TPU v7x, 32 devices: a whole 2x2x4 slice. The times are simulated.
32 devices in a mesh: seq: 8 (over z, x), exp: 4 (over y, core).
Axes of the slice: x: 2, y: 2, z: 4, core: 2. Of those that a mesh axis runs over, the one named last changes fastest.
Arguments:
- tokens: bfloat16 [8192, 2560], P(('seq', 'exp')), may hold values from -6 to 6
- routes: int32 [8192, 1], P(('seq', 'exp')), may hold values from 0 to 15; in each aligned block of 256 rows (0 to 255, 256 to 511, ...) at most 32 rows name the same one
- gate_inner_weight: bfloat16 [2560, 2, 3072], P(None, None, 'exp'), may hold values from -0.125 to 0.125
- state_map_weight: bfloat16 [2560, 256], replicated, may hold values from -0.125 to 0.125
- step_size_weight: bfloat16 [2560, 48], P(None, 'exp'), may hold values from -0.125 to 0.125
- adapter_down_weight: bfloat16 [2560, 128], P(None, 'exp'), may hold values from -0.125 to 0.125
- adapter_up_weight: bfloat16 [128, 2, 3072], P(None, None, 'exp'), may hold values from -1.5 to 1.5
- inner_conv_taps: float32 [4, 3072], P(None, 'exp'), may hold values from -3 to 3
- state_map_taps: float32 [4, 256], replicated, may hold values from -3 to 3
- inner_conv_bias: float32 [3072], P('exp'), may hold values from -3 to 3
- state_map_conv_bias: float32 [256], replicated, may hold values from -3 to 3
- step_size_bias: float32 [48], P('exp'), may hold values from -6 to -3
- head_decay_rate: float32 [48], P('exp'), may hold values from 7.4505806e-05 to 8
- direct_head_scale: float32 [48], P('exp'), may hold values from 0.5 to 2
- gated_norm_scale: float32 [3072], P('exp'), may hold values from 0.5 to 1.5
Outputs:
- mixed: bfloat16 [8192, 3072], P('seq', 'exp')
Inputs may be any that keep to these rules, and one draw needn't show every extreme that they name: `routes`: among the rows of one device no expert is named more than 32 times.
All inputs are finite; a program needn't handle non-finite values.
Results may differ from a plain program's by a relative error of at most 0.0034.
Values may be sent and summed in bfloat16 or wider, within the bound.
No kernel may reach another device: no remote copies, remote signals or barrier semaphores. Data moves between devices by JAX's collectives and lax.ppermute only.
A program may use at most 64 MiB of HBM per device.

v0:
```python
import functools

import jax
import jax.numpy as jnp
from jax import lax
from jax.experimental import pallas as pl
from jax.experimental.pallas import tpu as pltpu
from jax.sharding import PartitionSpec as P


STATE = 128
HEADDIM = 64
CHUNK = 128
LANES = 128
F32 = jnp.float32
BF16 = jnp.bfloat16


def swap(block, axis, mask):
    return lax.ppermute(block, axis, [(i, i ^ mask) for i in range(lax.axis_size(axis))])


def split3(value):
    hi = value.astype(BF16)
    rest = value - hi.astype(F32)
    mid = rest.astype(BF16)
    lo = (rest - mid.astype(F32)).astype(BF16)
    return hi, mid, lo


def split2(value):
    hi = value.astype(BF16)
    return hi, (value - hi.astype(F32)).astype(BF16)


def mm(a, b):
    return jnp.dot(a, b, preferred_element_type=F32)


def mm_nt(a, b):
    return lax.dot_general(a, b, (((1,), (1,)), ((), ())), preferred_element_type=F32)


def silu(v):
    return v / (1.0 + jnp.exp(-v))


def route_mask(e, route_row, experts_dev, rank):
    column = lax.broadcasted_iota(jnp.int32, (LANES, route_row.shape[1]), 0)
    per_dev = experts_dev * rank
    expert = ((column // per_dev) ^ e) * experts_dev + (column % per_dev) // rank
    return jnp.where(expert.astype(F32) == route_row, 1.0, 0.0)


def once(shape, const):
    return pl.BlockSpec(shape, const, pipeline_mode=pl.Buffered(1))


def up_specs(up, devices, tn, column):
    cols = up.shape[0] // devices
    return [
        pl.BlockSpec((cols, tn), lambda t, i, r=r: (i[0] ^ r, column(t))) for r in range(devices)
    ]


def project_kernel(cfg, index_ref, *refs):
    counts, route_from, devices, cols, rank, inner_tiles, aliased, pair = cfg
    x_refs, refs = refs[: len(counts)], refs[len(counts):]
    d_refs, refs = refs[:devices], refs[devices:]
    dt_ref, w_ref, wbc_ref = refs[:3]
    up_refs, refs = refs[3 : 3 + devices], refs[3 + devices:]
    z_ref, dto_ref, lift_ref, tail_ref, x_scr, w_scr = refs[aliased:]
    tile = pl.program_id(0)
    e = index_ref[0]

    @pl.when(tile == 0)
    def _():
        at = 0
        for x_ref, n in zip(x_refs, counts):
            x_scr[at : at + n, :] = x_ref[...]
            at += n
        w_scr[LANES:, :] = jnp.zeros((w_scr.shape[0] - LANES, w_scr.shape[1]), BF16)
        w_scr[LANES : LANES + dt_ref.shape[0], :] = dt_ref[...]
        for r in range(devices):
            w_scr[r * cols : (r + 1) * cols, :] = d_refs[r][0:cols, :]
        small = mm_nt(x_scr[...], w_scr[...])
        masks = []
        for r, first, n in route_from:
            for lane in range(first, first + n, LANES):
                row = d_refs[r][cols : cols + 1, lane : lane + LANES].astype(F32)
                masks.append(route_mask(e, row, cols // rank, rank).T)
        mask = jnp.concatenate(masks, axis=0)
        lift_ref[...] = jnp.where(mask > 0.5, small[:, :LANES], 0.0).astype(BF16)
        pad = jnp.zeros((small.shape[0], 2 * LANES - small.shape[1]), F32)
        dto_ref[...] = jnp.concatenate([small[:, LANES:], pad], axis=1)

    @pl.when(tile < inner_tiles)
    def _():
        up = jnp.concatenate([r[...] for r in up_refs], axis=0)
        z_ref[...] = mm(x_scr[...], w_ref[...]) + mm(lift_ref[...], up)

    @pl.when(tile >= inner_tiles)
    def _():
        z_ref[...] = mm(x_scr[...], wbc_ref[...])

    half = counts[0]
    start = ((devices - 1) ^ e) % 2 * half + half - 8
    tail = z_ref[pl.ds(pl.multiple_of(start, 8), 8), :]
    if aliased == 4:
        old_ref = refs[3]
        tail = jnp.where(((devices - 1) ^ e) // 2 == pair, tail, old_ref[...])
    tail_ref[...] = tail


def project(index, xs, route_from, downs, dt_t, wz, wbc, up, rank, total, row_block, buffers, tail, pair):
    counts = tuple(x.shape[0] for x in xs)
    rows = sum(counts)
    features = wz.shape[0]
    inner = up.shape[1] // 2
    width = inner + wbc.shape[1]
    tn = 256 if inner % 256 == 0 and width % 256 == 0 else 128
    inner_tiles = inner // tn
    devices = len(downs)
    const = lambda t, i: (0, 0)
    in_specs = (
        [once(x.shape, const) for x in xs]
        + [once(d.shape, const) for d in downs]
        + [
            once(dt_t.shape, const),
            pl.BlockSpec((features, tn), lambda t, i: (0, inner_tiles + jnp.minimum(t, inner_tiles - 1))),
            pl.BlockSpec((features, tn), lambda t, i: (0, jnp.maximum(t - inner_tiles, 0))),
        ]
        + up_specs(up, devices, tn, lambda t: inner_tiles + jnp.minimum(t, inner_tiles - 1))
    )
    args = list(xs) + list(downs) + [dt_t, wz, wbc] + [up] * devices
    aliases = {}
    if buffers is not None:
        for n, buffer in enumerate(buffers):
            aliases[1 + len(args)] = n
            args.append(buffer)
            in_specs.append(pl.BlockSpec(memory_space=pl.ANY))
    extra = len(aliases)
    if tail is not None:
        args.append(tail)
        in_specs.append(pl.BlockSpec((8, tn), lambda t, i: (0, t)))
        extra += 1
    cfg = (counts, route_from, devices, LANES // devices, rank, inner_tiles, extra, pair)
    return pl.pallas_call(
        functools.partial(project_kernel, cfg),
        out_shape=(
            jax.ShapeDtypeStruct((total, width), F32),
            jax.ShapeDtypeStruct((total, LANES), F32),
            jax.ShapeDtypeStruct((total, LANES), BF16),
            jax.ShapeDtypeStruct((8, width), F32),
        ),
        grid_spec=pltpu.PrefetchScalarGridSpec(
            num_scalar_prefetch=1,
            grid=(width // tn,),
            in_specs=in_specs,
            out_specs=(
                pl.BlockSpec((rows, tn), lambda t, i: (row_block, t)),
                pl.BlockSpec((rows, LANES), lambda t, i: (row_block, 0)),
                pl.BlockSpec((rows, LANES), lambda t, i: (row_block, 0)),
                pl.BlockSpec((8, tn), lambda t, i: (0, t)),
            ),
            scratch_shapes=[
                pltpu.VMEM((rows, features), BF16),
                pltpu.VMEM((LANES + 16, features), BF16),
            ],
        ),
        input_output_aliases=aliases,
        cost_estimate=pl.CostEstimate(
            flops=2 * rows * features * (width + 256),
            transcendentals=0,
            bytes_accessed=2 * features * (width + rows) + 4 * rows * width,
        ),
        compiler_params=pltpu.CompilerParams(
            dimension_semantics=("arbitrary",), vmem_limit_bytes=16 << 20
        ),
        name="project",
    )(index, *args)


def gate_kernel(counts, devices, index_ref, *refs):
    x_refs, refs = refs[: len(counts)], refs[len(counts):]
    lift_ref, w_ref = refs[:2]
    up_refs = refs[2 : 2 + devices]
    g_ref, x_scr = refs[-2:]

    @pl.when(pl.program_id(0) == 0)
    def _():
        at = 0
        for x_ref, n in zip(x_refs, counts):
            x_scr[at : at + n, :] = x_ref[...]
            at += n

    up = jnp.concatenate([r[...] for r in up_refs], axis=0)
    g_ref[...] = mm(x_scr[...], w_ref[...]) + mm(lift_ref[...], up)


def gate_project(index, xs, lift, wz, up, devices, total, row_block, buffer):
    counts = tuple(x.shape[0] for x in xs)
    rows = sum(counts)
    features = wz.shape[0]
    width = up.shape[1] // 2
    tn = 256 if width % 256 == 0 else 128
    const = lambda t, i: (0, 0)
    in_specs = [once(x.shape, const) for x in xs] + [
        pl.BlockSpec((rows, lift.shape[1]), lambda t, i: (row_block, 0), pipeline_mode=pl.Buffered(1)),
        pl.BlockSpec((features, tn), lambda t, i: (0, t)),
    ]
    in_specs += up_specs(up, devices, tn, lambda t: t)
    args = list(xs) + [lift, wz] + [up] * devices
    aliases = {}
    if buffer is not None:
        aliases[1 + len(args)] = 0
        args.append(buffer)
        in_specs.append(pl.BlockSpec(memory_space=pl.ANY))
    return pl.pallas_call(
        functools.partial(gate_kernel, counts, devices),
        out_shape=jax.ShapeDtypeStruct((total, width), F32),
        grid_spec=pltpu.PrefetchScalarGridSpec(
            num_scalar_prefetch=1,
            grid=(width // tn,),
            in_specs=in_specs,
            out_specs=pl.BlockSpec((rows, tn), lambda t, i: (row_block, t)),
            scratch_shapes=[pltpu.VMEM((rows, features), BF16)],
        ),
        input_output_aliases=aliases,
        cost_estimate=pl.CostEstimate(
            flops=2 * rows * features * width,
            transcendentals=0,
            bytes_accessed=2 * features * (width + rows) + 4 * rows * width,
        ),
        compiler_params=pltpu.CompilerParams(
            dimension_semantics=("arbitrary",), vmem_limit_bytes=12 << 20
        ),
        name="gate_project",
    )(index, *args)


def spread(value, width):
    rows = value.shape[0]
    left = lax.broadcasted_iota(jnp.int32, (rows, LANES), 1) < HEADDIM
    parts = []
    for p in range(width // LANES):
        a = jnp.broadcast_to(value[:, 2 * p : 2 * p + 1], (rows, LANES))
        b = jnp.broadcast_to(value[:, 2 * p + 1 : 2 * p + 2], (rows, LANES))
        parts.append(jnp.where(left, a, b))
    return jnp.concatenate(parts, axis=1)


def pad_lanes(row):
    return jnp.concatenate([row, jnp.zeros((1, LANES - row.shape[1]), F32)], axis=1)


def state_kernel(
    width, index_ref, z_ref, d_ref, rim_ref, taps_ref, mtaps_ref, bias_ref, mbias_ref, dtb_ref, rate_ref,
    xc_ref, cum_ref, step_ref, before_ref, local_ref, final_ref, log_ref, send_ref, prefix_ref, plog_ref,
    ext, state, offset,
):
    c = pl.program_id(0)

    @pl.when(c == 0)
    def _():
        ext[0:8, :] = jnp.where(index_ref[1] == 0, 0.0, rim_ref[...])
        state[...] = jnp.zeros_like(state)
        offset[...] = jnp.zeros_like(offset)

    ext[8 : 8 + CHUNK, :] = z_ref[...]
    taps = taps_ref.shape[0]
    outs = []
    for tr, br, lanes in (
        (taps_ref, bias_ref, slice(0, width)),
        (mtaps_ref, mbias_ref, slice(width, width + 2 * STATE)),
    ):
        acc = br[...] + tr[taps - 1 : taps, :] * ext[8 : 8 + CHUNK, lanes]
        for k in range(taps - 1):
            start = 8 - (taps - 1) + k
            acc = acc + tr[k : k + 1, :] * ext[start : start + CHUNK, lanes]
        out = silu(acc)
        xc_ref[:, lanes] = out
        outs.append(out)
    x, maps = outs
    ext[0:8, :] = ext[CHUNK : CHUNK + 8, :]

    raw = d_ref[...] + pad_lanes(dtb_ref[...])
    step = jnp.maximum(raw, 0.0) + jnp.log1p(jnp.exp(-jnp.abs(raw)))
    decay = -pad_lanes(rate_ref[...]) * step
    rows = lax.broadcasted_iota(jnp.int32, (CHUNK, CHUNK), 0)
    cols = lax.broadcasted_iota(jnp.int32, (CHUNK, CHUNK), 1)
    lower = jnp.where(rows >= cols, 1.0, 0.0).astype(BF16)
    sums = mm(lower, jnp.concatenate(split3(decay), axis=1))
    cum = sums[:, :LANES] + sums[:, LANES : 2 * LANES] + sums[:, 2 * LANES :]
    total = cum[CHUNK - 1 : CHUNK, :]
    before = offset[0:1, :]
    cum_ref[...] = cum
    step_ref[...] = step
    before_ref[0] = offset[...]
    after = jnp.broadcast_to(before + total, offset.shape)
    offset[...] = after

    xs = (spread(jnp.exp(total - cum) * step, width) * x).astype(BF16)
    b_hi, b_lo = split2(maps[:, :STATE].T)
    update = mm(jnp.concatenate([b_hi, b_lo], axis=1), jnp.concatenate([xs, xs], axis=0))
    old = state[...]
    local_ref[0] = old.astype(BF16)
    new = spread(jnp.broadcast_to(jnp.exp(total), (8, LANES)), width)[0:1, :] * old + update
    state[...] = new

    @pl.when(c == pl.num_programs(0) - 1)
    def _():
        final_ref[...] = new
        wide = spread(after, width)
        log_ref[...] = wide
        send_ref[0:STATE, :] = new.astype(BF16)
        send_ref[STATE : STATE + 8, :] = pack_logs(wide)
        prefix_ref[...] = jnp.zeros_like(new)
        plog_ref[...] = jnp.zeros_like(wide)


def piece_index(block, q, e, per):
    r = block ^ e
    far = 2 * per + ((r // 2 - 1) * per + q) * 2 + r % 2
    return jnp.where(r < 2, r * per + q, far)


def piece_map(per):
    def index(c, index_ref):
        return (piece_index(c // per, c % per, index_ref[0], per), 0)

    return index


def run_states(index, z, dt, rim, params, width, local):
    total, wide = z.shape
    chunks = total // CHUNK
    per = local // CHUNK
    const = lambda c, i: (0, 0)
    row = lambda c, i: (c, 0)
    deep = lambda c, i: (c, 0, 0)
    return pl.pallas_call(
        functools.partial(state_kernel, width),
        out_shape=(
            jax.ShapeDtypeStruct((total, wide), F32),
            jax.ShapeDtypeStruct((total, LANES), F32),
            jax.ShapeDtypeStruct((total, LANES), F32),
            jax.ShapeDtypeStruct((chunks, 8, LANES), F32),
            jax.ShapeDtypeStruct((chunks, STATE, width), BF16),
            jax.ShapeDtypeStruct((STATE, width), F32),
            jax.ShapeDtypeStruct((8, width), F32),
            jax.ShapeDtypeStruct((STATE + 8, width), BF16),
            jax.ShapeDtypeStruct((STATE, width), F32),
            jax.ShapeDtypeStruct((8, width), F32),
        ),
        grid_spec=pltpu.PrefetchScalarGridSpec(
            num_scalar_prefetch=1,
            grid=(chunks,),
            in_specs=[
                pl.BlockSpec((CHUNK, wide), piece_map(per)),
                pl.BlockSpec((CHUNK, LANES), piece_map(per)),
                pl.BlockSpec(rim.shape, const),
            ]
            + [pl.BlockSpec(p.shape, const) for p in params],
            out_specs=(
                pl.BlockSpec((CHUNK, wide), row),
                pl.BlockSpec((CHUNK, LANES), row),
                pl.BlockSpec((CHUNK, LANES), row),
                pl.BlockSpec((1, 8, LANES), deep),
                pl.BlockSpec((1, STATE, width), deep),
                pl.BlockSpec((STATE, width), const),
                pl.BlockSpec((8, width), const),
                pl.BlockSpec((STATE + 8, width), const),
                pl.BlockSpec((STATE, width), const),
                pl.BlockSpec((8, width), const),
            ),
            scratch_shapes=[
                pltpu.VMEM((CHUNK + 8, wide), F32),
                pltpu.VMEM((STATE, width), F32),
                pltpu.VMEM((8, LANES), F32),
            ],
        ),
        cost_estimate=pl.CostEstimate(
            flops=2 * total * width * 1000, transcendentals=total * wide, bytes_accessed=12 * total * wide
        ),
        compiler_params=pltpu.CompilerParams(
            dimension_semantics=("arbitrary",), vmem_limit_bytes=12 << 20
        ),
        name="run_states",
    )(index, z, dt, rim, *params)


def output_kernel(
    width, index_ref, xc_ref, cum_ref, step_ref, before_ref, local_ref, g_ref, direct_ref,
    a_ref, b_ref, c_ref,
):
    bmap = xc_ref[:, width : width + STATE]
    cmap = xc_ref[:, width + STATE :]
    cum = cum_ref[...]
    b_hi, b_lo = split2(bmap)
    c_hi, c_lo = split2(cmap)
    c_ref[...] = c_hi
    gram = mm_nt(jnp.concatenate([c_hi, c_lo], axis=1), jnp.concatenate([b_hi, b_hi], axis=1))
    gram = gram + mm_nt(c_hi, b_lo)
    cum_t = cum.T
    step_t = step_ref[...].T
    rows = lax.broadcasted_iota(jnp.int32, (CHUNK, CHUNK), 0)
    cols = lax.broadcasted_iota(jnp.int32, (CHUNK, CHUNK), 1)
    causal = rows >= cols
    left = cols < HEADDIM
    direct = pad_lanes(direct_ref[...])
    for p in range(width // LANES):
        lanes = slice(p * LANES, (p + 1) * LANES)
        ws, cs = [], []
        for h in (2 * p, 2 * p + 1):
            column = jnp.broadcast_to(cum[:, h : h + 1], (CHUNK, CHUNK))
            differ = jnp.where(causal, column - cum_t[h : h + 1, :], -jnp.inf)
            ws.append((jnp.exp(differ) * (gram * step_t[h : h + 1, :])).astype(BF16))
            cs.append(column)
        x = xc_ref[:, lanes]
        xb = jnp.concatenate([jnp.where(left, x, 0.0), jnp.where(left, 0.0, x)], axis=0)
        both = lambda v: jnp.where(
            left[0:1, :],
            jnp.broadcast_to(v[:, 2 * p : 2 * p + 1], (1, LANES)),
            jnp.broadcast_to(v[:, 2 * p + 1 : 2 * p + 2], (1, LANES)),
        )
        inside = mm(jnp.concatenate(ws, axis=1), xb.astype(BF16))
        fade = jnp.exp(jnp.where(left, cs[0], cs[1]))
        y = inside + fade * mm(c_hi, local_ref[0, :, lanes]) + both(direct) * x
        gate = silu(g_ref[:, lanes])
        a_ref[:, lanes] = y * gate
        b_ref[:, lanes] = fade * jnp.exp(both(before_ref[0, 0:1, :])) * gate


def run_outputs(index, xc, cum, step, before, local_states, gate, direct, local):
    total, wide = xc.shape
    width = gate.shape[1]
    chunks = total // CHUNK
    per = local // CHUNK
    const = lambda c, i: (0, 0)
    row = lambda c, i: (c, 0)
    deep = lambda c, i: (c, 0, 0)
    return pl.pallas_call(
        functools.partial(output_kernel, width),
        out_shape=(
            jax.ShapeDtypeStruct((total, width), F32),
            jax.ShapeDtypeStruct((total, width), F32),
            jax.ShapeDtypeStruct((total, STATE), BF16),
        ),
        grid_spec=pltpu.PrefetchScalarGridSpec(
            num_scalar_prefetch=1,
            grid=(chunks,),
            in_specs=[
                pl.BlockSpec((CHUNK, wide), row),
                pl.BlockSpec((CHUNK, LANES), row),
                pl.BlockSpec((CHUNK, LANES), row),
                pl.BlockSpec((1, 8, LANES), deep),
                pl.BlockSpec((1, STATE, width), deep),
                pl.BlockSpec((CHUNK, width), piece_map(per)),
                pl.BlockSpec(direct.shape, const),
            ],
            out_specs=(
                pl.BlockSpec((CHUNK, width), row),
                pl.BlockSpec((CHUNK, width), row),
                pl.BlockSpec((CHUNK, STATE), row),
            ),
        ),
        cost_estimate=pl.CostEstimate(
            flops=2 * total * width * 1500, transcendentals=total * width * 4, bytes_accessed=16 * total * width
        ),
        compiler_params=pltpu.CompilerParams(
            dimension_semantics=("arbitrary",), vmem_limit_bytes=12 << 20
        ),
        name="run_outputs",
    )(index, xc, cum, step, before, local_states, gate, direct)


def pack_logs(wide):
    hi, mid, lo = split3(wide)
    row = lax.broadcasted_iota(jnp.int32, wide.shape, 0)
    lo = jnp.where(row == 2, lo.astype(F32), 0.0)
    return jnp.where(row == 0, hi.astype(F32), jnp.where(row == 1, mid.astype(F32), lo)).astype(BF16)


def unpack(got_ref):
    other = got_ref[0:STATE, :].astype(F32)
    logs = got_ref[STATE : STATE + 8, :].astype(F32)
    log = logs[0:1, :] + logs[1:2, :] + logs[2:3, :]
    return other, log


def combine_kernel(
    d, index_ref, got_ref, group_ref, glog_ref, prefix_ref, plog_ref,
    send_ref, group_out, glog_out, prefix_out, plog_out,
):
    upper = (index_ref[1] & d) != 0
    other, other_log = unpack(got_ref)
    group, group_log = group_ref[...], glog_ref[0:1, :]
    prefix, prefix_log = prefix_ref[...], plog_ref[0:1, :]
    prefix_out[...] = jnp.where(upper, prefix + jnp.exp(prefix_log) * other, prefix)
    new_plog = jnp.where(upper, prefix_log + other_log, prefix_log)
    plog_out[...] = jnp.broadcast_to(new_plog, plog_out.shape)
    late = jnp.where(upper, group, other)
    early = jnp.where(upper, other, group)
    late_log = jnp.where(upper, group_log, other_log)
    new = late + jnp.exp(late_log) * early
    new_log = jnp.broadcast_to(group_log + other_log, glog_out.shape)
    group_out[...] = new
    glog_out[...] = new_log
    send_ref[0:STATE, :] = new.astype(BF16)
    send_ref[STATE : STATE + 8, :] = pack_logs(new_log)


def combine(index, d, got, group, glog, prefix, plog):
    state = jax.ShapeDtypeStruct(group.shape, F32)
    log = jax.ShapeDtypeStruct(glog.shape, F32)
    full = lambda x: pl.BlockSpec(x.shape, lambda i, s: (0, 0))
    outs = (jax.ShapeDtypeStruct(got.shape, BF16), state, log, state, log)
    return pl.pallas_call(
        functools.partial(combine_kernel, d),
        out_shape=outs,
        grid_spec=pltpu.PrefetchScalarGridSpec(
            num_scalar_prefetch=1,
            grid=(1,),
            in_specs=[full(x) for x in (got, group, glog, prefix, plog)],
            out_specs=tuple(full(x) for x in outs),
        ),
        compiler_params=pltpu.CompilerParams(vmem_limit_bytes=8 << 20),
        name="combine",
    )(index, got, group, glog, prefix, plog)


def join_kernel(d, index_ref, a_ref, b_ref, c_ref, got_ref, prefix_ref, plog_ref, o_ref, ss_ref, s_scr):
    @pl.when(pl.program_id(0) == 0)
    def _():
        other, _ = unpack(got_ref)
        prefix = prefix_ref[...]
        upper = (index_ref[1] & d) != 0
        entering = jnp.where(upper, prefix + jnp.exp(plog_ref[0:1, :]) * other, prefix)
        s_scr[...] = entering.astype(BF16)

    gated = a_ref[...] + b_ref[...] * mm(c_ref[...], s_scr[...])
    o_ref[...] = gated
    hi, lo = split2(gated * gated)
    ones = jnp.ones((8, 2 * hi.shape[1]), BF16)
    ss_ref[...] = mm_nt(ones, jnp.concatenate([hi, lo], axis=1))[0:1]


def join(index, d, a, b, c, got, prefix, plog):
    total, width = a.shape
    rows = 256
    row = lambda i, s: (i, 0)
    full = lambda x: pl.BlockSpec(x.shape, lambda i, s: (0, 0))
    return pl.pallas_call(
        functools.partial(join_kernel, d),
        out_shape=(jax.ShapeDtypeStruct((total, width), F32), jax.ShapeDtypeStruct((1, total), F32)),
        grid_spec=pltpu.PrefetchScalarGridSpec(
            num_scalar_prefetch=1,
            grid=(total // rows,),
            in_specs=[
                pl.BlockSpec((rows, width), row),
                pl.BlockSpec((rows, width), row),
                pl.BlockSpec((rows, STATE), row),
                full(got),
                full(prefix),
                full(plog),
            ],
            out_specs=(
                pl.BlockSpec((rows, width), row),
                pl.BlockSpec((1, rows), lambda i, s: (0, i)),
            ),
            scratch_shapes=[pltpu.VMEM((STATE, width), BF16)],
        ),
        compiler_params=pltpu.CompilerParams(
            dimension_semantics=("arbitrary",), vmem_limit_bytes=10 << 20
        ),
        name="join",
    )(index, a, b, c, got, prefix, plog)


def norm_kernel(inner_width, g_ref, mine_ref, other_ref, gain_ref, o_ref):
    scale = lax.rsqrt((mine_ref[...] + other_ref[...]) / inner_width + 1e-05)
    width = g_ref.shape[1]
    for part in range(g_ref.shape[0] // LANES):
        rows = slice(part * LANES, (part + 1) * LANES)
        column = jnp.broadcast_to(scale[:, rows], (LANES, LANES)).T
        for lane in range(width // LANES):
            lanes = slice(lane * LANES, (lane + 1) * LANES)
            o_ref[rows, lanes] = (g_ref[rows, lanes] * column * gain_ref[:, lanes]).astype(BF16)


def norm(gated, mine, other, gain, inner_width):
    total, width = gated.shape
    rows = 256
    return pl.pallas_call(
        functools.partial(norm_kernel, inner_width),
        out_shape=jax.ShapeDtypeStruct((total, width), BF16),
        grid=(total // rows,),
        in_specs=[
            pl.BlockSpec((rows, width), lambda i: (i, 0)),
            pl.BlockSpec((1, rows), lambda i: (0, i)),
            pl.BlockSpec((1, rows), lambda i: (0, i)),
            pl.BlockSpec(gain.shape, lambda i: (0, 0)),
        ],
        out_specs=pl.BlockSpec((rows, width), lambda i: (i, 0)),
        compiler_params=pltpu.CompilerParams(
            dimension_semantics=("arbitrary",), vmem_limit_bytes=8 << 20
        ),
        name="norm",
    )(gated, mine, other, gain)


def body(
    tokens,
    routes,
    gate_inner_weight,
    state_map_weight,
    step_size_weight,
    adapter_down_weight,
    adapter_up_weight,
    inner_conv_taps,
    state_map_taps,
    inner_conv_bias,
    state_map_conv_bias,
    step_size_bias,
    head_decay_rate,
    direct_head_scale,
    gated_norm_scale,
):
    n = lax.axis_size("exp")
    shards = lax.axis_size("seq")
    local, features = tokens.shape
    total = local * n
    width = gate_inner_weight.shape[2]
    experts = adapter_up_weight.shape[0]
    rank = 8
    e = lax.axis_index("exp")
    index = jnp.stack([e, lax.axis_index("seq")]).astype(jnp.int32)
    per = local // CHUNK

    route_row = jnp.pad(routes.reshape(1, local).astype(BF16), ((0, 0), (0, features - local)))
    down = {0: jnp.concatenate([adapter_down_weight.T, route_row], axis=0)}
    far = {}
    for k in range(2, n, 2):
        down[k] = swap(down[0], "exp", k)
    for k in range(2, n, 2):
        for q in reversed(range(per)):
            far[k, q] = swap(tokens[q * CHUNK : (q + 1) * CHUNK], "exp", k)
    sibling = swap(tokens, "exp", 1)
    for k in range(0, n, 2):
        down[k + 1] = swap(down[k], "exp", 1)
    downs = [down[k] for k in range(n)]
    wz = gate_inner_weight.reshape(features, 2 * width)
    up = adapter_up_weight.reshape(experts, 2 * width)
    call = functools.partial(
        project, index, downs=downs, dt_t=step_size_weight.T, wz=wz, wbc=state_map_weight,
        up=up, rank=rank, total=total,
    )
    *buffers, tail = call(
        [tokens, sibling], route_from=((0, 0, local), (1, 0, local)), row_block=0, buffers=None,
        tail=None, pair=0,
    )
    gate = gate_project(index, [tokens, sibling], buffers[2], wz, up, n, total, 0, None)
    far_rows = {}
    for k in range(2, n, 2):
        for q in reversed(range(per)):
            mine = far[k, q]
            other = swap(mine, "exp", 1)
            block = per + (k // 2 - 1) * per + q
            *buffers, new_tail = call(
                [mine, other],
                route_from=((k, q * CHUNK, CHUNK), (k + 1, q * CHUNK, CHUNK)),
                row_block=block,
                buffers=buffers,
                tail=tail if q == per - 1 else None,
                pair=k // 2,
            )
            if q == per - 1:
                tail = new_tail
            far_rows[k, q] = (mine, other)
        if k == n - 2:
            rim = lax.ppermute(tail, "seq", [(i, (i + 1) % shards) for i in range(shards)])
    z, dt, lift = buffers

    params = [
        inner_conv_taps, state_map_taps, inner_conv_bias[None, :], state_map_conv_bias[None, :],
        step_size_bias[None, :], head_decay_rate[None, :],
    ]
    xc, cum, step, before, states, group, glog, send, prefix, plog = run_states(
        index, z, dt, rim, params, width, local
    )
    d = 1
    while True:
        got = swap(send, "seq", d)
        if 2 * d >= shards:
            break
        send, group, glog, prefix, plog = combine(index, d, got, group, glog, prefix, plog)
        d *= 2
    for k in range(2, n, 2):
        xs = []
        for q in range(per):
            xs.extend(far_rows[k, q])
        gate = gate_project(index, xs, lift, wz, up, n, total, k // 2, gate)
    a, b, c = run_outputs(
        index, xc, cum, step, before, states, gate, direct_head_scale[None, :], local
    )
    gated, mine = join(index, d, a, b, c, got, prefix, plog)
    d = 1
    while 2 * d < n:
        mine = mine + swap(mine, "exp", d)
        d *= 2
    return norm(gated, mine, swap(mine, "exp", d), gated_norm_scale[None, :], width * n)


def solution(mesh):
    in_specs = (
        P(("seq", "exp"), None),
        P(("seq", "exp"), None),
        P(None, None, "exp"),
        P(),
        P(None, "exp"),
        P(None, "exp"),
        P(None, None, "exp"),
        P(None, "exp"),
        P(),
        P("exp"),
        P(),
        P("exp"),
        P("exp"),
        P("exp"),
        P("exp"),
    )
    out_specs = P("seq", "exp")

    return jax.shard_map(body, mesh=mesh, in_specs=in_specs, out_specs=out_specs, check_vma=False)
```

profile of v0, /device:TPU:0, one launch (start us, length us, event | category | flops | bytes accessed | tf_op | source)
XLA Modules:
  0.0 117.5 jit_solution(9950939594613288704)
XLA Ops:
  0.0 0.5 collective-permute-start.7
  0.5 2.2 %fusion.2 = (bf16[128,2560]{1,0:T(8,128)(2,1)S(1)}, bf16[128,2560]{1,0:T(8,128)(2,1)}) fusion(bf16[256,2560]{1,0:T(8,128)(2,1)} %refs_0_.3), kind=kLoop, calls=%fused_computation.5 | loop fusion | bytes 2621440 | tf_op jit(solution)/shard_map/slice | solution.py:648
  2.7 2.6 %collective-permute-start.5 = (bf16[128,2560]{1,0:T(8,128)(2,1)S(1)}, bf16[128,2560]{1,0:T(8,128)(2,1)}, u32[]{:S(2)}, u32[]{:S(2)}) collective-permute-start(bf16[128,2560]{1,0:T(8,128)(2,1)S(1)} %get-tuple-element.73), channel_id=1, source_target_pairs={{0,2},{1,3},{2,0},{3,1},{4,6},{5,7},{6,4},{7,5},{8,10},{9,11},{10,... | collective-permute-start | bytes 1966088 | tf_op jit(solution)/shard_map/ppermute | solution.py:20
  5.3 0.0 collective-permute-start
  5.3 0.7 convert_bitcast_fusion
  6.0 0.9 fusion.1.refs_2_
  6.9 2.1 %collective-permute-start.3 = (bf16[33,2560]{1,0:T(8,128)(2,1)S(1)}, bf16[33,2560]{1,0:T(8,128)(2,1)}, u32[]{:S(2)}, u32[]{:S(2)}) collective-permute-start(bf16[33,2560]{1,0:T(8,128)(2,1)S(1)} %fusion.1.refs_2_), channel_id=1, source_target_pairs={{0,2},{1,3},{2,0},{3,1},{4,6},{5,7},{6,4},{7,5},{8,10},{9,11},{10,... | collective-permute-start | bytes 506888 | tf_op jit(solution)/shard_map/ppermute | solution.py:20
  9.0 0.0 collective-permute-start.2
  9.0 30.2 %collective-permute-done.3.refs_4_ = bf16[33,2560]{1,0:T(8,128)(2,1)} collective-permute-done((bf16[33,2560]{1,0:T(8,128)(2,1)S(1)}, bf16[33,2560]{1,0:T(8,128)(2,1)}, u32[]{:S(2)}, u32[]{:S(2)}) %collective-permute-start.3) | collective-permute-done | bytes 168992 | tf_op jit(solution)/shard_map/ppermute | solution.py:20
  39.1 0.0 collective-permute-start.4
  39.1 0.0 collective-permute-done.5.refs_0_.refs_2_
  39.2 0.5 collective-permute-start.6
  39.7 0.7 broadcast_in_dim.18.bias_ref
  40.4 0.0 copy-start
  40.4 0.0 copy-start.2
  40.4 4.7 %copy.23 = bf16[320,8,2,768]{3,1,2,0:T(8,128)(2,1)S(1)} copy(bf16[320,8,2,768]{3,2,1,0:T(2,128)(2,1)} %bitcast.46) | data formatting | bytes 15728640
  45.1 0.1 pad_add_fusion.index_ref
  45.2 0.0 collective-permute-start.1
  45.2 0.0 collective-permute-done.2.refs_3_
  45.2 0.0 collective-permute-done.4.refs_5_
  45.3 0.0 copy-start.1
  45.3 1.3 %copy-done.1 = bf16[256,2560]{1,0:T(8,128)(2,1)S(1)} copy-done((bf16[256,2560]{1,0:T(8,128)(2,1)S(1)}, bf16[256,2560]{1,0:T(8,128)(2,1)}, u32[]{:S(2)}) %copy-start.1) | copy-done | bytes 1310744
  46.6 7.2 %project.3 = (f32[1024,1024]{1,0:T(8,128)S(1)}, f32[1024,128]{1,0:T(8,128)S(1)}, bf16[1024,128]{1,0:T(8,128)(2,1)S(1)}, f32[8,1024]{1,0:T(8,128)S(1)}) custom-call(s32[2]{0:T(128)S(1)} %pad_add_fusion.index_ref, bf16[256,2560]{1,0:T(8,128)(2,1)S(1)} %copy-done.1, bf16[256,2560]{1,0:T(8,128)(2,1)} %collective-permute-done.7.refs_1_, ...), custom_call_target="tpu_custom_call" | custom-call | flops 3355443200 | bytes 9961472 | tf_op jit(solution)/shard_map/project/pallas_call | solution.py:148
  53.8 5.2 %gate_project.2.refs_10_ = f32[1024,768]{1,0:T(8,128)S(1)} custom-call(s32[2]{0:T(128)S(1)} %pad_add_fusion.index_ref, bf16[256,2560]{1,0:T(8,128)(2,1)S(1)} %copy-done.1, bf16[256,2560]{1,0:T(8,128)(2,1)} %collective-permute-done.7.refs_1_, bf16[1024,128]{1,0:T(8,128)(2,1)S(1)} %get-tuple-element.41.refs_15_.refs_2_, bf16[2560,1536]{1,0:T(8,128)(2,1)S(1)} %bitcast.15, ...), custom_call_target="tpu_custom_call" | custom-call | flops 2013265920 | bytes 8126464 | tf_op jit(solution)/shard_map/gate_project/pallas_call | solution.py:219
  59.0 0.0 collective-permute-done.6.refs_1_.refs_3_
  59.0 5.3 %project.4 = (f32[1024,1024]{1,0:T(8,128)S(1)}, f32[1024,128]{1,0:T(8,128)S(1)}, bf16[1024,128]{1,0:T(8,128)(2,1)S(1)}, f32[8,1024]{1,0:T(8,128)S(1)}) custom-call(s32[2]{0:T(128)S(1)} %pad_add_fusion.index_ref, bf16[128,2560]{1,0:T(8,128)(2,1)} %collective-permute-done.5.refs_0_.refs_2_, ...), custom_call_target="tpu_custom_call", output_to_operand_aliasing={{0}: (14, {}), {1}: (15, {}), {2}: (16, {})} | custom-call | flops 1677721600 | bytes 7602176 | tf_op jit(solution)/shard_map/project/pallas_call | solution.py:148
  64.3 1.8 %collective-permute-start.8 = (f32[8,1024]{1,0:T(8,128)S(1)}, f32[8,1024]{1,0:T(8,128)S(1)}, u32[]{:S(2)}, u32[]{:S(2)}) collective-permute-start(f32[8,1024]{1,0:T(8,128)S(1)} %get-tuple-element.48), channel_id=1, source_target_pairs={{0,4},{4,8},{8,12},{12,16},{16,20},{20,24},{24,28},{28,0},{1,5},{5... | collective-permute-start | bytes 98312 | tf_op jit(solution)/shard_map/ppermute | solution.py:682
  66.1 0.0 collective-permute-done.1.refs_1_
  66.1 0.0 copy-start.7
  66.1 0.0 copy-start.8
  66.2 5.8 %project.5 = (f32[1024,1024]{1,0:T(8,128)S(1)}, f32[1024,128]{1,0:T(8,128)S(1)}, bf16[1024,128]{1,0:T(8,128)(2,1)S(1)}, f32[8,1024]{1,0:T(8,128)}) custom-call(s32[2]{0:T(128)S(1)} %pad_add_fusion.index_ref, bf16[128,2560]{1,0:T(8,128)(2,1)} %collective-permute-done.refs_0_, ...), custom_call_target="tpu_custom_call", output_to_operand_aliasing={{0}: (14, {}), {1}: (15, {}), {2}: (16, {})} | custom-call | flops 1677721600 | bytes 7602176 | tf_op jit(solution)/shard_map/project/pallas_call | solution.py:148
  72.0 7.8 %run_states.1 = (f32[1024,1024]{1,0:T(8,128)S(1)}, f32[1024,128]{1,0:T(8,128)S(1)}, f32[1024,128]{1,0:T(8,128)S(1)}, f32[8,8,128]{2,1,0:T(8,128)S(1)}, bf16[8,12...) custom-call(s32[2]{0:T(128)S(1)} %pad_add_fusion.index_ref, ...), custom_call_target="tpu_custom_call" | custom-call | flops 1572864000 | bytes 12582912 | tf_op jit(solution)/shard_map/run_states/pallas_call | solution.py:342
  79.8 1.6 %collective-permute-start.9 = (bf16[136,768]{1,0:T(8,128)(2,1)S(1)}, bf16[136,768]{1,0:T(8,128)(2,1)S(1)}, u32[]{:S(2)}, u32[]{:S(2)}) collective-permute-start(bf16[136,768]{1,0:T(8,128)(2,1)S(1)} %get-tuple-element.58), channel_id=1, source_target_pairs={{0,4},{4,0},{8,12},{12,8},{16,20},{20,16},{24,28},{28,24},{1,5},{5... | collective-permute-start | bytes 626696 | tf_op jit(solution)/shard_map/ppermute | solution.py:20
  81.4 5.7 %collective-permute-done.9.got_ref = bf16[136,768]{1,0:T(8,128)(2,1)S(1)} collective-permute-done((bf16[136,768]{1,0:T(8,128)(2,1)S(1)}, bf16[136,768]{1,0:T(8,128)(2,1)S(1)}, u32[]{:S(2)}, u32[]{:S(2)}) %collective-permute-start.9) | collective-permute-done | bytes 208928 | tf_op jit(solution)/shard_map/ppermute | solution.py:20
  87.1 0.7 combine.2
  87.8 1.6 %collective-permute-start.10 = (bf16[136,768]{1,0:T(8,128)(2,1)S(1)}, bf16[136,768]{1,0:T(8,128)(2,1)S(1)}, u32[]{:S(2)}, u32[]{:S(2)}) collective-permute-start(bf16[136,768]{1,0:T(8,128)(2,1)S(1)} %get-tuple-element.63), channel_id=1, source_target_pairs={{0,8},{4,12},{8,0},{12,4},{16,24},{20,28},{24,16},{28,20},{1,9},{5... | collective-permute-start | bytes 626696 | tf_op jit(solution)/shard_map/ppermute | solution.py:20
  89.4 5.4 %gate_project.3.g_ref = f32[1024,768]{1,0:T(8,128)S(1)} custom-call(s32[2]{0:T(128)S(1)} %pad_add_fusion.index_ref, bf16[128,2560]{1,0:T(8,128)(2,1)} %collective-permute-done.refs_0_, bf16[128,2560]{1,0:T(8,128)(2,1)S(1)} %collective-permute-done.1.refs_1_, ...), custom_call_target="tpu_custom_call", output_to_operand_aliasing={{}: (11, {})} | custom-call | flops 2013265920 | bytes 8126464 | tf_op jit(solution)/shard_map/gate_project/pallas_call | solution.py:219
  94.8 0.0 collective-permute-done.10.got_ref
  94.8 1.4 %combine.3 = (bf16[136,768]{1,0:T(8,128)(2,1)S(1)}, f32[128,768]{1,0:T(8,128)}, f32[8,768]{1,0:T(8,128)}, f32[128,768]{1,0:T(8,128)S(1)}, f32[8,768]{1,0:T(8,128)S(1)}) custom-call(s32[2]{0:T(128)S(1)} %pad_add_fusion.index_ref, bf16[136,768]{1,0:T(8,128)(2,1)S(1)} %collective-permute-done.10.got_ref, f32[128,768]{1,0:T(8,128)S(1)} %get-tuple-element.64.group_ref, ...), custom_call_target="tpu_custom_call" | custom-call | tf_op jit(solution)/shard_map/combine/pallas_call | solution.py:519
  96.2 2.6 %collective-permute-start.11 = (bf16[136,768]{1,0:T(8,128)(2,1)S(1)}, bf16[136,768]{1,0:T(8,128)(2,1)S(1)}, u32[]{:S(2)}, u32[]{:S(2)}) collective-permute-start(bf16[136,768]{1,0:T(8,128)(2,1)S(1)} %get-tuple-element.68), channel_id=1, source_target_pairs={{0,16},{4,20},{8,24},{12,28},{16,0},{20,4},{24,8},{28,12},{1,17},{... | collective-permute-start | bytes 626696 | tf_op jit(solution)/shard_map/ppermute | solution.py:20
  98.8 5.5 %run_outputs.1 = (f32[1024,768]{1,0:T(8,128)S(1)}, f32[1024,768]{1,0:T(8,128)S(1)}, bf16[1024,128]{1,0:T(8,128)(2,1)S(1)}) custom-call(s32[2]{0:T(128)S(1)} %pad_add_fusion.index_ref, f32[1024,1024]{1,0:T(8,128)S(1)} %get-tuple-element.49.xc_ref, f32[1024,128]{1,0:T(8,128)S(1)} %get-tuple-element.50.cum_ref, f32[1024,128]{1,0:T(8,128)S(1)} %get-tuple-element.51.step_ref, ...), custom_call_target="tpu_custom_call" | custom-call | flops 2359296000 | bytes 12582912 | tf_op jit(solution)/shard_map/run_outputs/pallas_call | solution.py:443
  104.3 3.3 %collective-permute-done.11.got_ref = bf16[136,768]{1,0:T(8,128)(2,1)S(1)} collective-permute-done((bf16[136,768]{1,0:T(8,128)(2,1)S(1)}, bf16[136,768]{1,0:T(8,128)(2,1)S(1)}, u32[]{:S(2)}, u32[]{:S(2)}) %collective-permute-start.11) | collective-permute-done | bytes 208928 | tf_op jit(solution)/shard_map/ppermute | solution.py:20
  107.6 3.1 %join.1 = (f32[1024,768]{1,0:T(8,128)S(1)}, f32[1,1024]{1,0:T(1,128)S(1)}) custom-call(s32[2]{0:T(128)S(1)} %pad_add_fusion.index_ref, f32[1024,768]{1,0:T(8,128)S(1)} %get-tuple-element.55.a_ref, f32[1024,768]{1,0:T(8,128)S(1)} %get-tuple-element.56.b_ref, bf16[1024,128]{1,0:T(8,128)(2,1)S(1)} %get-tuple-element.57.c_ref, ...), custom_call_target="tpu_custom_call" | custom-call | tf_op jit(solution)/shard_map/join/pallas_call | solution.py:554
  110.7 0.0 collective-permute-start.12
  110.7 1.2 collective-permute-done.12
  111.9 1.5 %collective-permute-start.13 = (f32[1,1024]{1,0:T(1,128)S(1)}, f32[1,1024]{1,0:T(1,128)S(1)}, u32[]{:S(2)}, u32[]{:S(2)}) collective-permute-start(f32[1,1024]{1,0:T(1,128)S(1)} %add.5.mine_ref), channel_id=1, source_target_pairs={{0,2},{1,3},{2,0},{3,1},{4,6},{5,7},{6,4},{7,5},{8,10},{9,11},{10,... | collective-permute-start | bytes 12296 | tf_op jit(solution)/shard_map/ppermute | solution.py:20
  113.4 2.1 %collective-permute-done.13.other_ref = f32[1,1024]{1,0:T(1,128)S(1)} collective-permute-done((f32[1,1024]{1,0:T(1,128)S(1)}, f32[1,1024]{1,0:T(1,128)S(1)}, u32[]{:S(2)}, u32[]{:S(2)}) %collective-permute-start.13) | collective-permute-done | bytes 4128 | tf_op jit(solution)/shard_map/ppermute | solution.py:20
  115.5 2.0 %norm.1 = bf16[1024,768]{1,0:T(8,128)(2,1)} custom-call(f32[1024,768]{1,0:T(8,128)S(1)} %get-tuple-element.71.g_ref, f32[1,1024]{1,0:T(1,128)S(1)} %add.5.mine_ref, f32[1,1024]{1,0:T(1,128)S(1)} %collective-permute-done.13.other_ref, f32[1,768]{1,0:T(1,128)S(1)} %broadcast_in_dim.23.gain_ref), custom_call_target="tpu_custom_call" | custom-call | tf_op jit(solution)/shard_map/norm/pallas_call | solution.py:595
  (22 shorter events, 0.1 us)
Async XLA Ops:
  0.0 40.4 %copy-start.9 = (bf16[128,2,768]{2,1,0:T(2,128)(2,1)S(1)}, bf16[128,2,768]{2,1,0:T(2,128)(2,1)}, u32[]{:S(2)}) copy-start(bf16[128,2,768]{2,1,0:T(2,128)(2,1)} %param.21) | copy-start | bytes 1179652
  0.0 45.3 %collective-permute-start.7 = (bf16[256,2560]{1,0:T(8,128)(2,1)}, bf16[256,2560]{1,0:T(8,128)(2,1)}, u32[]{:S(2)}, u32[]{:S(2)}) collective-permute-start(bf16[256,2560]{1,0:T(8,128)(2,1)} %refs_0_.3), channel_id=1, source_target_pairs={{0,1},{1,0},{2,3},{3,2},{4,5},{5,4},{6,7},{7,6},{8,9},{9,8},{10,11... | collective-permute-start | bytes 3932168 | tf_op jit(solution)/shard_map/ppermute | solution.py:20
  2.7 36.5 %collective-permute-start.5 = (bf16[128,2560]{1,0:T(8,128)(2,1)S(1)}, bf16[128,2560]{1,0:T(8,128)(2,1)}, u32[]{:S(2)}, u32[]{:S(2)}) collective-permute-start(bf16[128,2560]{1,0:T(8,128)(2,1)S(1)} %get-tuple-element.73), channel_id=1, source_target_pairs={{0,2},{1,3},{2,0},{3,1},{4,6},{5,7},{6,4},{7,5},{8,10},{9,11},{10,... | collective-permute-start | bytes 1966088 | tf_op jit(solution)/shard_map/ppermute | solution.py:20
  5.3 39.9 %collective-permute-start = (bf16[128,2560]{1,0:T(8,128)(2,1)}, bf16[128,2560]{1,0:T(8,128)(2,1)}, u32[]{:S(2)}, u32[]{:S(2)}) collective-permute-start(bf16[128,2560]{1,0:T(8,128)(2,1)} %get-tuple-element.74), channel_id=1, source_target_pairs={{0,2},{1,3},{2,0},{3,1},{4,6},{5,7},{6,4},{7,5},{8,10},{9,11},{10,... | collective-permute-start | bytes 1966088 | tf_op jit(solution)/shard_map/ppermute | solution.py:20
  6.9 32.2 %collective-permute-start.3 = (bf16[33,2560]{1,0:T(8,128)(2,1)S(1)}, bf16[33,2560]{1,0:T(8,128)(2,1)}, u32[]{:S(2)}, u32[]{:S(2)}) collective-permute-start(bf16[33,2560]{1,0:T(8,128)(2,1)S(1)} %fusion.1.refs_2_), channel_id=1, source_target_pairs={{0,2},{1,3},{2,0},{3,1},{4,6},{5,7},{6,4},{7,5},{8,10},{9,11},{10,... | collective-permute-start | bytes 506888 | tf_op jit(solution)/shard_map/ppermute | solution.py:20
  9.0 36.3 %collective-permute-start.2 = (bf16[33,2560]{1,0:T(8,128)(2,1)S(1)}, bf16[33,2560]{1,0:T(8,128)(2,1)}, u32[]{:S(2)}, u32[]{:S(2)}) collective-permute-start(bf16[33,2560]{1,0:T(8,128)(2,1)S(1)} %fusion.1.refs_2_), channel_id=1, source_target_pairs={{0,1},{1,0},{2,3},{3,2},{4,5},{5,4},{6,7},{7,6},{8,9},{9,8},{10,11... | collective-permute-start | bytes 506888 | tf_op jit(solution)/shard_map/ppermute | solution.py:20
  39.1 6.1 %collective-permute-start.4 = (bf16[33,2560]{1,0:T(8,128)(2,1)}, bf16[33,2560]{1,0:T(8,128)(2,1)}, u32[]{:S(2)}, u32[]{:S(2)}) collective-permute-start(bf16[33,2560]{1,0:T(8,128)(2,1)} %collective-permute-done.3.refs_4_), channel_id=1, source_target_pairs={{0,1},{1,0},{2,3},{3,2},{4,5},{5,4},{6,7},{7,6},{8,9},{9,8},{10,11... | collective-permute-start | bytes 506888 | tf_op jit(solution)/shard_map/ppermute | solution.py:20
  39.2 19.9 %collective-permute-start.6 = (bf16[128,2560]{1,0:T(8,128)(2,1)}, bf16[128,2560]{1,0:T(8,128)(2,1)}, u32[]{:S(2)}, u32[]{:S(2)}) collective-permute-start(bf16[128,2560]{1,0:T(8,128)(2,1)} %collective-permute-done.5.refs_0_.refs_2_), channel_id=1, source_target_pairs={{0,1},{1,0},{2,3},{3,2},{4,5},{5,4},{6,7},{7,6},{8,9},{9,8},{10,11... | collective-permute-start | bytes 1966088 | tf_op jit(solution)/shard_map/ppermute | solution.py:20
  40.4 4.9 %copy-start = (bf16[2560,256]{1,0:T(8,128)(2,1)S(1)}, bf16[2560,256]{1,0:T(8,128)(2,1)}, u32[]{:S(2)}) copy-start(bf16[2560,256]{1,0:T(8,128)(2,1)} %refs_8_.5) | copy-start | bytes 3932164
  40.4 4.9 %copy-start.2 = (bf16[2560,12]{0,1:T(8,128)(2,1)S(1)}, bf16[2560,12]{0,1:T(8,128)(2,1)}, u32[]{:S(2)}) copy-start(bf16[2560,12]{0,1:T(8,128)(2,1)} %param.19) | copy-start | bytes 184324
  45.2 20.9 %collective-permute-start.1 = (bf16[128,2560]{1,0:T(8,128)(2,1)}, bf16[128,2560]{1,0:T(8,128)(2,1)S(1)}, u32[]{:S(2)}, u32[]{:S(2)}) collective-permute-start(bf16[128,2560]{1,0:T(8,128)(2,1)} %collective-permute-done.refs_0_), channel_id=1, source_target_pairs={{0,1},{1,0},{2,3},{3,2},{4,5},{5,4},{6,7},{7,6},{8,9},{9,8},{10,11... | collective-permute-start | bytes 1966088 | tf_op jit(solution)/shard_map/ppermute | solution.py:20
  45.3 1.3 %copy-start.1 = (bf16[256,2560]{1,0:T(8,128)(2,1)S(1)}, bf16[256,2560]{1,0:T(8,128)(2,1)}, u32[]{:S(2)}) copy-start(bf16[256,2560]{1,0:T(8,128)(2,1)} %refs_0_.3) | copy-start | bytes 3932164
  64.3 7.6 %collective-permute-start.8 = (f32[8,1024]{1,0:T(8,128)S(1)}, f32[8,1024]{1,0:T(8,128)S(1)}, u32[]{:S(2)}, u32[]{:S(2)}) collective-permute-start(f32[8,1024]{1,0:T(8,128)S(1)} %get-tuple-element.48), channel_id=1, source_target_pairs={{0,4},{4,8},{8,12},{12,16},{16,20},{20,24},{24,28},{28,0},{1,5},{5... | collective-permute-start | bytes 98312 | tf_op jit(solution)/shard_map/ppermute | solution.py:682
  66.1 5.8 %copy-start.4 = (f32[4,768]{1,0:T(4,128)S(1)}, f32[4,768]{1,0:T(4,128)}, u32[]{:S(2)}) copy-start(f32[4,768]{1,0:T(4,128)} %taps_ref.1) | copy-start | bytes 36868
  66.1 5.8 %copy-start.5 = (f32[4,256]{1,0:T(4,128)S(1)}, f32[4,256]{1,0:T(4,128)}, u32[]{:S(2)}) copy-start(f32[4,256]{1,0:T(4,128)} %mtaps_ref.1) | copy-start | bytes 12292
  66.1 5.8 %copy-start.6 = (f32[256]{0:T(256)S(1)}, f32[256]{0:T(256)}, u32[]{:S(2)}) copy-start(f32[256]{0:T(256)} %param.25) | copy-start | bytes 3076
  66.1 5.8 %copy-start.7 = (f32[12]{0:T(128)S(1)}, f32[12]{0:T(128)}, u32[]{:S(2)}) copy-start(f32[12]{0:T(128)} %param.26) | copy-start | bytes 148
  66.1 5.8 %copy-start.8 = (f32[12]{0:T(128)S(1)}, f32[12]{0:T(128)}, u32[]{:S(2)}) copy-start(f32[12]{0:T(128)} %param.27) | copy-start | bytes 148
  79.8 7.3 %collective-permute-start.9 = (bf16[136,768]{1,0:T(8,128)(2,1)S(1)}, bf16[136,768]{1,0:T(8,128)(2,1)S(1)}, u32[]{:S(2)}, u32[]{:S(2)}) collective-permute-start(bf16[136,768]{1,0:T(8,128)(2,1)S(1)} %get-tuple-element.58), channel_id=1, source_target_pairs={{0,4},{4,0},{8,12},{12,8},{16,20},{20,16},{24,28},{28,24},{1,5},{5... | collective-permute-start | bytes 626696 | tf_op jit(solution)/shard_map/ppermute | solution.py:20
  87.8 7.0 %collective-permute-start.10 = (bf16[136,768]{1,0:T(8,128)(2,1)S(1)}, bf16[136,768]{1,0:T(8,128)(2,1)S(1)}, u32[]{:S(2)}, u32[]{:S(2)}) collective-permute-start(bf16[136,768]{1,0:T(8,128)(2,1)S(1)} %get-tuple-element.63), channel_id=1, source_target_pairs={{0,8},{4,12},{8,0},{12,4},{16,24},{20,28},{24,16},{28,20},{1,9},{5... | collective-permute-start | bytes 626696 | tf_op jit(solution)/shard_map/ppermute | solution.py:20
  89.4 9.4 %copy-start.3 = (f32[12]{0:T(128)S(1)}, f32[12]{0:T(128)}, u32[]{:S(2)}) copy-start(f32[12]{0:T(128)} %param.28) | copy-start | bytes 148
  96.2 11.4 %collective-permute-start.11 = (bf16[136,768]{1,0:T(8,128)(2,1)S(1)}, bf16[136,768]{1,0:T(8,128)(2,1)S(1)}, u32[]{:S(2)}, u32[]{:S(2)}) collective-permute-start(bf16[136,768]{1,0:T(8,128)(2,1)S(1)} %get-tuple-element.68), channel_id=1, source_target_pairs={{0,16},{4,20},{8,24},{12,28},{16,0},{20,4},{24,8},{28,12},{1,17},{... | collective-permute-start | bytes 626696 | tf_op jit(solution)/shard_map/ppermute | solution.py:20
  107.6 5.8 %copy-start.10 = (f32[768]{0:T(1024)S(1)}, f32[768]{0:T(1024)}, u32[]{:S(2)}) copy-start(f32[768]{0:T(1024)} %param.29) | copy-start | bytes 9220
  110.7 1.2 %collective-permute-start.12 = (f32[1,1024]{1,0:T(1,128)S(1)}, f32[1,1024]{1,0:T(1,128)S(1)}, u32[]{:S(2)}, u32[]{:S(2)}) collective-permute-start(f32[1,1024]{1,0:T(1,128)S(1)} %get-tuple-element.72), channel_id=1, source_target_pairs={{0,1},{1,0},{2,3},{3,2},{4,5},{5,4},{6,7},{7,6},{8,9},{9,8},{10,11... | collective-permute-start | bytes 12296 | tf_op jit(solution)/shard_map/ppermute | solution.py:20
  111.9 3.6 %collective-permute-start.13 = (f32[1,1024]{1,0:T(1,128)S(1)}, f32[1,1024]{1,0:T(1,128)S(1)}, u32[]{:S(2)}, u32[]{:S(2)}) collective-permute-start(f32[1,1024]{1,0:T(1,128)S(1)} %add.5.mine_ref), channel_id=1, source_target_pairs={{0,2},{1,3},{2,0},{3,1},{4,6},{5,7},{6,4},{7,5},{8,10},{9,11},{10,... | collective-permute-start | bytes 12296 | tf_op jit(solution)/shard_map/ppermute | solution.py:20
where the time goes:
time: 118 us; the launch traced here: 117 us
  Pallas kernels  49.3 us (42%)
  waiting for transfers between devices  42.5 us (36%)
  starting transfers between devices  14.8 us (13%)
  local copies, waits for them, and re-layouts  9 us (8%)
  other arithmetic  1.7 us (1%)
    ppermute x13, waiting for transfers between devices, swap(): lax.ppermute(block, axis, [(i, i ^ mask) for i in range(lax.axis_size(axi...  42.4 us
    pallas_call x3, Pallas kernels, project(): pl.pallas_call(functools.partial(project_kernel, cfg), out_shape=(jax.Sha...  18.3 us
    ppermute x13, starting transfers between devices, swap(): lax.ppermute(block, axis, [(i, i ^ mask) for i in range(lax.axis_size(axi...  13.1 us
    pallas_call x2, Pallas kernels, gate_project(): pl.pallas_call(functools.partial(gate_kernel, counts, devices), out_shape...  10.5 us
    pallas_call x1, Pallas kernels, run_states(): pl.pallas_call(functools.partial(state_kernel, width), out_shape=(jax.Sha...  7.76 us
    unnamed x24, local copies, waits for them, and re-layouts  6.1 us
    pallas_call x1, Pallas kernels, run_outputs(): pl.pallas_call(functools.partial(output_kernel, width), out_shape=(jax.Sh...  5.48 us
    pallas_call x1, Pallas kernels, join(): pl.pallas_call(functools.partial(join_kernel, d), out_shape=(jax.ShapeDty...  3.08 us
  transfers between devices with their start and end apart: 14, of which 5 were waited for; matrix products, arithmetic and copies ran while one was open for 8% of the time, Pallas kernels for 29%

commit v1 on v0

--- a/solution.py
+++ b/solution.py
@@ -52,121 +52,126 @@
     return jnp.where(expert.astype(F32) == route_row, 1.0, 0.0)
 
 
-def once(shape, const):
-    return pl.BlockSpec(shape, const, pipeline_mode=pl.Buffered(1))
-
-
-def up_specs(up, devices, tn, column):
-    cols = up.shape[0] // devices
-    return [
-        pl.BlockSpec((cols, tn), lambda t, i, r=r: (i[0] ^ r, column(t))) for r in range(devices)
-    ]
+VMEM = pl.BlockSpec(memory_space=pltpu.VMEM)
+
+
+def up_rows(up_ref, e, devices, lanes):
+    cols = up_ref.shape[0] // devices
+    return jnp.concatenate(
+        [up_ref[pl.ds(pl.multiple_of((e ^ r) * cols, cols), cols), lanes] for r in range(devices)], axis=0
+    )
 
 
 def project_kernel(cfg, index_ref, *refs):
-    counts, route_from, devices, cols, rank, inner_tiles, aliased, pair = cfg
+    counts, route_from, devices, cols, rank, aliased = cfg
     x_refs, refs = refs[: len(counts)], refs[len(counts):]
     d_refs, refs = refs[:devices], refs[devices:]
-    dt_ref, w_ref, wbc_ref = refs[:3]
-    up_refs, refs = refs[3 : 3 + devices], refs[3 + devices:]
-    z_ref, dto_ref, lift_ref, tail_ref, x_scr, w_scr = refs[aliased:]
-    tile = pl.program_id(0)
+    dt_ref, w_ref, wbc_ref, up_ref = refs[:4]
+    if aliased:
+        z_ref, dto_ref, lift_ref, x_scr, w_scr = refs[4 + aliased:]
+        lift_scr = lift_ref
+    else:
+        z_ref, dto_ref, lift_ref, tails_ref, rim_ref, x_scr, w_scr, lift_scr = refs[4:]
     e = index_ref[0]
-
-    @pl.when(tile == 0)
-    def _():
-        at = 0
-        for x_ref, n in zip(x_refs, counts):
-            x_scr[at : at + n, :] = x_ref[...]
-            at += n
-        w_scr[LANES:, :] = jnp.zeros((w_scr.shape[0] - LANES, w_scr.shape[1]), BF16)
-        w_scr[LANES : LANES + dt_ref.shape[0], :] = dt_ref[...]
+    rows = sum(counts)
+
+    at = 0
+    for x_ref, n in zip(x_refs, counts):
+        x_scr[at : at + n, :] = x_ref[...]
+        at += n
+    if not aliased:
         for r in range(devices):
-            w_scr[r * cols : (r + 1) * cols, :] = d_refs[r][0:cols, :]
-        small = mm_nt(x_scr[...], w_scr[...])
-        masks = []
-        for r, first, n in route_from:
-            for lane in range(first, first + n, LANES):
-                row = d_refs[r][cols : cols + 1, lane : lane + LANES].astype(F32)
-                masks.append(route_mask(e, row, cols // rank, rank).T)
-        mask = jnp.concatenate(masks, axis=0)
-        lift_ref[...] = jnp.where(mask > 0.5, small[:, :LANES], 0.0).astype(BF16)
-        pad = jnp.zeros((small.shape[0], 2 * LANES - small.shape[1]), F32)
-        dto_ref[...] = jnp.concatenate([small[:, LANES:], pad], axis=1)
-
-    @pl.when(tile < inner_tiles)
-    def _():
-        up = jnp.concatenate([r[...] for r in up_refs], axis=0)
-        z_ref[...] = mm(x_scr[...], w_ref[...]) + mm(lift_ref[...], up)
-
-    @pl.when(tile >= inner_tiles)
-    def _():
-        z_ref[...] = mm(x_scr[...], wbc_ref[...])
-
-    half = counts[0]
-    start = ((devices - 1) ^ e) % 2 * half + half - 8
-    tail = z_ref[pl.ds(pl.multiple_of(start, 8), 8), :]
-    if aliased == 4:
-        old_ref = refs[3]
-        tail = jnp.where(((devices - 1) ^ e) // 2 == pair, tail, old_ref[...])
-    tail_ref[...] = tail
-
-
-def project(index, xs, route_from, downs, dt_t, wz, wbc, up, rank, total, row_block, buffers, tail, pair):
+            x_scr[at + 8 * r : at + 8 * r + 8, :] = d_refs[r][cols : cols + 8, :]
+    w_scr[LANES:, :] = jnp.zeros((w_scr.shape[0] - LANES, w_scr.shape[1]), BF16)
+    w_scr[LANES : LANES + dt_ref.shape[0], :] = dt_ref[...]
+    for r in range(devices):
+        w_scr[r * cols : (r + 1) * cols, :] = d_refs[r][0:cols, :]
+    small = mm_nt(x_scr[...], w_scr[...])
+
+    def mask_of(r, lane):
+        row = d_refs[r][cols : cols + 1, lane : lane + LANES].astype(F32)
+        return route_mask(e, row, cols // rank, rank).T
+
+    masks = []
+    for r, first, n in route_from:
+        for lane in range(first, first + n, LANES):
+            masks.append(mask_of(r, lane))
+    if not aliased:
+        last = route_from[0][1] + route_from[0][2] - LANES
+        for r in range(devices):
+            masks.append(mask_of(r, last)[LANES - 8 :, :])
+    lift = jnp.where(jnp.concatenate(masks, axis=0) > 0.5, small[:, :LANES], 0.0).astype(BF16)
+    lift_scr[...] = lift
+    pad = jnp.zeros((rows, 2 * LANES - small.shape[1]), F32)
+    dto_ref[...] = jnp.concatenate([small[:rows, LANES:], pad], axis=1)
+    if not aliased:
+        lift_ref[...] = lift[:rows]
+
+    def put(lanes, value):
+        z_ref[:, lanes] = value[:rows]
+        if not aliased:
+            tails_ref[:, lanes] = value[rows:]
+
+    width = z_ref.shape[1]
+    inner = up_ref.shape[1] // 2
+    tn = 256 if inner % 256 == 0 else 128
+    for at in range(0, inner, tn):
+        lanes = slice(inner + at, inner + at + tn)
+        up = up_rows(up_ref, e, devices, lanes)
+        put(slice(at, at + tn), mm(x_scr[...], w_ref[:, lanes]) + mm(lift_scr[...], up))
+    for at in range(0, width - inner, tn):
+        put(slice(inner + at, inner + at + tn), mm(x_scr[...], wbc_ref[:, at : at + tn]))
+    if not aliased:
+        row = ((devices - 1) ^ e) * 8
+        rim_ref[...] = tails_ref[pl.ds(pl.multiple_of(row, 8), 8), :]
+
+
+def project(index, xs, route_from, downs, dt_t, wz, wbc, up, rank, total, row_block, buffers):
     counts = tuple(x.shape[0] for x in xs)
     rows = sum(counts)
     features = wz.shape[0]
-    inner = up.shape[1] // 2
-    width = inner + wbc.shape[1]
-    tn = 256 if inner % 256 == 0 and width % 256 == 0 else 128
-    inner_tiles = inner // tn
+    width = up.shape[1] // 2 + wbc.shape[1]
     devices = len(downs)
-    const = lambda t, i: (0, 0)
-    in_specs = (
-        [once(x.shape, const) for x in xs]
-        + [once(d.shape, const) for d in downs]
-        + [
-            once(dt_t.shape, const),
-            pl.BlockSpec((features, tn), lambda t, i: (0, inner_tiles + jnp.minimum(t, inner_tiles - 1))),
-            pl.BlockSpec((features, tn), lambda t, i: (0, jnp.maximum(t - inner_tiles, 0))),
+    args = list(xs) + list(downs) + [dt_t, wz, wbc, up]
+    in_specs = [VMEM] * len(args)
+    out_shape = [
+        jax.ShapeDtypeStruct((total, width), F32),
+        jax.ShapeDtypeStruct((total, LANES), F32),
+        jax.ShapeDtypeStruct((total, LANES), BF16),
+    ]
+    out_specs = [
+        pl.BlockSpec((rows, width), lambda t, i: (row_block, 0)),
+        pl.BlockSpec((rows, LANES), lambda t, i: (row_block, 0)),
+        pl.BlockSpec((rows, LANES), lambda t, i: (row_block, 0)),
+    ]
+    extra = 8 * devices if buffers is None else 0
+    scratch = [
+        pltpu.VMEM((rows + extra, features), BF16),
+        pltpu.VMEM((LANES + 16, features), BF16),
+    ]
+    aliases = {}
+    if buffers is None:
+        out_shape += [jax.ShapeDtypeStruct((extra, width), F32), jax.ShapeDtypeStruct((8, width), F32)]
+        out_specs += [
+            pl.BlockSpec((extra, width), lambda t, i: (0, 0)),
+            pl.BlockSpec((8, width), lambda t, i: (0, 0)),
         ]
-        + up_specs(up, devices, tn, lambda t: inner_tiles + jnp.minimum(t, inner_tiles - 1))
-    )
-    args = list(xs) + list(downs) + [dt_t, wz, wbc] + [up] * devices
-    aliases = {}
-    if buffers is not None:
+        scratch.append(pltpu.VMEM((rows + extra, LANES), BF16))
+    else:
         for n, buffer in enumerate(buffers):
             aliases[1 + len(args)] = n
             args.append(buffer)
             in_specs.append(pl.BlockSpec(memory_space=pl.ANY))
-    extra = len(aliases)
-    if tail is not None:
-        args.append(tail)
-        in_specs.append(pl.BlockSpec((8, tn), lambda t, i: (0, t)))
-        extra += 1
-    cfg = (counts, route_from, devices, LANES // devices, rank, inner_tiles, extra, pair)
+    cfg = (counts, route_from, devices, LANES // devices, rank, len(aliases))
     return pl.pallas_call(
         functools.partial(project_kernel, cfg),
-        out_shape=(
-            jax.ShapeDtypeStruct((total, width), F32),
-            jax.ShapeDtypeStruct((total, LANES), F32),
-            jax.ShapeDtypeStruct((total, LANES), BF16),
-            jax.ShapeDtypeStruct((8, width), F32),
-        ),
+        out_shape=tuple(out_shape),
         grid_spec=pltpu.PrefetchScalarGridSpec(
             num_scalar_prefetch=1,
-            grid=(width // tn,),
+            grid=(1,),
             in_specs=in_specs,
-            out_specs=(
-                pl.BlockSpec((rows, tn), lambda t, i: (row_block, t)),
-                pl.BlockSpec((rows, LANES), lambda t, i: (row_block, 0)),
-                pl.BlockSpec((rows, LANES), lambda t, i: (row_block, 0)),
-                pl.BlockSpec((8, tn), lambda t, i: (0, t)),
-            ),
-            scratch_shapes=[
-                pltpu.VMEM((rows, features), BF16),
-                pltpu.VMEM((LANES + 16, features), BF16),
-            ],
+            out_specs=tuple(out_specs),
+            scratch_shapes=scratch,
         ),
         input_output_aliases=aliases,
         cost_estimate=pl.CostEstimate(
@@ -183,19 +188,18 @@
 
 def gate_kernel(counts, devices, index_ref, *refs):
     x_refs, refs = refs[: len(counts)], refs[len(counts):]
-    lift_ref, w_ref = refs[:2]
-    up_refs = refs[2 : 2 + devices]
+    lift_ref, w_ref, up_ref = refs[:3]
     g_ref, x_scr = refs[-2:]
-
-    @pl.when(pl.program_id(0) == 0)
-    def _():
-        at = 0
-        for x_ref, n in zip(x_refs, counts):
-            x_scr[at : at + n, :] = x_ref[...]
-            at += n
-
-    up = jnp.concatenate([r[...] for r in up_refs], axis=0)
-    g_ref[...] = mm(x_scr[...], w_ref[...]) + mm(lift_ref[...], up)
+    at = 0
+    for x_ref, n in zip(x_refs, counts):
+        x_scr[at : at + n, :] = x_ref[...]
+        at += n
+    width = g_ref.shape[1]
+    tn = 256 if width % 256 == 0 else 128
+    for at in range(0, width, tn):
+        lanes = slice(at, at + tn)
+        up = up_rows(up_ref, index_ref[0], devices, lanes)
+        g_ref[:, lanes] = mm(x_scr[...], w_ref[:, lanes]) + mm(lift_ref[...], up)
 
 
 def gate_project(index, xs, lift, wz, up, devices, total, row_block, buffer):
@@ -203,14 +207,9 @@
     rows = sum(counts)
     features = wz.shape[0]
     width = up.shape[1] // 2
-    tn = 256 if width % 256 == 0 else 128
-    const = lambda t, i: (0, 0)
-    in_specs = [once(x.shape, const) for x in xs] + [
-        pl.BlockSpec((rows, lift.shape[1]), lambda t, i: (row_block, 0), pipeline_mode=pl.Buffered(1)),
-        pl.BlockSpec((features, tn), lambda t, i: (0, t)),
-    ]
-    in_specs += up_specs(up, devices, tn, lambda t: t)
-    args = list(xs) + [lift, wz] + [up] * devices
+    block = lambda t, i: (row_block, 0)
+    in_specs = [VMEM] * len(xs) + [pl.BlockSpec((rows, lift.shape[1]), block), VMEM, VMEM]
+    args = list(xs) + [lift, wz, up]
     aliases = {}
     if buffer is not None:
         aliases[1 + len(args)] = 0
@@ -221,9 +220,9 @@
         out_shape=jax.ShapeDtypeStruct((total, width), F32),
         grid_spec=pltpu.PrefetchScalarGridSpec(
             num_scalar_prefetch=1,
-            grid=(width // tn,),
+            grid=(1,),
             in_specs=in_specs,
-            out_specs=pl.BlockSpec((rows, tn), lambda t, i: (row_block, t)),
+            out_specs=pl.BlockSpec((rows, width), block),
             scratch_shapes=[pltpu.VMEM((rows, features), BF16)],
         ),
         input_output_aliases=aliases,
@@ -255,18 +254,18 @@
 
 
 def state_kernel(
-    width, index_ref, z_ref, d_ref, rim_ref, taps_ref, mtaps_ref, bias_ref, mbias_ref, dtb_ref, rate_ref,
-    xc_ref, cum_ref, step_ref, before_ref, local_ref, final_ref, log_ref, send_ref, prefix_ref, plog_ref,
-    ext, state, offset,
+    cfg, index_ref, z_ref, d_ref, prev_ref, tails_ref, rim_ref,
+    taps_ref, mtaps_ref, bias_ref, mbias_ref, dtb_ref, rate_ref, *refs,
 ):
-    c = pl.program_id(0)
-
-    @pl.when(c == 0)
-    def _():
-        ext[0:8, :] = jnp.where(index_ref[1] == 0, 0.0, rim_ref[...])
-        state[...] = jnp.zeros_like(state)
-        offset[...] = jnp.zeros_like(offset)
-
+    width, where_am_i = cfg
+    xc_ref, cum_ref, step_ref, update_ref, total_ref, ext = refs[-6:]
+    e = index_ref[0]
+    r, q = where_am_i(pl.program_id(0))
+    block = r ^ e
+    before = pl.multiple_of((jnp.maximum(block - 1, 0) ^ e) * 8, 8)
+    rim = jnp.where(index_ref[1] == 0, 0.0, rim_ref[...])
+    first = jnp.where(block == 0, rim, tails_ref[pl.ds(before, 8), :])
+    ext[0:8, :] = jnp.where(q == 0, first, prev_ref[...])
     ext[8 : 8 + CHUNK, :] = z_ref[...]
     taps = taps_ref.shape[0]
     outs = []
@@ -282,7 +281,6 @@
         xc_ref[:, lanes] = out
         outs.append(out)
     x, maps = outs
-    ext[0:8, :] = ext[CHUNK : CHUNK + 8, :]
 
     raw = d_ref[...] + pad_lanes(dtb_ref[...])
     step = jnp.maximum(raw, 0.0) + jnp.log1p(jnp.exp(-jnp.abs(raw)))
@@ -293,101 +291,131 @@
     sums = mm(lower, jnp.concatenate(split3(decay), axis=1))
     cum = sums[:, :LANES] + sums[:, LANES : 2 * LANES] + sums[:, 2 * LANES :]
     total = cum[CHUNK - 1 : CHUNK, :]
-    before = offset[0:1, :]
     cum_ref[...] = cum
     step_ref[...] = step
-    before_ref[0] = offset[...]
-    after = jnp.broadcast_to(before + total, offset.shape)
-    offset[...] = after
+    total_ref[0] = jnp.broadcast_to(total, total_ref.shape[1:])
 
     xs = (spread(jnp.exp(total - cum) * step, width) * x).astype(BF16)
     b_hi, b_lo = split2(maps[:, :STATE].T)
-    update = mm(jnp.concatenate([b_hi, b_lo], axis=1), jnp.concatenate([xs, xs], axis=0))
-    old = state[...]
-    local_ref[0] = old.astype(BF16)
-    new = spread(jnp.broadcast_to(jnp.exp(total), (8, LANES)), width)[0:1, :] * old + update
-    state[...] = new
-
-    @pl.when(c == pl.num_programs(0) - 1)
-    def _():
-        final_ref[...] = new
-        wide = spread(after, width)
-        log_ref[...] = wide
-        send_ref[0:STATE, :] = new.astype(BF16)
-        send_ref[STATE : STATE + 8, :] = pack_logs(wide)
-        prefix_ref[...] = jnp.zeros_like(new)
-        plog_ref[...] = jnp.zeros_like(wide)
-
-
-def piece_index(block, q, e, per):
-    r = block ^ e
+    update_ref[0] = mm(jnp.concatenate([b_hi, b_lo], axis=1), jnp.concatenate([xs, xs], axis=0))
+
+
+def piece_index(r, q, per):
+    if isinstance(r, int):
+        return r * per + q if r < 2 else 2 * per + ((r // 2 - 1) * per + q) * 2 + r % 2
     far = 2 * per + ((r // 2 - 1) * per + q) * 2 + r % 2
     return jnp.where(r < 2, r * per + q, far)
 
 
-def piece_map(per):
-    def index(c, index_ref):
-        return (piece_index(c // per, c % per, index_ref[0], per), 0)
-
-    return index
-
-
-def run_states(index, z, dt, rim, params, width, local):
+def run_states(index, z, dt, tails, rim, params, width, per, far, buffers):
     total, wide = z.shape
     chunks = total // CHUNK
-    per = local // CHUNK
-    const = lambda c, i: (0, 0)
-    row = lambda c, i: (c, 0)
-    deep = lambda c, i: (c, 0, 0)
+    if far is None:
+        steps = 2 * per
+        at = lambda c: (c // per, c % per)
+    else:
+        steps = 2
+        at = lambda c: (far[0] + c, far[1])
+
+    def piece(c, i):
+        r, q = at(c)
+        return (piece_index(r, q, per), 0)
+
+    def previous(c, i):
+        r, q = at(c)
+        return (piece_index(r, jnp.maximum(q - 1, 0), per) * (CHUNK // 8) + CHUNK // 8 - 1, 0)
+
+    def place(c, i):
+        r, q = at(c)
+        return (r ^ i[0]) * per + q
+
+    row = lambda c, i: (place(c, i), 0)
+    deep = lambda c, i: (place(c, i), 0, 0)
+    args = [z, dt, z, tails, rim, *params]
+    in_specs = [
+        pl.BlockSpec((CHUNK, wide), piece),
+        pl.BlockSpec((CHUNK, LANES), piece),
+        pl.BlockSpec((8, wide), previous),
+    ] + [VMEM] * (2 + len(params))
+    aliases = {}
+    if buffers is not None:
+        for n, buffer in enumerate(buffers):
+            aliases[1 + len(args)] = n
+            args.append(buffer)
+            in_specs.append(pl.BlockSpec(memory_space=pl.ANY))
     return pl.pallas_call(
-        functools.partial(state_kernel, width),
+        functools.partial(state_kernel, (width, at)),
         out_shape=(
             jax.ShapeDtypeStruct((total, wide), F32),
             jax.ShapeDtypeStruct((total, LANES), F32),
             jax.ShapeDtypeStruct((total, LANES), F32),
+            jax.ShapeDtypeStruct((chunks, STATE, width), F32),
             jax.ShapeDtypeStruct((chunks, 8, LANES), F32),
-            jax.ShapeDtypeStruct((chunks, STATE, width), BF16),
-            jax.ShapeDtypeStruct((STATE, width), F32),
-            jax.ShapeDtypeStruct((8, width), F32),
-            jax.ShapeDtypeStruct((STATE + 8, width), BF16),
-            jax.ShapeDtypeStruct((STATE, width), F32),
-            jax.ShapeDtypeStruct((8, width), F32),
         ),
         grid_spec=pltpu.PrefetchScalarGridSpec(
             num_scalar_prefetch=1,
-            grid=(chunks,),
-            in_specs=[
-                pl.BlockSpec((CHUNK, wide), piece_map(per)),
-                pl.BlockSpec((CHUNK, LANES), piece_map(per)),
-                pl.BlockSpec(rim.shape, const),
-            ]
-            + [pl.BlockSpec(p.shape, const) for p in params],
+            grid=(steps,),
+            in_specs=in_specs,
             out_specs=(
                 pl.BlockSpec((CHUNK, wide), row),
                 pl.BlockSpec((CHUNK, LANES), row),
                 pl.BlockSpec((CHUNK, LANES), row),
+                pl.BlockSpec((1, STATE, width), deep),
                 pl.BlockSpec((1, 8, LANES), deep),
-                pl.BlockSpec((1, STATE, width), deep),
-                pl.BlockSpec((STATE, width), const),
-                pl.BlockSpec((8, width), const),
-                pl.BlockSpec((STATE + 8, width), const),
-                pl.BlockSpec((STATE, width), const),
-                pl.BlockSpec((8, width), const),
             ),
-            scratch_shapes=[
-                pltpu.VMEM((CHUNK + 8, wide), F32),
-                pltpu.VMEM((STATE, width), F32),
-                pltpu.VMEM((8, LANES), F32),
-            ],
-        ),
+            scratch_shapes=[pltpu.VMEM((CHUNK + 8, wide), F32)],
+        ),
+        input_output_aliases=aliases,
         cost_estimate=pl.CostEstimate(
-            flops=2 * total * width * 1000, transcendentals=total * wide, bytes_accessed=12 * total * wide
+            flops=2 * steps * CHUNK * width * 1000, transcendentals=steps * CHUNK * wide,
+            bytes_accessed=12 * steps * CHUNK * wide,
         ),
         compiler_params=pltpu.CompilerParams(
             dimension_semantics=("arbitrary",), vmem_limit_bytes=12 << 20
         ),
         name="run_states",
-    )(index, z, dt, rim, *params)
+    )(index, *args)
+
+
+def stitch_kernel(
+    width, update_ref, total_ref, entry_ref, before_ref, group_ref, glog_ref, send_ref, prefix_ref, plog_ref,
+):
+    chunks = update_ref.shape[0]
+    state = jnp.zeros(group_ref.shape, F32)
+    log = jnp.zeros(total_ref.shape[1:], F32)
+    for c in range(chunks):
+        entry_ref[c] = state.astype(BF16)
+        before_ref[c] = log
+        total = total_ref[c]
+        state = spread(jnp.exp(total), width)[0:1, :] * state + update_ref[c]
+        log = log + total
+    group_ref[...] = state
+    wide = spread(log, width)
+    glog_ref[...] = wide
+    send_ref[0:STATE, :] = state.astype(BF16)
+    send_ref[STATE : STATE + 8, :] = pack_logs(wide)
+    prefix_ref[...] = jnp.zeros_like(state)
+    plog_ref[...] = jnp.zeros_like(wide)
+
+
+def stitch(updates, totals):
+    _, state, width = updates.shape
+    return pl.pallas_call(
+        functools.partial(stitch_kernel, width),
+        out_shape=(
+            jax.ShapeDtypeStruct(updates.shape, BF16),
+            jax.ShapeDtypeStruct(totals.shape, F32),
+            jax.ShapeDtypeStruct((state, width), F32),
+            jax.ShapeDtypeStruct((8, width), F32),
+            jax.ShapeDtypeStruct((state + 8, width), BF16),
+            jax.ShapeDtypeStruct((state, width), F32),
+            jax.ShapeDtypeStruct((8, width), F32),
+        ),
+        in_specs=[VMEM, VMEM],
+        out_specs=(VMEM,) * 7,
+        compiler_params=pltpu.CompilerParams(vmem_limit_bytes=8 << 20),
+        name="stitch",
+    )(updates, totals)
 
 
 def output_kernel(
@@ -456,7 +484,7 @@
                 pl.BlockSpec((CHUNK, LANES), row),
                 pl.BlockSpec((1, 8, LANES), deep),
                 pl.BlockSpec((1, STATE, width), deep),
-                pl.BlockSpec((CHUNK, width), piece_map(per)),
+                pl.BlockSpec((CHUNK, width), lambda c, i: (piece_index((c // per) ^ i[0], c % per, per), 0)),
                 pl.BlockSpec(direct.shape, const),
             ],
             out_specs=(
@@ -639,12 +667,12 @@
     per = local // CHUNK
 
     route_row = jnp.pad(routes.reshape(1, local).astype(BF16), ((0, 0), (0, features - local)))
-    down = {0: jnp.concatenate([adapter_down_weight.T, route_row], axis=0)}
+    down = {0: jnp.concatenate([adapter_down_weight.T, route_row, tokens[local - 7 :]], axis=0)}
     far = {}
     for k in range(2, n, 2):
         down[k] = swap(down[0], "exp", k)
-    for k in range(2, n, 2):
-        for q in reversed(range(per)):
+    for q in range(per):
+        for k in range(2, n, 2):
             far[k, q] = swap(tokens[q * CHUNK : (q + 1) * CHUNK], "exp", k)
     sibling = swap(tokens, "exp", 1)
     for k in range(0, n, 2):
@@ -656,39 +684,33 @@
         project, index, downs=downs, dt_t=step_size_weight.T, wz=wz, wbc=state_map_weight,
         up=up, rank=rank, total=total,
     )
-    *buffers, tail = call(
-        [tokens, sibling], route_from=((0, 0, local), (1, 0, local)), row_block=0, buffers=None,
-        tail=None, pair=0,
+    *buffers, tails, rim = call(
+        [tokens, sibling], route_from=((0, 0, local), (1, 0, local)), row_block=0, buffers=None
     )
-    gate = gate_project(index, [tokens, sibling], buffers[2], wz, up, n, total, 0, None)
-    far_rows = {}
-    for k in range(2, n, 2):
-        for q in reversed(range(per)):
-            mine = far[k, q]
-            other = swap(mine, "exp", 1)
-            block = per + (k // 2 - 1) * per + q
-            *buffers, new_tail = call(
-                [mine, other],
-                route_from=((k, q * CHUNK, CHUNK), (k + 1, q * CHUNK, CHUNK)),
-                row_block=block,
-                buffers=buffers,
-                tail=tail if q == per - 1 else None,
-                pair=k // 2,
-            )
-            if q == per - 1:
-                tail = new_tail
-            far_rows[k, q] = (mine, other)
-        if k == n - 2:
-            rim = lax.ppermute(tail, "seq", [(i, (i + 1) % shards) for i in range(shards)])
-    z, dt, lift = buffers
-
+    rim = lax.ppermute(rim, "seq", [(i, (i + 1) % shards) for i in range(shards)])
     params = [
         inner_conv_taps, state_map_taps, inner_conv_bias[None, :], state_map_conv_bias[None, :],
         step_size_bias[None, :], head_decay_rate[None, :],
     ]
-    xc, cum, step, before, states, group, glog, send, prefix, plog = run_states(
-        index, z, dt, rim, params, width, local
-    )
+    kept = run_states(index, buffers[0], buffers[1], tails, rim, params, width, per, None, None)
+    far_rows = {}
+    for q in range(per):
+        for k in range(2, n, 2):
+            mine = far[k, q]
+            other = swap(mine, "exp", 1)
+            far_rows[k, q] = (mine, other)
+            buffers = call(
+                [mine, other],
+                route_from=((k, q * CHUNK, CHUNK), (k + 1, q * CHUNK, CHUNK)),
+                row_block=per + (k // 2 - 1) * per + q,
+                buffers=buffers,
+            )
+            kept = run_states(
+                index, buffers[0], buffers[1], tails, rim, params, width, per, (k, q), kept
+            )
+    xc, cum, step, updates, totals = kept
+    lift = buffers[2]
+    states, before, group, glog, send, prefix, plog = stitch(updates, totals)
     d = 1
     while True:
         got = swap(send, "seq", d)
@@ -696,6 +718,7 @@
             break
         send, group, glog, prefix, plog = combine(index, d, got, group, glog, prefix, plog)
         d *= 2
+    gate = gate_project(index, [tokens, sibling], lift, wz, up, n, total, 0, None)
     for k in range(2, n, 2):
         xs = []
         for q in range(per):

time: 118 us -> 115 us (0.975)
  Pallas kernels: 49.3 us -> 44.7 us
  waiting for transfers between devices: 42.5 us -> 46.5 us
  starting transfers between devices: 14.8 us -> 11.9 us
    ppermute x1, waiting for transfers between devices: 0.01 us -> 4.92 us  [body(): lax.ppermute(rim, 'seq', [(i, (i + 1) % shards) for i in range(shards)])]
    ppermute x13, starting transfers between devices: 13.1 us -> 9.93 us  [swap(): lax.ppermute(block, axis, [(i, i ^ mask) for i in range(lax.axis_size(axi...]
    pallas_call x4 -> x7, Pallas kernels: 26.1 us -> 23.4 us  [the longest x3 14.1 us: project(): pl.pallas_call(functools.partial(project_kernel, cfg), out_shape=tuple(ou...]
    pallas_call x2, Pallas kernels: 10.5 us -> 8.84 us  [gate_project(): pl.pallas_call(functools.partial(gate_kernel, counts, devices), out_shape...]
    unnamed x24 -> x26, local copies, waits for them, and re-layouts: 6.1 us -> 7.1 us
  transfers between devices with their start and end apart: 14 -> 14, of which waited for: 5 -> 7; matrix products, arithmetic and copies ran while one was open for 8% -> 8% of each run, Pallas kernels for 29% -> 27%
where the time goes in v1:
time: 115 us; the launch traced here: 114 us
  waiting for transfers between devices  46.5 us (40%)
  Pallas kernels  44.7 us (39%)
  starting transfers between devices  11.9 us (10%)
  local copies, waits for them, and re-layouts  9.27 us (8%)
  other arithmetic  1.7 us (1%)
    ppermute x13, waiting for transfers between devices, swap(): lax.ppermute(block, axis, [(i, i ^ mask) for i in range(lax.axis_size(axi...  41.6 us
    pallas_call x3, Pallas kernels, project(): pl.pallas_call(functools.partial(project_kernel, cfg), out_shape=tuple(ou...  14.1 us
    ppermute x13, starting transfers between devices, swap(): lax.ppermute(block, axis, [(i, i ^ mask) for i in range(lax.axis_size(axi...  9.93 us
    pallas_call x3, Pallas kernels, run_states(): pl.pallas_call(functools.partial(state_kernel, (width, at)), out_shape=(j...  8.88 us
    pallas_call x2, Pallas kernels, gate_project(): pl.pallas_call(functools.partial(gate_kernel, counts, devices), out_shape...  8.84 us
    unnamed x26, local copies, waits for them, and re-layouts  7.1 us
    pallas_call x1, Pallas kernels, run_outputs(): pl.pallas_call(functools.partial(output_kernel, width), out_shape=(jax.Sh...  5.35 us
    ppermute x1, waiting for transfers between devices, body(): lax.ppermute(rim, 'seq', [(i, (i + 1) % shards) for i in range(shards)])  4.92 us
  transfers between devices with their start and end apart: 14, of which 7 were waited for; matrix products, arithmetic and copies ran while one was open for 8% of the time, Pallas kernels for 27%

profile of v1, /device:TPU:0, one launch (start us, length us, event | category | flops | bytes accessed | tf_op | source)
XLA Modules:
  0.0 114.3 jit_solution(12083475885893048334)
XLA Ops:
  0.0 0.5 collective-permute-start.7
  0.5 1.4 %fusion.4 = (bf16[128,2560]{1,0:T(8,128)(2,1)S(1)}, bf16[128,2560]{1,0:T(8,128)(2,1)S(1)}) fusion(bf16[256,2560]{1,0:T(8,128)(2,1)} %refs_0_.3), kind=kLoop, calls=%fused_computation.8 | loop fusion | bytes 2621440 | tf_op jit(solution)/shard_map/slice | solution.py:676
  1.9 2.6 %collective-permute-start.5 = (bf16[128,2560]{1,0:T(8,128)(2,1)S(1)}, bf16[128,2560]{1,0:T(8,128)(2,1)}, u32[]{:S(2)}, u32[]{:S(2)}) collective-permute-start(bf16[128,2560]{1,0:T(8,128)(2,1)S(1)} %get-tuple-element.97), channel_id=1, source_target_pairs={{0,2},{1,3},{2,0},{3,1},{4,6},{5,7},{6,4},{7,5},{8,10},{9,11},{10,... | collective-permute-start | bytes 1966088 | tf_op jit(solution)/shard_map/ppermute | solution.py:20
  4.4 0.1 collective-permute-start
  4.5 0.7 convert_bitcast_fusion
  5.2 0.8 slice.10
  6.0 0.9 fusion.3.refs_2_
  6.9 2.0 %collective-permute-start.3 = (bf16[40,2560]{1,0:T(8,128)(2,1)S(1)}, bf16[40,2560]{1,0:T(8,128)(2,1)S(1)}, u32[]{:S(2)}, u32[]{:S(2)}) collective-permute-start(bf16[40,2560]{1,0:T(8,128)(2,1)S(1)} %fusion.3.refs_2_), channel_id=1, source_target_pairs={{0,2},{1,3},{2,0},{3,1},{4,6},{5,7},{6,4},{7,5},{8,10},{9,11},{10,... | collective-permute-start | bytes 614408 | tf_op jit(solution)/shard_map/ppermute | solution.py:20
  8.9 11.2 %collective-permute-done.5.refs_0_ = bf16[128,2560]{1,0:T(8,128)(2,1)} collective-permute-done((bf16[128,2560]{1,0:T(8,128)(2,1)S(1)}, bf16[128,2560]{1,0:T(8,128)(2,1)}, u32[]{:S(2)}, u32[]{:S(2)}) %collective-permute-start.5) | collective-permute-done | bytes 655392 | tf_op jit(solution)/shard_map/ppermute | solution.py:20
  20.1 0.0 collective-permute-start.6
  20.1 0.5 collective-permute-start.2
  20.6 17.6 %collective-permute-done.3.refs_4_ = bf16[40,2560]{1,0:T(8,128)(2,1)S(1)} collective-permute-done((bf16[40,2560]{1,0:T(8,128)(2,1)S(1)}, bf16[40,2560]{1,0:T(8,128)(2,1)S(1)}, u32[]{:S(2)}, u32[]{:S(2)}) %collective-permute-start.3) | collective-permute-done | bytes 204832 | tf_op jit(solution)/shard_map/ppermute | solution.py:20
  38.3 0.5 collective-permute-start.1
  38.8 0.1 pad_add_fusion.index_ref
  38.9 4.7 %copy.33 = bf16[320,8,2,768]{3,1,2,0:T(8,128)(2,1)S(1)} copy(bf16[320,8,2,768]{3,2,1,0:T(2,128)(2,1)} %bitcast.37) | data formatting | bytes 15728640
  43.6 1.0 copy.34
  44.6 0.0 collective-permute-done.2.refs_3_
  44.7 0.0 copy-start.1
  44.7 1.3 %copy-done.1 = bf16[2560,256]{1,0:T(8,128)(2,1)S(1)} copy-done((bf16[2560,256]{1,0:T(8,128)(2,1)S(1)}, bf16[2560,256]{1,0:T(8,128)(2,1)}, u32[]{:S(2)}) %copy-start.1) | copy-done | bytes 1310744
  46.0 0.0 copy-start.7
  46.0 0.0 copy-start.8
  46.0 6.0 %project.3 = (f32[1024,1024]{1,0:T(8,128)S(1)}, f32[1024,128]{1,0:T(8,128)S(1)}, bf16[1024,128]{1,0:T(8,128)(2,1)S(1)}, f32[32,1024]{1,0:T(8,128)S(1)}, f32[8,1024]{1,0:T(8,128)S(1)}) custom-call(s32[2]{0:T(128)S(1)} %pad_add_fusion.index_ref, bf16[256,2560]{1,0:T(8,128)(2,1)S(1)} %copy-done, bf16[256,2560]{1,0:T(8,128)(2,1)} %collective-permute-done.7.refs_1_, ...), custom_call_target="tpu_custom_call" | custom-call | flops 3355443200 | bytes 9961472 | tf_op jit(solution)/shard_map/project/pallas_call | solution.py:166
  52.0 1.9 %collective-permute-start.8 = (f32[8,1024]{1,0:T(8,128)S(1)}, f32[8,1024]{1,0:T(8,128)S(1)}, u32[]{:S(2)}, u32[]{:S(2)}) collective-permute-start(f32[8,1024]{1,0:T(8,128)S(1)} %get-tuple-element.60), channel_id=1, source_target_pairs={{0,4},{4,8},{8,12},{12,16},{16,20},{20,24},{24,28},{28,0},{1,5},{5... | collective-permute-start | bytes 98312 | tf_op jit(solution)/shard_map/ppermute | solution.py:690
  54.0 4.9 %collective-permute-done.8.rim_ref = f32[8,1024]{1,0:T(8,128)S(1)} collective-permute-done((f32[8,1024]{1,0:T(8,128)S(1)}, f32[8,1024]{1,0:T(8,128)S(1)}, u32[]{:S(2)}, u32[]{:S(2)}) %collective-permute-start.8) | collective-permute-done | bytes 32800 | tf_op jit(solution)/shard_map/ppermute | solution.py:690
  59.0 0.0 copy-start.2
  59.0 4.2 %run_states.3 = (f32[1024,1024]{1,0:T(8,128)S(1)}, f32[1024,128]{1,0:T(8,128)S(1)}, f32[1024,128]{1,0:T(8,128)S(1)}, f32[8,128,768]{2,1,0:T(8,128)S(1)}, f32[8,8,128]{2,1,0:T(8,128)S(1)}) custom-call(s32[2]{0:T(128)S(1)} %pad_add_fusion.index_ref, f32[1024,1024]{1,0:T(8,128)S(1)} %get-tuple-element.51.refs_10_.z_ref.prev_ref, ...), custom_call_target="tpu_custom_call" | custom-call | flops 786432000 | bytes 6291456 | tf_op jit(solution)/shard_map/run_states/pallas_call | solution.py:346
  63.1 0.0 collective-permute-done.6.refs_1_
  63.2 4.0 %project.4 = (f32[1024,1024]{1,0:T(8,128)S(1)}, f32[1024,128]{1,0:T(8,128)S(1)}, bf16[1024,128]{1,0:T(8,128)(2,1)S(1)}) custom-call(s32[2]{0:T(128)S(1)} %pad_add_fusion.index_ref, bf16[128,2560]{1,0:T(8,128)(2,1)} %collective-permute-done.5.refs_0_, ...), custom_call_target="tpu_custom_call", output_to_operand_aliasing={{0}: (11, {}), {1}: (12, {}), {2}: (13, {})} | custom-call | flops 1677721600 | bytes 7602176 | tf_op jit(solution)/shard_map/project/pallas_call | solution.py:166
  67.2 2.4 %run_states.4 = (f32[1024,1024]{1,0:T(8,128)S(1)}, f32[1024,128]{1,0:T(8,128)S(1)}, f32[1024,128]{1,0:T(8,128)S(1)}, f32[8,128,768]{2,1,0:T(8,128)S(1)}, f32[8,8,128]{2,1,0:T(8,128)S(1)}) custom-call(s32[2]{0:T(128)S(1)} %pad_add_fusion.index_ref, ...), custom_call_target="tpu_custom_call", output_to_operand_aliasing={{0}: (12, {}), {1}: (13, {}), {2}: (14, {}), {3}: (15, {}),... | custom-call | flops 393216000 | bytes 3145728 | tf_op jit(solution)/shard_map/run_states/pallas_call | solution.py:346
  69.6 4.0 %project.5 = (f32[1024,1024]{1,0:T(8,128)S(1)}, f32[1024,128]{1,0:T(8,128)S(1)}, bf16[1024,128]{1,0:T(8,128)(2,1)S(1)}) custom-call(s32[2]{0:T(128)S(1)} %pad_add_fusion.index_ref, bf16[128,2560]{1,0:T(8,128)(2,1)} %collective-permute-done.refs_0_.refs_2_, ...), custom_call_target="tpu_custom_call", output_to_operand_aliasing={{0}: (11, {}), {1}: (12, {}), {2}: (13, {})} | custom-call | flops 1677721600 | bytes 7602176 | tf_op jit(solution)/shard_map/project/pallas_call | solution.py:166
  73.6 2.3 %run_states.5 = (f32[1024,1024]{1,0:T(8,128)S(1)}, f32[1024,128]{1,0:T(8,128)S(1)}, f32[1024,128]{1,0:T(8,128)S(1)}, f32[8,128,768]{2,1,0:T(8,128)S(1)}, f32[8,8,128]{2,1,0:T(8,128)S(1)}) custom-call(s32[2]{0:T(128)S(1)} %pad_add_fusion.index_ref, ...), custom_call_target="tpu_custom_call", output_to_operand_aliasing={{0}: (12, {}), {1}: (13, {}), {2}: (14, {}), {3}: (15, {}),... | custom-call | flops 393216000 | bytes 3145728 | tf_op jit(solution)/shard_map/run_states/pallas_call | solution.py:346
  75.9 0.5 stitch.1
  76.4 0.1 collective-permute-start.9
  76.5 6.2 %collective-permute-done.9.got_ref = bf16[136,768]{1,0:T(8,128)(2,1)S(1)} collective-permute-done((bf16[136,768]{1,0:T(8,128)(2,1)S(1)}, bf16[136,768]{1,0:T(8,128)(2,1)S(1)}, u32[]{:S(2)}, u32[]{:S(2)}) %collective-permute-start.9) | collective-permute-done | bytes 208928 | tf_op jit(solution)/shard_map/ppermute | solution.py:20
  82.7 0.7 combine.2
  83.4 0.1 collective-permute-start.10
  83.4 4.2 %gate_project.2.refs_7_ = f32[1024,768]{1,0:T(8,128)S(1)} custom-call(s32[2]{0:T(128)S(1)} %pad_add_fusion.index_ref, bf16[256,2560]{1,0:T(8,128)(2,1)S(1)} %copy-done, bf16[256,2560]{1,0:T(8,128)(2,1)} %collective-permute-done.7.refs_1_, bf16[1024,128]{1,0:T(8,128)(2,1)S(1)} %get-tuple-element.78.refs_2_.refs_4_, bf16[2560,1536]{1,0:T(8,128)(2,1)S(1)} %bitcast.17, ...), custom_call_target="tpu_custom_call" | custom-call | flops 2013265920 | bytes 8126464 | tf_op jit(solution)/shard_map/gate_project/pallas_call | solution.py:218
  87.7 0.0 copy-start.9
  87.7 4.6 %gate_project.3.g_ref = f32[1024,768]{1,0:T(8,128)S(1)} custom-call(s32[2]{0:T(128)S(1)} %pad_add_fusion.index_ref, bf16[128,2560]{1,0:T(8,128)(2,1)} %collective-permute-done.5.refs_0_, bf16[128,2560]{1,0:T(8,128)(2,1)} %collective-permute-done.6.refs_1_, bf16[128,2560]{1,0:T(8,128)(2,1)} %collective-permute-done.refs_0_.refs_2_, ...), custom_call_target="tpu_custom_call", output_to_operand_aliasing={{}: (8, {})} | custom-call | flops 2013265920 | bytes 8126464 | tf_op jit(solution)/shard_map/gate_project/pallas_call | solution.py:218
  92.3 1.4 %combine.3 = (bf16[136,768]{1,0:T(8,128)(2,1)S(1)}, f32[128,768]{1,0:T(8,128)}, f32[8,768]{1,0:T(8,128)}, f32[128,768]{1,0:T(8,128)S(1)}, f32[8,768]{1,0:T(8,128)S(1)}) custom-call(s32[2]{0:T(128)S(1)} %pad_add_fusion.index_ref, bf16[136,768]{1,0:T(8,128)(2,1)S(1)} %collective-permute-done.10.got_ref, f32[128,768]{1,0:T(8,128)S(1)} %get-tuple-element.88.group_ref, ...), custom_call_target="tpu_custom_call" | custom-call | tf_op jit(solution)/shard_map/combine/pallas_call | solution.py:547
  93.7 2.3 %collective-permute-start.11 = (bf16[136,768]{1,0:T(8,128)(2,1)S(1)}, bf16[136,768]{1,0:T(8,128)(2,1)S(1)}, u32[]{:S(2)}, u32[]{:S(2)}) collective-permute-start(bf16[136,768]{1,0:T(8,128)(2,1)S(1)} %get-tuple-element.92), channel_id=1, source_target_pairs={{0,16},{4,20},{8,24},{12,28},{16,0},{20,4},{24,8},{28,12},{1,17},{... | collective-permute-start | bytes 626696 | tf_op jit(solution)/shard_map/ppermute | solution.py:20
  96.0 5.3 %run_outputs.1 = (f32[1024,768]{1,0:T(8,128)S(1)}, f32[1024,768]{1,0:T(8,128)S(1)}, bf16[1024,128]{1,0:T(8,128)(2,1)S(1)}) custom-call(s32[2]{0:T(128)S(1)} %pad_add_fusion.index_ref, f32[1024,1024]{1,0:T(8,128)S(1)} %get-tuple-element.71.xc_ref, f32[1024,128]{1,0:T(8,128)S(1)} %get-tuple-element.72.cum_ref, f32[1024,128]{1,0:T(8,128)S(1)} %get-tuple-element.73.step_ref, ...), custom_call_target="tpu_custom_call" | custom-call | flops 2359296000 | bytes 12582912 | tf_op jit(solution)/shard_map/run_outputs/pallas_call | solution.py:471
  101.3 3.1 %collective-permute-done.11.got_ref = bf16[136,768]{1,0:T(8,128)(2,1)S(1)} collective-permute-done((bf16[136,768]{1,0:T(8,128)(2,1)S(1)}, bf16[136,768]{1,0:T(8,128)(2,1)S(1)}, u32[]{:S(2)}, u32[]{:S(2)}) %collective-permute-start.11) | collective-permute-done | bytes 208928 | tf_op jit(solution)/shard_map/ppermute | solution.py:20
  104.4 3.1 %join.1 = (f32[1024,768]{1,0:T(8,128)S(1)}, f32[1,1024]{1,0:T(1,128)S(1)}) custom-call(s32[2]{0:T(128)S(1)} %pad_add_fusion.index_ref, f32[1024,768]{1,0:T(8,128)S(1)} %get-tuple-element.79.a_ref, f32[1024,768]{1,0:T(8,128)S(1)} %get-tuple-element.80.b_ref, bf16[1024,128]{1,0:T(8,128)(2,1)S(1)} %get-tuple-element.81.c_ref, ...), custom_call_target="tpu_custom_call" | custom-call | tf_op jit(solution)/shard_map/join/pallas_call | solution.py:582
  107.5 1.2 %collective-permute-done.12 = f32[1,1024]{1,0:T(1,128)S(1)} collective-permute-done((f32[1,1024]{1,0:T(1,128)S(1)}, f32[1,1024]{1,0:T(1,128)S(1)}, u32[]{:S(2)}, u32[]{:S(2)}) %collective-permute-start.12) | collective-permute-done | bytes 4128 | tf_op jit(solution)/shard_map/ppermute | solution.py:20
  108.7 1.4 %collective-permute-start.13 = (f32[1,1024]{1,0:T(1,128)S(1)}, f32[1,1024]{1,0:T(1,128)S(1)}, u32[]{:S(2)}, u32[]{:S(2)}) collective-permute-start(f32[1,1024]{1,0:T(1,128)S(1)} %add.5.mine_ref), channel_id=1, source_target_pairs={{0,2},{1,3},{2,0},{3,1},{4,6},{5,7},{6,4},{7,5},{8,10},{9,11},{10,... | collective-permute-start | bytes 12296 | tf_op jit(solution)/shard_map/ppermute | solution.py:20
  110.0 2.2 %collective-permute-done.13.other_ref = f32[1,1024]{1,0:T(1,128)S(1)} collective-permute-done((f32[1,1024]{1,0:T(1,128)S(1)}, f32[1,1024]{1,0:T(1,128)S(1)}, u32[]{:S(2)}, u32[]{:S(2)}) %collective-permute-start.13) | collective-permute-done | bytes 4128 | tf_op jit(solution)/shard_map/ppermute | solution.py:20
  112.3 2.0 %norm.1 = bf16[1024,768]{1,0:T(8,128)(2,1)} custom-call(f32[1024,768]{1,0:T(8,128)S(1)} %get-tuple-element.95.g_ref, f32[1,1024]{1,0:T(1,128)S(1)} %add.5.mine_ref, f32[1,1024]{1,0:T(1,128)S(1)} %collective-permute-done.13.other_ref, f32[1,768]{1,0:T(1,128)S(1)} %broadcast_in_dim.23.gain_ref), custom_call_target="tpu_custom_call" | custom-call | tf_op jit(solution)/shard_map/norm/pallas_call | solution.py:623
  (28 shorter events, 0.1 us)
Async XLA Ops:
  0.0 44.6 %collective-permute-start.7 = (bf16[256,2560]{1,0:T(8,128)(2,1)}, bf16[256,2560]{1,0:T(8,128)(2,1)}, u32[]{:S(2)}, u32[]{:S(2)}) collective-permute-start(bf16[256,2560]{1,0:T(8,128)(2,1)} %refs_0_.3), channel_id=1, source_target_pairs={{0,1},{1,0},{2,3},{3,2},{4,5},{5,4},{6,7},{7,6},{8,9},{9,8},{10,11... | collective-permute-start | bytes 3932168 | tf_op jit(solution)/shard_map/ppermute | solution.py:20
  1.9 18.3 %collective-permute-start.5 = (bf16[128,2560]{1,0:T(8,128)(2,1)S(1)}, bf16[128,2560]{1,0:T(8,128)(2,1)}, u32[]{:S(2)}, u32[]{:S(2)}) collective-permute-start(bf16[128,2560]{1,0:T(8,128)(2,1)S(1)} %get-tuple-element.97), channel_id=1, source_target_pairs={{0,2},{1,3},{2,0},{3,1},{4,6},{5,7},{6,4},{7,5},{8,10},{9,11},{10,... | collective-permute-start | bytes 1966088 | tf_op jit(solution)/shard_map/ppermute | solution.py:20
  4.4 33.8 %collective-permute-start = (bf16[128,2560]{1,0:T(8,128)(2,1)S(1)}, bf16[128,2560]{1,0:T(8,128)(2,1)}, u32[]{:S(2)}, u32[]{:S(2)}) collective-permute-start(bf16[128,2560]{1,0:T(8,128)(2,1)S(1)} %get-tuple-element.98), channel_id=1, source_target_pairs={{0,2},{1,3},{2,0},{3,1},{4,6},{5,7},{6,4},{7,5},{8,10},{9,11},{10,... | collective-permute-start | bytes 1966088 | tf_op jit(solution)/shard_map/ppermute | solution.py:20
  6.9 31.3 %collective-permute-start.3 = (bf16[40,2560]{1,0:T(8,128)(2,1)S(1)}, bf16[40,2560]{1,0:T(8,128)(2,1)S(1)}, u32[]{:S(2)}, u32[]{:S(2)}) collective-permute-start(bf16[40,2560]{1,0:T(8,128)(2,1)S(1)} %fusion.3.refs_2_), channel_id=1, source_target_pairs={{0,2},{1,3},{2,0},{3,1},{4,6},{5,7},{6,4},{7,5},{8,10},{9,11},{10,... | collective-permute-start | bytes 614408 | tf_op jit(solution)/shard_map/ppermute | solution.py:20
  20.1 43.0 %collective-permute-start.6 = (bf16[128,2560]{1,0:T(8,128)(2,1)}, bf16[128,2560]{1,0:T(8,128)(2,1)}, u32[]{:S(2)}, u32[]{:S(2)}) collective-permute-start(bf16[128,2560]{1,0:T(8,128)(2,1)} %collective-permute-done.5.refs_0_), channel_id=1, source_target_pairs={{0,1},{1,0},{2,3},{3,2},{4,5},{5,4},{6,7},{7,6},{8,9},{9,8},{10,11... | collective-permute-start | bytes 1966088 | tf_op jit(solution)/shard_map/ppermute | solution.py:20
  20.1 24.5 %collective-permute-start.2 = (bf16[40,2560]{1,0:T(8,128)(2,1)S(1)}, bf16[40,2560]{1,0:T(8,128)(2,1)S(1)}, u32[]{:S(2)}, u32[]{:S(2)}) collective-permute-start(bf16[40,2560]{1,0:T(8,128)(2,1)S(1)} %fusion.3.refs_2_), channel_id=1, source_target_pairs={{0,1},{1,0},{2,3},{3,2},{4,5},{5,4},{6,7},{7,6},{8,9},{9,8},{10,11... | collective-permute-start | bytes 614408 | tf_op jit(solution)/shard_map/ppermute | solution.py:20
  38.3 6.4 %collective-permute-start.4 = (bf16[40,2560]{1,0:T(8,128)(2,1)S(1)}, bf16[40,2560]{1,0:T(8,128)(2,1)}, u32[]{:S(2)}, u32[]{:S(2)}) collective-permute-start(bf16[40,2560]{1,0:T(8,128)(2,1)S(1)} %collective-permute-done.3.refs_4_), channel_id=1, source_target_pairs={{0,1},{1,0},{2,3},{3,2},{4,5},{5,4},{6,7},{7,6},{8,9},{9,8},{10,11... | collective-permute-start | bytes 614408 | tf_op jit(solution)/shard_map/ppermute | solution.py:20
  38.3 31.3 %collective-permute-start.1 = (bf16[128,2560]{1,0:T(8,128)(2,1)}, bf16[128,2560]{1,0:T(8,128)(2,1)}, u32[]{:S(2)}, u32[]{:S(2)}) collective-permute-start(bf16[128,2560]{1,0:T(8,128)(2,1)} %collective-permute-done.refs_0_.refs_2_), channel_id=1, source_target_pairs={{0,1},{1,0},{2,3},{3,2},{4,5},{5,4},{6,7},{7,6},{8,9},{9,8},{10,11... | collective-permute-start | bytes 1966088 | tf_op jit(solution)/shard_map/ppermute | solution.py:20
  38.9 5.8 %copy-start = (bf16[256,2560]{1,0:T(8,128)(2,1)S(1)}, bf16[256,2560]{1,0:T(8,128)(2,1)}, u32[]{:S(2)}) copy-start(bf16[256,2560]{1,0:T(8,128)(2,1)} %refs_0_.3) | copy-start | bytes 3932164
  38.9 5.8 %copy-start.3 = (bf16[2560,12]{0,1:T(8,128)(2,1)S(1)}, bf16[2560,12]{0,1:T(8,128)(2,1)}, u32[]{:S(2)}) copy-start(bf16[2560,12]{0,1:T(8,128)(2,1)} %param.19) | copy-start | bytes 184324
  44.7 1.3 %copy-start.1 = (bf16[2560,256]{1,0:T(8,128)(2,1)S(1)}, bf16[2560,256]{1,0:T(8,128)(2,1)}, u32[]{:S(2)}) copy-start(bf16[2560,256]{1,0:T(8,128)(2,1)} %refs_8_.5) | copy-start | bytes 3932164
  46.0 8.0 %copy-start.10 = (f32[768]{0:T(1024)S(1)}, f32[768]{0:T(1024)}, u32[]{:S(2)}) copy-start(f32[768]{0:T(1024)} %param.24) | copy-start | bytes 9220
  46.0 12.9 %copy-start.4 = (f32[4,768]{1,0:T(4,128)S(1)}, f32[4,768]{1,0:T(4,128)}, u32[]{:S(2)}) copy-start(f32[4,768]{1,0:T(4,128)} %taps_ref.5) | copy-start | bytes 36868
  46.0 12.9 %copy-start.5 = (f32[4,256]{1,0:T(4,128)S(1)}, f32[4,256]{1,0:T(4,128)}, u32[]{:S(2)}) copy-start(f32[4,256]{1,0:T(4,128)} %mtaps_ref.5) | copy-start | bytes 12292
  46.0 12.9 %copy-start.6 = (f32[256]{0:T(256)S(1)}, f32[256]{0:T(256)}, u32[]{:S(2)}) copy-start(f32[256]{0:T(256)} %param.25) | copy-start | bytes 3076
  46.0 12.9 %copy-start.7 = (f32[12]{0:T(128)S(1)}, f32[12]{0:T(128)}, u32[]{:S(2)}) copy-start(f32[12]{0:T(128)} %param.26) | copy-start | bytes 148
  46.0 12.9 %copy-start.8 = (f32[12]{0:T(128)S(1)}, f32[12]{0:T(128)}, u32[]{:S(2)}) copy-start(f32[12]{0:T(128)} %param.27) | copy-start | bytes 148
  52.0 6.9 %collective-permute-start.8 = (f32[8,1024]{1,0:T(8,128)S(1)}, f32[8,1024]{1,0:T(8,128)S(1)}, u32[]{:S(2)}, u32[]{:S(2)}) collective-permute-start(f32[8,1024]{1,0:T(8,128)S(1)} %get-tuple-element.60), channel_id=1, source_target_pairs={{0,4},{4,8},{8,12},{12,16},{16,20},{20,24},{24,28},{28,0},{1,5},{5... | collective-permute-start | bytes 98312 | tf_op jit(solution)/shard_map/ppermute | solution.py:690
  59.0 4.2 %copy-start.2 = (bf16[2560,256]{1,0:T(8,128)(2,1)S(1)}, bf16[2560,256]{1,0:T(8,128)(2,1)}, u32[]{:S(2)}) copy-start(bf16[2560,256]{1,0:T(8,128)(2,1)} %refs_8_.5) | copy-start | bytes 3932164
  76.4 6.3 %collective-permute-start.9 = (bf16[136,768]{1,0:T(8,128)(2,1)S(1)}, bf16[136,768]{1,0:T(8,128)(2,1)S(1)}, u32[]{:S(2)}, u32[]{:S(2)}) collective-permute-start(bf16[136,768]{1,0:T(8,128)(2,1)S(1)} %get-tuple-element.82), channel_id=1, source_target_pairs={{0,4},{4,0},{8,12},{12,8},{16,20},{20,16},{24,28},{28,24},{1,5},{5... | collective-permute-start | bytes 626696 | tf_op jit(solution)/shard_map/ppermute | solution.py:20
  83.4 8.9 %collective-permute-start.10 = (bf16[136,768]{1,0:T(8,128)(2,1)S(1)}, bf16[136,768]{1,0:T(8,128)(2,1)S(1)}, u32[]{:S(2)}, u32[]{:S(2)}) collective-permute-start(bf16[136,768]{1,0:T(8,128)(2,1)S(1)} %get-tuple-element.87), channel_id=1, source_target_pairs={{0,8},{4,12},{8,0},{12,4},{16,24},{20,28},{24,16},{28,20},{1,9},{5... | collective-permute-start | bytes 626696 | tf_op jit(solution)/shard_map/ppermute | solution.py:20
  87.7 8.3 %copy-start.9 = (f32[12]{0:T(128)S(1)}, f32[12]{0:T(128)}, u32[]{:S(2)}) copy-start(f32[12]{0:T(128)} %param.28) | copy-start | bytes 148
  93.7 10.7 %collective-permute-start.11 = (bf16[136,768]{1,0:T(8,128)(2,1)S(1)}, bf16[136,768]{1,0:T(8,128)(2,1)S(1)}, u32[]{:S(2)}, u32[]{:S(2)}) collective-permute-start(bf16[136,768]{1,0:T(8,128)(2,1)S(1)} %get-tuple-element.92), channel_id=1, source_target_pairs={{0,16},{4,20},{8,24},{12,28},{16,0},{20,4},{24,8},{28,12},{1,17},{... | collective-permute-start | bytes 626696 | tf_op jit(solution)/shard_map/ppermute | solution.py:20
  104.4 5.6 %copy-start.11 = (f32[768]{0:T(1024)S(1)}, f32[768]{0:T(1024)}, u32[]{:S(2)}) copy-start(f32[768]{0:T(1024)} %param.29) | copy-start | bytes 9220
  107.5 1.2 %collective-permute-start.12 = (f32[1,1024]{1,0:T(1,128)S(1)}, f32[1,1024]{1,0:T(1,128)S(1)}, u32[]{:S(2)}, u32[]{:S(2)}) collective-permute-start(f32[1,1024]{1,0:T(1,128)S(1)} %get-tuple-element.96), channel_id=1, source_target_pairs={{0,1},{1,0},{2,3},{3,2},{4,5},{5,4},{6,7},{7,6},{8,9},{9,8},{10,11... | collective-permute-start | bytes 12296 | tf_op jit(solution)/shard_map/ppermute | solution.py:20
  108.7 3.6 %collective-permute-start.13 = (f32[1,1024]{1,0:T(1,128)S(1)}, f32[1,1024]{1,0:T(1,128)S(1)}, u32[]{:S(2)}, u32[]{:S(2)}) collective-permute-start(f32[1,1024]{1,0:T(1,128)S(1)} %add.5.mine_ref), channel_id=1, source_target_pairs={{0,2},{1,3},{2,0},{3,1},{4,6},{5,7},{6,4},{7,5},{8,10},{9,11},{10,... | collective-permute-start | bytes 12296 | tf_op jit(solution)/shard_map/ppermute | solution.py:20

commit v2 on v1

--- a/solution.py
+++ b/solution.py
@@ -42,7 +42,8 @@
 
 
 def silu(v):
-    return v / (1.0 + jnp.exp(-v))
+    half = 0.5 * v
+    return half + half * jnp.tanh(half)
 
 
 def route_mask(e, route_row, experts_dev, rank):
@@ -62,16 +63,53 @@
     )
 
 
+def pack_kernel(tokens_ref, route_ref, *refs):
+    halves, (note_ref, tail, sems) = refs[:-3], refs[-3:]
+    rows = halves[0].shape[0]
+    copies = [
+        pltpu.make_async_copy(tokens_ref.at[q * rows : (q + 1) * rows], half, sems.at[q])
+        for q, half in enumerate(halves)
+    ]
+    last = tokens_ref.shape[0] - 8
+    copies.append(pltpu.make_async_copy(tokens_ref.at[last:], tail, sems.at[len(halves)]))
+    for copy in copies[::-1]:
+        copy.start()
+    copies[-1].wait()
+    route = route_ref[...].astype(F32)
+    route = jnp.concatenate([route, jnp.zeros((1, tail.shape[1] - route.shape[1]), F32)], axis=1)
+    row = lax.broadcasted_iota(jnp.int32, tail.shape, 0)
+    note_ref[...] = jnp.where(row == 0, route, tail[...].astype(F32)).astype(BF16)
+    for copy in copies[:-1]:
+        copy.wait()
+
+
+def pack(tokens, route_row, per):
+    features = tokens.shape[1]
+    anywhere = pl.BlockSpec(memory_space=pl.ANY)
+    piece = jax.ShapeDtypeStruct((CHUNK, features), BF16)
+    return pl.pallas_call(
+        pack_kernel,
+        out_shape=(piece,) * per + (jax.ShapeDtypeStruct((8, features), BF16),),
+        in_specs=[anywhere, VMEM],
+        out_specs=(VMEM,) * (per + 1),
+        scratch_shapes=[pltpu.VMEM((8, features), BF16), pltpu.SemaphoreType.DMA((per + 1,))],
+        compiler_params=pltpu.CompilerParams(vmem_limit_bytes=4 << 20),
+        name="pack",
+    )(tokens, route_row)
+
+
 def project_kernel(cfg, index_ref, *refs):
-    counts, route_from, devices, cols, rank, aliased = cfg
+    counts, route_from, devices, cols, rank, near = cfg
     x_refs, refs = refs[: len(counts)], refs[len(counts):]
-    d_refs, refs = refs[:devices], refs[devices:]
-    dt_ref, w_ref, wbc_ref, up_ref = refs[:4]
-    if aliased:
-        z_ref, dto_ref, lift_ref, x_scr, w_scr = refs[4 + aliased:]
+    n_refs, refs = refs[:devices], refs[devices:]
+    w_ref, wbc_ref, up_ref = refs[:3]
+    refs = refs[3:]
+    if near:
+        dt_ref, d_refs, refs = refs[0], refs[1 : 1 + devices], refs[1 + devices:]
+        z_ref, dto_ref, lift_ref, tails_ref, rim_ref, wsm_ref, x_scr, lift_scr = refs
+    else:
+        wsm_ref, z_ref, dto_ref, lift_ref, x_scr = refs
         lift_scr = lift_ref
-    else:
-        z_ref, dto_ref, lift_ref, tails_ref, rim_ref, x_scr, w_scr, lift_scr = refs[4:]
     e = index_ref[0]
     rows = sum(counts)
 
@@ -79,24 +117,24 @@
     for x_ref, n in zip(x_refs, counts):
         x_scr[at : at + n, :] = x_ref[...]
         at += n
-    if not aliased:
+    if near:
         for r in range(devices):
-            x_scr[at + 8 * r : at + 8 * r + 8, :] = d_refs[r][cols : cols + 8, :]
-    w_scr[LANES:, :] = jnp.zeros((w_scr.shape[0] - LANES, w_scr.shape[1]), BF16)
-    w_scr[LANES : LANES + dt_ref.shape[0], :] = dt_ref[...]
-    for r in range(devices):
-        w_scr[r * cols : (r + 1) * cols, :] = d_refs[r][0:cols, :]
-    small = mm_nt(x_scr[...], w_scr[...])
+            x_scr[at + 8 * r : at + 8 * r + 8, :] = n_refs[r][...]
+        wsm_ref[LANES:, :] = jnp.zeros((wsm_ref.shape[0] - LANES, wsm_ref.shape[1]), BF16)
+        wsm_ref[LANES : LANES + dt_ref.shape[0], :] = dt_ref[...]
+        for r in range(devices):
+            wsm_ref[r * cols : (r + 1) * cols, :] = d_refs[r][...]
+    small = mm_nt(x_scr[...], wsm_ref[...])
 
     def mask_of(r, lane):
-        row = d_refs[r][cols : cols + 1, lane : lane + LANES].astype(F32)
+        row = n_refs[r][0:1, lane : lane + LANES].astype(F32)
         return route_mask(e, row, cols // rank, rank).T
 
     masks = []
     for r, first, n in route_from:
         for lane in range(first, first + n, LANES):
             masks.append(mask_of(r, lane))
-    if not aliased:
+    if near:
         last = route_from[0][1] + route_from[0][2] - LANES
         for r in range(devices):
             masks.append(mask_of(r, last)[LANES - 8 :, :])
@@ -104,12 +142,12 @@
     lift_scr[...] = lift
     pad = jnp.zeros((rows, 2 * LANES - small.shape[1]), F32)
     dto_ref[...] = jnp.concatenate([small[:rows, LANES:], pad], axis=1)
-    if not aliased:
+    if near:
         lift_ref[...] = lift[:rows]
 
     def put(lanes, value):
         z_ref[:, lanes] = value[:rows]
-        if not aliased:
+        if near:
             tails_ref[:, lanes] = value[rows:]
 
     width = z_ref.shape[1]
@@ -121,59 +159,42 @@
         put(slice(at, at + tn), mm(x_scr[...], w_ref[:, lanes]) + mm(lift_scr[...], up))
     for at in range(0, width - inner, tn):
         put(slice(inner + at, inner + at + tn), mm(x_scr[...], wbc_ref[:, at : at + tn]))
-    if not aliased:
+    if near:
         row = ((devices - 1) ^ e) * 8
         rim_ref[...] = tails_ref[pl.ds(pl.multiple_of(row, 8), 8), :]
 
 
-def project(index, xs, route_from, downs, dt_t, wz, wbc, up, rank, total, row_block, buffers):
+def project(index, xs, route_from, notes, wz, wbc, up, rank, dt_t=None, downs=None, wsm=None):
     counts = tuple(x.shape[0] for x in xs)
     rows = sum(counts)
     features = wz.shape[0]
     width = up.shape[1] // 2 + wbc.shape[1]
-    devices = len(downs)
-    args = list(xs) + list(downs) + [dt_t, wz, wbc, up]
-    in_specs = [VMEM] * len(args)
+    devices = len(notes)
+    near = wsm is None
+    args = list(xs) + list(notes) + [wz, wbc, up]
+    args += [dt_t, *downs] if near else [wsm]
     out_shape = [
-        jax.ShapeDtypeStruct((total, width), F32),
-        jax.ShapeDtypeStruct((total, LANES), F32),
-        jax.ShapeDtypeStruct((total, LANES), BF16),
+        jax.ShapeDtypeStruct((rows, width), F32),
+        jax.ShapeDtypeStruct((rows, LANES), F32),
+        jax.ShapeDtypeStruct((rows, LANES), BF16),
     ]
-    out_specs = [
-        pl.BlockSpec((rows, width), lambda t, i: (row_block, 0)),
-        pl.BlockSpec((rows, LANES), lambda t, i: (row_block, 0)),
-        pl.BlockSpec((rows, LANES), lambda t, i: (row_block, 0)),
-    ]
-    extra = 8 * devices if buffers is None else 0
-    scratch = [
-        pltpu.VMEM((rows + extra, features), BF16),
-        pltpu.VMEM((LANES + 16, features), BF16),
-    ]
-    aliases = {}
-    if buffers is None:
+    extra = 8 * devices if near else 0
+    scratch = [pltpu.VMEM((rows + extra, features), BF16)]
+    if near:
         out_shape += [jax.ShapeDtypeStruct((extra, width), F32), jax.ShapeDtypeStruct((8, width), F32)]
-        out_specs += [
-            pl.BlockSpec((extra, width), lambda t, i: (0, 0)),
-            pl.BlockSpec((8, width), lambda t, i: (0, 0)),
-        ]
+        out_shape.append(jax.ShapeDtypeStruct((LANES + 16, features), BF16))
         scratch.append(pltpu.VMEM((rows + extra, LANES), BF16))
-    else:
-        for n, buffer in enumerate(buffers):
-            aliases[1 + len(args)] = n
-            args.append(buffer)
-            in_specs.append(pl.BlockSpec(memory_space=pl.ANY))
-    cfg = (counts, route_from, devices, LANES // devices, rank, len(aliases))
+    cfg = (counts, route_from, devices, LANES // devices, rank, near)
     return pl.pallas_call(
         functools.partial(project_kernel, cfg),
         out_shape=tuple(out_shape),
         grid_spec=pltpu.PrefetchScalarGridSpec(
             num_scalar_prefetch=1,
             grid=(1,),
-            in_specs=in_specs,
-            out_specs=tuple(out_specs),
+            in_specs=[VMEM] * len(args),
+            out_specs=(VMEM,) * len(out_shape),
             scratch_shapes=scratch,
         ),
-        input_output_aliases=aliases,
         cost_estimate=pl.CostEstimate(
             flops=2 * rows * features * (width + 256),
             transcendentals=0,
@@ -186,9 +207,10 @@
     )(index, *args)
 
 
-def gate_kernel(counts, devices, index_ref, *refs):
+def gate_kernel(counts, devices, lifts, index_ref, *refs):
     x_refs, refs = refs[: len(counts)], refs[len(counts):]
-    lift_ref, w_ref, up_ref = refs[:3]
+    lift = jnp.concatenate([r[...] for r in refs[:lifts]], axis=0)
+    w_ref, up_ref = refs[lifts : lifts + 2]
     g_ref, x_scr = refs[-2:]
     at = 0
     for x_ref, n in zip(x_refs, counts):
@@ -199,24 +221,24 @@
     for at in range(0, width, tn):
         lanes = slice(at, at + tn)
         up = up_rows(up_ref, index_ref[0], devices, lanes)
-        g_ref[:, lanes] = mm(x_scr[...], w_ref[:, lanes]) + mm(lift_ref[...], up)
-
-
-def gate_project(index, xs, lift, wz, up, devices, total, row_block, buffer):
+        g_ref[:, lanes] = mm(x_scr[...], w_ref[:, lanes]) + mm(lift, up)
+
+
+def gate_project(index, xs, lifts, wz, up, devices, total, row_block, buffer):
     counts = tuple(x.shape[0] for x in xs)
     rows = sum(counts)
     features = wz.shape[0]
     width = up.shape[1] // 2
     block = lambda t, i: (row_block, 0)
-    in_specs = [VMEM] * len(xs) + [pl.BlockSpec((rows, lift.shape[1]), block), VMEM, VMEM]
-    args = list(xs) + [lift, wz, up]
+    args = list(xs) + list(lifts) + [wz, up]
+    in_specs = [VMEM] * len(args)
     aliases = {}
     if buffer is not None:
         aliases[1 + len(args)] = 0
         args.append(buffer)
         in_specs.append(pl.BlockSpec(memory_space=pl.ANY))
     return pl.pallas_call(
-        functools.partial(gate_kernel, counts, devices),
+        functools.partial(gate_kernel, counts, devices, len(lifts)),
         out_shape=jax.ShapeDtypeStruct((total, width), F32),
         grid_spec=pltpu.PrefetchScalarGridSpec(
             num_scalar_prefetch=1,
@@ -254,14 +276,23 @@
 
 
 def state_kernel(
-    cfg, index_ref, z_ref, d_ref, prev_ref, tails_ref, rim_ref,
+    cfg, index_ref, z_all, d_all, older_all, tails_ref, rim_ref,
     taps_ref, mtaps_ref, bias_ref, mbias_ref, dtb_ref, rate_ref, *refs,
 ):
-    width, where_am_i = cfg
-    xc_ref, cum_ref, step_ref, update_ref, total_ref, ext = refs[-6:]
+    width, per, far, where_am_i = cfg
+    xc_all, cum_all, step_all, update_all, total_all, ext = refs[-6:]
     e = index_ref[0]
     r, q = where_am_i(pl.program_id(0))
     block = r ^ e
+    at = pl.program_id(0) * CHUNK
+    there = pl.ds(pl.multiple_of(at, CHUNK), CHUNK)
+    z_ref, d_ref = z_all.at[there], d_all.at[there]
+    older = at + CHUNK - 8 if far else jnp.maximum(at - 8, 0)
+    prev_ref = older_all.at[pl.ds(pl.multiple_of(older, 8), 8)]
+    chunk = block * per + q
+    here = pl.ds(pl.multiple_of(chunk * CHUNK, CHUNK), CHUNK)
+    xc_ref, cum_ref, step_ref = xc_all.at[here], cum_all.at[here], step_all.at[here]
+    update_ref, total_ref = update_all.at[pl.ds(chunk, 1)], total_all.at[pl.ds(chunk, 1)]
     before = pl.multiple_of((jnp.maximum(block - 1, 0) ^ e) * 8, 8)
     rim = jnp.where(index_ref[1] == 0, 0.0, rim_ref[...])
     first = jnp.where(block == 0, rim, tails_ref[pl.ds(before, 8), :])
@@ -307,8 +338,8 @@
     return jnp.where(r < 2, r * per + q, far)
 
 
-def run_states(index, z, dt, tails, rim, params, width, per, far, buffers):
-    total, wide = z.shape
+def run_states(index, total, z, dt, older, tails, rim, params, width, per, far, buffers):
+    wide = z.shape[1]
     chunks = total // CHUNK
     if far is None:
         steps = 2 * per
@@ -317,34 +348,16 @@
         steps = 2
         at = lambda c: (far[0] + c, far[1])
 
-    def piece(c, i):
-        r, q = at(c)
-        return (piece_index(r, q, per), 0)
-
-    def previous(c, i):
-        r, q = at(c)
-        return (piece_index(r, jnp.maximum(q - 1, 0), per) * (CHUNK // 8) + CHUNK // 8 - 1, 0)
-
-    def place(c, i):
-        r, q = at(c)
-        return (r ^ i[0]) * per + q
-
-    row = lambda c, i: (place(c, i), 0)
-    deep = lambda c, i: (place(c, i), 0, 0)
-    args = [z, dt, z, tails, rim, *params]
-    in_specs = [
-        pl.BlockSpec((CHUNK, wide), piece),
-        pl.BlockSpec((CHUNK, LANES), piece),
-        pl.BlockSpec((8, wide), previous),
-    ] + [VMEM] * (2 + len(params))
+    args = [z, dt, older, tails, rim, *params]
+    in_specs = [VMEM] * len(args)
     aliases = {}
     if buffers is not None:
         for n, buffer in enumerate(buffers):
             aliases[1 + len(args)] = n
             args.append(buffer)
-            in_specs.append(pl.BlockSpec(memory_space=pl.ANY))
-    return pl.pallas_call(
-        functools.partial(state_kernel, (width, at)),
+            in_specs.append(VMEM)
+    return pl.pallas_call(
+        functools.partial(state_kernel, (width, per, far is not None, at)),
         out_shape=(
             jax.ShapeDtypeStruct((total, wide), F32),
             jax.ShapeDtypeStruct((total, LANES), F32),
@@ -356,13 +369,7 @@
             num_scalar_prefetch=1,
             grid=(steps,),
             in_specs=in_specs,
-            out_specs=(
-                pl.BlockSpec((CHUNK, wide), row),
-                pl.BlockSpec((CHUNK, LANES), row),
-                pl.BlockSpec((CHUNK, LANES), row),
-                pl.BlockSpec((1, STATE, width), deep),
-                pl.BlockSpec((1, 8, LANES), deep),
-            ),
+            out_specs=(VMEM,) * 5,
             scratch_shapes=[pltpu.VMEM((CHUNK + 8, wide), F32)],
         ),
         input_output_aliases=aliases,
@@ -419,9 +426,16 @@
 
 
 def output_kernel(
-    width, index_ref, xc_ref, cum_ref, step_ref, before_ref, local_ref, g_ref, direct_ref,
-    a_ref, b_ref, c_ref,
+    width, per, index_ref, xc_all, cum_all, step_all, before_all, local_all, g_all, direct_ref,
+    a_all, b_all, c_all,
 ):
+    c = pl.program_id(0)
+    here = pl.ds(pl.multiple_of(c * CHUNK, CHUNK), CHUNK)
+    piece = piece_index((c // per) ^ index_ref[0], c % per, per)
+    there = pl.ds(pl.multiple_of(piece * CHUNK, CHUNK), CHUNK)
+    xc_ref, cum_ref, step_ref, g_ref = xc_all.at[here], cum_all.at[here], step_all.at[here], g_all.at[there]
+    before_ref, local_ref = before_all.at[pl.ds(c, 1)], local_all.at[pl.ds(c, 1)]
+    a_ref, b_ref, c_ref = a_all.at[here], b_all.at[here], c_all.at[here]
     bmap = xc_ref[:, width : width + STATE]
     cmap = xc_ref[:, width + STATE :]
     cum = cum_ref[...]
@@ -461,15 +475,12 @@
 
 
 def run_outputs(index, xc, cum, step, before, local_states, gate, direct, local):
-    total, wide = xc.shape
+    total, _ = xc.shape
     width = gate.shape[1]
     chunks = total // CHUNK
     per = local // CHUNK
-    const = lambda c, i: (0, 0)
-    row = lambda c, i: (c, 0)
-    deep = lambda c, i: (c, 0, 0)
-    return pl.pallas_call(
-        functools.partial(output_kernel, width),
+    return pl.pallas_call(
+        functools.partial(output_kernel, width, per),
         out_shape=(
             jax.ShapeDtypeStruct((total, width), F32),
             jax.ShapeDtypeStruct((total, width), F32),
@@ -478,20 +489,8 @@
         grid_spec=pltpu.PrefetchScalarGridSpec(
             num_scalar_prefetch=1,
             grid=(chunks,),
-            in_specs=[
-                pl.BlockSpec((CHUNK, wide), row),
-                pl.BlockSpec((CHUNK, LANES), row),
-                pl.BlockSpec((CHUNK, LANES), row),
-                pl.BlockSpec((1, 8, LANES), deep),
-                pl.BlockSpec((1, STATE, width), deep),
-                pl.BlockSpec((CHUNK, width), lambda c, i: (piece_index((c // per) ^ i[0], c % per, per), 0)),
-                pl.BlockSpec(direct.shape, const),
-            ],
-            out_specs=(
-                pl.BlockSpec((CHUNK, width), row),
-                pl.BlockSpec((CHUNK, width), row),
-                pl.BlockSpec((CHUNK, STATE), row),
-            ),
+            in_specs=[VMEM] * 7,
+            out_specs=(VMEM,) * 3,
         ),
         cost_estimate=pl.CostEstimate(
             flops=2 * total * width * 1500, transcendentals=total * width * 4, bytes_accessed=16 * total * width
@@ -559,44 +558,32 @@
 
 
 def join_kernel(d, index_ref, a_ref, b_ref, c_ref, got_ref, prefix_ref, plog_ref, o_ref, ss_ref, s_scr):
-    @pl.when(pl.program_id(0) == 0)
-    def _():
-        other, _ = unpack(got_ref)
-        prefix = prefix_ref[...]
-        upper = (index_ref[1] & d) != 0
-        entering = jnp.where(upper, prefix + jnp.exp(plog_ref[0:1, :]) * other, prefix)
-        s_scr[...] = entering.astype(BF16)
-
-    gated = a_ref[...] + b_ref[...] * mm(c_ref[...], s_scr[...])
-    o_ref[...] = gated
-    hi, lo = split2(gated * gated)
-    ones = jnp.ones((8, 2 * hi.shape[1]), BF16)
-    ss_ref[...] = mm_nt(ones, jnp.concatenate([hi, lo], axis=1))[0:1]
+    other, _ = unpack(got_ref)
+    prefix = prefix_ref[...]
+    upper = (index_ref[1] & d) != 0
+    entering = jnp.where(upper, prefix + jnp.exp(plog_ref[0:1, :]) * other, prefix)
+    s_scr[...] = entering.astype(BF16)
+
+    part = 256
+    ones = jnp.ones((8, 2 * o_ref.shape[1]), BF16)
+    for at in range(0, o_ref.shape[0], part):
+        rows = slice(at, at + part)
+        gated = a_ref[rows, :] + b_ref[rows, :] * mm(c_ref[rows, :], s_scr[...])
+        o_ref[rows, :] = gated
+        hi, lo = split2(gated * gated)
+        ss_ref[:, rows] = mm_nt(ones, jnp.concatenate([hi, lo], axis=1))[0:1]
 
 
 def join(index, d, a, b, c, got, prefix, plog):
     total, width = a.shape
-    rows = 256
-    row = lambda i, s: (i, 0)
-    full = lambda x: pl.BlockSpec(x.shape, lambda i, s: (0, 0))
     return pl.pallas_call(
         functools.partial(join_kernel, d),
         out_shape=(jax.ShapeDtypeStruct((total, width), F32), jax.ShapeDtypeStruct((1, total), F32)),
         grid_spec=pltpu.PrefetchScalarGridSpec(
             num_scalar_prefetch=1,
-            grid=(total // rows,),
-            in_specs=[
-                pl.BlockSpec((rows, width), row),
-                pl.BlockSpec((rows, width), row),
-                pl.BlockSpec((rows, STATE), row),
-                full(got),
-                full(prefix),
-                full(plog),
-            ],
-            out_specs=(
-                pl.BlockSpec((rows, width), row),
-                pl.BlockSpec((1, rows), lambda i, s: (0, i)),
-            ),
+            grid=(1,),
+            in_specs=[VMEM] * 6,
+            out_specs=(VMEM, VMEM),
             scratch_shapes=[pltpu.VMEM((STATE, width), BF16)],
         ),
         compiler_params=pltpu.CompilerParams(
@@ -606,36 +593,35 @@
     )(index, a, b, c, got, prefix, plog)
 
 
-def norm_kernel(inner_width, g_ref, mine_ref, other_ref, gain_ref, o_ref):
-    scale = lax.rsqrt((mine_ref[...] + other_ref[...]) / inner_width + 1e-05)
-    width = g_ref.shape[1]
-    for part in range(g_ref.shape[0] // LANES):
-        rows = slice(part * LANES, (part + 1) * LANES)
-        column = jnp.broadcast_to(scale[:, rows], (LANES, LANES)).T
+def norm_kernel(inner_width, g_ref, gain_ref, *refs):
+    *squares_refs, o_ref = refs
+    rows, width = o_ref.shape
+    base = pl.program_id(0) * rows
+    for part in range(rows // LANES):
+        at = pl.multiple_of(base + part * LANES, LANES)
+        squares = sum(r[:, pl.ds(at, LANES)] for r in squares_refs)
+        scale = lax.rsqrt(squares / inner_width + 1e-05)
+        column = jnp.broadcast_to(scale, (LANES, LANES)).T
         for lane in range(width // LANES):
             lanes = slice(lane * LANES, (lane + 1) * LANES)
-            o_ref[rows, lanes] = (g_ref[rows, lanes] * column * gain_ref[:, lanes]).astype(BF16)
-
-
-def norm(gated, mine, other, gain, inner_width):
+            value = g_ref[pl.ds(at, LANES), lanes] * column * gain_ref[:, lanes]
+            o_ref[part * LANES : (part + 1) * LANES, lanes] = value.astype(BF16)
+
+
+def norm(gated, squares, gain, inner_width):
     total, width = gated.shape
     rows = 256
     return pl.pallas_call(
         functools.partial(norm_kernel, inner_width),
         out_shape=jax.ShapeDtypeStruct((total, width), BF16),
         grid=(total // rows,),
-        in_specs=[
-            pl.BlockSpec((rows, width), lambda i: (i, 0)),
-            pl.BlockSpec((1, rows), lambda i: (0, i)),
-            pl.BlockSpec((1, rows), lambda i: (0, i)),
-            pl.BlockSpec(gain.shape, lambda i: (0, 0)),
-        ],
+        in_specs=[VMEM] * (2 + len(squares)),
         out_specs=pl.BlockSpec((rows, width), lambda i: (i, 0)),
         compiler_params=pltpu.CompilerParams(
             dimension_semantics=("arbitrary",), vmem_limit_bytes=8 << 20
         ),
         name="norm",
-    )(gated, mine, other, gain)
+    )(gated, gain, *squares)
 
 
 def body(
@@ -666,50 +652,55 @@
     index = jnp.stack([e, lax.axis_index("seq")]).astype(jnp.int32)
     per = local // CHUNK
 
-    route_row = jnp.pad(routes.reshape(1, local).astype(BF16), ((0, 0), (0, features - local)))
-    down = {0: jnp.concatenate([adapter_down_weight.T, route_row, tokens[local - 7 :]], axis=0)}
+    down = {0: adapter_down_weight.T}
+    for k in range(2, n, 2):
+        down[k] = swap(down[0], "exp", k)
+    *pieces, note = pack(tokens, routes.reshape(1, local), per)
+    notes = {0: note}
     far = {}
     for k in range(2, n, 2):
-        down[k] = swap(down[0], "exp", k)
+        notes[k] = swap(note, "exp", k)
     for q in range(per):
         for k in range(2, n, 2):
-            far[k, q] = swap(tokens[q * CHUNK : (q + 1) * CHUNK], "exp", k)
+            far[k, q] = swap(pieces[q], "exp", k)
     sibling = swap(tokens, "exp", 1)
     for k in range(0, n, 2):
         down[k + 1] = swap(down[k], "exp", 1)
+        notes[k + 1] = swap(notes[k], "exp", 1)
     downs = [down[k] for k in range(n)]
+    notes = [notes[k] for k in range(n)]
     wz = gate_inner_weight.reshape(features, 2 * width)
     up = adapter_up_weight.reshape(experts, 2 * width)
     call = functools.partial(
-        project, index, downs=downs, dt_t=step_size_weight.T, wz=wz, wbc=state_map_weight,
-        up=up, rank=rank, total=total,
+        project, index, notes=notes, wz=wz, wbc=state_map_weight, up=up, rank=rank
     )
-    *buffers, tails, rim = call(
-        [tokens, sibling], route_from=((0, 0, local), (1, 0, local)), row_block=0, buffers=None
+    z, dt, lift, tails, rim, wsm = call(
+        [tokens, sibling], route_from=((0, 0, local), (1, 0, local)),
+        dt_t=step_size_weight.T, downs=downs,
     )
+    gate = gate_project(index, [tokens, sibling], [lift], wz, up, n, total, 0, None)
     rim = lax.ppermute(rim, "seq", [(i, (i + 1) % shards) for i in range(shards)])
     params = [
         inner_conv_taps, state_map_taps, inner_conv_bias[None, :], state_map_conv_bias[None, :],
         step_size_bias[None, :], head_decay_rate[None, :],
     ]
-    kept = run_states(index, buffers[0], buffers[1], tails, rim, params, width, per, None, None)
+    kept = run_states(index, total, z, dt, z, tails, rim, params, width, per, None, None)
     far_rows = {}
     for q in range(per):
         for k in range(2, n, 2):
             mine = far[k, q]
             other = swap(mine, "exp", 1)
-            far_rows[k, q] = (mine, other)
-            buffers = call(
+            z, dt, lift = call(
                 [mine, other],
                 route_from=((k, q * CHUNK, CHUNK), (k + 1, q * CHUNK, CHUNK)),
-                row_block=per + (k // 2 - 1) * per + q,
-                buffers=buffers,
+                wsm=wsm,
             )
+            far_rows[k, q] = (mine, other, z, lift)
+            older = far_rows[k, max(q - 1, 0)][2]
             kept = run_states(
-                index, buffers[0], buffers[1], tails, rim, params, width, per, (k, q), kept
+                index, total, z, dt, older, tails, rim, params, width, per, (k, q), kept
             )
     xc, cum, step, updates, totals = kept
-    lift = buffers[2]
     states, before, group, glog, send, prefix, plog = stitch(updates, totals)
     d = 1
     while True:
@@ -718,21 +709,16 @@
             break
         send, group, glog, prefix, plog = combine(index, d, got, group, glog, prefix, plog)
         d *= 2
-    gate = gate_project(index, [tokens, sibling], lift, wz, up, n, total, 0, None)
     for k in range(2, n, 2):
-        xs = []
-        for q in range(per):
-            xs.extend(far_rows[k, q])
-        gate = gate_project(index, xs, lift, wz, up, n, total, k // 2, gate)
+        xs = [row for q in range(per) for row in far_rows[k, q][:2]]
+        lifts = [far_rows[k, q][3] for q in range(per)]
+        gate = gate_project(index, xs, lifts, wz, up, n, total, k // 2, gate)
     a, b, c = run_outputs(
         index, xc, cum, step, before, states, gate, direct_head_scale[None, :], local
     )
     gated, mine = join(index, d, a, b, c, got, prefix, plog)
-    d = 1
-    while 2 * d < n:
-        mine = mine + swap(mine, "exp", d)
-        d *= 2
-    return norm(gated, mine, swap(mine, "exp", d), gated_norm_scale[None, :], width * n)
+    others = [swap(mine, "exp", k) for k in range(1, n)]
+    return norm(gated, [mine, *others], gated_norm_scale[None, :], width * n)
 
 
 def solution(mesh):

time: 115 us -> 117 us (1.017)
  starting transfers between devices: 11.9 us -> 15.9 us
  other arithmetic: 1.7 us -> 0.08 us
  waiting for transfers between devices: 46.5 us -> 45 us
  local copies, waits for them, and re-layouts: 9.27 us -> 10.7 us
    ppermute x1, waiting for transfers between devices: 4.92 us -> 0.01 us  [body(): lax.ppermute(rim, 'seq', [(i, (i + 1) % shards) for i in range(shards)])]
    ppermute x13 -> x17, starting transfers between devices: 9.93 us -> 13.9 us  [swap(): lax.ppermute(block, axis, [(i, i ^ mask) for i in range(lax.axis_size(axi...]
    ppermute x13 -> x17, waiting for transfers between devices: 41.6 us -> 45 us  [swap(): lax.ppermute(block, axis, [(i, i ^ mask) for i in range(lax.axis_size(axi...]
    unnamed x26 -> x30, local copies, waits for them, and re-layouts: 7.1 us -> 9.99 us
    slice x2 -> x0, local copies, waits for them, and re-layouts: 2.16 us -> none  [the longest x1 1.37 us: body(): far[k, q] = swap(tokens[q * CHUNK:(q + 1) * CHUNK], 'exp', k)]
    pallas_call x6 -> x7, Pallas kernels: 23.1 us -> 23.5 us  [the longest x2 8.85 us: gate_project(): pl.pallas_call(functools.partial(gate_kernel, counts, devices, len(lifts)...]
  transfers between devices with their start and end apart: 14 -> 18, of which waited for: 7 -> 8; matrix products, arithmetic and copies ran while one was open for 8% -> 6% of each run, Pallas kernels for 27% -> 25%
where the time goes in v2:
time: 117 us; the launch traced here: 116 us
  waiting for transfers between devices  45 us (38%)
  Pallas kernels  44.2 us (38%)
  starting transfers between devices  15.9 us (14%)
  local copies, waits for them, and re-layouts  10.7 us (9%)
    ppermute x17, waiting for transfers between devices, swap(): lax.ppermute(block, axis, [(i, i ^ mask) for i in range(lax.axis_size(axi...  45 us
    pallas_call x3, Pallas kernels, project(): pl.pallas_call(functools.partial(project_kernel, cfg), out_shape=tuple(ou...  14.2 us
    ppermute x17, starting transfers between devices, swap(): lax.ppermute(block, axis, [(i, i ^ mask) for i in range(lax.axis_size(axi...  13.9 us
    unnamed x30, local copies, waits for them, and re-layouts  9.99 us
    pallas_call x2, Pallas kernels, gate_project(): pl.pallas_call(functools.partial(gate_kernel, counts, devices, len(lifts)...  8.85 us
    pallas_call x3, Pallas kernels, run_states(): pl.pallas_call(functools.partial(state_kernel, (width, per, far is not No...  8.68 us
    pallas_call x1, Pallas kernels, run_outputs(): pl.pallas_call(functools.partial(output_kernel, width, per), out_shape=(j...  5.46 us
  transfers between devices with their start and end apart: 18, of which 8 were waited for; matrix products, arithmetic and copies ran while one was open for 6% of the time, Pallas kernels for 25%

profile of v2, /device:TPU:0, one launch (start us, length us, event | category | flops | bytes accessed | tf_op | source)
XLA Modules:
  0.0 116.1 jit_solution(10548079879478761139)
XLA Ops:
  0.0 0.5 collective-permute-start.5
  0.5 1.3 %copy-done.1 = bf16[256,2560]{1,0:T(8,128)(2,1)S(1)} copy-done((bf16[256,2560]{1,0:T(8,128)(2,1)S(1)}, bf16[256,2560]{1,0:T(8,128)(2,1)}, u32[]{:S(2)}) %copy-start.1) | copy-done | bytes 1310744
  1.8 0.7 copy-done.11
  2.5 0.5 pack.1
  3.0 2.6 %collective-permute-start.9 = (bf16[128,2560]{1,0:T(8,128)(2,1)S(1)}, bf16[128,2560]{1,0:T(8,128)(2,1)}, u32[]{:S(2)}, u32[]{:S(2)}) collective-permute-start(bf16[128,2560]{1,0:T(8,128)(2,1)S(1)} %get-tuple-element.60), channel_id=1, source_target_pairs={{0,2},{1,3},{2,0},{3,1},{4,6},{5,7},{6,4},{7,5},{8,10},{9,11},{10,... | collective-permute-start | bytes 1966088 | tf_op jit(solution)/shard_map/ppermute | solution.py:20
  5.5 0.1 collective-permute-start
  5.6 15.6 %collective-permute-done.9.refs_0_ = bf16[128,2560]{1,0:T(8,128)(2,1)} collective-permute-done((bf16[128,2560]{1,0:T(8,128)(2,1)S(1)}, bf16[128,2560]{1,0:T(8,128)(2,1)}, u32[]{:S(2)}, u32[]{:S(2)}) %collective-permute-start.9) | collective-permute-done | bytes 655392 | tf_op jit(solution)/shard_map/ppermute | solution.py:20
  21.2 2.0 %collective-permute-start.7 = (bf16[32,2560]{1,0:T(8,128)(2,1)}, bf16[32,2560]{1,0:T(8,128)(2,1)}, u32[]{:S(2)}, u32[]{:S(2)}) collective-permute-start(bf16[32,2560]{1,0:T(8,128)(2,1)} %bitcast.23), channel_id=1, source_target_pairs={{0,2},{1,3},{2,0},{3,1},{4,6},{5,7},{6,4},{7,5},{8,10},{9,11},{10,... | collective-permute-start | bytes 491528 | tf_op jit(solution)/shard_map/ppermute | solution.py:20
  23.3 0.0 collective-permute-start.3
  23.3 16.1 %collective-permute-done.3.refs_4_ = bf16[8,2560]{1,0:T(8,128)(2,1)S(1)} collective-permute-done((bf16[8,2560]{1,0:T(8,128)(2,1)S(1)}, bf16[8,2560]{1,0:T(8,128)(2,1)S(1)}, u32[]{:S(2)}, u32[]{:S(2)}) %collective-permute-start.3) | collective-permute-done | bytes 40992 | tf_op jit(solution)/shard_map/ppermute | solution.py:20
  39.4 1.2 %collective-permute-done.2.refs_3_ = bf16[8,2560]{1,0:T(8,128)(2,1)S(1)} collective-permute-done((bf16[8,2560]{1,0:T(8,128)(2,1)S(1)}, bf16[8,2560]{1,0:T(8,128)(2,1)S(1)}, u32[]{:S(2)}, u32[]{:S(2)}) %collective-permute-start.2) | collective-permute-done | bytes 40992 | tf_op jit(solution)/shard_map/ppermute | solution.py:20
  40.6 0.2 collective-permute-start.4
  40.8 0.3 collective-permute-start.1
  41.1 0.7 collective-permute-done.4.refs_5_
  41.8 0.2 collective-permute-start.6
  42.0 0.3 collective-permute-start.8
  42.3 0.7 broadcast_in_dim.18.bias_ref
  43.0 1.0 copy.28
  44.1 0.0 copy-start
  44.1 4.7 %copy.27 = bf16[320,8,2,768]{3,1,2,0:T(8,128)(2,1)S(1)} copy(bf16[320,8,2,768]{3,2,1,0:T(2,128)(2,1)} %bitcast.38) | data formatting | bytes 15728640
  48.8 0.1 pad_add_fusion.index_ref
  48.9 1.3 %copy-done.2 = bf16[256,2560]{1,0:T(8,128)(2,1)S(1)} copy-done((bf16[256,2560]{1,0:T(8,128)(2,1)S(1)}, bf16[256,2560]{1,0:T(8,128)(2,1)}, u32[]{:S(2)}) %copy-start.2) | copy-done | bytes 1310744
  50.2 0.9 copy-done.6
  51.1 6.3 %project.3 = (f32[512,1024]{1,0:T(8,128)S(1)}, f32[512,128]{1,0:T(8,128)S(1)}, bf16[512,128]{1,0:T(8,128)(2,1)S(1)}, f32[32,1024]{1,0:T(8,128)S(1)}, f32[8,1024]...) custom-call(s32[2]{0:T(128)S(1)} %pad_add_fusion.index_ref, bf16[256,2560]{1,0:T(8,128)(2,1)S(1)} %copy-done.2, ...), custom_call_target="tpu_custom_call" | custom-call | flops 3355443200 | bytes 9961472 | tf_op jit(solution)/shard_map/project/pallas_call | solution.py:188
  57.4 1.9 %collective-permute-start.11 = (f32[8,1024]{1,0:T(8,128)S(1)}, f32[8,1024]{1,0:T(8,128)S(1)}, u32[]{:S(2)}, u32[]{:S(2)}) collective-permute-start(f32[8,1024]{1,0:T(8,128)S(1)} %get-tuple-element.63), channel_id=1, source_target_pairs={{0,4},{4,8},{8,12},{12,16},{16,20},{20,24},{24,28},{28,0},{1,5},{5... | collective-permute-start | bytes 98312 | tf_op jit(solution)/shard_map/ppermute | solution.py:682
  59.3 4.0 %project.5 = (f32[256,1024]{1,0:T(8,128)S(1)}, f32[256,128]{1,0:T(8,128)S(1)}, bf16[256,128]{1,0:T(8,128)(2,1)S(1)}) custom-call(s32[2]{0:T(128)S(1)} %pad_add_fusion.index_ref, bf16[128,2560]{1,0:T(8,128)(2,1)} %collective-permute-done.9.refs_0_, bf16[128,2560]{1,0:T(8,128)(2,1)} %collective-permute-done.10.refs_1_, ...), custom_call_target="tpu_custom_call" | custom-call | flops 1677721600 | bytes 7602176 | tf_op jit(solution)/shard_map/project/pallas_call | solution.py:188
  63.4 4.0 %project.4 = (f32[256,1024]{1,0:T(8,128)S(1)}, f32[256,128]{1,0:T(8,128)S(1)}, bf16[256,128]{1,0:T(8,128)(2,1)S(1)}) custom-call(s32[2]{0:T(128)S(1)} %pad_add_fusion.index_ref, bf16[128,2560]{1,0:T(8,128)(2,1)} %collective-permute-done.refs_0_.refs_2_, bf16[128,2560]{1,0:T(8,128)(2,1)} %collective-permute-done.1.refs_1_.refs_3_, ...), custom_call_target="tpu_custom_call" | custom-call | flops 1677721600 | bytes 7602176 | tf_op jit(solution)/shard_map/project/pallas_call | solution.py:188
  67.4 4.1 %run_states.3 = (f32[1024,1024]{1,0:T(8,128)S(1)}, f32[1024,128]{1,0:T(8,128)S(1)}, f32[1024,128]{1,0:T(8,128)S(1)}, f32[8,128,768]{2,1,0:T(8,128)S(1)}, f32[8,8,128]{2,1,0:T(8,128)S(1)}) custom-call(s32[2]{0:T(128)S(1)} %pad_add_fusion.index_ref, f32[512,1024]{1,0:T(8,128)S(1)} %get-tuple-element.65.z_all.older_all, ...), custom_call_target="tpu_custom_call" | custom-call | flops 786432000 | bytes 6291456 | tf_op jit(solution)/shard_map/run_states/pallas_call | solution.py:359
  71.5 2.3 %run_states.4 = (f32[1024,1024]{1,0:T(8,128)S(1)}, f32[1024,128]{1,0:T(8,128)S(1)}, f32[1024,128]{1,0:T(8,128)S(1)}, f32[8,128,768]{2,1,0:T(8,128)S(1)}, f32[8,8,128]{2,1,0:T(8,128)S(1)}) custom-call(s32[2]{0:T(128)S(1)} %pad_add_fusion.index_ref, ...), custom_call_target="tpu_custom_call", output_to_operand_aliasing={{0}: (12, {}), {1}: (13, {}), {2}: (14, {}), {3}: (15, {}),... | custom-call | flops 393216000 | bytes 3145728 | tf_op jit(solution)/shard_map/run_states/pallas_call | solution.py:359
  73.8 2.3 %run_states.5 = (f32[1024,1024]{1,0:T(8,128)S(1)}, f32[1024,128]{1,0:T(8,128)S(1)}, f32[1024,128]{1,0:T(8,128)S(1)}, f32[8,128,768]{2,1,0:T(8,128)S(1)}, f32[8,8,128]{2,1,0:T(8,128)S(1)}) custom-call(s32[2]{0:T(128)S(1)} %pad_add_fusion.index_ref, ...), custom_call_target="tpu_custom_call", output_to_operand_aliasing={{0}: (12, {}), {1}: (13, {}), {2}: (14, {}), {3}: (15, {}),... | custom-call | flops 393216000 | bytes 3145728 | tf_op jit(solution)/shard_map/run_states/pallas_call | solution.py:359
  76.2 0.5 stitch.1
  76.6 1.6 %collective-permute-start.12 = (bf16[136,768]{1,0:T(8,128)(2,1)S(1)}, bf16[136,768]{1,0:T(8,128)(2,1)S(1)}, u32[]{:S(2)}, u32[]{:S(2)}) collective-permute-start(bf16[136,768]{1,0:T(8,128)(2,1)S(1)} %get-tuple-element.90), channel_id=1, source_target_pairs={{0,4},{4,0},{8,12},{12,8},{16,20},{20,16},{24,28},{28,24},{1,5},{5... | collective-permute-start | bytes 626696 | tf_op jit(solution)/shard_map/ppermute | solution.py:20
  78.2 5.4 %collective-permute-done.12.got_ref = bf16[136,768]{1,0:T(8,128)(2,1)S(1)} collective-permute-done((bf16[136,768]{1,0:T(8,128)(2,1)S(1)}, bf16[136,768]{1,0:T(8,128)(2,1)S(1)}, u32[]{:S(2)}, u32[]{:S(2)}) %collective-permute-start.12) | collective-permute-done | bytes 208928 | tf_op jit(solution)/shard_map/ppermute | solution.py:20
  83.6 0.7 combine.2
  84.3 1.6 %collective-permute-start.13 = (bf16[136,768]{1,0:T(8,128)(2,1)S(1)}, bf16[136,768]{1,0:T(8,128)(2,1)S(1)}, u32[]{:S(2)}, u32[]{:S(2)}) collective-permute-start(bf16[136,768]{1,0:T(8,128)(2,1)S(1)} %get-tuple-element.95), channel_id=1, source_target_pairs={{0,8},{4,12},{8,0},{12,4},{16,24},{20,28},{24,16},{28,20},{1,9},{5... | collective-permute-start | bytes 626696 | tf_op jit(solution)/shard_map/ppermute | solution.py:20
  86.0 4.2 %gate_project.2.refs_8_ = f32[1024,768]{1,0:T(8,128)S(1)} custom-call(s32[2]{0:T(128)S(1)} %pad_add_fusion.index_ref, bf16[256,2560]{1,0:T(8,128)(2,1)S(1)} %copy-done.3, bf16[256,2560]{1,0:T(8,128)(2,1)} %collective-permute-done.5.refs_1_, bf16[512,128]{1,0:T(8,128)(2,1)S(1)} %get-tuple-element.86.refs_2_, bf16[2560,1536]{1,0:T(8,128)(2,1)S(1)} %bitcast.16, ...), custom_call_target="tpu_custom_call" | custom-call | flops 2013265920 | bytes 8126464 | tf_op jit(solution)/shard_map/gate_project/pallas_call | solution.py:240
  90.2 4.6 %gate_project.3.g_all = f32[1024,768]{1,0:T(8,128)S(1)} custom-call(s32[2]{0:T(128)S(1)} %pad_add_fusion.index_ref, bf16[128,2560]{1,0:T(8,128)(2,1)} %collective-permute-done.9.refs_0_, bf16[128,2560]{1,0:T(8,128)(2,1)} %collective-permute-done.10.refs_1_, bf16[128,2560]{1,0:T(8,128)(2,1)} %collective-permute-done.refs_0_.refs_2_, ...), custom_call_target="tpu_custom_call", output_to_operand_aliasing={{}: (9, {})} | custom-call | flops 2013265920 | bytes 8126464 | tf_op jit(solution)/shard_map/gate_project/pallas_call | solution.py:240
  94.9 1.4 %combine.3 = (bf16[136,768]{1,0:T(8,128)(2,1)S(1)}, f32[128,768]{1,0:T(8,128)}, f32[8,768]{1,0:T(8,128)}, f32[128,768]{1,0:T(8,128)S(1)}, f32[8,768]{1,0:T(8,128)S(1)}) custom-call(s32[2]{0:T(128)S(1)} %pad_add_fusion.index_ref, bf16[136,768]{1,0:T(8,128)(2,1)S(1)} %collective-permute-done.13.got_ref, f32[128,768]{1,0:T(8,128)S(1)} %get-tuple-element.96.group_ref, ...), custom_call_target="tpu_custom_call" | custom-call | tf_op jit(solution)/shard_map/combine/pallas_call | solution.py:546
  96.2 2.6 %collective-permute-start.14 = (bf16[136,768]{1,0:T(8,128)(2,1)S(1)}, bf16[136,768]{1,0:T(8,128)(2,1)S(1)}, u32[]{:S(2)}, u32[]{:S(2)}) collective-permute-start(bf16[136,768]{1,0:T(8,128)(2,1)S(1)} %get-tuple-element.100), channel_id=1, source_target_pairs={{0,16},{4,20},{8,24},{12,28},{16,0},{20,4},{24,8},{28,12},{1,17},{... | collective-permute-start | bytes 626696 | tf_op jit(solution)/shard_map/ppermute | solution.py:20
  98.9 5.5 %run_outputs.1 = (f32[1024,768]{1,0:T(8,128)S(1)}, f32[1024,768]{1,0:T(8,128)S(1)}, bf16[1024,128]{1,0:T(8,128)(2,1)S(1)}) custom-call(s32[2]{0:T(128)S(1)} %pad_add_fusion.index_ref, f32[1024,1024]{1,0:T(8,128)S(1)} %get-tuple-element.77.xc_all, f32[1024,128]{1,0:T(8,128)S(1)} %get-tuple-element.78.cum_all, f32[1024,128]{1,0:T(8,128)S(1)} %get-tuple-element.79.step_all, ...), custom_call_target="tpu_custom_call" | custom-call | flops 2359296000 | bytes 12582912 | tf_op jit(solution)/shard_map/run_outputs/pallas_call | solution.py:482
  104.3 3.0 %collective-permute-done.14.got_ref = bf16[136,768]{1,0:T(8,128)(2,1)S(1)} collective-permute-done((bf16[136,768]{1,0:T(8,128)(2,1)S(1)}, bf16[136,768]{1,0:T(8,128)(2,1)S(1)}, u32[]{:S(2)}, u32[]{:S(2)}) %collective-permute-start.14) | collective-permute-done | bytes 208928 | tf_op jit(solution)/shard_map/ppermute | solution.py:20
  107.4 1.9 %join.1 = (f32[1024,768]{1,0:T(8,128)S(1)}, f32[1,1024]{1,0:T(1,128)S(1)}) custom-call(s32[2]{0:T(128)S(1)} %pad_add_fusion.index_ref, f32[1024,768]{1,0:T(8,128)S(1)} %get-tuple-element.87.a_ref, f32[1024,768]{1,0:T(8,128)S(1)} %get-tuple-element.88.b_ref, bf16[1024,128]{1,0:T(8,128)(2,1)S(1)} %get-tuple-element.89.c_ref, ...), custom_call_target="tpu_custom_call" | custom-call | tf_op jit(solution)/shard_map/join/pallas_call | solution.py:579
  109.3 1.2 collective-permute-start.17
  110.4 0.5 collective-permute-start.16
  110.9 0.2 collective-permute-start.15
  111.2 1.2 %collective-permute-done.17.refs_3_ = f32[1,1024]{1,0:T(1,128)S(1)} collective-permute-done((f32[1,1024]{1,0:T(1,128)S(1)}, f32[1,1024]{1,0:T(1,128)S(1)}, u32[]{:S(2)}, u32[]{:S(2)}) %collective-permute-start.17) | collective-permute-done | bytes 4128 | tf_op jit(solution)/shard_map/ppermute | solution.py:20
  112.3 1.7 %collective-permute-done.16.refs_2_ = f32[1,1024]{1,0:T(1,128)S(1)} collective-permute-done((f32[1,1024]{1,0:T(1,128)S(1)}, f32[1,1024]{1,0:T(1,128)S(1)}, u32[]{:S(2)}, u32[]{:S(2)}) %collective-permute-start.16) | collective-permute-done | bytes 4128 | tf_op jit(solution)/shard_map/ppermute | solution.py:20
  114.0 2.0 %norm.1 = bf16[1024,768]{1,0:T(8,128)(2,1)} custom-call(f32[1024,768]{1,0:T(8,128)S(1)} %get-tuple-element.103.g_ref, f32[1,768]{1,0:T(1,128)S(1)} %broadcast_in_dim.23.gain_ref, f32[1,1024]{1,0:T(1,128)S(1)} %get-tuple-element.104.refs_0_, f32[1,1024]{1,0:T(1,128)S(1)} %collective-permute-done.15.refs_1_, f32[1,1024]{1,0:T(1,128)S(1)} %collective-permute-done.16.refs_2_, ...), custom_call_target="tpu_custom_call" | custom-call | tf_op jit(solution)/shard_map/norm/pallas_call | solution.py:614
  (36 shorter events, 0.1 us)
Async XLA Ops:
  0.0 48.9 %collective-permute-start.5 = (bf16[256,2560]{1,0:T(8,128)(2,1)}, bf16[256,2560]{1,0:T(8,128)(2,1)}, u32[]{:S(2)}, u32[]{:S(2)}) collective-permute-start(bf16[256,2560]{1,0:T(8,128)(2,1)} %refs_0_.3), channel_id=1, source_target_pairs={{0,1},{1,0},{2,3},{3,2},{4,5},{5,4},{6,7},{7,6},{8,9},{9,8},{10,11... | collective-permute-start | bytes 3932168 | tf_op jit(solution)/shard_map/ppermute | solution.py:20
  0.5 1.3 %copy-start.1 = (bf16[256,2560]{1,0:T(8,128)(2,1)S(1)}, bf16[256,2560]{1,0:T(8,128)(2,1)}, u32[]{:S(2)}) copy-start(bf16[256,2560]{1,0:T(8,128)(2,1)} %refs_0_.3) | copy-start | bytes 3932164
  1.8 0.7 copy-start.11
  3.0 18.3 %collective-permute-start.9 = (bf16[128,2560]{1,0:T(8,128)(2,1)S(1)}, bf16[128,2560]{1,0:T(8,128)(2,1)}, u32[]{:S(2)}, u32[]{:S(2)}) collective-permute-start(bf16[128,2560]{1,0:T(8,128)(2,1)S(1)} %get-tuple-element.60), channel_id=1, source_target_pairs={{0,2},{1,3},{2,0},{3,1},{4,6},{5,7},{6,4},{7,5},{8,10},{9,11},{10,... | collective-permute-start | bytes 1966088 | tf_op jit(solution)/shard_map/ppermute | solution.py:20
  5.5 35.2 %collective-permute-start = (bf16[128,2560]{1,0:T(8,128)(2,1)S(1)}, bf16[128,2560]{1,0:T(8,128)(2,1)}, u32[]{:S(2)}, u32[]{:S(2)}) collective-permute-start(bf16[128,2560]{1,0:T(8,128)(2,1)S(1)} %get-tuple-element.55), channel_id=1, source_target_pairs={{0,2},{1,3},{2,0},{3,1},{4,6},{5,7},{6,4},{7,5},{8,10},{9,11},{10,... | collective-permute-start | bytes 1966088 | tf_op jit(solution)/shard_map/ppermute | solution.py:20
  21.2 38.1 %collective-permute-start.10 = (bf16[128,2560]{1,0:T(8,128)(2,1)}, bf16[128,2560]{1,0:T(8,128)(2,1)}, u32[]{:S(2)}, u32[]{:S(2)}) collective-permute-start(bf16[128,2560]{1,0:T(8,128)(2,1)} %collective-permute-done.9.refs_0_), channel_id=1, source_target_pairs={{0,1},{1,0},{2,3},{3,2},{4,5},{5,4},{6,7},{7,6},{8,9},{9,8},{10,11... | collective-permute-start | bytes 1966088 | tf_op jit(solution)/shard_map/ppermute | solution.py:20
  21.2 20.7 %collective-permute-start.7 = (bf16[32,2560]{1,0:T(8,128)(2,1)}, bf16[32,2560]{1,0:T(8,128)(2,1)}, u32[]{:S(2)}, u32[]{:S(2)}) collective-permute-start(bf16[32,2560]{1,0:T(8,128)(2,1)} %bitcast.23), channel_id=1, source_target_pairs={{0,2},{1,3},{2,0},{3,1},{4,6},{5,7},{6,4},{7,5},{8,10},{9,11},{10,... | collective-permute-start | bytes 491528 | tf_op jit(solution)/shard_map/ppermute | solution.py:20
  23.3 16.1 %collective-permute-start.3 = (bf16[8,2560]{1,0:T(8,128)(2,1)S(1)}, bf16[8,2560]{1,0:T(8,128)(2,1)S(1)}, u32[]{:S(2)}, u32[]{:S(2)}) collective-permute-start(bf16[8,2560]{1,0:T(8,128)(2,1)S(1)} %get-tuple-element.56.refs_2_), channel_id=1, source_target_pairs={{0,2},{1,3},{2,0},{3,1},{4,6},{5,7},{6,4},{7,5},{8,10},{9,11},{10,... | collective-permute-start | bytes 122888 | tf_op jit(solution)/shard_map/ppermute | solution.py:20
  39.4 1.2 %collective-permute-start.2 = (bf16[8,2560]{1,0:T(8,128)(2,1)S(1)}, bf16[8,2560]{1,0:T(8,128)(2,1)S(1)}, u32[]{:S(2)}, u32[]{:S(2)}) collective-permute-start(bf16[8,2560]{1,0:T(8,128)(2,1)S(1)} %get-tuple-element.56.refs_2_), channel_id=1, source_target_pairs={{0,1},{1,0},{2,3},{3,2},{4,5},{5,4},{6,7},{7,6},{8,9},{9,8},{10,11... | collective-permute-start | bytes 122888 | tf_op jit(solution)/shard_map/ppermute | solution.py:20
  40.6 1.2 %collective-permute-start.4 = (bf16[8,2560]{1,0:T(8,128)(2,1)S(1)}, bf16[8,2560]{1,0:T(8,128)(2,1)S(1)}, u32[]{:S(2)}, u32[]{:S(2)}) collective-permute-start(bf16[8,2560]{1,0:T(8,128)(2,1)S(1)} %collective-permute-done.3.refs_4_), channel_id=1, source_target_pairs={{0,1},{1,0},{2,3},{3,2},{4,5},{5,4},{6,7},{7,6},{8,9},{9,8},{10,11... | collective-permute-start | bytes 122888 | tf_op jit(solution)/shard_map/ppermute | solution.py:20
  40.8 22.6 %collective-permute-start.1 = (bf16[128,2560]{1,0:T(8,128)(2,1)}, bf16[128,2560]{1,0:T(8,128)(2,1)}, u32[]{:S(2)}, u32[]{:S(2)}) collective-permute-start(bf16[128,2560]{1,0:T(8,128)(2,1)} %collective-permute-done.refs_0_.refs_2_), channel_id=1, source_target_pairs={{0,1},{1,0},{2,3},{3,2},{4,5},{5,4},{6,7},{7,6},{8,9},{9,8},{10,11... | collective-permute-start | bytes 1966088 | tf_op jit(solution)/shard_map/ppermute | solution.py:20
  41.8 7.1 %collective-permute-start.6 = (bf16[32,2560]{1,0:T(8,128)(2,1)}, bf16[32,2560]{1,0:T(8,128)(2,1)}, u32[]{:S(2)}, u32[]{:S(2)}) collective-permute-start(bf16[32,2560]{1,0:T(8,128)(2,1)} %bitcast.24), channel_id=1, source_target_pairs={{0,1},{1,0},{2,3},{3,2},{4,5},{5,4},{6,7},{7,6},{8,9},{9,8},{10,11... | collective-permute-start | bytes 491528 | tf_op jit(solution)/shard_map/ppermute | solution.py:20
  42.0 6.9 %collective-permute-start.8 = (bf16[32,2560]{1,0:T(8,128)(2,1)}, bf16[32,2560]{1,0:T(8,128)(2,1)}, u32[]{:S(2)}, u32[]{:S(2)}) collective-permute-start(bf16[32,2560]{1,0:T(8,128)(2,1)} %collective-permute-done.7.refs_12_), channel_id=1, source_target_pairs={{0,1},{1,0},{2,3},{3,2},{4,5},{5,4},{6,7},{7,6},{8,9},{9,8},{10,11... | collective-permute-start | bytes 491528 | tf_op jit(solution)/shard_map/ppermute | solution.py:20
  44.1 4.8 %copy-start = (bf16[2560,256]{1,0:T(8,128)(2,1)S(1)}, bf16[2560,256]{1,0:T(8,128)(2,1)}, u32[]{:S(2)}) copy-start(bf16[2560,256]{1,0:T(8,128)(2,1)} %refs_7_.5) | copy-start | bytes 3932164
  44.1 4.8 %copy-start.4 = (bf16[2560,32]{0,1:T(8,128)(2,1)S(1)}, bf16[2560,32]{0,1:T(8,128)(2,1)}, u32[]{:S(2)}) copy-start(bf16[2560,32]{0,1:T(8,128)(2,1)} %param.20) | copy-start | bytes 491524
  48.9 1.3 %copy-start.2 = (bf16[256,2560]{1,0:T(8,128)(2,1)S(1)}, bf16[256,2560]{1,0:T(8,128)(2,1)}, u32[]{:S(2)}) copy-start(bf16[256,2560]{1,0:T(8,128)(2,1)} %refs_0_.3) | copy-start | bytes 3932164
  50.2 0.9 copy-start.6
  57.4 10.0 %collective-permute-start.11 = (f32[8,1024]{1,0:T(8,128)S(1)}, f32[8,1024]{1,0:T(8,128)S(1)}, u32[]{:S(2)}, u32[]{:S(2)}) collective-permute-start(f32[8,1024]{1,0:T(8,128)S(1)} %get-tuple-element.63), channel_id=1, source_target_pairs={{0,4},{4,8},{8,12},{12,16},{16,20},{20,24},{24,28},{28,0},{1,5},{5... | collective-permute-start | bytes 98312 | tf_op jit(solution)/shard_map/ppermute | solution.py:682
  63.3 4.1 %copy-start.5 = (f32[4,768]{1,0:T(4,128)S(1)}, f32[4,768]{1,0:T(4,128)}, u32[]{:S(2)}) copy-start(f32[4,768]{1,0:T(4,128)} %taps_ref.5) | copy-start | bytes 36868
  63.3 4.1 %copy-start.7 = (f32[4,256]{1,0:T(4,128)S(1)}, f32[4,256]{1,0:T(4,128)}, u32[]{:S(2)}) copy-start(f32[4,256]{1,0:T(4,128)} %mtaps_ref.5) | copy-start | bytes 12292
  63.3 4.1 %copy-start.8 = (f32[256]{0:T(256)S(1)}, f32[256]{0:T(256)}, u32[]{:S(2)}) copy-start(f32[256]{0:T(256)} %param.25) | copy-start | bytes 3076
  63.4 4.1 %copy-start.9 = (f32[12]{0:T(128)S(1)}, f32[12]{0:T(128)}, u32[]{:S(2)}) copy-start(f32[12]{0:T(128)} %param.26) | copy-start | bytes 148
  63.4 4.1 %copy-start.10 = (f32[12]{0:T(128)S(1)}, f32[12]{0:T(128)}, u32[]{:S(2)}) copy-start(f32[12]{0:T(128)} %param.27) | copy-start | bytes 148
  76.1 9.8 %copy-start.3 = (bf16[256,2560]{1,0:T(8,128)(2,1)S(1)}, bf16[256,2560]{1,0:T(8,128)(2,1)}, u32[]{:S(2)}) copy-start(bf16[256,2560]{1,0:T(8,128)(2,1)} %refs_0_.3) | copy-start | bytes 3932164
  76.6 7.0 %collective-permute-start.12 = (bf16[136,768]{1,0:T(8,128)(2,1)S(1)}, bf16[136,768]{1,0:T(8,128)(2,1)S(1)}, u32[]{:S(2)}, u32[]{:S(2)}) collective-permute-start(bf16[136,768]{1,0:T(8,128)(2,1)S(1)} %get-tuple-element.90), channel_id=1, source_target_pairs={{0,4},{4,0},{8,12},{12,8},{16,20},{20,16},{24,28},{28,24},{1,5},{5... | collective-permute-start | bytes 626696 | tf_op jit(solution)/shard_map/ppermute | solution.py:20
  84.3 10.5 %collective-permute-start.13 = (bf16[136,768]{1,0:T(8,128)(2,1)S(1)}, bf16[136,768]{1,0:T(8,128)(2,1)S(1)}, u32[]{:S(2)}, u32[]{:S(2)}) collective-permute-start(bf16[136,768]{1,0:T(8,128)(2,1)S(1)} %get-tuple-element.95), channel_id=1, source_target_pairs={{0,8},{4,12},{8,0},{12,4},{16,24},{20,28},{24,16},{28,20},{1,9},{5... | collective-permute-start | bytes 626696 | tf_op jit(solution)/shard_map/ppermute | solution.py:20
  90.2 8.6 %copy-start.12 = (f32[12]{0:T(128)S(1)}, f32[12]{0:T(128)}, u32[]{:S(2)}) copy-start(f32[12]{0:T(128)} %param.28) | copy-start | bytes 148
  96.2 11.1 %collective-permute-start.14 = (bf16[136,768]{1,0:T(8,128)(2,1)S(1)}, bf16[136,768]{1,0:T(8,128)(2,1)S(1)}, u32[]{:S(2)}, u32[]{:S(2)}) collective-permute-start(bf16[136,768]{1,0:T(8,128)(2,1)S(1)} %get-tuple-element.100), channel_id=1, source_target_pairs={{0,16},{4,20},{8,24},{12,28},{16,0},{20,4},{24,8},{28,12},{1,17},{... | collective-permute-start | bytes 626696 | tf_op jit(solution)/shard_map/ppermute | solution.py:20
  107.3 3.8 %copy-start.13 = (f32[768]{0:T(1024)S(1)}, f32[768]{0:T(1024)}, u32[]{:S(2)}) copy-start(f32[768]{0:T(1024)} %param.29) | copy-start | bytes 9220
  109.3 3.1 %collective-permute-start.17 = (f32[1,1024]{1,0:T(1,128)S(1)}, f32[1,1024]{1,0:T(1,128)S(1)}, u32[]{:S(2)}, u32[]{:S(2)}) collective-permute-start(f32[1,1024]{1,0:T(1,128)S(1)} %get-tuple-element.104.refs_0_), channel_id=1, source_target_pairs={{0,3},{1,2},{2,1},{3,0},{4,7},{5,6},{6,5},{7,4},{8,11},{9,10},{10,... | collective-permute-start | bytes 12296 | tf_op jit(solution)/shard_map/ppermute | solution.py:20
  110.4 3.6 %collective-permute-start.16 = (f32[1,1024]{1,0:T(1,128)S(1)}, f32[1,1024]{1,0:T(1,128)S(1)}, u32[]{:S(2)}, u32[]{:S(2)}) collective-permute-start(f32[1,1024]{1,0:T(1,128)S(1)} %get-tuple-element.104.refs_0_), channel_id=1, source_target_pairs={{0,2},{1,3},{2,0},{3,1},{4,6},{5,7},{6,4},{7,5},{8,10},{9,11},{10,... | collective-permute-start | bytes 12296 | tf_op jit(solution)/shard_map/ppermute | solution.py:20
  110.9 3.1 %collective-permute-start.15 = (f32[1,1024]{1,0:T(1,128)S(1)}, f32[1,1024]{1,0:T(1,128)S(1)}, u32[]{:S(2)}, u32[]{:S(2)}) collective-permute-start(f32[1,1024]{1,0:T(1,128)S(1)} %get-tuple-element.104.refs_0_), channel_id=1, source_target_pairs={{0,1},{1,0},{2,3},{3,2},{4,5},{5,4},{6,7},{7,6},{8,9},{9,8},{10,11... | collective-permute-start | bytes 12296 | tf_op jit(solution)/shard_map/ppermute | solution.py:20

commit v3 on v2

--- a/solution.py
+++ b/solution.py
@@ -41,9 +41,12 @@
     return lax.dot_general(a, b, (((1,), (1,)), ((), ())), preferred_element_type=F32)
 
 
+def silu_of_double(half):
+    return half + half * jnp.tanh(half)
+
+
 def silu(v):
-    half = 0.5 * v
-    return half + half * jnp.tanh(half)
+    return silu_of_double(0.5 * v)
 
 
 def route_mask(e, route_row, experts_dev, rank):
@@ -64,7 +67,7 @@
 
 
 def pack_kernel(tokens_ref, route_ref, *refs):
-    halves, (note_ref, tail, sems) = refs[:-3], refs[-3:]
+    halves, (note_ref, tail, route, sems) = refs[:-4], refs[-4:]
     rows = halves[0].shape[0]
     copies = [
         pltpu.make_async_copy(tokens_ref.at[q * rows : (q + 1) * rows], half, sems.at[q])
@@ -72,14 +75,16 @@
     ]
     last = tokens_ref.shape[0] - 8
     copies.append(pltpu.make_async_copy(tokens_ref.at[last:], tail, sems.at[len(halves)]))
+    copies.append(pltpu.make_async_copy(route_ref, route, sems.at[len(halves) + 1]))
     for copy in copies[::-1]:
         copy.start()
     copies[-1].wait()
-    route = route_ref[...].astype(F32)
+    copies[-2].wait()
+    route = route[...].astype(F32)
     route = jnp.concatenate([route, jnp.zeros((1, tail.shape[1] - route.shape[1]), F32)], axis=1)
     row = lax.broadcasted_iota(jnp.int32, tail.shape, 0)
     note_ref[...] = jnp.where(row == 0, route, tail[...].astype(F32)).astype(BF16)
-    for copy in copies[:-1]:
+    for copy in copies[:-2]:
         copy.wait()
 
 
@@ -90,15 +95,19 @@
     return pl.pallas_call(
         pack_kernel,
         out_shape=(piece,) * per + (jax.ShapeDtypeStruct((8, features), BF16),),
-        in_specs=[anywhere, VMEM],
+        in_specs=[anywhere, anywhere],
         out_specs=(VMEM,) * (per + 1),
-        scratch_shapes=[pltpu.VMEM((8, features), BF16), pltpu.SemaphoreType.DMA((per + 1,))],
+        scratch_shapes=[
+            pltpu.VMEM((8, features), BF16),
+            pltpu.VMEM(route_row.shape, route_row.dtype),
+            pltpu.SemaphoreType.DMA((per + 2,)),
+        ],
         compiler_params=pltpu.CompilerParams(vmem_limit_bytes=4 << 20),
         name="pack",
     )(tokens, route_row)
 
 
-def project_kernel(cfg, index_ref, *refs):
+def project_kernel(cfg, *refs):
     counts, route_from, devices, cols, rank, near = cfg
     x_refs, refs = refs[: len(counts)], refs[len(counts):]
     n_refs, refs = refs[:devices], refs[devices:]
@@ -106,11 +115,11 @@
     refs = refs[3:]
     if near:
         dt_ref, d_refs, refs = refs[0], refs[1 : 1 + devices], refs[1 + devices:]
-        z_ref, dto_ref, lift_ref, tails_ref, rim_ref, wsm_ref, x_scr, lift_scr = refs
+        z_ref, dto_ref, lift_ref, x_scr, tails_ref, rim_ref, wsm_ref, lift_scr = refs
     else:
         wsm_ref, z_ref, dto_ref, lift_ref, x_scr = refs
         lift_scr = lift_ref
-    e = index_ref[0]
+    e = lax.axis_index("exp")
     rows = sum(counts)
 
     at = 0
@@ -164,7 +173,7 @@
         rim_ref[...] = tails_ref[pl.ds(pl.multiple_of(row, 8), 8), :]
 
 
-def project(index, xs, route_from, notes, wz, wbc, up, rank, dt_t=None, downs=None, wsm=None):
+def project(xs, route_from, notes, wz, wbc, up, rank, dt_t=None, downs=None, wsm=None):
     counts = tuple(x.shape[0] for x in xs)
     rows = sum(counts)
     features = wz.shape[0]
@@ -179,7 +188,8 @@
         jax.ShapeDtypeStruct((rows, LANES), BF16),
     ]
     extra = 8 * devices if near else 0
-    scratch = [pltpu.VMEM((rows + extra, features), BF16)]
+    out_shape.append(jax.ShapeDtypeStruct((rows + extra, features), BF16))
+    scratch = []
     if near:
         out_shape += [jax.ShapeDtypeStruct((extra, width), F32), jax.ShapeDtypeStruct((8, width), F32)]
         out_shape.append(jax.ShapeDtypeStruct((LANES + 16, features), BF16))
@@ -189,7 +199,7 @@
         functools.partial(project_kernel, cfg),
         out_shape=tuple(out_shape),
         grid_spec=pltpu.PrefetchScalarGridSpec(
-            num_scalar_prefetch=1,
+            num_scalar_prefetch=0,
             grid=(1,),
             in_specs=[VMEM] * len(args),
             out_specs=(VMEM,) * len(out_shape),
@@ -204,60 +214,42 @@
             dimension_semantics=("arbitrary",), vmem_limit_bytes=16 << 20
         ),
         name="project",
-    )(index, *args)
-
-
-def gate_kernel(counts, devices, lifts, index_ref, *refs):
-    x_refs, refs = refs[: len(counts)], refs[len(counts):]
-    lift = jnp.concatenate([r[...] for r in refs[:lifts]], axis=0)
-    w_ref, up_ref = refs[lifts : lifts + 2]
-    g_ref, x_scr = refs[-2:]
-    at = 0
-    for x_ref, n in zip(x_refs, counts):
-        x_scr[at : at + n, :] = x_ref[...]
-        at += n
+    )(*args)
+
+
+def gate_kernel(rows, devices, *refs):
+    x_refs, lift_refs = refs[: len(rows)], refs[len(rows) : 2 * len(rows)]
+    w_ref, up_ref, g_ref = refs[-3:]
     width = g_ref.shape[1]
     tn = 256 if width % 256 == 0 else 128
-    for at in range(0, width, tn):
-        lanes = slice(at, at + tn)
-        up = up_rows(up_ref, index_ref[0], devices, lanes)
-        g_ref[:, lanes] = mm(x_scr[...], w_ref[:, lanes]) + mm(lift, up)
-
-
-def gate_project(index, xs, lifts, wz, up, devices, total, row_block, buffer):
-    counts = tuple(x.shape[0] for x in xs)
+    for lane in range(0, width, tn):
+        lanes = slice(lane, lane + tn)
+        up = up_rows(up_ref, lax.axis_index("exp"), devices, lanes)
+        at = 0
+        for x_ref, lift_ref, n in zip(x_refs, lift_refs, rows):
+            g_ref[at : at + n, lanes] = mm(x_ref[0:n, :], w_ref[:, lanes]) + mm(lift_ref[...], up)
+            at += n
+
+
+def gate_project(xs, lifts, wz, up, devices):
+    counts = tuple(lift.shape[0] for lift in lifts)
     rows = sum(counts)
     features = wz.shape[0]
     width = up.shape[1] // 2
-    block = lambda t, i: (row_block, 0)
     args = list(xs) + list(lifts) + [wz, up]
-    in_specs = [VMEM] * len(args)
-    aliases = {}
-    if buffer is not None:
-        aliases[1 + len(args)] = 0
-        args.append(buffer)
-        in_specs.append(pl.BlockSpec(memory_space=pl.ANY))
     return pl.pallas_call(
-        functools.partial(gate_kernel, counts, devices, len(lifts)),
-        out_shape=jax.ShapeDtypeStruct((total, width), F32),
-        grid_spec=pltpu.PrefetchScalarGridSpec(
-            num_scalar_prefetch=1,
-            grid=(1,),
-            in_specs=in_specs,
-            out_specs=pl.BlockSpec((rows, width), block),
-            scratch_shapes=[pltpu.VMEM((rows, features), BF16)],
-        ),
-        input_output_aliases=aliases,
+        functools.partial(gate_kernel, counts, devices),
+        out_shape=jax.ShapeDtypeStruct((rows, width), F32),
+        in_specs=[VMEM] * len(args),
+        out_specs=VMEM,
         cost_estimate=pl.CostEstimate(
             flops=2 * rows * features * width,
             transcendentals=0,
             bytes_accessed=2 * features * (width + rows) + 4 * rows * width,
         ),
-        compiler_params=pltpu.CompilerParams(
-            dimension_semantics=("arbitrary",), vmem_limit_bytes=12 << 20
-        ),
+        compiler_params=pltpu.CompilerParams(vmem_limit_bytes=12 << 20),
         name="gate_project",
-    )(index, *args)
+    )(*args)
 
 
 def spread(value, width):
@@ -276,12 +268,12 @@
 
 
 def state_kernel(
-    cfg, index_ref, z_all, d_all, older_all, tails_ref, rim_ref,
+    cfg, z_all, d_all, older_all, tails_ref, rim_ref,
     taps_ref, mtaps_ref, bias_ref, mbias_ref, dtb_ref, rate_ref, *refs,
 ):
     width, per, far, where_am_i = cfg
     xc_all, cum_all, step_all, update_all, total_all, ext = refs[-6:]
-    e = index_ref[0]
+    e = lax.axis_index("exp")
     r, q = where_am_i(pl.program_id(0))
     block = r ^ e
     at = pl.program_id(0) * CHUNK
@@ -294,7 +286,7 @@
     xc_ref, cum_ref, step_ref = xc_all.at[here], cum_all.at[here], step_all.at[here]
     update_ref, total_ref = update_all.at[pl.ds(chunk, 1)], total_all.at[pl.ds(chunk, 1)]
     before = pl.multiple_of((jnp.maximum(block - 1, 0) ^ e) * 8, 8)
-    rim = jnp.where(index_ref[1] == 0, 0.0, rim_ref[...])
+    rim = jnp.where(lax.axis_index("seq") == 0, 0.0, rim_ref[...])
     first = jnp.where(block == 0, rim, tails_ref[pl.ds(before, 8), :])
     ext[0:8, :] = jnp.where(q == 0, first, prev_ref[...])
     ext[8 : 8 + CHUNK, :] = z_ref[...]
@@ -304,11 +296,12 @@
         (taps_ref, bias_ref, slice(0, width)),
         (mtaps_ref, mbias_ref, slice(width, width + 2 * STATE)),
     ):
-        acc = br[...] + tr[taps - 1 : taps, :] * ext[8 : 8 + CHUNK, lanes]
+        halved = 0.5 * tr[...]
+        acc = 0.5 * br[...] + halved[taps - 1 : taps, :] * ext[8 : 8 + CHUNK, lanes]
         for k in range(taps - 1):
             start = 8 - (taps - 1) + k
-            acc = acc + tr[k : k + 1, :] * ext[start : start + CHUNK, lanes]
-        out = silu(acc)
+            acc = acc + halved[k : k + 1, :] * ext[start : start + CHUNK, lanes]
+        out = silu_of_double(acc)
         xc_ref[:, lanes] = out
         outs.append(out)
     x, maps = outs
@@ -331,14 +324,7 @@
     update_ref[0] = mm(jnp.concatenate([b_hi, b_lo], axis=1), jnp.concatenate([xs, xs], axis=0))
 
 
-def piece_index(r, q, per):
-    if isinstance(r, int):
-        return r * per + q if r < 2 else 2 * per + ((r // 2 - 1) * per + q) * 2 + r % 2
-    far = 2 * per + ((r // 2 - 1) * per + q) * 2 + r % 2
-    return jnp.where(r < 2, r * per + q, far)
-
-
-def run_states(index, total, z, dt, older, tails, rim, params, width, per, far, buffers):
+def run_states(total, z, dt, older, tails, rim, params, width, per, far, buffers):
     wide = z.shape[1]
     chunks = total // CHUNK
     if far is None:
@@ -353,7 +339,7 @@
     aliases = {}
     if buffers is not None:
         for n, buffer in enumerate(buffers):
-            aliases[1 + len(args)] = n
+            aliases[len(args)] = n
             args.append(buffer)
             in_specs.append(VMEM)
     return pl.pallas_call(
@@ -366,7 +352,7 @@
             jax.ShapeDtypeStruct((chunks, 8, LANES), F32),
         ),
         grid_spec=pltpu.PrefetchScalarGridSpec(
-            num_scalar_prefetch=1,
+            num_scalar_prefetch=0,
             grid=(steps,),
             in_specs=in_specs,
             out_specs=(VMEM,) * 5,
@@ -381,14 +367,17 @@
             dimension_semantics=("arbitrary",), vmem_limit_bytes=12 << 20
         ),
         name="run_states",
-    )(index, *args)
-
-
-def stitch_kernel(
-    width, update_ref, total_ref, entry_ref, before_ref, group_ref, glog_ref, send_ref, prefix_ref, plog_ref,
-):
+    )(*args)
+
+
+def part_lanes(width):
+    middle = (width // LANES + 1) // 2 * LANES
+    return [slice(0, middle), slice(middle, width)]
+
+
+def stitch_kernel(width, update_ref, total_ref, entry_ref, before_ref, *refs):
     chunks = update_ref.shape[0]
-    state = jnp.zeros(group_ref.shape, F32)
+    state = jnp.zeros(update_ref.shape[1:], F32)
     log = jnp.zeros(total_ref.shape[1:], F32)
     for c in range(chunks):
         entry_ref[c] = state.astype(BF16)
@@ -396,44 +385,50 @@
         total = total_ref[c]
         state = spread(jnp.exp(total), width)[0:1, :] * state + update_ref[c]
         log = log + total
-    group_ref[...] = state
     wide = spread(log, width)
-    glog_ref[...] = wide
-    send_ref[0:STATE, :] = state.astype(BF16)
-    send_ref[STATE : STATE + 8, :] = pack_logs(wide)
-    prefix_ref[...] = jnp.zeros_like(state)
-    plog_ref[...] = jnp.zeros_like(wide)
+    for p, lanes in enumerate(part_lanes(width)):
+        send_ref, group_ref, glog_ref, prefix_ref, plog_ref = refs[5 * p : 5 * p + 5]
+        group_ref[...] = state[:, lanes]
+        glog_ref[...] = wide[:, lanes]
+        send_ref[0:STATE, :] = state[:, lanes].astype(BF16)
+        send_ref[STATE : STATE + 8, :] = pack_logs(wide[:, lanes])
+        prefix_ref[...] = jnp.zeros(prefix_ref.shape, F32)
+        plog_ref[...] = jnp.zeros(plog_ref.shape, F32)
 
 
 def stitch(updates, totals):
     _, state, width = updates.shape
-    return pl.pallas_call(
+    outs = [jax.ShapeDtypeStruct(updates.shape, BF16), jax.ShapeDtypeStruct(totals.shape, F32)]
+    for lanes in part_lanes(width):
+        wide = lanes.stop - lanes.start
+        outs += [
+            jax.ShapeDtypeStruct((state + 8, wide), BF16),
+            jax.ShapeDtypeStruct((state, wide), F32),
+            jax.ShapeDtypeStruct((8, wide), F32),
+            jax.ShapeDtypeStruct((state, wide), F32),
+            jax.ShapeDtypeStruct((8, wide), F32),
+        ]
+    entry, before, *rest = pl.pallas_call(
         functools.partial(stitch_kernel, width),
-        out_shape=(
-            jax.ShapeDtypeStruct(updates.shape, BF16),
-            jax.ShapeDtypeStruct(totals.shape, F32),
-            jax.ShapeDtypeStruct((state, width), F32),
-            jax.ShapeDtypeStruct((8, width), F32),
-            jax.ShapeDtypeStruct((state + 8, width), BF16),
-            jax.ShapeDtypeStruct((state, width), F32),
-            jax.ShapeDtypeStruct((8, width), F32),
-        ),
+        out_shape=tuple(outs),
         in_specs=[VMEM, VMEM],
-        out_specs=(VMEM,) * 7,
+        out_specs=(VMEM,) * len(outs),
         compiler_params=pltpu.CompilerParams(vmem_limit_bytes=8 << 20),
         name="stitch",
     )(updates, totals)
+    return entry, before, [rest[:5], rest[5:]]
 
 
 def output_kernel(
-    width, per, index_ref, xc_all, cum_all, step_all, before_all, local_all, g_all, direct_ref,
-    a_all, b_all, c_all,
+    width, per, xc_all, cum_all, step_all, before_all, local_all, direct_ref, *refs,
 ):
+    g_refs, (a_all, b_all, c_all) = refs[:-3], refs[-3:]
     c = pl.program_id(0)
     here = pl.ds(pl.multiple_of(c * CHUNK, CHUNK), CHUNK)
-    piece = piece_index((c // per) ^ index_ref[0], c % per, per)
+    r, q = (c // per) ^ lax.axis_index("exp"), c % per
+    piece = jnp.where(r < 2, r * per + q, q * 2 + r % 2)
     there = pl.ds(pl.multiple_of(piece * CHUNK, CHUNK), CHUNK)
-    xc_ref, cum_ref, step_ref, g_ref = xc_all.at[here], cum_all.at[here], step_all.at[here], g_all.at[there]
+    xc_ref, cum_ref, step_ref = xc_all.at[here], cum_all.at[here], step_all.at[here]
     before_ref, local_ref = before_all.at[pl.ds(c, 1)], local_all.at[pl.ds(c, 1)]
     a_ref, b_ref, c_ref = a_all.at[here], b_all.at[here], c_all.at[here]
     bmap = xc_ref[:, width : width + STATE]
@@ -469,14 +464,17 @@
         inside = mm(jnp.concatenate(ws, axis=1), xb.astype(BF16))
         fade = jnp.exp(jnp.where(left, cs[0], cs[1]))
         y = inside + fade * mm(c_hi, local_ref[0, :, lanes]) + both(direct) * x
-        gate = silu(g_ref[:, lanes])
+        gate = g_refs[0][there, lanes]
+        for k, g_ref in enumerate(g_refs[1:]):
+            gate = jnp.where(r // 2 == k + 1, g_ref[there, lanes], gate)
+        gate = silu(gate)
         a_ref[:, lanes] = y * gate
         b_ref[:, lanes] = fade * jnp.exp(both(before_ref[0, 0:1, :])) * gate
 
 
-def run_outputs(index, xc, cum, step, before, local_states, gate, direct, local):
+def run_outputs(xc, cum, step, before, local_states, gates, direct, local):
     total, _ = xc.shape
-    width = gate.shape[1]
+    width = gates[0].shape[1]
     chunks = total // CHUNK
     per = local // CHUNK
     return pl.pallas_call(
@@ -487,9 +485,9 @@
             jax.ShapeDtypeStruct((total, STATE), BF16),
         ),
         grid_spec=pltpu.PrefetchScalarGridSpec(
-            num_scalar_prefetch=1,
+            num_scalar_prefetch=0,
             grid=(chunks,),
-            in_specs=[VMEM] * 7,
+            in_specs=[VMEM] * (6 + len(gates)),
             out_specs=(VMEM,) * 3,
         ),
         cost_estimate=pl.CostEstimate(
@@ -499,7 +497,7 @@
             dimension_semantics=("arbitrary",), vmem_limit_bytes=12 << 20
         ),
         name="run_outputs",
-    )(index, xc, cum, step, before, local_states, gate, direct)
+    )(xc, cum, step, before, local_states, direct, *gates)
 
 
 def pack_logs(wide):
@@ -517,52 +515,71 @@
 
 
 def combine_kernel(
-    d, index_ref, got_ref, group_ref, glog_ref, prefix_ref, plog_ref,
-    send_ref, group_out, glog_out, prefix_out, plog_out,
+    d, radix, *refs,
 ):
-    upper = (index_ref[1] & d) != 0
-    other, other_log = unpack(got_ref)
-    group, group_log = group_ref[...], glog_ref[0:1, :]
-    prefix, prefix_log = prefix_ref[...], plog_ref[0:1, :]
-    prefix_out[...] = jnp.where(upper, prefix + jnp.exp(prefix_log) * other, prefix)
-    new_plog = jnp.where(upper, prefix_log + other_log, prefix_log)
-    plog_out[...] = jnp.broadcast_to(new_plog, plog_out.shape)
-    late = jnp.where(upper, group, other)
-    early = jnp.where(upper, other, group)
-    late_log = jnp.where(upper, group_log, other_log)
-    new = late + jnp.exp(late_log) * early
-    new_log = jnp.broadcast_to(group_log + other_log, glog_out.shape)
-    group_out[...] = new
+    got_refs, refs = refs[: radix - 1], refs[radix - 1 :]
+    group_ref, glog_ref, prefix_ref, plog_ref = refs[:4]
+    send_ref, group_out, glog_out, prefix_out, plog_out, states, logs = refs[4:]
+    mine = (lax.axis_index("seq") // d) % radix
+    states[0] = group_ref[...]
+    logs[0] = glog_ref[...]
+    for k, got_ref in enumerate(got_refs):
+        other, other_log = unpack(got_ref)
+        states[k + 1] = other
+        logs[k + 1] = jnp.broadcast_to(other_log, logs.shape[1:])
+    total = jnp.zeros(group_ref.shape, F32)
+    total_log = jnp.zeros((1, total.shape[1]), F32)
+    early, early_log = total, total_log
+    for m in range(radix):
+        state = states[pl.ds(m ^ mine, 1)][0]
+        log = logs[pl.ds(m ^ mine, 1)][0, 0:1]
+        if m:
+            early = jnp.where(mine == m, total, early)
+            early_log = jnp.where(mine == m, total_log, early_log)
+            state = jnp.exp(log) * total + state
+        total = state
+        total_log = total_log + log
+    prefix_log = plog_ref[0:1, :]
+    prefix_out[...] = prefix_ref[...] + jnp.exp(prefix_log) * early
+    plog_out[...] = jnp.broadcast_to(prefix_log + early_log, plog_out.shape)
+    new_log = jnp.broadcast_to(total_log, glog_out.shape)
+    group_out[...] = total
     glog_out[...] = new_log
-    send_ref[0:STATE, :] = new.astype(BF16)
+    send_ref[0:STATE, :] = total.astype(BF16)
     send_ref[STATE : STATE + 8, :] = pack_logs(new_log)
 
 
-def combine(index, d, got, group, glog, prefix, plog):
+def combine(d, got, group, glog, prefix, plog):
+    radix = len(got) + 1
     state = jax.ShapeDtypeStruct(group.shape, F32)
     log = jax.ShapeDtypeStruct(glog.shape, F32)
-    full = lambda x: pl.BlockSpec(x.shape, lambda i, s: (0, 0))
-    outs = (jax.ShapeDtypeStruct(got.shape, BF16), state, log, state, log)
     return pl.pallas_call(
-        functools.partial(combine_kernel, d),
-        out_shape=outs,
+        functools.partial(combine_kernel, d, radix),
+        out_shape=(jax.ShapeDtypeStruct(got[0].shape, BF16), state, log, state, log),
         grid_spec=pltpu.PrefetchScalarGridSpec(
-            num_scalar_prefetch=1,
+            num_scalar_prefetch=0,
             grid=(1,),
-            in_specs=[full(x) for x in (got, group, glog, prefix, plog)],
-            out_specs=tuple(full(x) for x in outs),
+            in_specs=[VMEM] * (radix + 3),
+            out_specs=(VMEM,) * 5,
+            scratch_shapes=[
+                pltpu.VMEM((radix, *group.shape), F32),
+                pltpu.VMEM((radix, *glog.shape), F32),
+            ],
         ),
         compiler_params=pltpu.CompilerParams(vmem_limit_bytes=8 << 20),
         name="combine",
-    )(index, got, group, glog, prefix, plog)
-
-
-def join_kernel(d, index_ref, a_ref, b_ref, c_ref, got_ref, prefix_ref, plog_ref, o_ref, ss_ref, s_scr):
-    other, _ = unpack(got_ref)
-    prefix = prefix_ref[...]
-    upper = (index_ref[1] & d) != 0
-    entering = jnp.where(upper, prefix + jnp.exp(plog_ref[0:1, :]) * other, prefix)
-    s_scr[...] = entering.astype(BF16)
+    )(*got, group, glog, prefix, plog)
+
+
+def join_kernel(d, a_ref, b_ref, c_ref, *refs):
+    o_ref, ss_ref, s_scr = refs[-3:]
+    upper = (lax.axis_index("seq") & d) != 0
+    for p, lanes in enumerate(part_lanes(o_ref.shape[1])):
+        got_ref, prefix_ref, plog_ref = refs[3 * p : 3 * p + 3]
+        other, _ = unpack(got_ref)
+        prefix = prefix_ref[...]
+        entering = jnp.where(upper, prefix + jnp.exp(plog_ref[0:1, :]) * other, prefix)
+        s_scr[:, lanes] = entering.astype(BF16)
 
     part = 256
     ones = jnp.ones((8, 2 * o_ref.shape[1]), BF16)
@@ -574,15 +591,15 @@
         ss_ref[:, rows] = mm_nt(ones, jnp.concatenate([hi, lo], axis=1))[0:1]
 
 
-def join(index, d, a, b, c, got, prefix, plog):
+def join(d, a, b, c, entering):
     total, width = a.shape
     return pl.pallas_call(
         functools.partial(join_kernel, d),
         out_shape=(jax.ShapeDtypeStruct((total, width), F32), jax.ShapeDtypeStruct((1, total), F32)),
         grid_spec=pltpu.PrefetchScalarGridSpec(
-            num_scalar_prefetch=1,
+            num_scalar_prefetch=0,
             grid=(1,),
-            in_specs=[VMEM] * 6,
+            in_specs=[VMEM] * (3 + len(entering)),
             out_specs=(VMEM, VMEM),
             scratch_shapes=[pltpu.VMEM((STATE, width), BF16)],
         ),
@@ -590,7 +607,7 @@
             dimension_semantics=("arbitrary",), vmem_limit_bytes=10 << 20
         ),
         name="join",
-    )(index, a, b, c, got, prefix, plog)
+    )(a, b, c, *entering)
 
 
 def norm_kernel(inner_width, g_ref, gain_ref, *refs):
@@ -622,6 +639,15 @@
         ),
         name="norm",
     )(gated, gain, *squares)
+
+
+def stages(shards):
+    out, d = [], 1
+    while d < shards:
+        radix = 4 if 8 * d <= shards else 2
+        out.append((d, radix))
+        d *= radix
+    return out
 
 
 def body(
@@ -648,8 +674,6 @@
     width = gate_inner_weight.shape[2]
     experts = adapter_up_weight.shape[0]
     rank = 8
-    e = lax.axis_index("exp")
-    index = jnp.stack([e, lax.axis_index("seq")]).astype(jnp.int32)
     per = local // CHUNK
 
     down = {0: adapter_down_weight.T}
@@ -672,51 +696,55 @@
     wz = gate_inner_weight.reshape(features, 2 * width)
     up = adapter_up_weight.reshape(experts, 2 * width)
     call = functools.partial(
-        project, index, notes=notes, wz=wz, wbc=state_map_weight, up=up, rank=rank
+        project, notes=notes, wz=wz, wbc=state_map_weight, up=up, rank=rank
     )
-    z, dt, lift, tails, rim, wsm = call(
+    z, dt, lift, rows, tails, rim, wsm = call(
         [tokens, sibling], route_from=((0, 0, local), (1, 0, local)),
         dt_t=step_size_weight.T, downs=downs,
     )
-    gate = gate_project(index, [tokens, sibling], [lift], wz, up, n, total, 0, None)
+    gates = [gate_project([rows], [lift], wz, up, n)]
     rim = lax.ppermute(rim, "seq", [(i, (i + 1) % shards) for i in range(shards)])
     params = [
         inner_conv_taps, state_map_taps, inner_conv_bias[None, :], state_map_conv_bias[None, :],
         step_size_bias[None, :], head_decay_rate[None, :],
     ]
-    kept = run_states(index, total, z, dt, z, tails, rim, params, width, per, None, None)
+    kept = run_states(total, z, dt, z, tails, rim, params, width, per, None, None)
     far_rows = {}
     for q in range(per):
         for k in range(2, n, 2):
             mine = far[k, q]
             other = swap(mine, "exp", 1)
-            z, dt, lift = call(
+            z, dt, lift, rows = call(
                 [mine, other],
                 route_from=((k, q * CHUNK, CHUNK), (k + 1, q * CHUNK, CHUNK)),
                 wsm=wsm,
             )
-            far_rows[k, q] = (mine, other, z, lift)
+            far_rows[k, q] = (rows, lift, z)
             older = far_rows[k, max(q - 1, 0)][2]
             kept = run_states(
-                index, total, z, dt, older, tails, rim, params, width, per, (k, q), kept
+                total, z, dt, older, tails, rim, params, width, per, (k, q), kept
             )
     xc, cum, step, updates, totals = kept
-    states, before, group, glog, send, prefix, plog = stitch(updates, totals)
-    d = 1
-    while True:
-        got = swap(send, "seq", d)
-        if 2 * d >= shards:
-            break
-        send, group, glog, prefix, plog = combine(index, d, got, group, glog, prefix, plog)
-        d *= 2
+    states, before, parts = stitch(updates, totals)
+    for d, radix in stages(shards):
+        last = 2 * d == shards
+        got = {}
+        for p, part in enumerate(parts):
+            for k in range(1, radix):
+                got[p, k] = swap(part[0], "seq", d * k)
+        for p, part in enumerate(parts):
+            arrived = [got[p, k] for k in range(1, radix)]
+            if last:
+                parts[p] = [arrived[0], *part[3:]]
+            else:
+                parts[p] = combine(d, arrived, *part[1:])
+    entering = [x for part in parts for x in part]
     for k in range(2, n, 2):
-        xs = [row for q in range(per) for row in far_rows[k, q][:2]]
-        lifts = [far_rows[k, q][3] for q in range(per)]
-        gate = gate_project(index, xs, lifts, wz, up, n, total, k // 2, gate)
-    a, b, c = run_outputs(
-        index, xc, cum, step, before, states, gate, direct_head_scale[None, :], local
-    )
-    gated, mine = join(index, d, a, b, c, got, prefix, plog)
+        xs = [far_rows[k, q][0] for q in range(per)]
+        lifts = [far_rows[k, q][1] for q in range(per)]
+        gates.append(gate_project(xs, lifts, wz, up, n))
+    a, b, c = run_outputs(xc, cum, step, before, states, gates, direct_head_scale[None, :], local)
+    gated, mine = join(shards // 2, a, b, c, entering)
     others = [swap(mine, "exp", k) for k in range(1, n)]
     return norm(gated, [mine, *others], gated_norm_scale[None, :], width * n)
 

time: 117 us -> 106 us (0.906)
  Pallas kernels: 44.2 us -> 35.3 us
  waiting for transfers between devices: 45 us -> 38.4 us
  starting transfers between devices: 15.9 us -> 20.7 us
    ppermute x17 -> x22, waiting for transfers between devices: 45 us -> 38.4 us  [swap(): lax.ppermute(block, axis, [(i, i ^ mask) for i in range(lax.axis_size(axi...]
    ppermute x17 -> x22, starting transfers between devices: 13.9 us -> 18.8 us  [swap(): lax.ppermute(block, axis, [(i, i ^ mask) for i in range(lax.axis_size(axi...]
    pallas_call x5, Pallas kernels: 11.4 us -> 7.01 us  [the longest x2 4.78 us: gate_project(): pl.pallas_call(functools.partial(gate_kernel, counts, devices), out_shape...]
    pallas_call x3, Pallas kernels: 8.68 us -> 6.85 us  [run_states(): pl.pallas_call(functools.partial(state_kernel, (width, per, far is not No...]
    pallas_call x3, Pallas kernels: 14.2 us -> 12.7 us  [project(): pl.pallas_call(functools.partial(project_kernel, cfg), out_shape=tuple(ou...]
    unnamed x30 -> x28, local copies, waits for them, and re-layouts: 9.99 us -> 9.98 us
  transfers between devices with their start and end apart: 18 -> 23, of which waited for: 8 -> 9; matrix products, arithmetic and copies ran while one was open for 6% -> 6% of each run, Pallas kernels for 25% -> 23%
where the time goes in v3:
time: 106 us; the launch traced here: 105 us
  waiting for transfers between devices  38.4 us (36%)
  Pallas kernels  35.3 us (33%)
  starting transfers between devices  20.7 us (20%)
  local copies, waits for them, and re-layouts  10.7 us (10%)
    ppermute x22, waiting for transfers between devices, swap(): lax.ppermute(block, axis, [(i, i ^ mask) for i in range(lax.axis_size(axi...  38.4 us
    ppermute x22, starting transfers between devices, swap(): lax.ppermute(block, axis, [(i, i ^ mask) for i in range(lax.axis_size(axi...  18.8 us
    pallas_call x3, Pallas kernels, project(): pl.pallas_call(functools.partial(project_kernel, cfg), out_shape=tuple(ou...  12.7 us
    unnamed x28, local copies, waits for them, and re-layouts  9.98 us
    pallas_call x3, Pallas kernels, run_states(): pl.pallas_call(functools.partial(state_kernel, (width, per, far is not No...  6.85 us
    pallas_call x1, Pallas kernels, run_outputs(): pl.pallas_call(functools.partial(output_kernel, width, per), out_shape=(j...  4.9 us
    pallas_call x2, Pallas kernels, gate_project(): pl.pallas_call(functools.partial(gate_kernel, counts, devices), out_shape...  4.78 us
  transfers between devices with their start and end apart: 23, of which 9 were waited for; matrix products, arithmetic and copies ran while one was open for 6% of the time, Pallas kernels for 23%

profile of v3, /device:TPU:0, one launch (start us, length us, event | category | flops | bytes accessed | tf_op | source)
XLA Modules:
  0.0 105.4 jit_solution(10402405450864179057)
XLA Ops:
  0.0 0.5 collective-permute-start.5
  0.5 1.3 %copy-done.1 = bf16[256,2560]{1,0:T(8,128)(2,1)S(1)} copy-done((bf16[256,2560]{1,0:T(8,128)(2,1)S(1)}, bf16[256,2560]{1,0:T(8,128)(2,1)}, u32[]{:S(2)}) %copy-start.1) | copy-done | bytes 1310744
  1.8 0.7 copy-done.10
  2.5 0.5 pack.1
  3.0 2.6 %collective-permute-start.9 = (bf16[128,2560]{1,0:T(8,128)(2,1)S(1)}, bf16[128,2560]{1,0:T(8,128)(2,1)}, u32[]{:S(2)}, u32[]{:S(2)}) collective-permute-start(bf16[128,2560]{1,0:T(8,128)(2,1)S(1)} %get-tuple-element.66), channel_id=1, source_target_pairs={{0,2},{1,3},{2,0},{3,1},{4,6},{5,7},{6,4},{7,5},{8,10},{9,11},{10,... | collective-permute-start | bytes 1966088 | tf_op jit(solution)/shard_map/ppermute | solution.py:20
  5.6 15.6 %collective-permute-done.9.refs_0_ = bf16[128,2560]{1,0:T(8,128)(2,1)} collective-permute-done((bf16[128,2560]{1,0:T(8,128)(2,1)S(1)}, bf16[128,2560]{1,0:T(8,128)(2,1)}, u32[]{:S(2)}, u32[]{:S(2)}) %collective-permute-start.9) | collective-permute-done | bytes 655392 | tf_op jit(solution)/shard_map/ppermute | solution.py:20
  21.3 2.0 %collective-permute-start.7 = (bf16[32,2560]{1,0:T(8,128)(2,1)}, bf16[32,2560]{1,0:T(8,128)(2,1)}, u32[]{:S(2)}, u32[]{:S(2)}) collective-permute-start(bf16[32,2560]{1,0:T(8,128)(2,1)} %bitcast.21), channel_id=1, source_target_pairs={{0,2},{1,3},{2,0},{3,1},{4,6},{5,7},{6,4},{7,5},{8,10},{9,11},{10,... | collective-permute-start | bytes 491528 | tf_op jit(solution)/shard_map/ppermute | solution.py:20
  23.3 16.1 %collective-permute-done.3.refs_4_ = bf16[8,2560]{1,0:T(8,128)(2,1)S(1)} collective-permute-done((bf16[8,2560]{1,0:T(8,128)(2,1)S(1)}, bf16[8,2560]{1,0:T(8,128)(2,1)S(1)}, u32[]{:S(2)}, u32[]{:S(2)}) %collective-permute-start.3) | collective-permute-done | bytes 40992 | tf_op jit(solution)/shard_map/ppermute | solution.py:20
  39.4 1.2 %collective-permute-done.2.refs_3_ = bf16[8,2560]{1,0:T(8,128)(2,1)S(1)} collective-permute-done((bf16[8,2560]{1,0:T(8,128)(2,1)S(1)}, bf16[8,2560]{1,0:T(8,128)(2,1)S(1)}, u32[]{:S(2)}, u32[]{:S(2)}) %collective-permute-start.2) | collective-permute-done | bytes 40992 | tf_op jit(solution)/shard_map/ppermute | solution.py:20
  40.8 0.3 collective-permute-start.1
  41.1 0.7 collective-permute-done.4.refs_5_
  42.0 0.3 collective-permute-start.8
  42.4 0.7 broadcast_in_dim.18.bias_ref
  43.0 1.0 copy.27
  44.1 4.7 %copy.26 = bf16[320,8,2,768]{3,1,2,0:T(8,128)(2,1)S(1)} copy(bf16[320,8,2,768]{3,2,1,0:T(2,128)(2,1)} %bitcast.36) | data formatting | bytes 15728640
  48.9 1.3 %copy-done.2 = bf16[256,2560]{1,0:T(8,128)(2,1)S(1)} copy-done((bf16[256,2560]{1,0:T(8,128)(2,1)S(1)}, bf16[256,2560]{1,0:T(8,128)(2,1)}, u32[]{:S(2)}) %copy-start.2) | copy-done | bytes 1310744
  50.2 0.9 copy-done.5
  51.1 5.8 %project.3 = (f32[512,1024]{1,0:T(8,128)S(1)}, f32[512,128]{1,0:T(8,128)S(1)}, bf16[512,128]{1,0:T(8,128)(2,1)S(1)}, bf16[544,2560]{1,0:T(8,128)(2,1)S(1)}, f32[...) custom-call(bf16[256,2560]{1,0:T(8,128)(2,1)S(1)} %copy-done.2, ...), custom_call_target="tpu_custom_call" | custom-call | flops 3355443200 | bytes 9961472 | tf_op jit(solution)/shard_map/project/pallas_call | solution.py:198
  56.9 1.9 %collective-permute-start.11 = (f32[8,1024]{1,0:T(8,128)S(1)}, f32[8,1024]{1,0:T(8,128)S(1)}, u32[]{:S(2)}, u32[]{:S(2)}) collective-permute-start(f32[8,1024]{1,0:T(8,128)S(1)} %get-tuple-element.69), channel_id=1, source_target_pairs={{0,4},{4,8},{8,12},{12,16},{16,20},{20,24},{24,28},{28,0},{1,5},{5... | collective-permute-start | bytes 98312 | tf_op jit(solution)/shard_map/ppermute | solution.py:706
  58.8 3.4 %project.5 = (f32[256,1024]{1,0:T(8,128)S(1)}, f32[256,128]{1,0:T(8,128)S(1)}, bf16[256,128]{1,0:T(8,128)(2,1)S(1)}, bf16[256,2560]{1,0:T(8,128)(2,1)S(1)}) custom-call(bf16[128,2560]{1,0:T(8,128)(2,1)} %collective-permute-done.9.refs_0_, bf16[128,2560]{1,0:T(8,128)(2,1)} %collective-permute-done.10.refs_1_, bf16[8,2560]{1,0:T(8,128)(2,1)S(1)} %get-tuple-element.62.refs_2_, ...), custom_call_target="tpu_custom_call" | custom-call | flops 1677721600 | bytes 7602176 | tf_op jit(solution)/shard_map/project/pallas_call | solution.py:198
  62.3 3.5 %project.4 = (f32[256,1024]{1,0:T(8,128)S(1)}, f32[256,128]{1,0:T(8,128)S(1)}, bf16[256,128]{1,0:T(8,128)(2,1)S(1)}, bf16[256,2560]{1,0:T(8,128)(2,1)S(1)}) custom-call(bf16[128,2560]{1,0:T(8,128)(2,1)} %collective-permute-done.refs_0_, bf16[128,2560]{1,0:T(8,128)(2,1)} %collective-permute-done.1.refs_1_, bf16[8,2560]{1,0:T(8,128)(2,1)S(1)} %get-tuple-element.62.refs_2_, ...), custom_call_target="tpu_custom_call" | custom-call | flops 1677721600 | bytes 7602176 | tf_op jit(solution)/shard_map/project/pallas_call | solution.py:198
  65.8 3.4 %run_states.3 = (f32[1024,1024]{1,0:T(8,128)S(1)}, f32[1024,128]{1,0:T(8,128)S(1)}, f32[1024,128]{1,0:T(8,128)S(1)}, f32[8,128,768]{2,1,0:T(8,128)S(1)}, f32[8,8,128]{2,1,0:T(8,128)S(1)}) custom-call(f32[512,1024]{1,0:T(8,128)S(1)} %get-tuple-element.71.z_all.older_all, f32[512,128]{1,0:T(8,128)S(1)} %get-tuple-element.72.d_all, ...), custom_call_target="tpu_custom_call" | custom-call | flops 786432000 | bytes 6291456 | tf_op jit(solution)/shard_map/run_states/pallas_call | solution.py:345
  69.3 1.7 %run_states.4 = (f32[1024,1024]{1,0:T(8,128)S(1)}, f32[1024,128]{1,0:T(8,128)S(1)}, f32[1024,128]{1,0:T(8,128)S(1)}, f32[8,128,768]{2,1,0:T(8,128)S(1)}, f32[8,8,128]{2,1,0:T(8,128)S(1)}) custom-call(f32[256,1024]{1,0:T(8,128)S(1)} %get-tuple-element.67.z_all.older_all, ...), custom_call_target="tpu_custom_call", output_to_operand_aliasing={{0}: (11, {}), {1}: (12, {}), {2}: (13, {}), {3}: (14, {}),... | custom-call | flops 393216000 | bytes 3145728 | tf_op jit(solution)/shard_map/run_states/pallas_call | solution.py:345
  71.0 1.7 %run_states.5 = (f32[1024,1024]{1,0:T(8,128)S(1)}, f32[1024,128]{1,0:T(8,128)S(1)}, f32[1024,128]{1,0:T(8,128)S(1)}, f32[8,128,768]{2,1,0:T(8,128)S(1)}, f32[8,8,128]{2,1,0:T(8,128)S(1)}) custom-call(f32[256,1024]{1,0:T(8,128)S(1)} %get-tuple-element.64.z_all, ...), custom_call_target="tpu_custom_call", output_to_operand_aliasing={{0}: (11, {}), {1}: (12, {}), {2}: (13, {}), {3}: (14, {}),... | custom-call | flops 393216000 | bytes 3145728 | tf_op jit(solution)/shard_map/run_states/pallas_call | solution.py:345
  72.7 0.5 stitch.1
  73.2 2.6 %collective-permute-start.14 = (bf16[136,384]{1,0:T(8,128)(2,1)S(1)}, bf16[136,384]{1,0:T(8,128)(2,1)S(1)}, u32[]{:S(2)}, u32[]{:S(2)}) collective-permute-start(bf16[136,384]{1,0:T(8,128)(2,1)S(1)} %get-tuple-element.99), channel_id=1, source_target_pairs={{0,12},{4,8},{8,4},{12,0},{16,28},{20,24},{24,20},{28,16},{1,13},{... | collective-permute-start | bytes 313352 | tf_op jit(solution)/shard_map/ppermute | solution.py:20
  75.9 2.4 %gate_project.2.refs_0_ = f32[512,768]{1,0:T(8,128)S(1)} custom-call(bf16[544,2560]{1,0:T(8,128)(2,1)S(1)} %get-tuple-element.90.refs_0_, bf16[512,128]{1,0:T(8,128)(2,1)S(1)} %get-tuple-element.91.refs_1_, bf16[2560,1536]{1,0:T(8,128)(2,1)S(1)} %bitcast.14, bf16[128,1536]{1,0:T(8,128)(2,1)S(1)} %bitcast.19), custom_call_target="tpu_custom_call" | custom-call | flops 2013265920 | bytes 8126464 | tf_op jit(solution)/shard_map/gate_project/pallas_call | solution.py:240
  78.2 0.5 collective-permute-start.13
  78.8 0.5 collective-permute-start.12
  79.2 2.6 %collective-permute-start.18 = (bf16[136,384]{1,0:T(8,128)(2,1)S(1)}, bf16[136,384]{1,0:T(8,128)(2,1)S(1)}, u32[]{:S(2)}, u32[]{:S(2)}) collective-permute-start(bf16[136,384]{1,0:T(8,128)(2,1)S(1)} %get-tuple-element.107), channel_id=1, source_target_pairs={{0,12},{4,8},{8,4},{12,0},{16,28},{20,24},{24,20},{28,16},{1,13},{... | collective-permute-start | bytes 313352 | tf_op jit(solution)/shard_map/ppermute | solution.py:20
  81.8 0.4 collective-permute-start.17
  82.3 0.5 collective-permute-start.16
  82.7 2.4 %gate_project.3.refs_1_ = f32[512,768]{1,0:T(8,128)S(1)} custom-call(bf16[256,2560]{1,0:T(8,128)(2,1)S(1)} %get-tuple-element.92.refs_0_, bf16[256,2560]{1,0:T(8,128)(2,1)S(1)} %get-tuple-element.93.refs_1_, bf16[256,128]{1,0:T(8,128)(2,1)S(1)} %get-tuple-element.94.refs_2_, bf16[256,128]{1,0:T(8,128)(2,1)S(1)} %get-tuple-element.95.refs_3_, ...), custom_call_target="tpu_custom_call" | custom-call | flops 2013265920 | bytes 8126464 | tf_op jit(solution)/shard_map/gate_project/pallas_call | solution.py:240
  85.1 0.6 collective-permute-done.12.refs_0_
  85.8 0.9 combine.2
  86.6 2.6 %collective-permute-start.15 = (bf16[136,384]{1,0:T(8,128)(2,1)S(1)}, bf16[136,384]{1,0:T(8,128)(2,1)S(1)}, u32[]{:S(2)}, u32[]{:S(2)}) collective-permute-start(bf16[136,384]{1,0:T(8,128)(2,1)S(1)} %get-tuple-element.104), channel_id=1, source_target_pairs={{0,16},{4,20},{8,24},{12,28},{16,0},{20,4},{24,8},{28,12},{1,17},{... | collective-permute-start | bytes 313352 | tf_op jit(solution)/shard_map/ppermute | solution.py:20
  89.2 0.9 combine.3
  90.1 1.0 collective-permute-start.19
  91.1 4.9 %run_outputs.1 = (f32[1024,768]{1,0:T(8,128)S(1)}, f32[1024,768]{1,0:T(8,128)S(1)}, bf16[1024,128]{1,0:T(8,128)(2,1)S(1)}) custom-call(f32[1024,1024]{1,0:T(8,128)S(1)} %get-tuple-element.83.xc_all, f32[1024,128]{1,0:T(8,128)S(1)} %get-tuple-element.84.cum_all, f32[1024,128]{1,0:T(8,128)S(1)} %get-tuple-element.85.step_all, ...), custom_call_target="tpu_custom_call" | custom-call | flops 2359296000 | bytes 12582912 | tf_op jit(solution)/shard_map/run_outputs/pallas_call | solution.py:480
  96.0 0.3 collective-permute-done.15.refs_0_
  96.3 1.5 %collective-permute-done.19.refs_3_ = bf16[136,384]{1,0:T(8,128)(2,1)S(1)} collective-permute-done((bf16[136,384]{1,0:T(8,128)(2,1)S(1)}, bf16[136,384]{1,0:T(8,128)(2,1)S(1)}, u32[]{:S(2)}, u32[]{:S(2)}) %collective-permute-start.19) | collective-permute-done | bytes 104480 | tf_op jit(solution)/shard_map/ppermute | solution.py:20
  97.8 1.4 %join.1 = (f32[1024,768]{1,0:T(8,128)S(1)}, f32[1,1024]{1,0:T(1,128)S(1)}) custom-call(f32[1024,768]{1,0:T(8,128)S(1)} %get-tuple-element.96.a_ref, f32[1024,768]{1,0:T(8,128)S(1)} %get-tuple-element.97.b_ref, bf16[1024,128]{1,0:T(8,128)(2,1)S(1)} %get-tuple-element.98.c_ref, bf16[136,384]{1,0:T(8,128)(2,1)S(1)} %collective-permute-done.15.refs_0_, ...), custom_call_target="tpu_custom_call" | custom-call | tf_op jit(solution)/shard_map/join/pallas_call | solution.py:596
  99.2 0.5 collective-permute-start.22
  99.7 1.1 %collective-permute-start.21 = (f32[1,1024]{1,0:T(1,128)S(1)}, f32[1,1024]{1,0:T(1,128)S(1)}, u32[]{:S(2)}, u32[]{:S(2)}) collective-permute-start(f32[1,1024]{1,0:T(1,128)S(1)} %get-tuple-element.116.refs_0_), channel_id=1, source_target_pairs={{0,2},{1,3},{2,0},{3,1},{4,6},{5,7},{6,4},{7,5},{8,10},{9,11},{10,... | collective-permute-start | bytes 12296 | tf_op jit(solution)/shard_map/ppermute | solution.py:20
  100.8 0.3 collective-permute-start.20
  101.1 1.2 %collective-permute-done.22.refs_3_ = f32[1,1024]{1,0:T(1,128)S(1)} collective-permute-done((f32[1,1024]{1,0:T(1,128)S(1)}, f32[1,1024]{1,0:T(1,128)S(1)}, u32[]{:S(2)}, u32[]{:S(2)}) %collective-permute-start.22) | collective-permute-done | bytes 4128 | tf_op jit(solution)/shard_map/ppermute | solution.py:20
  102.3 1.1 %collective-permute-done.21.refs_2_ = f32[1,1024]{1,0:T(1,128)S(1)} collective-permute-done((f32[1,1024]{1,0:T(1,128)S(1)}, f32[1,1024]{1,0:T(1,128)S(1)}, u32[]{:S(2)}, u32[]{:S(2)}) %collective-permute-start.21) | collective-permute-done | bytes 4128 | tf_op jit(solution)/shard_map/ppermute | solution.py:20
  103.4 2.0 %norm.1 = bf16[1024,768]{1,0:T(8,128)(2,1)} custom-call(f32[1024,768]{1,0:T(8,128)S(1)} %get-tuple-element.115.g_ref, f32[1,768]{1,0:T(1,128)S(1)} %broadcast_in_dim.23.gain_ref, f32[1,1024]{1,0:T(1,128)S(1)} %get-tuple-element.116.refs_0_, f32[1,1024]{1,0:T(1,128)S(1)} %collective-permute-done.20.refs_1_, f32[1,1024]{1,0:T(1,128)S(1)} %collective-permute-done.21.refs_2_, ...), custom_call_target="tpu_custom_call" | custom-call | tf_op jit(solution)/shard_map/norm/pallas_call | solution.py:631
  (43 shorter events, 0.5 us)
Async XLA Ops:
  0.0 48.8 %collective-permute-start.5 = (bf16[256,2560]{1,0:T(8,128)(2,1)}, bf16[256,2560]{1,0:T(8,128)(2,1)}, u32[]{:S(2)}, u32[]{:S(2)}) collective-permute-start(bf16[256,2560]{1,0:T(8,128)(2,1)} %refs_0_.1), channel_id=1, source_target_pairs={{0,1},{1,0},{2,3},{3,2},{4,5},{5,4},{6,7},{7,6},{8,9},{9,8},{10,11... | collective-permute-start | bytes 3932168 | tf_op jit(solution)/shard_map/ppermute | solution.py:20
  0.5 1.3 %copy-start.1 = (bf16[256,2560]{1,0:T(8,128)(2,1)S(1)}, bf16[256,2560]{1,0:T(8,128)(2,1)}, u32[]{:S(2)}) copy-start(bf16[256,2560]{1,0:T(8,128)(2,1)} %refs_0_.1) | copy-start | bytes 3932164
  1.8 0.7 copy-start.10
  3.0 18.3 %collective-permute-start.9 = (bf16[128,2560]{1,0:T(8,128)(2,1)S(1)}, bf16[128,2560]{1,0:T(8,128)(2,1)}, u32[]{:S(2)}, u32[]{:S(2)}) collective-permute-start(bf16[128,2560]{1,0:T(8,128)(2,1)S(1)} %get-tuple-element.66), channel_id=1, source_target_pairs={{0,2},{1,3},{2,0},{3,1},{4,6},{5,7},{6,4},{7,5},{8,10},{9,11},{10,... | collective-permute-start | bytes 1966088 | tf_op jit(solution)/shard_map/ppermute | solution.py:20
  5.6 35.2 %collective-permute-start = (bf16[128,2560]{1,0:T(8,128)(2,1)S(1)}, bf16[128,2560]{1,0:T(8,128)(2,1)}, u32[]{:S(2)}, u32[]{:S(2)}) collective-permute-start(bf16[128,2560]{1,0:T(8,128)(2,1)S(1)} %get-tuple-element.61), channel_id=1, source_target_pairs={{0,2},{1,3},{2,0},{3,1},{4,6},{5,7},{6,4},{7,5},{8,10},{9,11},{10,... | collective-permute-start | bytes 1966088 | tf_op jit(solution)/shard_map/ppermute | solution.py:20
  21.2 37.5 %collective-permute-start.10 = (bf16[128,2560]{1,0:T(8,128)(2,1)}, bf16[128,2560]{1,0:T(8,128)(2,1)}, u32[]{:S(2)}, u32[]{:S(2)}) collective-permute-start(bf16[128,2560]{1,0:T(8,128)(2,1)} %collective-permute-done.9.refs_0_), channel_id=1, source_target_pairs={{0,1},{1,0},{2,3},{3,2},{4,5},{5,4},{6,7},{7,6},{8,9},{9,8},{10,11... | collective-permute-start | bytes 1966088 | tf_op jit(solution)/shard_map/ppermute | solution.py:20
  21.3 20.7 %collective-permute-start.7 = (bf16[32,2560]{1,0:T(8,128)(2,1)}, bf16[32,2560]{1,0:T(8,128)(2,1)}, u32[]{:S(2)}, u32[]{:S(2)}) collective-permute-start(bf16[32,2560]{1,0:T(8,128)(2,1)} %bitcast.21), channel_id=1, source_target_pairs={{0,2},{1,3},{2,0},{3,1},{4,6},{5,7},{6,4},{7,5},{8,10},{9,11},{10,... | collective-permute-start | bytes 491528 | tf_op jit(solution)/shard_map/ppermute | solution.py:20
  23.3 16.1 %collective-permute-start.3 = (bf16[8,2560]{1,0:T(8,128)(2,1)S(1)}, bf16[8,2560]{1,0:T(8,128)(2,1)S(1)}, u32[]{:S(2)}, u32[]{:S(2)}) collective-permute-start(bf16[8,2560]{1,0:T(8,128)(2,1)S(1)} %get-tuple-element.62.refs_2_), channel_id=1, source_target_pairs={{0,2},{1,3},{2,0},{3,1},{4,6},{5,7},{6,4},{7,5},{8,10},{9,11},{10,... | collective-permute-start | bytes 122888 | tf_op jit(solution)/shard_map/ppermute | solution.py:20
  39.4 1.2 %collective-permute-start.2 = (bf16[8,2560]{1,0:T(8,128)(2,1)S(1)}, bf16[8,2560]{1,0:T(8,128)(2,1)S(1)}, u32[]{:S(2)}, u32[]{:S(2)}) collective-permute-start(bf16[8,2560]{1,0:T(8,128)(2,1)S(1)} %get-tuple-element.62.refs_2_), channel_id=1, source_target_pairs={{0,1},{1,0},{2,3},{3,2},{4,5},{5,4},{6,7},{7,6},{8,9},{9,8},{10,11... | collective-permute-start | bytes 122888 | tf_op jit(solution)/shard_map/ppermute | solution.py:20
  40.6 1.2 %collective-permute-start.4 = (bf16[8,2560]{1,0:T(8,128)(2,1)S(1)}, bf16[8,2560]{1,0:T(8,128)(2,1)S(1)}, u32[]{:S(2)}, u32[]{:S(2)}) collective-permute-start(bf16[8,2560]{1,0:T(8,128)(2,1)S(1)} %collective-permute-done.3.refs_4_), channel_id=1, source_target_pairs={{0,1},{1,0},{2,3},{3,2},{4,5},{5,4},{6,7},{7,6},{8,9},{9,8},{10,11... | collective-permute-start | bytes 122888 | tf_op jit(solution)/shard_map/ppermute | solution.py:20
  40.8 21.5 %collective-permute-start.1 = (bf16[128,2560]{1,0:T(8,128)(2,1)}, bf16[128,2560]{1,0:T(8,128)(2,1)}, u32[]{:S(2)}, u32[]{:S(2)}) collective-permute-start(bf16[128,2560]{1,0:T(8,128)(2,1)} %collective-permute-done.refs_0_), channel_id=1, source_target_pairs={{0,1},{1,0},{2,3},{3,2},{4,5},{5,4},{6,7},{7,6},{8,9},{9,8},{10,11... | collective-permute-start | bytes 1966088 | tf_op jit(solution)/shard_map/ppermute | solution.py:20
  41.8 7.0 %collective-permute-start.6 = (bf16[32,2560]{1,0:T(8,128)(2,1)}, bf16[32,2560]{1,0:T(8,128)(2,1)}, u32[]{:S(2)}, u32[]{:S(2)}) collective-permute-start(bf16[32,2560]{1,0:T(8,128)(2,1)} %bitcast.22), channel_id=1, source_target_pairs={{0,1},{1,0},{2,3},{3,2},{4,5},{5,4},{6,7},{7,6},{8,9},{9,8},{10,11... | collective-permute-start | bytes 491528 | tf_op jit(solution)/shard_map/ppermute | solution.py:20
  42.0 6.8 %collective-permute-start.8 = (bf16[32,2560]{1,0:T(8,128)(2,1)}, bf16[32,2560]{1,0:T(8,128)(2,1)}, u32[]{:S(2)}, u32[]{:S(2)}) collective-permute-start(bf16[32,2560]{1,0:T(8,128)(2,1)} %collective-permute-done.7.refs_12_), channel_id=1, source_target_pairs={{0,1},{1,0},{2,3},{3,2},{4,5},{5,4},{6,7},{7,6},{8,9},{9,8},{10,11... | collective-permute-start | bytes 491528 | tf_op jit(solution)/shard_map/ppermute | solution.py:20
  44.1 4.8 %copy-start = (bf16[2560,256]{1,0:T(8,128)(2,1)S(1)}, bf16[2560,256]{1,0:T(8,128)(2,1)}, u32[]{:S(2)}) copy-start(bf16[2560,256]{1,0:T(8,128)(2,1)} %refs_7_.5) | copy-start | bytes 3932164
  44.1 4.8 %copy-start.3 = (bf16[2560,32]{0,1:T(8,128)(2,1)S(1)}, bf16[2560,32]{0,1:T(8,128)(2,1)}, u32[]{:S(2)}) copy-start(bf16[2560,32]{0,1:T(8,128)(2,1)} %param.20) | copy-start | bytes 491524
  48.9 1.3 %copy-start.2 = (bf16[256,2560]{1,0:T(8,128)(2,1)S(1)}, bf16[256,2560]{1,0:T(8,128)(2,1)}, u32[]{:S(2)}) copy-start(bf16[256,2560]{1,0:T(8,128)(2,1)} %refs_0_.1) | copy-start | bytes 3932164
  50.2 0.9 copy-start.5
  56.9 8.9 %collective-permute-start.11 = (f32[8,1024]{1,0:T(8,128)S(1)}, f32[8,1024]{1,0:T(8,128)S(1)}, u32[]{:S(2)}, u32[]{:S(2)}) collective-permute-start(f32[8,1024]{1,0:T(8,128)S(1)} %get-tuple-element.69), channel_id=1, source_target_pairs={{0,4},{4,8},{8,12},{12,16},{16,20},{20,24},{24,28},{28,0},{1,5},{5... | collective-permute-start | bytes 98312 | tf_op jit(solution)/shard_map/ppermute | solution.py:706
  62.2 3.5 %copy-start.4 = (f32[4,768]{1,0:T(4,128)S(1)}, f32[4,768]{1,0:T(4,128)}, u32[]{:S(2)}) copy-start(f32[4,768]{1,0:T(4,128)} %taps_ref.5) | copy-start | bytes 36868
  62.3 3.5 %copy-start.6 = (f32[4,256]{1,0:T(4,128)S(1)}, f32[4,256]{1,0:T(4,128)}, u32[]{:S(2)}) copy-start(f32[4,256]{1,0:T(4,128)} %mtaps_ref.5) | copy-start | bytes 12292
  62.3 3.5 %copy-start.7 = (f32[256]{0:T(256)S(1)}, f32[256]{0:T(256)}, u32[]{:S(2)}) copy-start(f32[256]{0:T(256)} %param.25) | copy-start | bytes 3076
  62.3 3.5 %copy-start.8 = (f32[12]{0:T(128)S(1)}, f32[12]{0:T(128)}, u32[]{:S(2)}) copy-start(f32[12]{0:T(128)} %param.26) | copy-start | bytes 148
  62.3 3.5 %copy-start.9 = (f32[12]{0:T(128)S(1)}, f32[12]{0:T(128)}, u32[]{:S(2)}) copy-start(f32[12]{0:T(128)} %param.27) | copy-start | bytes 148
  73.2 9.0 %collective-permute-start.14 = (bf16[136,384]{1,0:T(8,128)(2,1)S(1)}, bf16[136,384]{1,0:T(8,128)(2,1)S(1)}, u32[]{:S(2)}, u32[]{:S(2)}) collective-permute-start(bf16[136,384]{1,0:T(8,128)(2,1)S(1)} %get-tuple-element.99), channel_id=1, source_target_pairs={{0,12},{4,8},{8,4},{12,0},{16,28},{20,24},{24,20},{28,16},{1,13},{... | collective-permute-start | bytes 313352 | tf_op jit(solution)/shard_map/ppermute | solution.py:20
  78.2 6.9 %collective-permute-start.13 = (bf16[136,384]{1,0:T(8,128)(2,1)S(1)}, bf16[136,384]{1,0:T(8,128)(2,1)S(1)}, u32[]{:S(2)}, u32[]{:S(2)}) collective-permute-start(bf16[136,384]{1,0:T(8,128)(2,1)S(1)} %get-tuple-element.99), channel_id=1, source_target_pairs={{0,8},{4,12},{8,0},{12,4},{16,24},{20,28},{24,16},{28,20},{1,9},{5... | collective-permute-start | bytes 313352 | tf_op jit(solution)/shard_map/ppermute | solution.py:20
  78.8 7.0 %collective-permute-start.12 = (bf16[136,384]{1,0:T(8,128)(2,1)S(1)}, bf16[136,384]{1,0:T(8,128)(2,1)S(1)}, u32[]{:S(2)}, u32[]{:S(2)}) collective-permute-start(bf16[136,384]{1,0:T(8,128)(2,1)S(1)} %get-tuple-element.99), channel_id=1, source_target_pairs={{0,4},{4,0},{8,12},{12,8},{16,20},{20,16},{24,28},{28,24},{1,5},{5... | collective-permute-start | bytes 313352 | tf_op jit(solution)/shard_map/ppermute | solution.py:20
  79.2 10.0 %collective-permute-start.18 = (bf16[136,384]{1,0:T(8,128)(2,1)S(1)}, bf16[136,384]{1,0:T(8,128)(2,1)S(1)}, u32[]{:S(2)}, u32[]{:S(2)}) collective-permute-start(bf16[136,384]{1,0:T(8,128)(2,1)S(1)} %get-tuple-element.107), channel_id=1, source_target_pairs={{0,12},{4,8},{8,4},{12,0},{16,28},{20,24},{24,20},{28,16},{1,13},{... | collective-permute-start | bytes 313352 | tf_op jit(solution)/shard_map/ppermute | solution.py:20
  81.8 7.4 %collective-permute-start.17 = (bf16[136,384]{1,0:T(8,128)(2,1)S(1)}, bf16[136,384]{1,0:T(8,128)(2,1)S(1)}, u32[]{:S(2)}, u32[]{:S(2)}) collective-permute-start(bf16[136,384]{1,0:T(8,128)(2,1)S(1)} %get-tuple-element.107), channel_id=1, source_target_pairs={{0,8},{4,12},{8,0},{12,4},{16,24},{20,28},{24,16},{28,20},{1,9},{5... | collective-permute-start | bytes 313352 | tf_op jit(solution)/shard_map/ppermute | solution.py:20
  82.3 6.9 %collective-permute-start.16 = (bf16[136,384]{1,0:T(8,128)(2,1)S(1)}, bf16[136,384]{1,0:T(8,128)(2,1)S(1)}, u32[]{:S(2)}, u32[]{:S(2)}) collective-permute-start(bf16[136,384]{1,0:T(8,128)(2,1)S(1)} %get-tuple-element.107), channel_id=1, source_target_pairs={{0,4},{4,0},{8,12},{12,8},{16,20},{20,16},{24,28},{28,24},{1,5},{5... | collective-permute-start | bytes 313352 | tf_op jit(solution)/shard_map/ppermute | solution.py:20
  82.7 8.4 %copy-start.11 = (f32[12]{0:T(128)S(1)}, f32[12]{0:T(128)}, u32[]{:S(2)}) copy-start(f32[12]{0:T(128)} %param.28) | copy-start | bytes 148
  86.6 9.7 %collective-permute-start.15 = (bf16[136,384]{1,0:T(8,128)(2,1)S(1)}, bf16[136,384]{1,0:T(8,128)(2,1)S(1)}, u32[]{:S(2)}, u32[]{:S(2)}) collective-permute-start(bf16[136,384]{1,0:T(8,128)(2,1)S(1)} %get-tuple-element.104), channel_id=1, source_target_pairs={{0,16},{4,20},{8,24},{12,28},{16,0},{20,4},{24,8},{28,12},{1,17},{... | collective-permute-start | bytes 313352 | tf_op jit(solution)/shard_map/ppermute | solution.py:20
  90.1 7.7 %collective-permute-start.19 = (bf16[136,384]{1,0:T(8,128)(2,1)S(1)}, bf16[136,384]{1,0:T(8,128)(2,1)S(1)}, u32[]{:S(2)}, u32[]{:S(2)}) collective-permute-start(bf16[136,384]{1,0:T(8,128)(2,1)S(1)} %get-tuple-element.112), channel_id=1, source_target_pairs={{0,16},{4,20},{8,24},{12,28},{16,0},{20,4},{24,8},{28,12},{1,17},{... | collective-permute-start | bytes 313352 | tf_op jit(solution)/shard_map/ppermute | solution.py:20
  97.8 3.3 %copy-start.12 = (f32[768]{0:T(1024)S(1)}, f32[768]{0:T(1024)}, u32[]{:S(2)}) copy-start(f32[768]{0:T(1024)} %param.29) | copy-start | bytes 9220
  99.2 3.1 %collective-permute-start.22 = (f32[1,1024]{1,0:T(1,128)S(1)}, f32[1,1024]{1,0:T(1,128)S(1)}, u32[]{:S(2)}, u32[]{:S(2)}) collective-permute-start(f32[1,1024]{1,0:T(1,128)S(1)} %get-tuple-element.116.refs_0_), channel_id=1, source_target_pairs={{0,3},{1,2},{2,1},{3,0},{4,7},{5,6},{6,5},{7,4},{8,11},{9,10},{10,... | collective-permute-start | bytes 12296 | tf_op jit(solution)/shard_map/ppermute | solution.py:20
  99.7 3.6 %collective-permute-start.21 = (f32[1,1024]{1,0:T(1,128)S(1)}, f32[1,1024]{1,0:T(1,128)S(1)}, u32[]{:S(2)}, u32[]{:S(2)}) collective-permute-start(f32[1,1024]{1,0:T(1,128)S(1)} %get-tuple-element.116.refs_0_), channel_id=1, source_target_pairs={{0,2},{1,3},{2,0},{3,1},{4,6},{5,7},{6,4},{7,5},{8,10},{9,11},{10,... | collective-permute-start | bytes 12296 | tf_op jit(solution)/shard_map/ppermute | solution.py:20
  100.8 2.5 %collective-permute-start.20 = (f32[1,1024]{1,0:T(1,128)S(1)}, f32[1,1024]{1,0:T(1,128)S(1)}, u32[]{:S(2)}, u32[]{:S(2)}) collective-permute-start(f32[1,1024]{1,0:T(1,128)S(1)} %get-tuple-element.116.refs_0_), channel_id=1, source_target_pairs={{0,1},{1,0},{2,3},{3,2},{4,5},{5,4},{6,7},{7,6},{8,9},{9,8},{10,11... | collective-permute-start | bytes 12296 | tf_op jit(solution)/shard_map/ppermute | solution.py:20

commit v4 on v3

--- a/solution.py
+++ b/solution.py
@@ -11,6 +11,7 @@
 STATE = 128
 HEADDIM = 64
 CHUNK = 128
+HEADS_PAD = 16
 LANES = 128
 F32 = jnp.float32
 BF16 = jnp.bfloat16
@@ -107,17 +108,40 @@
     )(tokens, route_row)
 
 
+def pad_lanes(row):
+    pad = LANES - row.shape[1]
+    return jnp.concatenate([row, jnp.zeros((row.shape[0], pad), F32)], axis=1)
+
+
+def step_chain(raw, bias, rate):
+    column = lambda row: jnp.broadcast_to(pad_lanes(row), (LANES, LANES)).T[:HEADS_PAD]
+    raw = pad_lanes(raw).T[:HEADS_PAD] + column(bias)
+    step = jnp.maximum(raw, 0.0) + jnp.log1p(jnp.exp(-jnp.abs(raw)))
+    decay = -column(rate) * step
+    rows = lax.broadcasted_iota(jnp.int32, (CHUNK, CHUNK), 0)
+    cols = lax.broadcasted_iota(jnp.int32, (CHUNK, CHUNK), 1)
+    upper = jnp.where(rows <= cols, 1.0, 0.0).astype(BF16)
+    sums = mm(jnp.concatenate(split3(decay), axis=0), upper)
+    cum_t = sums[:HEADS_PAD] + sums[HEADS_PAD : 2 * HEADS_PAD] + sums[2 * HEADS_PAD :]
+    carried = jnp.exp(jnp.broadcast_to(cum_t[:, CHUNK - 1 :], cum_t.shape) - cum_t) * step
+    blank = jnp.zeros((LANES - 2 * HEADS_PAD, CHUNK), F32)
+    return jnp.concatenate([cum_t, carried, blank], axis=0).T, cum_t, step
+
+
 def project_kernel(cfg, *refs):
     counts, route_from, devices, cols, rank, near = cfg
     x_refs, refs = refs[: len(counts)], refs[len(counts):]
-    n_refs, refs = refs[:devices], refs[devices:]
-    w_ref, wbc_ref, up_ref = refs[:3]
-    refs = refs[3:]
+    if near:
+        n_refs, refs = refs[:devices], refs[devices:]
+    else:
+        route_ref, refs = refs[0], refs[1:]
+    w_ref, wbc_ref, up_ref, dtb_ref, rate_ref = refs[:5]
+    refs = refs[5:]
     if near:
         dt_ref, d_refs, refs = refs[0], refs[1 : 1 + devices], refs[1 + devices:]
-        z_ref, dto_ref, lift_ref, x_scr, tails_ref, rim_ref, wsm_ref, lift_scr = refs
+        z_ref, cum_ref, cum_t_ref, step_t_ref, lift_ref, x_scr, tails_ref, rim_ref, wsm_ref, route_ref, lift_scr = refs
     else:
-        wsm_ref, z_ref, dto_ref, lift_ref, x_scr = refs
+        wsm_ref, z_ref, cum_ref, cum_t_ref, step_t_ref, lift_ref, x_scr = refs
         lift_scr = lift_ref
     e = lax.axis_index("exp")
     rows = sum(counts)
@@ -140,17 +164,26 @@
         return route_mask(e, row, cols // rank, rank).T
 
     masks = []
-    for r, first, n in route_from:
-        for lane in range(first, first + n, LANES):
-            masks.append(mask_of(r, lane))
     if near:
-        last = route_from[0][1] + route_from[0][2] - LANES
+        whole = route_ref.shape[0] // devices
         for r in range(devices):
-            masks.append(mask_of(r, last)[LANES - 8 :, :])
+            for lane in range(0, whole, LANES):
+                mask = mask_of(r, lane)
+                route_ref[r * whole + lane : r * whole + lane + LANES, :] = mask.astype(BF16)
+                if r < 2:
+                    masks.append(mask)
+        for r in range(devices):
+            masks.append(route_ref[(r + 1) * whole - 16 : (r + 1) * whole, :].astype(F32)[8:])
+    else:
+        masks = [route_ref[first : first + n, :].astype(F32) for first, n in route_from]
     lift = jnp.where(jnp.concatenate(masks, axis=0) > 0.5, small[:, :LANES], 0.0).astype(BF16)
     lift_scr[...] = lift
-    pad = jnp.zeros((rows, 2 * LANES - small.shape[1]), F32)
-    dto_ref[...] = jnp.concatenate([small[:rows, LANES:], pad], axis=1)
+    for c in range(rows // CHUNK):
+        here = slice(c * CHUNK, (c + 1) * CHUNK)
+        both, cum_t, step_t = step_chain(small[here, LANES:], dtb_ref[...], rate_ref[...])
+        cum_ref[here, :] = both
+        cum_t_ref[c] = cum_t
+        step_t_ref[c] = step_t
     if near:
         lift_ref[...] = lift[:rows]
 
@@ -173,18 +206,19 @@
         rim_ref[...] = tails_ref[pl.ds(pl.multiple_of(row, 8), 8), :]
 
 
-def project(xs, route_from, notes, wz, wbc, up, rank, dt_t=None, downs=None, wsm=None):
+def project(xs, wz, wbc, up, dtb, rate, rank, devices, notes=None, dt_t=None, downs=None, route_from=None, routes=None, wsm=None):
     counts = tuple(x.shape[0] for x in xs)
     rows = sum(counts)
     features = wz.shape[0]
     width = up.shape[1] // 2 + wbc.shape[1]
-    devices = len(notes)
     near = wsm is None
-    args = list(xs) + list(notes) + [wz, wbc, up]
+    args = list(xs) + (list(notes) if near else [routes]) + [wz, wbc, up, dtb, rate]
     args += [dt_t, *downs] if near else [wsm]
     out_shape = [
         jax.ShapeDtypeStruct((rows, width), F32),
         jax.ShapeDtypeStruct((rows, LANES), F32),
+        jax.ShapeDtypeStruct((rows // CHUNK, HEADS_PAD, CHUNK), F32),
+        jax.ShapeDtypeStruct((rows // CHUNK, HEADS_PAD, CHUNK), F32),
         jax.ShapeDtypeStruct((rows, LANES), BF16),
     ]
     extra = 8 * devices if near else 0
@@ -193,6 +227,7 @@
     if near:
         out_shape += [jax.ShapeDtypeStruct((extra, width), F32), jax.ShapeDtypeStruct((8, width), F32)]
         out_shape.append(jax.ShapeDtypeStruct((LANES + 16, features), BF16))
+        out_shape.append(jax.ShapeDtypeStruct((devices * counts[0], LANES), BF16))
         scratch.append(pltpu.VMEM((rows + extra, LANES), BF16))
     cfg = (counts, route_from, devices, LANES // devices, rank, near)
     return pl.pallas_call(
@@ -263,27 +298,24 @@
     return jnp.concatenate(parts, axis=1)
 
 
-def pad_lanes(row):
-    return jnp.concatenate([row, jnp.zeros((1, LANES - row.shape[1]), F32)], axis=1)
-
-
 def state_kernel(
-    cfg, z_all, d_all, older_all, tails_ref, rim_ref,
-    taps_ref, mtaps_ref, bias_ref, mbias_ref, dtb_ref, rate_ref, *refs,
+    cfg, z_all, sums_all, sums_t_all, steps_t_all, older_all, tails_ref, rim_ref,
+    taps_ref, mtaps_ref, bias_ref, mbias_ref, *refs,
 ):
     width, per, far, where_am_i = cfg
-    xc_all, cum_all, step_all, update_all, total_all, ext = refs[-6:]
+    xc_all, cum_all, cum_t_all, step_t_all, update_all, total_all, ext = refs[-7:]
     e = lax.axis_index("exp")
     r, q = where_am_i(pl.program_id(0))
     block = r ^ e
     at = pl.program_id(0) * CHUNK
     there = pl.ds(pl.multiple_of(at, CHUNK), CHUNK)
-    z_ref, d_ref = z_all.at[there], d_all.at[there]
-    older = at + CHUNK - 8 if far else jnp.maximum(at - 8, 0)
+    z_ref = z_all.at[there]
+    older = r % 2 * CHUNK + CHUNK - 8 if far else jnp.maximum(at - 8, 0)
     prev_ref = older_all.at[pl.ds(pl.multiple_of(older, 8), 8)]
     chunk = block * per + q
     here = pl.ds(pl.multiple_of(chunk * CHUNK, CHUNK), CHUNK)
-    xc_ref, cum_ref, step_ref = xc_all.at[here], cum_all.at[here], step_all.at[here]
+    xc_ref, cum_ref = xc_all.at[here], cum_all.at[here]
+    cum_t_ref, step_t_ref = cum_t_all.at[pl.ds(chunk, 1)], step_t_all.at[pl.ds(chunk, 1)]
     update_ref, total_ref = update_all.at[pl.ds(chunk, 1)], total_all.at[pl.ds(chunk, 1)]
     before = pl.multiple_of((jnp.maximum(block - 1, 0) ^ e) * 8, 8)
     rim = jnp.where(lax.axis_index("seq") == 0, 0.0, rim_ref[...])
@@ -306,35 +338,28 @@
         outs.append(out)
     x, maps = outs
 
-    raw = d_ref[...] + pad_lanes(dtb_ref[...])
-    step = jnp.maximum(raw, 0.0) + jnp.log1p(jnp.exp(-jnp.abs(raw)))
-    decay = -pad_lanes(rate_ref[...]) * step
-    rows = lax.broadcasted_iota(jnp.int32, (CHUNK, CHUNK), 0)
-    cols = lax.broadcasted_iota(jnp.int32, (CHUNK, CHUNK), 1)
-    lower = jnp.where(rows >= cols, 1.0, 0.0).astype(BF16)
-    sums = mm(lower, jnp.concatenate(split3(decay), axis=1))
-    cum = sums[:, :LANES] + sums[:, LANES : 2 * LANES] + sums[:, 2 * LANES :]
-    total = cum[CHUNK - 1 : CHUNK, :]
-    cum_ref[...] = cum
-    step_ref[...] = step
-    total_ref[0] = jnp.broadcast_to(total, total_ref.shape[1:])
-
-    xs = (spread(jnp.exp(total - cum) * step, width) * x).astype(BF16)
+    both = sums_all[there, :]
+    cum_ref[...] = both
+    cum_t_ref[0] = sums_t_all[pl.ds(pl.program_id(0), 1)][0]
+    step_t_ref[0] = steps_t_all[pl.ds(pl.program_id(0), 1)][0]
+    total_ref[0] = jnp.broadcast_to(both[CHUNK - 1 : CHUNK, :], total_ref.shape[1:])
+
+    xs = (spread(both[:, HEADS_PAD:], width) * x).astype(BF16)
     b_hi, b_lo = split2(maps[:, :STATE].T)
     update_ref[0] = mm(jnp.concatenate([b_hi, b_lo], axis=1), jnp.concatenate([xs, xs], axis=0))
 
 
-def run_states(total, z, dt, older, tails, rim, params, width, per, far, buffers):
+def run_states(total, z, sums, older, tails, rim, params, width, per, far, buffers):
     wide = z.shape[1]
     chunks = total // CHUNK
     if far is None:
         steps = 2 * per
         at = lambda c: (c // per, c % per)
     else:
-        steps = 2
+        steps = z.shape[0] // CHUNK
         at = lambda c: (far[0] + c, far[1])
 
-    args = [z, dt, older, tails, rim, *params]
+    args = [z, *sums, older, tails, rim, *params]
     in_specs = [VMEM] * len(args)
     aliases = {}
     if buffers is not None:
@@ -347,7 +372,8 @@
         out_shape=(
             jax.ShapeDtypeStruct((total, wide), F32),
             jax.ShapeDtypeStruct((total, LANES), F32),
-            jax.ShapeDtypeStruct((total, LANES), F32),
+            jax.ShapeDtypeStruct((chunks, HEADS_PAD, CHUNK), F32),
+            jax.ShapeDtypeStruct((chunks, HEADS_PAD, CHUNK), F32),
             jax.ShapeDtypeStruct((chunks, STATE, width), F32),
             jax.ShapeDtypeStruct((chunks, 8, LANES), F32),
         ),
@@ -355,7 +381,7 @@
             num_scalar_prefetch=0,
             grid=(steps,),
             in_specs=in_specs,
-            out_specs=(VMEM,) * 5,
+            out_specs=(VMEM,) * 6,
             scratch_shapes=[pltpu.VMEM((CHUNK + 8, wide), F32)],
         ),
         input_output_aliases=aliases,
@@ -420,7 +446,7 @@
 
 
 def output_kernel(
-    width, per, xc_all, cum_all, step_all, before_all, local_all, direct_ref, *refs,
+    width, per, xc_all, cum_all, cum_t_all, step_t_all, before_all, local_all, direct_ref, *refs,
 ):
     g_refs, (a_all, b_all, c_all) = refs[:-3], refs[-3:]
     c = pl.program_id(0)
@@ -428,7 +454,7 @@
     r, q = (c // per) ^ lax.axis_index("exp"), c % per
     piece = jnp.where(r < 2, r * per + q, q * 2 + r % 2)
     there = pl.ds(pl.multiple_of(piece * CHUNK, CHUNK), CHUNK)
-    xc_ref, cum_ref, step_ref = xc_all.at[here], cum_all.at[here], step_all.at[here]
+    xc_ref, cum_ref = xc_all.at[here], cum_all.at[here]
     before_ref, local_ref = before_all.at[pl.ds(c, 1)], local_all.at[pl.ds(c, 1)]
     a_ref, b_ref, c_ref = a_all.at[here], b_all.at[here], c_all.at[here]
     bmap = xc_ref[:, width : width + STATE]
@@ -439,8 +465,8 @@
     c_ref[...] = c_hi
     gram = mm_nt(jnp.concatenate([c_hi, c_lo], axis=1), jnp.concatenate([b_hi, b_hi], axis=1))
     gram = gram + mm_nt(c_hi, b_lo)
-    cum_t = cum.T
-    step_t = step_ref[...].T
+    cum_t = cum_t_all[pl.ds(c, 1)][0]
+    step_t = step_t_all[pl.ds(c, 1)][0]
     rows = lax.broadcasted_iota(jnp.int32, (CHUNK, CHUNK), 0)
     cols = lax.broadcasted_iota(jnp.int32, (CHUNK, CHUNK), 1)
     causal = rows >= cols
@@ -472,7 +498,7 @@
         b_ref[:, lanes] = fade * jnp.exp(both(before_ref[0, 0:1, :])) * gate
 
 
-def run_outputs(xc, cum, step, before, local_states, gates, direct, local):
+def run_outputs(xc, cum, cum_t, step_t, before, local_states, gates, direct, local):
     total, _ = xc.shape
     width = gates[0].shape[1]
     chunks = total // CHUNK
@@ -487,7 +513,7 @@
         grid_spec=pltpu.PrefetchScalarGridSpec(
             num_scalar_prefetch=0,
             grid=(chunks,),
-            in_specs=[VMEM] * (6 + len(gates)),
+            in_specs=[VMEM] * (7 + len(gates)),
             out_specs=(VMEM,) * 3,
         ),
         cost_estimate=pl.CostEstimate(
@@ -497,7 +523,7 @@
             dimension_semantics=("arbitrary",), vmem_limit_bytes=12 << 20
         ),
         name="run_outputs",
-    )(xc, cum, step, before, local_states, direct, *gates)
+    )(xc, cum, cum_t, step_t, before, local_states, direct, *gates)
 
 
 def pack_logs(wide):
@@ -582,12 +608,14 @@
         s_scr[:, lanes] = entering.astype(BF16)
 
     part = 256
-    ones = jnp.ones((8, 2 * o_ref.shape[1]), BF16)
+    ones = jnp.ones((8, 2 * LANES), BF16)
     for at in range(0, o_ref.shape[0], part):
         rows = slice(at, at + part)
         gated = a_ref[rows, :] + b_ref[rows, :] * mm(c_ref[rows, :], s_scr[...])
         o_ref[rows, :] = gated
-        hi, lo = split2(gated * gated)
+        squared = gated * gated
+        folded = sum(squared[:, k : k + LANES] for k in range(0, squared.shape[1], LANES))
+        hi, lo = split2(folded)
         ss_ref[:, rows] = mm_nt(ones, jnp.concatenate([hi, lo], axis=1))[0:1]
 
 
@@ -611,32 +639,35 @@
 
 
 def norm_kernel(inner_width, g_ref, gain_ref, *refs):
-    *squares_refs, o_ref = refs
+    *squares_refs, o_hbm, o_ref, sems = refs
     rows, width = o_ref.shape
-    base = pl.program_id(0) * rows
+    copies = []
     for part in range(rows // LANES):
-        at = pl.multiple_of(base + part * LANES, LANES)
-        squares = sum(r[:, pl.ds(at, LANES)] for r in squares_refs)
+        here = slice(part * LANES, (part + 1) * LANES)
+        squares = sum(r[:, here] for r in squares_refs)
         scale = lax.rsqrt(squares / inner_width + 1e-05)
         column = jnp.broadcast_to(scale, (LANES, LANES)).T
         for lane in range(width // LANES):
             lanes = slice(lane * LANES, (lane + 1) * LANES)
-            value = g_ref[pl.ds(at, LANES), lanes] * column * gain_ref[:, lanes]
-            o_ref[part * LANES : (part + 1) * LANES, lanes] = value.astype(BF16)
+            o_ref[here, lanes] = (g_ref[here, lanes] * column * gain_ref[:, lanes]).astype(BF16)
+        copies.append(pltpu.make_async_copy(o_ref.at[here], o_hbm.at[here], sems.at[part]))
+        copies[-1].start()
+    for copy in copies:
+        copy.wait()
 
 
 def norm(gated, squares, gain, inner_width):
     total, width = gated.shape
-    rows = 256
     return pl.pallas_call(
         functools.partial(norm_kernel, inner_width),
         out_shape=jax.ShapeDtypeStruct((total, width), BF16),
-        grid=(total // rows,),
         in_specs=[VMEM] * (2 + len(squares)),
-        out_specs=pl.BlockSpec((rows, width), lambda i: (i, 0)),
-        compiler_params=pltpu.CompilerParams(
-            dimension_semantics=("arbitrary",), vmem_limit_bytes=8 << 20
-        ),
+        out_specs=pl.BlockSpec(memory_space=pl.ANY),
+        scratch_shapes=[
+            pltpu.VMEM((total, width), BF16),
+            pltpu.SemaphoreType.DMA((total // LANES,)),
+        ],
+        compiler_params=pltpu.CompilerParams(vmem_limit_bytes=8 << 20),
         name="norm",
     )(gated, gain, *squares)
 
@@ -679,12 +710,16 @@
     down = {0: adapter_down_weight.T}
     for k in range(2, n, 2):
         down[k] = swap(down[0], "exp", k)
-    *pieces, note = pack(tokens, routes.reshape(1, local), per)
+    *pieces, note = pack(tokens, routes.reshape(1, local), max(per - 1, 1))
     notes = {0: note}
     far = {}
     for k in range(2, n, 2):
         notes[k] = swap(note, "exp", k)
+    wz = gate_inner_weight.reshape(features, 2 * width)
     for q in range(per):
+        if q and q == per - 1:
+            late, wz = lax.optimization_barrier((tokens, wz))
+            pieces.append(late[q * CHUNK :])
         for k in range(2, n, 2):
             far[k, q] = swap(pieces[q], "exp", k)
     sibling = swap(tokens, "exp", 1)
@@ -693,38 +728,43 @@
         notes[k + 1] = swap(notes[k], "exp", 1)
     downs = [down[k] for k in range(n)]
     notes = [notes[k] for k in range(n)]
-    wz = gate_inner_weight.reshape(features, 2 * width)
     up = adapter_up_weight.reshape(experts, 2 * width)
     call = functools.partial(
-        project, notes=notes, wz=wz, wbc=state_map_weight, up=up, rank=rank
+        project, devices=n, wz=wz, wbc=state_map_weight, up=up, rank=rank,
+        dtb=step_size_bias[None, :], rate=head_decay_rate[None, :],
     )
-    z, dt, lift, rows, tails, rim, wsm = call(
-        [tokens, sibling], route_from=((0, 0, local), (1, 0, local)),
-        dt_t=step_size_weight.T, downs=downs,
+    z, *sums, lift, rows, tails, rim, wsm, masks = call(
+        [tokens, sibling], notes=notes, dt_t=step_size_weight.T, downs=downs
     )
     gates = [gate_project([rows], [lift], wz, up, n)]
     rim = lax.ppermute(rim, "seq", [(i, (i + 1) % shards) for i in range(shards)])
     params = [
         inner_conv_taps, state_map_taps, inner_conv_bias[None, :], state_map_conv_bias[None, :],
-        step_size_bias[None, :], head_decay_rate[None, :],
     ]
-    kept = run_states(total, z, dt, z, tails, rim, params, width, per, None, None)
+    kept = run_states(total, z, sums, z, tails, rim, params, width, per, None, None)
     far_rows = {}
     for q in range(per):
         for k in range(2, n, 2):
             mine = far[k, q]
             other = swap(mine, "exp", 1)
-            z, dt, lift, rows = call(
-                [mine, other],
-                route_from=((k, q * CHUNK, CHUNK), (k + 1, q * CHUNK, CHUNK)),
-                wsm=wsm,
-            )
-            far_rows[k, q] = (rows, lift, z)
-            older = far_rows[k, max(q - 1, 0)][2]
-            kept = run_states(
-                total, z, dt, older, tails, rim, params, width, per, (k, q), kept
-            )
-    xc, cum, step, updates, totals = kept
+            older = far_rows[k, q - 1][2] if q else z
+            pieces = [[mine, other]] if (k, q) != (n - 2, per - 1) else [[mine], [other]]
+            found = []
+            for p, piece in enumerate(pieces):
+                new_z, *sums, lift, rows = call(
+                    piece,
+                    route_from=tuple(
+                        ((k + p + m) * local + q * CHUNK, CHUNK) for m in range(len(piece))
+                    ),
+                    routes=masks,
+                    wsm=wsm,
+                )
+                kept = run_states(
+                    total, new_z, sums, older, tails, rim, params, width, per, (k + p, q), kept
+                )
+                found.append((rows, lift))
+            far_rows[k, q] = ([f[0] for f in found], [f[1] for f in found], new_z)
+    xc, cum, cum_t, step_t, updates, totals = kept
     states, before, parts = stitch(updates, totals)
     for d, radix in stages(shards):
         last = 2 * d == shards
@@ -740,10 +780,12 @@
                 parts[p] = combine(d, arrived, *part[1:])
     entering = [x for part in parts for x in part]
     for k in range(2, n, 2):
-        xs = [far_rows[k, q][0] for q in range(per)]
-        lifts = [far_rows[k, q][1] for q in range(per)]
+        xs = [x for q in range(per) for x in far_rows[k, q][0]]
+        lifts = [x for q in range(per) for x in far_rows[k, q][1]]
         gates.append(gate_project(xs, lifts, wz, up, n))
-    a, b, c = run_outputs(xc, cum, step, before, states, gates, direct_head_scale[None, :], local)
+    a, b, c = run_outputs(
+        xc, cum, cum_t, step_t, before, states, gates, direct_head_scale[None, :], local
+    )
     gated, mine = join(shards // 2, a, b, c, entering)
     others = [swap(mine, "exp", k) for k in range(1, n)]
     return norm(gated, [mine, *others], gated_norm_scale[None, :], width * n)

time: 106 us -> 98.6 us (0.930)
  waiting for transfers between devices: 38.4 us -> 33.2 us
  Pallas kernels: 35.3 us -> 32.3 us
  local copies, waits for them, and re-layouts: 10.7 us -> 12 us
    ppermute x22, waiting for transfers between devices: 38.4 us -> 33.2 us  [swap(): lax.ppermute(block, axis, [(i, i ^ mask) for i in range(lax.axis_size(axi...]
    pallas_call x3 -> x4, Pallas kernels: 6.85 us -> 5.08 us  [run_states(): pl.pallas_call(functools.partial(state_kernel, (width, per, far is not No...]
    pallas_call x3 -> x4, Pallas kernels: 12.7 us -> 11.4 us  [project(): pl.pallas_call(functools.partial(project_kernel, cfg), out_shape=tuple(ou...]
    slice x0 -> x1, local copies, waits for them, and re-layouts: none -> 1.13 us  [body(): pieces.append(late[q * CHUNK:])]
    unnamed x28 -> x30, local copies, waits for them, and re-layouts: 9.98 us -> 10.9 us
  transfers between devices with their start and end apart: 23 -> 23, of which waited for: 9 -> 10; matrix products, arithmetic and copies ran while one was open for 6% -> 7% of each run, Pallas kernels for 23% -> 24%
where the time goes in v4:
time: 98.6 us; the launch traced here: 98.3 us
  waiting for transfers between devices  33.2 us (34%)
  Pallas kernels  32.3 us (33%)
  starting transfers between devices  20.3 us (21%)
  local copies, waits for them, and re-layouts  12 us (12%)
    ppermute x22, waiting for transfers between devices, swap(): lax.ppermute(block, axis, [(i, i ^ mask) for i in range(lax.axis_size(axi...  33.2 us
    ppermute x22, starting transfers between devices, swap(): lax.ppermute(block, axis, [(i, i ^ mask) for i in range(lax.axis_size(axi...  18.6 us
    pallas_call x4, Pallas kernels, project(): pl.pallas_call(functools.partial(project_kernel, cfg), out_shape=tuple(ou...  11.4 us
    unnamed x30, local copies, waits for them, and re-layouts  10.9 us
    pallas_call x4, Pallas kernels, run_states(): pl.pallas_call(functools.partial(state_kernel, (width, per, far is not No...  5.08 us
    pallas_call x1, Pallas kernels, run_outputs(): pl.pallas_call(functools.partial(output_kernel, width, per), out_shape=(j...  4.88 us
    pallas_call x2, Pallas kernels, gate_project(): pl.pallas_call(functools.partial(gate_kernel, counts, devices), out_shape...  4.87 us
  transfers between devices with their start and end apart: 23, of which 10 were waited for; matrix products, arithmetic and copies ran while one was open for 7% of the time, Pallas kernels for 24%

profile of v4, /device:TPU:0, one launch (start us, length us, event | category | flops | bytes accessed | tf_op | source)
XLA Modules:
  0.0 98.3 jit_solution(10219403356707008936)
XLA Ops:
  0.0 0.5 collective-permute-start.2
  0.5 1.3 %copy-done.1 = bf16[256,2560]{1,0:T(8,128)(2,1)S(1)} copy-done((bf16[256,2560]{1,0:T(8,128)(2,1)S(1)}, bf16[256,2560]{1,0:T(8,128)(2,1)}, u32[]{:S(2)}) %copy-start.1) | copy-done | bytes 1310744
  1.8 0.7 copy-done.10
  2.5 1.1 %pack.1 = (bf16[128,2560]{1,0:T(8,128)(2,1)}, bf16[8,2560]{1,0:T(8,128)(2,1)S(1)}) custom-call(bf16[256,2560]{1,0:T(8,128)(2,1)S(1)} %copy-done.1, s32[1,256]{1,0:T(1,128)S(1)} %bitcast.39), custom_call_target="tpu_custom_call" | custom-call | tf_op jit(solution)/shard_map/pack/pallas_call | solution.py:96
  3.6 2.6 %collective-permute-start.9 = (bf16[128,2560]{1,0:T(8,128)(2,1)}, bf16[128,2560]{1,0:T(8,128)(2,1)S(1)}, u32[]{:S(2)}, u32[]{:S(2)}) collective-permute-start(bf16[128,2560]{1,0:T(8,128)(2,1)} %get-tuple-element.93), channel_id=1, source_target_pairs={{0,2},{1,3},{2,0},{3,1},{4,6},{5,7},{6,4},{7,5},{8,10},{9,11},{10,... | collective-permute-start | bytes 1966088 | tf_op jit(solution)/shard_map/ppermute | solution.py:21
  6.2 4.7 %copy.34 = bf16[320,8,2,768]{3,1,2,0:T(8,128)(2,1)S(1)} copy(bf16[320,8,2,768]{3,2,1,0:T(2,128)(2,1)} %bitcast.41) | data formatting | bytes 15728640
  10.9 1.1 %slice.3 = bf16[128,2560]{1,0:T(8,128)(2,1)S(1)} slice(bf16[256,2560]{1,0:T(8,128)(2,1)} %refs_0_.1), slice={[128:256], [0:2560]} | slice | bytes 1310720 | tf_op jit(solution)/shard_map/slice | solution.py:722
  12.1 2.0 %collective-permute-start.7 = (bf16[32,2560]{1,0:T(8,128)(2,1)}, bf16[32,2560]{1,0:T(8,128)(2,1)S(1)}, u32[]{:S(2)}, u32[]{:S(2)}) collective-permute-start(bf16[32,2560]{1,0:T(8,128)(2,1)} %bitcast.23), channel_id=1, source_target_pairs={{0,2},{1,3},{2,0},{3,1},{4,6},{5,7},{6,4},{7,5},{8,10},{9,11},{10,... | collective-permute-start | bytes 491528 | tf_op jit(solution)/shard_map/ppermute | solution.py:21
  14.2 7.8 %collective-permute-done.9.refs_0_ = bf16[128,2560]{1,0:T(8,128)(2,1)S(1)} collective-permute-done((bf16[128,2560]{1,0:T(8,128)(2,1)}, bf16[128,2560]{1,0:T(8,128)(2,1)S(1)}, u32[]{:S(2)}, u32[]{:S(2)}) %collective-permute-start.9) | collective-permute-done | bytes 655392 | tf_op jit(solution)/shard_map/ppermute | solution.py:21
  22.0 18.2 %collective-permute-done.4.refs_4_ = bf16[8,2560]{1,0:T(8,128)(2,1)S(1)} collective-permute-done((bf16[8,2560]{1,0:T(8,128)(2,1)S(1)}, bf16[8,2560]{1,0:T(8,128)(2,1)S(1)}, u32[]{:S(2)}, u32[]{:S(2)}) %collective-permute-start.4) | collective-permute-done | bytes 40992 | tf_op jit(solution)/shard_map/ppermute | solution.py:21
  40.2 1.2 %collective-permute-done.3.refs_3_ = bf16[8,2560]{1,0:T(8,128)(2,1)S(1)} collective-permute-done((bf16[8,2560]{1,0:T(8,128)(2,1)S(1)}, bf16[8,2560]{1,0:T(8,128)(2,1)S(1)}, u32[]{:S(2)}, u32[]{:S(2)}) %collective-permute-start.3) | collective-permute-done | bytes 40992 | tf_op jit(solution)/shard_map/ppermute | solution.py:21
  41.6 1.1 %collective-permute-done.5.refs_5_ = bf16[8,2560]{1,0:T(8,128)(2,1)S(1)} collective-permute-done((bf16[8,2560]{1,0:T(8,128)(2,1)S(1)}, bf16[8,2560]{1,0:T(8,128)(2,1)S(1)}, u32[]{:S(2)}, u32[]{:S(2)}) %collective-permute-start.5) | collective-permute-done | bytes 40992 | tf_op jit(solution)/shard_map/ppermute | solution.py:21
  42.8 0.3 collective-permute-start.8
  43.4 1.0 %copy.35 = bf16[16,8,2,768]{3,1,2,0:T(8,128)(2,1)S(1)} copy(bf16[16,8,2,768]{3,2,1,0:T(2,128)(2,1)} %bitcast.42) | data formatting | bytes 786432
  44.5 1.3 %copy-done.2 = bf16[256,2560]{1,0:T(8,128)(2,1)S(1)} copy-done((bf16[256,2560]{1,0:T(8,128)(2,1)S(1)}, bf16[256,2560]{1,0:T(8,128)(2,1)}, u32[]{:S(2)}) %copy-start.2) | copy-done | bytes 1310744
  45.8 0.9 copy-done.4
  46.8 0.9 copy-done.5
  47.7 5.7 %project.4 = (f32[512,1024]{1,0:T(8,128)S(1)}, f32[512,128]{1,0:T(8,128)S(1)}, f32[4,16,128]{2,1,0:T(8,128)S(1)}, f32[4,16,128]{2,1,0:T(8,128)S(1)}, bf16[512,12...) custom-call(bf16[256,2560]{1,0:T(8,128)(2,1)S(1)} %copy-done.2, ...), custom_call_target="tpu_custom_call" | custom-call | flops 3355443200 | bytes 9961472 | tf_op jit(solution)/shard_map/project/pallas_call | solution.py:233
  53.4 1.8 %collective-permute-start.11 = (f32[8,1024]{1,0:T(8,128)S(1)}, f32[8,1024]{1,0:T(8,128)S(1)}, u32[]{:S(2)}, u32[]{:S(2)}) collective-permute-start(f32[8,1024]{1,0:T(8,128)S(1)} %get-tuple-element.96), channel_id=1, source_target_pairs={{0,4},{4,8},{8,12},{12,16},{16,20},{20,24},{24,28},{28,0},{1,5},{5... | collective-permute-start | bytes 98312 | tf_op jit(solution)/shard_map/ppermute | solution.py:740
  55.2 1.7 %project.7 = (f32[128,1024]{1,0:T(8,128)S(1)}, f32[128,128]{1,0:T(8,128)S(1)}, f32[1,16,128]{2,1,0:T(8,128)S(1)}, f32[1,16,128]{2,1,0:T(8,128)S(1)}, bf16[128,12...) custom-call(bf16[128,2560]{1,0:T(8,128)(2,1)S(1)} %collective-permute-done.refs_0_, ...), custom_call_target="tpu_custom_call" | custom-call | flops 838860800 | bytes 6422528 | tf_op jit(solution)/shard_map/project/pallas_call | solution.py:233
  56.9 2.3 %project.6 = (f32[256,1024]{1,0:T(8,128)S(1)}, f32[256,128]{1,0:T(8,128)S(1)}, f32[2,16,128]{2,1,0:T(8,128)S(1)}, f32[2,16,128]{2,1,0:T(8,128)S(1)}, bf16[256,12...) custom-call(bf16[128,2560]{1,0:T(8,128)(2,1)S(1)} %collective-permute-done.9.refs_0_, ...), custom_call_target="tpu_custom_call" | custom-call | flops 1677721600 | bytes 7602176 | tf_op jit(solution)/shard_map/project/pallas_call | solution.py:233
  59.2 1.7 %project.5 = (f32[128,1024]{1,0:T(8,128)S(1)}, f32[128,128]{1,0:T(8,128)S(1)}, f32[1,16,128]{2,1,0:T(8,128)S(1)}, f32[1,16,128]{2,1,0:T(8,128)S(1)}, bf16[128,12...) custom-call(bf16[128,2560]{1,0:T(8,128)(2,1)S(1)} %collective-permute-done.1.refs_0_, ...), custom_call_target="tpu_custom_call" | custom-call | flops 838860800 | bytes 6422528 | tf_op jit(solution)/shard_map/project/pallas_call | solution.py:233
  60.9 2.7 %run_states.4 = (f32[1024,1024]{1,0:T(8,128)S(1)}, f32[1024,128]{1,0:T(8,128)S(1)}, f32[8,16,128]{2,1,0:T(8,128)S(1)}, f32[8,16,128]{2,1,0:T(8,128)S(1)}, f32[8,...) custom-call(f32[512,1024]{1,0:T(8,128)S(1)} %get-tuple-element.104.z_all.older_all, ...), custom_call_target="tpu_custom_call" | custom-call | flops 786432000 | bytes 6291456 | tf_op jit(solution)/shard_map/run_states/pallas_call | solution.py:370
  63.6 1.2 %run_states.5 = (f32[1024,1024]{1,0:T(8,128)S(1)}, f32[1024,128]{1,0:T(8,128)S(1)}, f32[8,16,128]{2,1,0:T(8,128)S(1)}, f32[8,16,128]{2,1,0:T(8,128)S(1)}, f32[8,...) custom-call(f32[256,1024]{1,0:T(8,128)S(1)} %get-tuple-element.94.z_, ...), custom_call_target="tpu_custom_call", output_to_operand_aliasing={{0}: (11, {}), {1}: (12, {}), {2}: (13, {}), {3}: (14, {}),... | custom-call | flops 393216000 | bytes 3145728 | tf_op jit(solution)/shard_map/run_states/pallas_call | solution.py:370
  64.9 0.6 run_states.6
  65.5 0.6 run_states.7
  66.1 0.5 stitch.1
  66.6 2.6 %collective-permute-start.14 = (bf16[136,384]{1,0:T(8,128)(2,1)S(1)}, bf16[136,384]{1,0:T(8,128)(2,1)S(1)}, u32[]{:S(2)}, u32[]{:S(2)}) collective-permute-start(bf16[136,384]{1,0:T(8,128)(2,1)S(1)} %get-tuple-element.145), channel_id=1, source_target_pairs={{0,12},{4,8},{8,4},{12,0},{16,28},{20,24},{24,20},{28,16},{1,13},{... | collective-permute-start | bytes 313352 | tf_op jit(solution)/shard_map/ppermute | solution.py:21
  69.2 2.4 %gate_project.2.refs_0_ = f32[512,768]{1,0:T(8,128)S(1)} custom-call(bf16[544,2560]{1,0:T(8,128)(2,1)S(1)} %get-tuple-element.134.refs_0_, bf16[512,128]{1,0:T(8,128)(2,1)S(1)} %get-tuple-element.135.refs_1_, bf16[2560,1536]{1,0:T(8,128)(2,1)S(1)} %bitcast.15, bf16[128,1536]{1,0:T(8,128)(2,1)S(1)} %bitcast.21), custom_call_target="tpu_custom_call" | custom-call | flops 2013265920 | bytes 8126464 | tf_op jit(solution)/shard_map/gate_project/pallas_call | solution.py:275
  71.6 0.5 collective-permute-start.13
  72.1 0.5 collective-permute-start.12
  72.6 2.6 %collective-permute-start.18 = (bf16[136,384]{1,0:T(8,128)(2,1)S(1)}, bf16[136,384]{1,0:T(8,128)(2,1)S(1)}, u32[]{:S(2)}, u32[]{:S(2)}) collective-permute-start(bf16[136,384]{1,0:T(8,128)(2,1)S(1)} %get-tuple-element.153), channel_id=1, source_target_pairs={{0,12},{4,8},{8,4},{12,0},{16,28},{20,24},{24,20},{28,16},{1,13},{... | collective-permute-start | bytes 313352 | tf_op jit(solution)/shard_map/ppermute | solution.py:21
  75.1 0.5 collective-permute-start.17
  75.6 0.5 collective-permute-start.16
  76.1 2.5 %gate_project.3.refs_1_ = f32[512,768]{1,0:T(8,128)S(1)} custom-call(bf16[256,2560]{1,0:T(8,128)(2,1)S(1)} %get-tuple-element.136.refs_0_, bf16[128,2560]{1,0:T(8,128)(2,1)S(1)} %get-tuple-element.137.refs_1_, bf16[128,2560]{1,0:T(8,128)(2,1)S(1)} %get-tuple-element.138.refs_2_, bf16[256,128]{1,0:T(8,128)(2,1)S(1)} %get-tuple-element.139.refs_3_, ...), custom_call_target="tpu_custom_call" | custom-call | flops 2013265920 | bytes 8126464 | tf_op jit(solution)/shard_map/gate_project/pallas_call | solution.py:275
  78.6 0.6 collective-permute-done.12.refs_0_
  79.2 0.9 combine.2
  80.1 2.6 %collective-permute-start.15 = (bf16[136,384]{1,0:T(8,128)(2,1)S(1)}, bf16[136,384]{1,0:T(8,128)(2,1)S(1)}, u32[]{:S(2)}, u32[]{:S(2)}) collective-permute-start(bf16[136,384]{1,0:T(8,128)(2,1)S(1)} %get-tuple-element.150), channel_id=1, source_target_pairs={{0,16},{4,20},{8,24},{12,28},{16,0},{20,4},{24,8},{28,12},{1,17},{... | collective-permute-start | bytes 313352 | tf_op jit(solution)/shard_map/ppermute | solution.py:21
  82.7 0.9 combine.3
  83.5 1.0 collective-permute-start.19
  84.5 4.9 %run_outputs.1 = (f32[1024,768]{1,0:T(8,128)S(1)}, f32[1024,768]{1,0:T(8,128)S(1)}, bf16[1024,128]{1,0:T(8,128)(2,1)S(1)}) custom-call(f32[1024,1024]{1,0:T(8,128)S(1)} %get-tuple-element.126.xc_all, f32[1024,128]{1,0:T(8,128)S(1)} %get-tuple-element.127.cum_all, f32[8,16,128]{2,1,0:T(8,128)S(1)} %get-tuple-element.128.cum_t_all, ...), custom_call_target="tpu_custom_call" | custom-call | flops 2359296000 | bytes 12582912 | tf_op jit(solution)/shard_map/run_outputs/pallas_call | solution.py:506
  89.7 1.5 %collective-permute-done.19.refs_3_ = bf16[136,384]{1,0:T(8,128)(2,1)S(1)} collective-permute-done((bf16[136,384]{1,0:T(8,128)(2,1)S(1)}, bf16[136,384]{1,0:T(8,128)(2,1)S(1)}, u32[]{:S(2)}, u32[]{:S(2)}) %collective-permute-start.19) | collective-permute-done | bytes 104480 | tf_op jit(solution)/shard_map/ppermute | solution.py:21
  91.3 1.3 %join.1 = (f32[1024,768]{1,0:T(8,128)S(1)}, f32[1,1024]{1,0:T(1,128)S(1)}) custom-call(f32[1024,768]{1,0:T(8,128)S(1)} %get-tuple-element.142.a_ref, f32[1024,768]{1,0:T(8,128)S(1)} %get-tuple-element.143.b_ref, bf16[1024,128]{1,0:T(8,128)(2,1)S(1)} %get-tuple-element.144.c_ref, bf16[136,384]{1,0:T(8,128)(2,1)S(1)} %collective-permute-done.15.refs_0_, ...), custom_call_target="tpu_custom_call" | custom-call | tf_op jit(solution)/shard_map/join/pallas_call | solution.py:624
  92.6 0.5 collective-permute-start.22
  93.1 1.0 %collective-permute-start.21 = (f32[1,1024]{1,0:T(1,128)S(1)}, f32[1,1024]{1,0:T(1,128)S(1)}, u32[]{:S(2)}, u32[]{:S(2)}) collective-permute-start(f32[1,1024]{1,0:T(1,128)S(1)} %get-tuple-element.162.refs_0_), channel_id=1, source_target_pairs={{0,2},{1,3},{2,0},{3,1},{4,6},{5,7},{6,4},{7,5},{8,10},{9,11},{10,... | collective-permute-start | bytes 12296 | tf_op jit(solution)/shard_map/ppermute | solution.py:21
  94.5 1.2 %collective-permute-done.22.refs_3_ = f32[1,1024]{1,0:T(1,128)S(1)} collective-permute-done((f32[1,1024]{1,0:T(1,128)S(1)}, f32[1,1024]{1,0:T(1,128)S(1)}, u32[]{:S(2)}, u32[]{:S(2)}) %collective-permute-start.22) | collective-permute-done | bytes 4128 | tf_op jit(solution)/shard_map/ppermute | solution.py:21
  95.6 1.1 %collective-permute-done.21.refs_2_ = f32[1,1024]{1,0:T(1,128)S(1)} collective-permute-done((f32[1,1024]{1,0:T(1,128)S(1)}, f32[1,1024]{1,0:T(1,128)S(1)}, u32[]{:S(2)}, u32[]{:S(2)}) %collective-permute-start.21) | collective-permute-done | bytes 4128 | tf_op jit(solution)/shard_map/ppermute | solution.py:21
  96.8 1.4 %norm.1 = bf16[1024,768]{1,0:T(8,128)(2,1)} custom-call(f32[1024,768]{1,0:T(8,128)S(1)} %get-tuple-element.161.g_ref, f32[1,768]{1,0:T(1,128)S(1)} %broadcast_in_dim.23.gain_ref, f32[1,1024]{1,0:T(1,128)S(1)} %get-tuple-element.162.refs_0_, f32[1,1024]{1,0:T(1,128)S(1)} %collective-permute-done.20.refs_1_, f32[1,1024]{1,0:T(1,128)S(1)} %collective-permute-done.21.refs_2_, ...), custom_call_target="tpu_custom_call" | custom-call | tf_op jit(solution)/shard_map/norm/pallas_call | solution.py:661
  (48 shorter events, 1.5 us)
Async XLA Ops:
  0.0 44.5 %collective-permute-start.2 = (bf16[256,2560]{1,0:T(8,128)(2,1)}, bf16[256,2560]{1,0:T(8,128)(2,1)}, u32[]{:S(2)}, u32[]{:S(2)}) collective-permute-start(bf16[256,2560]{1,0:T(8,128)(2,1)} %refs_0_.1), channel_id=1, source_target_pairs={{0,1},{1,0},{2,3},{3,2},{4,5},{5,4},{6,7},{7,6},{8,9},{9,8},{10,11... | collective-permute-start | bytes 3932168 | tf_op jit(solution)/shard_map/ppermute | solution.py:21
  0.5 1.3 %copy-start.1 = (bf16[256,2560]{1,0:T(8,128)(2,1)S(1)}, bf16[256,2560]{1,0:T(8,128)(2,1)}, u32[]{:S(2)}) copy-start(bf16[256,2560]{1,0:T(8,128)(2,1)} %refs_0_.1) | copy-start | bytes 3932164
  1.8 0.7 copy-start.10
  3.6 18.4 %collective-permute-start.9 = (bf16[128,2560]{1,0:T(8,128)(2,1)}, bf16[128,2560]{1,0:T(8,128)(2,1)S(1)}, u32[]{:S(2)}, u32[]{:S(2)}) collective-permute-start(bf16[128,2560]{1,0:T(8,128)(2,1)} %get-tuple-element.93), channel_id=1, source_target_pairs={{0,2},{1,3},{2,0},{3,1},{4,6},{5,7},{6,4},{7,5},{8,10},{9,11},{10,... | collective-permute-start | bytes 1966088 | tf_op jit(solution)/shard_map/ppermute | solution.py:21
  6.2 37.2 %copy-start.12 = (f32[768]{0:T(1024)S(1)}, f32[768]{0:T(1024)}, u32[]{:S(2)}) copy-start(f32[768]{0:T(1024)} %param.24) | copy-start | bytes 9220
  6.2 38.3 %copy-start = (bf16[2560,256]{1,0:T(8,128)(2,1)S(1)}, bf16[2560,256]{1,0:T(8,128)(2,1)}, u32[]{:S(2)}) copy-start(bf16[2560,256]{1,0:T(8,128)(2,1)} %refs_3_.3) | copy-start | bytes 3932164
  6.2 38.3 %copy-start.8 = (f32[12]{0:T(128)S(1)}, f32[12]{0:T(128)}, u32[]{:S(2)}) copy-start(f32[12]{0:T(128)} %param.26) | copy-start | bytes 148
  6.2 38.3 %copy-start.9 = (f32[12]{0:T(128)S(1)}, f32[12]{0:T(128)}, u32[]{:S(2)}) copy-start(f32[12]{0:T(128)} %param.27) | copy-start | bytes 148
  12.0 31.2 %collective-permute-start = (bf16[128,2560]{1,0:T(8,128)(2,1)S(1)}, bf16[128,2560]{1,0:T(8,128)(2,1)S(1)}, u32[]{:S(2)}, u32[]{:S(2)}) collective-permute-start(bf16[128,2560]{1,0:T(8,128)(2,1)S(1)} %slice.3), channel_id=1, source_target_pairs={{0,2},{1,3},{2,0},{3,1},{4,6},{5,7},{6,4},{7,5},{8,10},{9,11},{10,... | collective-permute-start | bytes 1966088 | tf_op jit(solution)/shard_map/ppermute | solution.py:21
  12.1 30.7 %collective-permute-start.7 = (bf16[32,2560]{1,0:T(8,128)(2,1)}, bf16[32,2560]{1,0:T(8,128)(2,1)S(1)}, u32[]{:S(2)}, u32[]{:S(2)}) collective-permute-start(bf16[32,2560]{1,0:T(8,128)(2,1)} %bitcast.23), channel_id=1, source_target_pairs={{0,2},{1,3},{2,0},{3,1},{4,6},{5,7},{6,4},{7,5},{8,10},{9,11},{10,... | collective-permute-start | bytes 491528 | tf_op jit(solution)/shard_map/ppermute | solution.py:21
  14.1 26.1 %collective-permute-start.4 = (bf16[8,2560]{1,0:T(8,128)(2,1)S(1)}, bf16[8,2560]{1,0:T(8,128)(2,1)S(1)}, u32[]{:S(2)}, u32[]{:S(2)}) collective-permute-start(bf16[8,2560]{1,0:T(8,128)(2,1)S(1)} %get-tuple-element.85.refs_2_), channel_id=1, source_target_pairs={{0,2},{1,3},{2,0},{3,1},{4,6},{5,7},{6,4},{7,5},{8,10},{9,11},{10,... | collective-permute-start | bytes 122888 | tf_op jit(solution)/shard_map/ppermute | solution.py:21
  22.0 34.9 %collective-permute-start.10 = (bf16[128,2560]{1,0:T(8,128)(2,1)S(1)}, bf16[128,2560]{1,0:T(8,128)(2,1)S(1)}, u32[]{:S(2)}, u32[]{:S(2)}) collective-permute-start(bf16[128,2560]{1,0:T(8,128)(2,1)S(1)} %collective-permute-done.9.refs_0_), channel_id=1, source_target_pairs={{0,1},{1,0},{2,3},{3,2},{4,5},{5,4},{6,7},{7,6},{8,9},{9,8},{10,11... | collective-permute-start | bytes 1966088 | tf_op jit(solution)/shard_map/ppermute | solution.py:21
  40.2 1.2 %collective-permute-start.3 = (bf16[8,2560]{1,0:T(8,128)(2,1)S(1)}, bf16[8,2560]{1,0:T(8,128)(2,1)S(1)}, u32[]{:S(2)}, u32[]{:S(2)}) collective-permute-start(bf16[8,2560]{1,0:T(8,128)(2,1)S(1)} %get-tuple-element.85.refs_2_), channel_id=1, source_target_pairs={{0,1},{1,0},{2,3},{3,2},{4,5},{5,4},{6,7},{7,6},{8,9},{9,8},{10,11... | collective-permute-start | bytes 122888 | tf_op jit(solution)/shard_map/ppermute | solution.py:21
  41.4 1.2 %collective-permute-start.5 = (bf16[8,2560]{1,0:T(8,128)(2,1)S(1)}, bf16[8,2560]{1,0:T(8,128)(2,1)S(1)}, u32[]{:S(2)}, u32[]{:S(2)}) collective-permute-start(bf16[8,2560]{1,0:T(8,128)(2,1)S(1)} %collective-permute-done.4.refs_4_), channel_id=1, source_target_pairs={{0,1},{1,0},{2,3},{3,2},{4,5},{5,4},{6,7},{7,6},{8,9},{9,8},{10,11... | collective-permute-start | bytes 122888 | tf_op jit(solution)/shard_map/ppermute | solution.py:21
  42.7 1.7 %collective-permute-start.6 = (bf16[32,2560]{1,0:T(8,128)(2,1)}, bf16[32,2560]{1,0:T(8,128)(2,1)S(1)}, u32[]{:S(2)}, u32[]{:S(2)}) collective-permute-start(bf16[32,2560]{1,0:T(8,128)(2,1)} %bitcast.24), channel_id=1, source_target_pairs={{0,1},{1,0},{2,3},{3,2},{4,5},{5,4},{6,7},{7,6},{8,9},{9,8},{10,11... | collective-permute-start | bytes 491528 | tf_op jit(solution)/shard_map/ppermute | solution.py:21
  42.8 1.7 %collective-permute-start.8 = (bf16[32,2560]{1,0:T(8,128)(2,1)S(1)}, bf16[32,2560]{1,0:T(8,128)(2,1)S(1)}, u32[]{:S(2)}, u32[]{:S(2)}) collective-permute-start(bf16[32,2560]{1,0:T(8,128)(2,1)S(1)} %collective-permute-done.7.refs_14_), channel_id=1, source_target_pairs={{0,1},{1,0},{2,3},{3,2},{4,5},{5,4},{6,7},{7,6},{8,9},{9,8},{10,11... | collective-permute-start | bytes 491528 | tf_op jit(solution)/shard_map/ppermute | solution.py:21
  43.2 16.0 %collective-permute-start.1 = (bf16[128,2560]{1,0:T(8,128)(2,1)S(1)}, bf16[128,2560]{1,0:T(8,128)(2,1)S(1)}, u32[]{:S(2)}, u32[]{:S(2)}) collective-permute-start(bf16[128,2560]{1,0:T(8,128)(2,1)S(1)} %collective-permute-done.refs_0_), channel_id=1, source_target_pairs={{0,1},{1,0},{2,3},{3,2},{4,5},{5,4},{6,7},{7,6},{8,9},{9,8},{10,11... | collective-permute-start | bytes 1966088 | tf_op jit(solution)/shard_map/ppermute | solution.py:21
  44.5 1.3 %copy-start.2 = (bf16[256,2560]{1,0:T(8,128)(2,1)S(1)}, bf16[256,2560]{1,0:T(8,128)(2,1)}, u32[]{:S(2)}) copy-start(bf16[256,2560]{1,0:T(8,128)(2,1)} %refs_0_.1) | copy-start | bytes 3932164
  45.8 0.9 copy-start.4
  46.8 0.9 copy-start.5
  53.4 7.5 %collective-permute-start.11 = (f32[8,1024]{1,0:T(8,128)S(1)}, f32[8,1024]{1,0:T(8,128)S(1)}, u32[]{:S(2)}, u32[]{:S(2)}) collective-permute-start(f32[8,1024]{1,0:T(8,128)S(1)} %get-tuple-element.96), channel_id=1, source_target_pairs={{0,4},{4,8},{8,12},{12,16},{16,20},{20,24},{24,28},{28,0},{1,5},{5... | collective-permute-start | bytes 98312 | tf_op jit(solution)/shard_map/ppermute | solution.py:740
  59.2 1.7 %copy-start.3 = (f32[4,768]{1,0:T(4,128)S(1)}, f32[4,768]{1,0:T(4,128)}, u32[]{:S(2)}) copy-start(f32[4,768]{1,0:T(4,128)} %taps_ref.7) | copy-start | bytes 36868
  59.2 1.7 %copy-start.6 = (f32[4,256]{1,0:T(4,128)S(1)}, f32[4,256]{1,0:T(4,128)}, u32[]{:S(2)}) copy-start(f32[4,256]{1,0:T(4,128)} %mtaps_ref.7) | copy-start | bytes 12292
  59.2 1.7 %copy-start.7 = (f32[256]{0:T(256)S(1)}, f32[256]{0:T(256)}, u32[]{:S(2)}) copy-start(f32[256]{0:T(256)} %param.25) | copy-start | bytes 3076
  66.6 9.0 %collective-permute-start.14 = (bf16[136,384]{1,0:T(8,128)(2,1)S(1)}, bf16[136,384]{1,0:T(8,128)(2,1)S(1)}, u32[]{:S(2)}, u32[]{:S(2)}) collective-permute-start(bf16[136,384]{1,0:T(8,128)(2,1)S(1)} %get-tuple-element.145), channel_id=1, source_target_pairs={{0,12},{4,8},{8,4},{12,0},{16,28},{20,24},{24,20},{28,16},{1,13},{... | collective-permute-start | bytes 313352 | tf_op jit(solution)/shard_map/ppermute | solution.py:21
  71.6 7.0 %collective-permute-start.13 = (bf16[136,384]{1,0:T(8,128)(2,1)S(1)}, bf16[136,384]{1,0:T(8,128)(2,1)S(1)}, u32[]{:S(2)}, u32[]{:S(2)}) collective-permute-start(bf16[136,384]{1,0:T(8,128)(2,1)S(1)} %get-tuple-element.145), channel_id=1, source_target_pairs={{0,8},{4,12},{8,0},{12,4},{16,24},{20,28},{24,16},{28,20},{1,9},{5... | collective-permute-start | bytes 313352 | tf_op jit(solution)/shard_map/ppermute | solution.py:21
  72.1 7.1 %collective-permute-start.12 = (bf16[136,384]{1,0:T(8,128)(2,1)S(1)}, bf16[136,384]{1,0:T(8,128)(2,1)S(1)}, u32[]{:S(2)}, u32[]{:S(2)}) collective-permute-start(bf16[136,384]{1,0:T(8,128)(2,1)S(1)} %get-tuple-element.145), channel_id=1, source_target_pairs={{0,4},{4,0},{8,12},{12,8},{16,20},{20,16},{24,28},{28,24},{1,5},{5... | collective-permute-start | bytes 313352 | tf_op jit(solution)/shard_map/ppermute | solution.py:21
  72.6 10.1 %collective-permute-start.18 = (bf16[136,384]{1,0:T(8,128)(2,1)S(1)}, bf16[136,384]{1,0:T(8,128)(2,1)S(1)}, u32[]{:S(2)}, u32[]{:S(2)}) collective-permute-start(bf16[136,384]{1,0:T(8,128)(2,1)S(1)} %get-tuple-element.153), channel_id=1, source_target_pairs={{0,12},{4,8},{8,4},{12,0},{16,28},{20,24},{24,20},{28,16},{1,13},{... | collective-permute-start | bytes 313352 | tf_op jit(solution)/shard_map/ppermute | solution.py:21
  75.1 7.5 %collective-permute-start.17 = (bf16[136,384]{1,0:T(8,128)(2,1)S(1)}, bf16[136,384]{1,0:T(8,128)(2,1)S(1)}, u32[]{:S(2)}, u32[]{:S(2)}) collective-permute-start(bf16[136,384]{1,0:T(8,128)(2,1)S(1)} %get-tuple-element.153), channel_id=1, source_target_pairs={{0,8},{4,12},{8,0},{12,4},{16,24},{20,28},{24,16},{28,20},{1,9},{5... | collective-permute-start | bytes 313352 | tf_op jit(solution)/shard_map/ppermute | solution.py:21
  75.6 7.1 %collective-permute-start.16 = (bf16[136,384]{1,0:T(8,128)(2,1)S(1)}, bf16[136,384]{1,0:T(8,128)(2,1)S(1)}, u32[]{:S(2)}, u32[]{:S(2)}) collective-permute-start(bf16[136,384]{1,0:T(8,128)(2,1)S(1)} %get-tuple-element.153), channel_id=1, source_target_pairs={{0,4},{4,0},{8,12},{12,8},{16,20},{20,16},{24,28},{28,24},{1,5},{5... | collective-permute-start | bytes 313352 | tf_op jit(solution)/shard_map/ppermute | solution.py:21
  76.1 8.4 %copy-start.11 = (f32[12]{0:T(128)S(1)}, f32[12]{0:T(128)}, u32[]{:S(2)}) copy-start(f32[12]{0:T(128)} %param.28) | copy-start | bytes 148
  80.1 9.6 %collective-permute-start.15 = (bf16[136,384]{1,0:T(8,128)(2,1)S(1)}, bf16[136,384]{1,0:T(8,128)(2,1)S(1)}, u32[]{:S(2)}, u32[]{:S(2)}) collective-permute-start(bf16[136,384]{1,0:T(8,128)(2,1)S(1)} %get-tuple-element.150), channel_id=1, source_target_pairs={{0,16},{4,20},{8,24},{12,28},{16,0},{20,4},{24,8},{28,12},{1,17},{... | collective-permute-start | bytes 313352 | tf_op jit(solution)/shard_map/ppermute | solution.py:21
  83.5 7.7 %collective-permute-start.19 = (bf16[136,384]{1,0:T(8,128)(2,1)S(1)}, bf16[136,384]{1,0:T(8,128)(2,1)S(1)}, u32[]{:S(2)}, u32[]{:S(2)}) collective-permute-start(bf16[136,384]{1,0:T(8,128)(2,1)S(1)} %get-tuple-element.158), channel_id=1, source_target_pairs={{0,16},{4,20},{8,24},{12,28},{16,0},{20,4},{24,8},{28,12},{1,17},{... | collective-permute-start | bytes 313352 | tf_op jit(solution)/shard_map/ppermute | solution.py:21
  91.3 3.2 %copy-start.13 = (f32[768]{0:T(1024)S(1)}, f32[768]{0:T(1024)}, u32[]{:S(2)}) copy-start(f32[768]{0:T(1024)} %param.29) | copy-start | bytes 9220
  92.6 3.0 %collective-permute-start.22 = (f32[1,1024]{1,0:T(1,128)S(1)}, f32[1,1024]{1,0:T(1,128)S(1)}, u32[]{:S(2)}, u32[]{:S(2)}) collective-permute-start(f32[1,1024]{1,0:T(1,128)S(1)} %get-tuple-element.162.refs_0_), channel_id=1, source_target_pairs={{0,3},{1,2},{2,1},{3,0},{4,7},{5,6},{6,5},{7,4},{8,11},{9,10},{10,... | collective-permute-start | bytes 12296 | tf_op jit(solution)/shard_map/ppermute | solution.py:21
  93.1 3.6 %collective-permute-start.21 = (f32[1,1024]{1,0:T(1,128)S(1)}, f32[1,1024]{1,0:T(1,128)S(1)}, u32[]{:S(2)}, u32[]{:S(2)}) collective-permute-start(f32[1,1024]{1,0:T(1,128)S(1)} %get-tuple-element.162.refs_0_), channel_id=1, source_target_pairs={{0,2},{1,3},{2,0},{3,1},{4,6},{5,7},{6,4},{7,5},{8,10},{9,11},{10,... | collective-permute-start | bytes 12296 | tf_op jit(solution)/shard_map/ppermute | solution.py:21
  94.1 2.6 %collective-permute-start.20 = (f32[1,1024]{1,0:T(1,128)S(1)}, f32[1,1024]{1,0:T(1,128)S(1)}, u32[]{:S(2)}, u32[]{:S(2)}) collective-permute-start(f32[1,1024]{1,0:T(1,128)S(1)} %get-tuple-element.162.refs_0_), channel_id=1, source_target_pairs={{0,1},{1,0},{2,3},{3,2},{4,5},{5,4},{6,7},{7,6},{8,9},{9,8},{10,11... | collective-permute-start | bytes 12296 | tf_op jit(solution)/shard_map/ppermute | solution.py:21

commit v5 on v4

--- a/solution.py
+++ b/solution.py
@@ -91,7 +91,7 @@
 
 def pack(tokens, route_row, per):
     features = tokens.shape[1]
-    anywhere = pl.BlockSpec(memory_space=pl.ANY)
+    anywhere = pl.BlockSpec(memory_space=pltpu.HBM)
     piece = jax.ShapeDtypeStruct((CHUNK, features), BF16)
     return pl.pallas_call(
         pack_kernel,
@@ -139,7 +139,7 @@
     refs = refs[5:]
     if near:
         dt_ref, d_refs, refs = refs[0], refs[1 : 1 + devices], refs[1 + devices:]
-        z_ref, cum_ref, cum_t_ref, step_t_ref, lift_ref, x_scr, tails_ref, rim_ref, wsm_ref, route_ref, lift_scr = refs
+        z_ref, cum_ref, cum_t_ref, step_t_ref, lift_ref, x_scr, tails_ref, rim_ref, wsm_t_ref, route_ref, lift_scr, wsm_ref = refs
     else:
         wsm_ref, z_ref, cum_ref, cum_t_ref, step_t_ref, lift_ref, x_scr = refs
         lift_scr = lift_ref
@@ -157,7 +157,18 @@
         wsm_ref[LANES : LANES + dt_ref.shape[0], :] = dt_ref[...]
         for r in range(devices):
             wsm_ref[r * cols : (r + 1) * cols, :] = d_refs[r][...]
-    small = mm_nt(x_scr[...], wsm_ref[...])
+    if near:
+        weights = jnp.concatenate([d[...] for d in d_refs], axis=0).astype(F32)
+        wide = 512
+        for at in range(0, weights.shape[1], wide):
+            wsm_t_ref[at : at + wide, :LANES] = weights[:, at : at + wide].T.astype(BF16)
+        small = mm_nt(x_scr[...], wsm_ref[...])
+        steps = wsm_ref[LANES:, :].astype(F32)
+        steps = jnp.concatenate([steps, jnp.zeros((LANES - 16, steps.shape[1]), F32)], axis=0)
+        for at in range(0, weights.shape[1], wide):
+            wsm_t_ref[at : at + wide, LANES:] = steps[:, at : at + wide].T.astype(BF16)
+    else:
+        small = mm(x_scr[...], wsm_ref[...])[:, : LANES + 16]
 
     def mask_of(r, lane):
         row = n_refs[r][0:1, lane : lane + LANES].astype(F32)
@@ -226,9 +237,10 @@
     scratch = []
     if near:
         out_shape += [jax.ShapeDtypeStruct((extra, width), F32), jax.ShapeDtypeStruct((8, width), F32)]
-        out_shape.append(jax.ShapeDtypeStruct((LANES + 16, features), BF16))
+        out_shape.append(jax.ShapeDtypeStruct((features, 2 * LANES), BF16))
         out_shape.append(jax.ShapeDtypeStruct((devices * counts[0], LANES), BF16))
         scratch.append(pltpu.VMEM((rows + extra, LANES), BF16))
+        scratch.append(pltpu.VMEM((LANES + 16, features), BF16))
     cfg = (counts, route_from, devices, LANES // devices, rank, near)
     return pl.pallas_call(
         functools.partial(project_kernel, cfg),
@@ -452,8 +464,8 @@
     c = pl.program_id(0)
     here = pl.ds(pl.multiple_of(c * CHUNK, CHUNK), CHUNK)
     r, q = (c // per) ^ lax.axis_index("exp"), c % per
-    piece = jnp.where(r < 2, r * per + q, q * 2 + r % 2)
-    there = pl.ds(pl.multiple_of(piece * CHUNK, CHUNK), CHUNK)
+    near = pl.ds(pl.multiple_of(jnp.where(r < 2, r * per + q, 0) * CHUNK, CHUNK), CHUNK)
+    far = pl.ds(pl.multiple_of(r % 2 * CHUNK, CHUNK), CHUNK)
     xc_ref, cum_ref = xc_all.at[here], cum_all.at[here]
     before_ref, local_ref = before_all.at[pl.ds(c, 1)], local_all.at[pl.ds(c, 1)]
     a_ref, b_ref, c_ref = a_all.at[here], b_all.at[here], c_all.at[here]
@@ -490,9 +502,10 @@
         inside = mm(jnp.concatenate(ws, axis=1), xb.astype(BF16))
         fade = jnp.exp(jnp.where(left, cs[0], cs[1]))
         y = inside + fade * mm(c_hi, local_ref[0, :, lanes]) + both(direct) * x
-        gate = g_refs[0][there, lanes]
+        gate = g_refs[0][near, lanes]
         for k, g_ref in enumerate(g_refs[1:]):
-            gate = jnp.where(r // 2 == k + 1, g_ref[there, lanes], gate)
+            found = (r // 2 == k // per + 1) & (q == k % per)
+            gate = jnp.where(found, g_ref[far, lanes], gate)
         gate = silu(gate)
         a_ref[:, lanes] = y * gate
         b_ref[:, lanes] = fade * jnp.exp(both(before_ref[0, 0:1, :])) * gate
@@ -780,14 +793,15 @@
                 parts[p] = combine(d, arrived, *part[1:])
     entering = [x for part in parts for x in part]
     for k in range(2, n, 2):
-        xs = [x for q in range(per) for x in far_rows[k, q][0]]
-        lifts = [x for q in range(per) for x in far_rows[k, q][1]]
-        gates.append(gate_project(xs, lifts, wz, up, n))
+        for q in range(per):
+            gates.append(gate_project(far_rows[k, q][0], far_rows[k, q][1], wz, up, n))
     a, b, c = run_outputs(
         xc, cum, cum_t, step_t, before, states, gates, direct_head_scale[None, :], local
     )
     gated, mine = join(shards // 2, a, b, c, entering)
-    others = [swap(mine, "exp", k) for k in range(1, n)]
+    others = []
+    for k in range(1, n):
+        others.append(swap(mine, "exp", k))
     return norm(gated, [mine, *others], gated_norm_scale[None, :], width * n)
 
 

time: 98.6 us -> 98.1 us (level)
    pallas_call x2 -> x3, Pallas kernels: 4.87 us -> 4.96 us  [gate_project(): pl.pallas_call(functools.partial(gate_kernel, counts, devices), out_shape...]
where the time goes in v5:
time: 98.1 us; the launch traced here: 97.8 us
  waiting for transfers between devices  32.9 us (34%)
  Pallas kernels  32.1 us (33%)
  starting transfers between devices  20.3 us (21%)
  local copies, waits for them, and re-layouts  12 us (12%)
    ppermute x22, waiting for transfers between devices, swap(): lax.ppermute(block, axis, [(i, i ^ mask) for i in range(lax.axis_size(axi...  32.9 us
    ppermute x22, starting transfers between devices, swap(): lax.ppermute(block, axis, [(i, i ^ mask) for i in range(lax.axis_size(axi...  18.6 us
    pallas_call x4, Pallas kernels, project(): pl.pallas_call(functools.partial(project_kernel, cfg), out_shape=tuple(ou...  11 us
    unnamed x30, local copies, waits for them, and re-layouts  10.9 us
    pallas_call x4, Pallas kernels, run_states(): pl.pallas_call(functools.partial(state_kernel, (width, per, far is not No...  5.1 us
    pallas_call x1, Pallas kernels, run_outputs(): pl.pallas_call(functools.partial(output_kernel, width, per), out_shape=(j...  5.09 us
    pallas_call x3, Pallas kernels, gate_project(): pl.pallas_call(functools.partial(gate_kernel, counts, devices), out_shape...  4.96 us
  transfers between devices with their start and end apart: 23, of which 10 were waited for; matrix products, arithmetic and copies ran while one was open for 7% of the time, Pallas kernels for 24%

profile of v5, /device:TPU:0, one launch (start us, length us, event | category | flops | bytes accessed | tf_op | source)
XLA Modules:
  0.0 97.8 jit_solution(15526629248909290614)
XLA Ops:
  0.0 0.5 collective-permute-start.2
  0.5 1.3 %copy-done.1 = bf16[256,2560]{1,0:T(8,128)(2,1)S(1)} copy-done((bf16[256,2560]{1,0:T(8,128)(2,1)S(1)}, bf16[256,2560]{1,0:T(8,128)(2,1)}, u32[]{:S(2)}) %copy-start.1) | copy-done | bytes 1310744
  1.8 0.7 copy-done.10
  2.5 1.1 %pack.1 = (bf16[128,2560]{1,0:T(8,128)(2,1)}, bf16[8,2560]{1,0:T(8,128)(2,1)S(1)}) custom-call(bf16[256,2560]{1,0:T(8,128)(2,1)S(1)} %copy-done.1, s32[1,256]{1,0:T(1,128)S(1)} %bitcast.41), custom_call_target="tpu_custom_call" | custom-call | tf_op jit(solution)/shard_map/pack/pallas_call | solution.py:96
  3.6 2.6 %collective-permute-start.9 = (bf16[128,2560]{1,0:T(8,128)(2,1)}, bf16[128,2560]{1,0:T(8,128)(2,1)S(1)}, u32[]{:S(2)}, u32[]{:S(2)}) collective-permute-start(bf16[128,2560]{1,0:T(8,128)(2,1)} %get-tuple-element.93), channel_id=1, source_target_pairs={{0,2},{1,3},{2,0},{3,1},{4,6},{5,7},{6,4},{7,5},{8,10},{9,11},{10,... | collective-permute-start | bytes 1966088 | tf_op jit(solution)/shard_map/ppermute | solution.py:21
  6.2 4.7 %copy.34 = bf16[320,8,2,768]{3,1,2,0:T(8,128)(2,1)S(1)} copy(bf16[320,8,2,768]{3,2,1,0:T(2,128)(2,1)} %bitcast.43) | data formatting | bytes 15728640
  10.9 1.1 %slice.3 = bf16[128,2560]{1,0:T(8,128)(2,1)S(1)} slice(bf16[256,2560]{1,0:T(8,128)(2,1)} %refs_0_.1), slice={[128:256], [0:2560]} | slice | bytes 1310720 | tf_op jit(solution)/shard_map/slice | solution.py:735
  12.1 2.0 %collective-permute-start.7 = (bf16[32,2560]{1,0:T(8,128)(2,1)}, bf16[32,2560]{1,0:T(8,128)(2,1)S(1)}, u32[]{:S(2)}, u32[]{:S(2)}) collective-permute-start(bf16[32,2560]{1,0:T(8,128)(2,1)} %bitcast.25), channel_id=1, source_target_pairs={{0,2},{1,3},{2,0},{3,1},{4,6},{5,7},{6,4},{7,5},{8,10},{9,11},{10,... | collective-permute-start | bytes 491528 | tf_op jit(solution)/shard_map/ppermute | solution.py:21
  14.2 7.8 %collective-permute-done.9.refs_0_ = bf16[128,2560]{1,0:T(8,128)(2,1)S(1)} collective-permute-done((bf16[128,2560]{1,0:T(8,128)(2,1)}, bf16[128,2560]{1,0:T(8,128)(2,1)S(1)}, u32[]{:S(2)}, u32[]{:S(2)}) %collective-permute-start.9) | collective-permute-done | bytes 655392 | tf_op jit(solution)/shard_map/ppermute | solution.py:21
  22.0 18.2 %collective-permute-done.4.refs_4_ = bf16[8,2560]{1,0:T(8,128)(2,1)S(1)} collective-permute-done((bf16[8,2560]{1,0:T(8,128)(2,1)S(1)}, bf16[8,2560]{1,0:T(8,128)(2,1)S(1)}, u32[]{:S(2)}, u32[]{:S(2)}) %collective-permute-start.4) | collective-permute-done | bytes 40992 | tf_op jit(solution)/shard_map/ppermute | solution.py:21
  40.2 1.2 %collective-permute-done.3.refs_3_ = bf16[8,2560]{1,0:T(8,128)(2,1)S(1)} collective-permute-done((bf16[8,2560]{1,0:T(8,128)(2,1)S(1)}, bf16[8,2560]{1,0:T(8,128)(2,1)S(1)}, u32[]{:S(2)}, u32[]{:S(2)}) %collective-permute-start.3) | collective-permute-done | bytes 40992 | tf_op jit(solution)/shard_map/ppermute | solution.py:21
  41.6 1.1 %collective-permute-done.5.refs_5_ = bf16[8,2560]{1,0:T(8,128)(2,1)S(1)} collective-permute-done((bf16[8,2560]{1,0:T(8,128)(2,1)S(1)}, bf16[8,2560]{1,0:T(8,128)(2,1)S(1)}, u32[]{:S(2)}, u32[]{:S(2)}) %collective-permute-start.5) | collective-permute-done | bytes 40992 | tf_op jit(solution)/shard_map/ppermute | solution.py:21
  43.4 1.0 %copy.35 = bf16[16,8,2,768]{3,1,2,0:T(8,128)(2,1)S(1)} copy(bf16[16,8,2,768]{3,2,1,0:T(2,128)(2,1)} %bitcast.44) | data formatting | bytes 786432
  44.5 1.3 %copy-done.2 = bf16[256,2560]{1,0:T(8,128)(2,1)S(1)} copy-done((bf16[256,2560]{1,0:T(8,128)(2,1)S(1)}, bf16[256,2560]{1,0:T(8,128)(2,1)}, u32[]{:S(2)}) %copy-start.2) | copy-done | bytes 1310744
  45.8 0.9 copy-done.4
  46.8 0.9 copy-done.5
  47.7 5.8 %project.4 = (f32[512,1024]{1,0:T(8,128)S(1)}, f32[512,128]{1,0:T(8,128)S(1)}, f32[4,16,128]{2,1,0:T(8,128)S(1)}, f32[4,16,128]{2,1,0:T(8,128)S(1)}, bf16[512,12...) custom-call(bf16[256,2560]{1,0:T(8,128)(2,1)S(1)} %copy-done.2, ...), custom_call_target="tpu_custom_call" | custom-call | flops 3355443200 | bytes 9961472 | tf_op jit(solution)/shard_map/project/pallas_call | solution.py:245
  53.5 1.8 %collective-permute-start.11 = (f32[8,1024]{1,0:T(8,128)S(1)}, f32[8,1024]{1,0:T(8,128)S(1)}, u32[]{:S(2)}, u32[]{:S(2)}) collective-permute-start(f32[8,1024]{1,0:T(8,128)S(1)} %get-tuple-element.96), channel_id=1, source_target_pairs={{0,4},{4,8},{8,12},{12,16},{16,20},{20,24},{24,28},{28,0},{1,5},{5... | collective-permute-start | bytes 98312 | tf_op jit(solution)/shard_map/ppermute | solution.py:753
  55.2 1.4 %project.7 = (f32[128,1024]{1,0:T(8,128)S(1)}, f32[128,128]{1,0:T(8,128)S(1)}, f32[1,16,128]{2,1,0:T(8,128)S(1)}, f32[1,16,128]{2,1,0:T(8,128)S(1)}, bf16[128,12...) custom-call(bf16[128,2560]{1,0:T(8,128)(2,1)S(1)} %collective-permute-done.refs_0_, ...), custom_call_target="tpu_custom_call" | custom-call | flops 838860800 | bytes 6422528 | tf_op jit(solution)/shard_map/project/pallas_call | solution.py:245
  56.7 2.3 %project.6 = (f32[256,1024]{1,0:T(8,128)S(1)}, f32[256,128]{1,0:T(8,128)S(1)}, f32[2,16,128]{2,1,0:T(8,128)S(1)}, f32[2,16,128]{2,1,0:T(8,128)S(1)}, bf16[256,12...) custom-call(bf16[128,2560]{1,0:T(8,128)(2,1)S(1)} %collective-permute-done.9.refs_0_, ...), custom_call_target="tpu_custom_call" | custom-call | flops 1677721600 | bytes 7602176 | tf_op jit(solution)/shard_map/project/pallas_call | solution.py:245
  59.0 1.4 %project.5 = (f32[128,1024]{1,0:T(8,128)S(1)}, f32[128,128]{1,0:T(8,128)S(1)}, f32[1,16,128]{2,1,0:T(8,128)S(1)}, f32[1,16,128]{2,1,0:T(8,128)S(1)}, bf16[128,12...) custom-call(bf16[128,2560]{1,0:T(8,128)(2,1)S(1)} %collective-permute-done.1.refs_0_, ...), custom_call_target="tpu_custom_call" | custom-call | flops 838860800 | bytes 6422528 | tf_op jit(solution)/shard_map/project/pallas_call | solution.py:245
  60.5 2.7 %run_states.4 = (f32[1024,1024]{1,0:T(8,128)S(1)}, f32[1024,128]{1,0:T(8,128)S(1)}, f32[8,16,128]{2,1,0:T(8,128)S(1)}, f32[8,16,128]{2,1,0:T(8,128)S(1)}, f32[8,...) custom-call(f32[512,1024]{1,0:T(8,128)S(1)} %get-tuple-element.104.z_all.older_all, ...), custom_call_target="tpu_custom_call" | custom-call | flops 786432000 | bytes 6291456 | tf_op jit(solution)/shard_map/run_states/pallas_call | solution.py:382
  63.2 1.2 %run_states.5 = (f32[1024,1024]{1,0:T(8,128)S(1)}, f32[1024,128]{1,0:T(8,128)S(1)}, f32[8,16,128]{2,1,0:T(8,128)S(1)}, f32[8,16,128]{2,1,0:T(8,128)S(1)}, f32[8,...) custom-call(f32[256,1024]{1,0:T(8,128)S(1)} %get-tuple-element.94.z_, ...), custom_call_target="tpu_custom_call", output_to_operand_aliasing={{0}: (11, {}), {1}: (12, {}), {2}: (13, {}), {3}: (14, {}),... | custom-call | flops 393216000 | bytes 3145728 | tf_op jit(solution)/shard_map/run_states/pallas_call | solution.py:382
  64.4 0.6 run_states.6
  65.0 0.6 run_states.7
  65.6 0.5 stitch.1
  66.1 2.6 %collective-permute-start.14 = (bf16[136,384]{1,0:T(8,128)(2,1)S(1)}, bf16[136,384]{1,0:T(8,128)(2,1)S(1)}, u32[]{:S(2)}, u32[]{:S(2)}) collective-permute-start(bf16[136,384]{1,0:T(8,128)(2,1)S(1)} %get-tuple-element.145), channel_id=1, source_target_pairs={{0,12},{4,8},{8,4},{12,0},{16,28},{20,24},{24,20},{28,16},{1,13},{... | collective-permute-start | bytes 313352 | tf_op jit(solution)/shard_map/ppermute | solution.py:21
  68.7 2.4 %gate_project.3.refs_0_ = f32[512,768]{1,0:T(8,128)S(1)} custom-call(bf16[544,2560]{1,0:T(8,128)(2,1)S(1)} %get-tuple-element.134.refs_0_, bf16[512,128]{1,0:T(8,128)(2,1)S(1)} %get-tuple-element.135.refs_1_, bf16[2560,1536]{1,0:T(8,128)(2,1)S(1)} %bitcast.15, bf16[128,1536]{1,0:T(8,128)(2,1)S(1)} %bitcast.22), custom_call_target="tpu_custom_call" | custom-call | flops 2013265920 | bytes 8126464 | tf_op jit(solution)/shard_map/gate_project/pallas_call | solution.py:287
  71.1 0.5 collective-permute-start.13
  71.6 0.5 collective-permute-start.12
  72.1 2.6 %collective-permute-start.18 = (bf16[136,384]{1,0:T(8,128)(2,1)S(1)}, bf16[136,384]{1,0:T(8,128)(2,1)S(1)}, u32[]{:S(2)}, u32[]{:S(2)}) collective-permute-start(bf16[136,384]{1,0:T(8,128)(2,1)S(1)} %get-tuple-element.153), channel_id=1, source_target_pairs={{0,12},{4,8},{8,4},{12,0},{16,28},{20,24},{24,20},{28,16},{1,13},{... | collective-permute-start | bytes 313352 | tf_op jit(solution)/shard_map/ppermute | solution.py:21
  74.7 0.4 collective-permute-start.17
  75.1 0.5 collective-permute-start.16
  75.6 1.3 %gate_project.4.refs_1_ = f32[256,768]{1,0:T(8,128)S(1)} custom-call(bf16[256,2560]{1,0:T(8,128)(2,1)S(1)} %get-tuple-element.136.refs_0_, bf16[256,128]{1,0:T(8,128)(2,1)S(1)} %get-tuple-element.137.refs_1_, bf16[2560,1536]{1,0:T(8,128)(2,1)S(1)} %bitcast.16, bf16[128,1536]{1,0:T(8,128)(2,1)S(1)} %bitcast.23), custom_call_target="tpu_custom_call" | custom-call | flops 1006632960 | bytes 6029312 | tf_op jit(solution)/shard_map/gate_project/pallas_call | solution.py:287
  76.9 1.3 %gate_project.5.refs_2_ = f32[256,768]{1,0:T(8,128)S(1)} custom-call(bf16[128,2560]{1,0:T(8,128)(2,1)S(1)} %get-tuple-element.138.refs_0_, bf16[128,2560]{1,0:T(8,128)(2,1)S(1)} %get-tuple-element.139.refs_1_, bf16[128,128]{1,0:T(8,128)(2,1)S(1)} %get-tuple-element.140.refs_2_, bf16[128,128]{1,0:T(8,128)(2,1)S(1)} %get-tuple-element.141.refs_3_, ...), custom_call_target="tpu_custom_call" | custom-call | flops 1006632960 | bytes 6029312 | tf_op jit(solution)/shard_map/gate_project/pallas_call | solution.py:287
  78.2 0.5 collective-permute-done.12.refs_0_
  78.8 0.9 combine.2
  79.6 2.6 %collective-permute-start.15 = (bf16[136,384]{1,0:T(8,128)(2,1)S(1)}, bf16[136,384]{1,0:T(8,128)(2,1)S(1)}, u32[]{:S(2)}, u32[]{:S(2)}) collective-permute-start(bf16[136,384]{1,0:T(8,128)(2,1)S(1)} %get-tuple-element.150), channel_id=1, source_target_pairs={{0,16},{4,20},{8,24},{12,28},{16,0},{20,4},{24,8},{28,12},{1,17},{... | collective-permute-start | bytes 313352 | tf_op jit(solution)/shard_map/ppermute | solution.py:21
  82.2 0.9 combine.3
  83.1 0.9 collective-permute-start.19
  84.0 5.1 %run_outputs.1 = (f32[1024,768]{1,0:T(8,128)S(1)}, f32[1024,768]{1,0:T(8,128)S(1)}, bf16[1024,128]{1,0:T(8,128)(2,1)S(1)}) custom-call(f32[1024,1024]{1,0:T(8,128)S(1)} %get-tuple-element.126.xc_all, f32[1024,128]{1,0:T(8,128)S(1)} %get-tuple-element.127.cum_all, f32[8,16,128]{2,1,0:T(8,128)S(1)} %get-tuple-element.128.cum_t_all, ...), custom_call_target="tpu_custom_call" | custom-call | flops 2359296000 | bytes 12582912 | tf_op jit(solution)/shard_map/run_outputs/pallas_call | solution.py:519
  89.3 1.5 %collective-permute-done.19.refs_3_ = bf16[136,384]{1,0:T(8,128)(2,1)S(1)} collective-permute-done((bf16[136,384]{1,0:T(8,128)(2,1)S(1)}, bf16[136,384]{1,0:T(8,128)(2,1)S(1)}, u32[]{:S(2)}, u32[]{:S(2)}) %collective-permute-start.19) | collective-permute-done | bytes 104480 | tf_op jit(solution)/shard_map/ppermute | solution.py:21
  90.8 1.3 %join.1 = (f32[1024,768]{1,0:T(8,128)S(1)}, f32[1,1024]{1,0:T(1,128)S(1)}) custom-call(f32[1024,768]{1,0:T(8,128)S(1)} %get-tuple-element.142.a_ref, f32[1024,768]{1,0:T(8,128)S(1)} %get-tuple-element.143.b_ref, bf16[1024,128]{1,0:T(8,128)(2,1)S(1)} %get-tuple-element.144.c_ref, bf16[136,384]{1,0:T(8,128)(2,1)S(1)} %collective-permute-done.15.refs_0_, ...), custom_call_target="tpu_custom_call" | custom-call | tf_op jit(solution)/shard_map/join/pallas_call | solution.py:637
  92.1 0.5 collective-permute-start.22
  92.7 1.0 %collective-permute-start.21 = (f32[1,1024]{1,0:T(1,128)S(1)}, f32[1,1024]{1,0:T(1,128)S(1)}, u32[]{:S(2)}, u32[]{:S(2)}) collective-permute-start(f32[1,1024]{1,0:T(1,128)S(1)} %get-tuple-element.162.refs_0_), channel_id=1, source_target_pairs={{0,2},{1,3},{2,0},{3,1},{4,6},{5,7},{6,4},{7,5},{8,10},{9,11},{10,... | collective-permute-start | bytes 12296 | tf_op jit(solution)/shard_map/ppermute | solution.py:21
  94.0 1.2 %collective-permute-done.22.refs_3_ = f32[1,1024]{1,0:T(1,128)S(1)} collective-permute-done((f32[1,1024]{1,0:T(1,128)S(1)}, f32[1,1024]{1,0:T(1,128)S(1)}, u32[]{:S(2)}, u32[]{:S(2)}) %collective-permute-start.22) | collective-permute-done | bytes 4128 | tf_op jit(solution)/shard_map/ppermute | solution.py:21
  95.2 1.1 %collective-permute-done.21.refs_2_ = f32[1,1024]{1,0:T(1,128)S(1)} collective-permute-done((f32[1,1024]{1,0:T(1,128)S(1)}, f32[1,1024]{1,0:T(1,128)S(1)}, u32[]{:S(2)}, u32[]{:S(2)}) %collective-permute-start.21) | collective-permute-done | bytes 4128 | tf_op jit(solution)/shard_map/ppermute | solution.py:21
  96.3 1.4 %norm.1 = bf16[1024,768]{1,0:T(8,128)(2,1)} custom-call(f32[1024,768]{1,0:T(8,128)S(1)} %get-tuple-element.161.g_ref, f32[1,768]{1,0:T(1,128)S(1)} %broadcast_in_dim.23.gain_ref, f32[1,1024]{1,0:T(1,128)S(1)} %get-tuple-element.162.refs_0_, f32[1,1024]{1,0:T(1,128)S(1)} %collective-permute-done.20.refs_1_, f32[1,1024]{1,0:T(1,128)S(1)} %collective-permute-done.21.refs_2_, ...), custom_call_target="tpu_custom_call" | custom-call | tf_op jit(solution)/shard_map/norm/pallas_call | solution.py:674
  (49 shorter events, 1.7 us)
Async XLA Ops:
  0.0 44.5 %collective-permute-start.2 = (bf16[256,2560]{1,0:T(8,128)(2,1)}, bf16[256,2560]{1,0:T(8,128)(2,1)}, u32[]{:S(2)}, u32[]{:S(2)}) collective-permute-start(bf16[256,2560]{1,0:T(8,128)(2,1)} %refs_0_.1), channel_id=1, source_target_pairs={{0,1},{1,0},{2,3},{3,2},{4,5},{5,4},{6,7},{7,6},{8,9},{9,8},{10,11... | collective-permute-start | bytes 3932168 | tf_op jit(solution)/shard_map/ppermute | solution.py:21
  0.5 1.3 %copy-start.1 = (bf16[256,2560]{1,0:T(8,128)(2,1)S(1)}, bf16[256,2560]{1,0:T(8,128)(2,1)}, u32[]{:S(2)}) copy-start(bf16[256,2560]{1,0:T(8,128)(2,1)} %refs_0_.1) | copy-start | bytes 3932164
  1.8 0.7 copy-start.10
  3.6 18.4 %collective-permute-start.9 = (bf16[128,2560]{1,0:T(8,128)(2,1)}, bf16[128,2560]{1,0:T(8,128)(2,1)S(1)}, u32[]{:S(2)}, u32[]{:S(2)}) collective-permute-start(bf16[128,2560]{1,0:T(8,128)(2,1)} %get-tuple-element.93), channel_id=1, source_target_pairs={{0,2},{1,3},{2,0},{3,1},{4,6},{5,7},{6,4},{7,5},{8,10},{9,11},{10,... | collective-permute-start | bytes 1966088 | tf_op jit(solution)/shard_map/ppermute | solution.py:21
  6.2 37.2 %copy-start.12 = (f32[768]{0:T(1024)S(1)}, f32[768]{0:T(1024)}, u32[]{:S(2)}) copy-start(f32[768]{0:T(1024)} %param.24) | copy-start | bytes 9220
  6.2 38.3 %copy-start = (bf16[2560,256]{1,0:T(8,128)(2,1)S(1)}, bf16[2560,256]{1,0:T(8,128)(2,1)}, u32[]{:S(2)}) copy-start(bf16[2560,256]{1,0:T(8,128)(2,1)} %refs_3_.3) | copy-start | bytes 3932164
  6.2 38.3 %copy-start.8 = (f32[12]{0:T(128)S(1)}, f32[12]{0:T(128)}, u32[]{:S(2)}) copy-start(f32[12]{0:T(128)} %param.26) | copy-start | bytes 148
  6.2 38.3 %copy-start.9 = (f32[12]{0:T(128)S(1)}, f32[12]{0:T(128)}, u32[]{:S(2)}) copy-start(f32[12]{0:T(128)} %param.27) | copy-start | bytes 148
  12.0 31.2 %collective-permute-start = (bf16[128,2560]{1,0:T(8,128)(2,1)S(1)}, bf16[128,2560]{1,0:T(8,128)(2,1)S(1)}, u32[]{:S(2)}, u32[]{:S(2)}) collective-permute-start(bf16[128,2560]{1,0:T(8,128)(2,1)S(1)} %slice.3), channel_id=1, source_target_pairs={{0,2},{1,3},{2,0},{3,1},{4,6},{5,7},{6,4},{7,5},{8,10},{9,11},{10,... | collective-permute-start | bytes 1966088 | tf_op jit(solution)/shard_map/ppermute | solution.py:21
  12.1 30.7 %collective-permute-start.7 = (bf16[32,2560]{1,0:T(8,128)(2,1)}, bf16[32,2560]{1,0:T(8,128)(2,1)S(1)}, u32[]{:S(2)}, u32[]{:S(2)}) collective-permute-start(bf16[32,2560]{1,0:T(8,128)(2,1)} %bitcast.25), channel_id=1, source_target_pairs={{0,2},{1,3},{2,0},{3,1},{4,6},{5,7},{6,4},{7,5},{8,10},{9,11},{10,... | collective-permute-start | bytes 491528 | tf_op jit(solution)/shard_map/ppermute | solution.py:21
  14.1 26.1 %collective-permute-start.4 = (bf16[8,2560]{1,0:T(8,128)(2,1)S(1)}, bf16[8,2560]{1,0:T(8,128)(2,1)S(1)}, u32[]{:S(2)}, u32[]{:S(2)}) collective-permute-start(bf16[8,2560]{1,0:T(8,128)(2,1)S(1)} %get-tuple-element.85.refs_2_), channel_id=1, source_target_pairs={{0,2},{1,3},{2,0},{3,1},{4,6},{5,7},{6,4},{7,5},{8,10},{9,11},{10,... | collective-permute-start | bytes 122888 | tf_op jit(solution)/shard_map/ppermute | solution.py:21
  22.0 34.7 %collective-permute-start.10 = (bf16[128,2560]{1,0:T(8,128)(2,1)S(1)}, bf16[128,2560]{1,0:T(8,128)(2,1)S(1)}, u32[]{:S(2)}, u32[]{:S(2)}) collective-permute-start(bf16[128,2560]{1,0:T(8,128)(2,1)S(1)} %collective-permute-done.9.refs_0_), channel_id=1, source_target_pairs={{0,1},{1,0},{2,3},{3,2},{4,5},{5,4},{6,7},{7,6},{8,9},{9,8},{10,11... | collective-permute-start | bytes 1966088 | tf_op jit(solution)/shard_map/ppermute | solution.py:21
  40.2 1.2 %collective-permute-start.3 = (bf16[8,2560]{1,0:T(8,128)(2,1)S(1)}, bf16[8,2560]{1,0:T(8,128)(2,1)S(1)}, u32[]{:S(2)}, u32[]{:S(2)}) collective-permute-start(bf16[8,2560]{1,0:T(8,128)(2,1)S(1)} %get-tuple-element.85.refs_2_), channel_id=1, source_target_pairs={{0,1},{1,0},{2,3},{3,2},{4,5},{5,4},{6,7},{7,6},{8,9},{9,8},{10,11... | collective-permute-start | bytes 122888 | tf_op jit(solution)/shard_map/ppermute | solution.py:21
  41.4 1.2 %collective-permute-start.5 = (bf16[8,2560]{1,0:T(8,128)(2,1)S(1)}, bf16[8,2560]{1,0:T(8,128)(2,1)S(1)}, u32[]{:S(2)}, u32[]{:S(2)}) collective-permute-start(bf16[8,2560]{1,0:T(8,128)(2,1)S(1)} %collective-permute-done.4.refs_4_), channel_id=1, source_target_pairs={{0,1},{1,0},{2,3},{3,2},{4,5},{5,4},{6,7},{7,6},{8,9},{9,8},{10,11... | collective-permute-start | bytes 122888 | tf_op jit(solution)/shard_map/ppermute | solution.py:21
  42.7 1.7 %collective-permute-start.6 = (bf16[32,2560]{1,0:T(8,128)(2,1)}, bf16[32,2560]{1,0:T(8,128)(2,1)S(1)}, u32[]{:S(2)}, u32[]{:S(2)}) collective-permute-start(bf16[32,2560]{1,0:T(8,128)(2,1)} %bitcast.26), channel_id=1, source_target_pairs={{0,1},{1,0},{2,3},{3,2},{4,5},{5,4},{6,7},{7,6},{8,9},{9,8},{10,11... | collective-permute-start | bytes 491528 | tf_op jit(solution)/shard_map/ppermute | solution.py:21
  42.8 1.7 %collective-permute-start.8 = (bf16[32,2560]{1,0:T(8,128)(2,1)S(1)}, bf16[32,2560]{1,0:T(8,128)(2,1)S(1)}, u32[]{:S(2)}, u32[]{:S(2)}) collective-permute-start(bf16[32,2560]{1,0:T(8,128)(2,1)S(1)} %collective-permute-done.7.refs_14_), channel_id=1, source_target_pairs={{0,1},{1,0},{2,3},{3,2},{4,5},{5,4},{6,7},{7,6},{8,9},{9,8},{10,11... | collective-permute-start | bytes 491528 | tf_op jit(solution)/shard_map/ppermute | solution.py:21
  43.2 15.9 %collective-permute-start.1 = (bf16[128,2560]{1,0:T(8,128)(2,1)S(1)}, bf16[128,2560]{1,0:T(8,128)(2,1)S(1)}, u32[]{:S(2)}, u32[]{:S(2)}) collective-permute-start(bf16[128,2560]{1,0:T(8,128)(2,1)S(1)} %collective-permute-done.refs_0_), channel_id=1, source_target_pairs={{0,1},{1,0},{2,3},{3,2},{4,5},{5,4},{6,7},{7,6},{8,9},{9,8},{10,11... | collective-permute-start | bytes 1966088 | tf_op jit(solution)/shard_map/ppermute | solution.py:21
  44.5 1.3 %copy-start.2 = (bf16[256,2560]{1,0:T(8,128)(2,1)S(1)}, bf16[256,2560]{1,0:T(8,128)(2,1)}, u32[]{:S(2)}) copy-start(bf16[256,2560]{1,0:T(8,128)(2,1)} %refs_0_.1) | copy-start | bytes 3932164
  45.8 0.9 copy-start.4
  46.8 0.9 copy-start.5
  53.5 7.0 %collective-permute-start.11 = (f32[8,1024]{1,0:T(8,128)S(1)}, f32[8,1024]{1,0:T(8,128)S(1)}, u32[]{:S(2)}, u32[]{:S(2)}) collective-permute-start(f32[8,1024]{1,0:T(8,128)S(1)} %get-tuple-element.96), channel_id=1, source_target_pairs={{0,4},{4,8},{8,12},{12,16},{16,20},{20,24},{24,28},{28,0},{1,5},{5... | collective-permute-start | bytes 98312 | tf_op jit(solution)/shard_map/ppermute | solution.py:753
  59.0 1.5 %copy-start.3 = (f32[4,768]{1,0:T(4,128)S(1)}, f32[4,768]{1,0:T(4,128)}, u32[]{:S(2)}) copy-start(f32[4,768]{1,0:T(4,128)} %taps_ref.7) | copy-start | bytes 36868
  59.0 1.5 %copy-start.6 = (f32[4,256]{1,0:T(4,128)S(1)}, f32[4,256]{1,0:T(4,128)}, u32[]{:S(2)}) copy-start(f32[4,256]{1,0:T(4,128)} %mtaps_ref.7) | copy-start | bytes 12292
  59.0 1.5 %copy-start.7 = (f32[256]{0:T(256)S(1)}, f32[256]{0:T(256)}, u32[]{:S(2)}) copy-start(f32[256]{0:T(256)} %param.25) | copy-start | bytes 3076
  66.1 9.0 %collective-permute-start.14 = (bf16[136,384]{1,0:T(8,128)(2,1)S(1)}, bf16[136,384]{1,0:T(8,128)(2,1)S(1)}, u32[]{:S(2)}, u32[]{:S(2)}) collective-permute-start(bf16[136,384]{1,0:T(8,128)(2,1)S(1)} %get-tuple-element.145), channel_id=1, source_target_pairs={{0,12},{4,8},{8,4},{12,0},{16,28},{20,24},{24,20},{28,16},{1,13},{... | collective-permute-start | bytes 313352 | tf_op jit(solution)/shard_map/ppermute | solution.py:21
  71.1 7.1 %collective-permute-start.13 = (bf16[136,384]{1,0:T(8,128)(2,1)S(1)}, bf16[136,384]{1,0:T(8,128)(2,1)S(1)}, u32[]{:S(2)}, u32[]{:S(2)}) collective-permute-start(bf16[136,384]{1,0:T(8,128)(2,1)S(1)} %get-tuple-element.145), channel_id=1, source_target_pairs={{0,8},{4,12},{8,0},{12,4},{16,24},{20,28},{24,16},{28,20},{1,9},{5... | collective-permute-start | bytes 313352 | tf_op jit(solution)/shard_map/ppermute | solution.py:21
  71.6 7.1 %collective-permute-start.12 = (bf16[136,384]{1,0:T(8,128)(2,1)S(1)}, bf16[136,384]{1,0:T(8,128)(2,1)S(1)}, u32[]{:S(2)}, u32[]{:S(2)}) collective-permute-start(bf16[136,384]{1,0:T(8,128)(2,1)S(1)} %get-tuple-element.145), channel_id=1, source_target_pairs={{0,4},{4,0},{8,12},{12,8},{16,20},{20,16},{24,28},{28,24},{1,5},{5... | collective-permute-start | bytes 313352 | tf_op jit(solution)/shard_map/ppermute | solution.py:21
  72.1 10.1 %collective-permute-start.18 = (bf16[136,384]{1,0:T(8,128)(2,1)S(1)}, bf16[136,384]{1,0:T(8,128)(2,1)S(1)}, u32[]{:S(2)}, u32[]{:S(2)}) collective-permute-start(bf16[136,384]{1,0:T(8,128)(2,1)S(1)} %get-tuple-element.153), channel_id=1, source_target_pairs={{0,12},{4,8},{8,4},{12,0},{16,28},{20,24},{24,20},{28,16},{1,13},{... | collective-permute-start | bytes 313352 | tf_op jit(solution)/shard_map/ppermute | solution.py:21
  74.7 7.5 %collective-permute-start.17 = (bf16[136,384]{1,0:T(8,128)(2,1)S(1)}, bf16[136,384]{1,0:T(8,128)(2,1)S(1)}, u32[]{:S(2)}, u32[]{:S(2)}) collective-permute-start(bf16[136,384]{1,0:T(8,128)(2,1)S(1)} %get-tuple-element.153), channel_id=1, source_target_pairs={{0,8},{4,12},{8,0},{12,4},{16,24},{20,28},{24,16},{28,20},{1,9},{5... | collective-permute-start | bytes 313352 | tf_op jit(solution)/shard_map/ppermute | solution.py:21
  75.1 7.1 %collective-permute-start.16 = (bf16[136,384]{1,0:T(8,128)(2,1)S(1)}, bf16[136,384]{1,0:T(8,128)(2,1)S(1)}, u32[]{:S(2)}, u32[]{:S(2)}) collective-permute-start(bf16[136,384]{1,0:T(8,128)(2,1)S(1)} %get-tuple-element.153), channel_id=1, source_target_pairs={{0,4},{4,0},{8,12},{12,8},{16,20},{20,16},{24,28},{28,24},{1,5},{5... | collective-permute-start | bytes 313352 | tf_op jit(solution)/shard_map/ppermute | solution.py:21
  76.9 7.1 %copy-start.11 = (f32[12]{0:T(128)S(1)}, f32[12]{0:T(128)}, u32[]{:S(2)}) copy-start(f32[12]{0:T(128)} %param.28) | copy-start | bytes 148
  79.6 9.7 %collective-permute-start.15 = (bf16[136,384]{1,0:T(8,128)(2,1)S(1)}, bf16[136,384]{1,0:T(8,128)(2,1)S(1)}, u32[]{:S(2)}, u32[]{:S(2)}) collective-permute-start(bf16[136,384]{1,0:T(8,128)(2,1)S(1)} %get-tuple-element.150), channel_id=1, source_target_pairs={{0,16},{4,20},{8,24},{12,28},{16,0},{20,4},{24,8},{28,12},{1,17},{... | collective-permute-start | bytes 313352 | tf_op jit(solution)/shard_map/ppermute | solution.py:21
  83.1 7.7 %collective-permute-start.19 = (bf16[136,384]{1,0:T(8,128)(2,1)S(1)}, bf16[136,384]{1,0:T(8,128)(2,1)S(1)}, u32[]{:S(2)}, u32[]{:S(2)}) collective-permute-start(bf16[136,384]{1,0:T(8,128)(2,1)S(1)} %get-tuple-element.158), channel_id=1, source_target_pairs={{0,16},{4,20},{8,24},{12,28},{16,0},{20,4},{24,8},{28,12},{1,17},{... | collective-permute-start | bytes 313352 | tf_op jit(solution)/shard_map/ppermute | solution.py:21
  90.8 3.2 %copy-start.13 = (f32[768]{0:T(1024)S(1)}, f32[768]{0:T(1024)}, u32[]{:S(2)}) copy-start(f32[768]{0:T(1024)} %param.29) | copy-start | bytes 9220
  92.1 3.0 %collective-permute-start.22 = (f32[1,1024]{1,0:T(1,128)S(1)}, f32[1,1024]{1,0:T(1,128)S(1)}, u32[]{:S(2)}, u32[]{:S(2)}) collective-permute-start(f32[1,1024]{1,0:T(1,128)S(1)} %get-tuple-element.162.refs_0_), channel_id=1, source_target_pairs={{0,3},{1,2},{2,1},{3,0},{4,7},{5,6},{6,5},{7,4},{8,11},{9,10},{10,... | collective-permute-start | bytes 12296 | tf_op jit(solution)/shard_map/ppermute | solution.py:21
  92.7 3.6 %collective-permute-start.21 = (f32[1,1024]{1,0:T(1,128)S(1)}, f32[1,1024]{1,0:T(1,128)S(1)}, u32[]{:S(2)}, u32[]{:S(2)}) collective-permute-start(f32[1,1024]{1,0:T(1,128)S(1)} %get-tuple-element.162.refs_0_), channel_id=1, source_target_pairs={{0,2},{1,3},{2,0},{3,1},{4,6},{5,7},{6,4},{7,5},{8,10},{9,11},{10,... | collective-permute-start | bytes 12296 | tf_op jit(solution)/shard_map/ppermute | solution.py:21
  93.7 2.6 %collective-permute-start.20 = (f32[1,1024]{1,0:T(1,128)S(1)}, f32[1,1024]{1,0:T(1,128)S(1)}, u32[]{:S(2)}, u32[]{:S(2)}) collective-permute-start(f32[1,1024]{1,0:T(1,128)S(1)} %get-tuple-element.162.refs_0_), channel_id=1, source_target_pairs={{0,1},{1,0},{2,3},{3,2},{4,5},{5,4},{6,7},{7,6},{8,9},{9,8},{10,11... | collective-permute-start | bytes 12296 | tf_op jit(solution)/shard_map/ppermute | solution.py:21

commit v6 on v5

--- a/solution.py
+++ b/solution.py
@@ -409,7 +409,7 @@
 
 
 def part_lanes(width):
-    middle = (width // LANES + 1) // 2 * LANES
+    middle = (width // LANES * 2 // 3) * LANES
     return [slice(0, middle), slice(middle, width)]
 
 
@@ -458,12 +458,14 @@
 
 
 def output_kernel(
-    width, per, xc_all, cum_all, cum_t_all, step_t_all, before_all, local_all, direct_ref, *refs,
+    cfg, xc_all, cum_all, cum_t_all, step_t_all, before_all, local_all, direct_ref, *refs,
 ):
-    g_refs, (a_all, b_all, c_all) = refs[:-3], refs[-3:]
-    c = pl.program_id(0)
+    width, per, gate_count, skip = cfg
+    g_refs, (a_all, b_all, c_all) = refs[:gate_count], refs[-3:]
+    turn = pl.program_id(0) + skip
+    r, q = turn // per, turn % per
+    c = (r ^ lax.axis_index("exp")) * per + q
     here = pl.ds(pl.multiple_of(c * CHUNK, CHUNK), CHUNK)
-    r, q = (c // per) ^ lax.axis_index("exp"), c % per
     near = pl.ds(pl.multiple_of(jnp.where(r < 2, r * per + q, 0) * CHUNK, CHUNK), CHUNK)
     far = pl.ds(pl.multiple_of(r % 2 * CHUNK, CHUNK), CHUNK)
     xc_ref, cum_ref = xc_all.at[here], cum_all.at[here]
@@ -511,13 +513,14 @@
         b_ref[:, lanes] = fade * jnp.exp(both(before_ref[0, 0:1, :])) * gate
 
 
-def run_outputs(xc, cum, cum_t, step_t, before, local_states, gates, direct, local):
+def run_outputs(xc, cum, cum_t, step_t, before, local_states, gates, direct, local, skip, count, buffers):
     total, _ = xc.shape
     width = gates[0].shape[1]
-    chunks = total // CHUNK
     per = local // CHUNK
+    args = [xc, cum, cum_t, step_t, before, local_states, direct, *gates]
+    aliases = {len(args) + k: k for k in range(len(buffers))}
     return pl.pallas_call(
-        functools.partial(output_kernel, width, per),
+        functools.partial(output_kernel, (width, per, len(gates), skip)),
         out_shape=(
             jax.ShapeDtypeStruct((total, width), F32),
             jax.ShapeDtypeStruct((total, width), F32),
@@ -525,10 +528,11 @@
         ),
         grid_spec=pltpu.PrefetchScalarGridSpec(
             num_scalar_prefetch=0,
-            grid=(chunks,),
-            in_specs=[VMEM] * (7 + len(gates)),
+            grid=(count,),
+            in_specs=[VMEM] * (len(args) + len(buffers)),
             out_specs=(VMEM,) * 3,
         ),
+        input_output_aliases=aliases,
         cost_estimate=pl.CostEstimate(
             flops=2 * total * width * 1500, transcendentals=total * width * 4, bytes_accessed=16 * total * width
         ),
@@ -536,7 +540,7 @@
             dimension_semantics=("arbitrary",), vmem_limit_bytes=12 << 20
         ),
         name="run_outputs",
-    )(xc, cum, cum_t, step_t, before, local_states, direct, *gates)
+    )(*args, *buffers)
 
 
 def pack_logs(wide):
@@ -795,9 +799,13 @@
     for k in range(2, n, 2):
         for q in range(per):
             gates.append(gate_project(far_rows[k, q][0], far_rows[k, q][1], wz, up, n))
-    a, b, c = run_outputs(
-        xc, cum, cum_t, step_t, before, states, gates, direct_head_scale[None, :], local
-    )
+    abc = ()
+    for skip, count, used in ((0, 2 * per, 1), (2 * per, (n - 2) * per, len(gates))):
+        abc = run_outputs(
+            xc, cum, cum_t, step_t, before, states, gates[:used], direct_head_scale[None, :],
+            local, skip, count, abc,
+        )
+    a, b, c = abc
     gated, mine = join(shards // 2, a, b, c, entering)
     others = []
     for k in range(1, n):

time: 98.1 us -> 102 us (1.040)
  waiting for transfers between devices: 32.9 us -> 35.4 us
  starting transfers between devices: 20.3 us -> 21.5 us
    ppermute x22, waiting for transfers between devices: 32.9 us -> 35.4 us  [swap(): lax.ppermute(block, axis, [(i, i ^ mask) for i in range(lax.axis_size(axi...]
    ppermute x22, starting transfers between devices: 18.6 us -> 19.8 us  [swap(): lax.ppermute(block, axis, [(i, i ^ mask) for i in range(lax.axis_size(axi...]
    pallas_call x1 -> x2, Pallas kernels: 5.09 us -> 5.01 us  [run_outputs(): pl.pallas_call(functools.partial(output_kernel, (width, per, len(gates),...]
  transfers between devices with their start and end apart: 23 -> 23, of which waited for: 10 -> 9; matrix products, arithmetic and copies ran while one was open for 7% -> 7% of each run, Pallas kernels for 24% -> 23%
where the time goes in v6:
time: 102 us; the launch traced here: 101 us
  waiting for transfers between devices  35.4 us (35%)
  Pallas kernels  31.9 us (31%)
  starting transfers between devices  21.5 us (21%)
  local copies, waits for them, and re-layouts  12 us (12%)
    ppermute x22, waiting for transfers between devices, swap(): lax.ppermute(block, axis, [(i, i ^ mask) for i in range(lax.axis_size(axi...  35.4 us
    ppermute x22, starting transfers between devices, swap(): lax.ppermute(block, axis, [(i, i ^ mask) for i in range(lax.axis_size(axi...  19.8 us
    unnamed x30, local copies, waits for them, and re-layouts  10.9 us
    pallas_call x4, Pallas kernels, project(): pl.pallas_call(functools.partial(project_kernel, cfg), out_shape=tuple(ou...  10.9 us
    pallas_call x4, Pallas kernels, run_states(): pl.pallas_call(functools.partial(state_kernel, (width, per, far is not No...  5.08 us
    pallas_call x2, Pallas kernels, run_outputs(): pl.pallas_call(functools.partial(output_kernel, (width, per, len(gates),...  5.01 us
    pallas_call x3, Pallas kernels, gate_project(): pl.pallas_call(functools.partial(gate_kernel, counts, devices), out_shape...  4.93 us
  transfers between devices with their start and end apart: 23, of which 9 were waited for; matrix products, arithmetic and copies ran while one was open for 7% of the time, Pallas kernels for 23%

profile of v6, /device:TPU:0, one launch (start us, length us, event | category | flops | bytes accessed | tf_op | source)
XLA Modules:
  0.0 101.3 jit_solution(10232098589419198196)
XLA Ops:
  0.0 0.5 collective-permute-start.2
  0.5 1.3 %copy-done.1 = bf16[256,2560]{1,0:T(8,128)(2,1)S(1)} copy-done((bf16[256,2560]{1,0:T(8,128)(2,1)S(1)}, bf16[256,2560]{1,0:T(8,128)(2,1)}, u32[]{:S(2)}) %copy-start.1) | copy-done | bytes 1310744
  1.8 0.7 copy-done.10
  2.5 1.1 %pack.1 = (bf16[128,2560]{1,0:T(8,128)(2,1)}, bf16[8,2560]{1,0:T(8,128)(2,1)S(1)}) custom-call(bf16[256,2560]{1,0:T(8,128)(2,1)S(1)} %copy-done.1, s32[1,256]{1,0:T(1,128)S(1)} %bitcast.41), custom_call_target="tpu_custom_call" | custom-call | tf_op jit(solution)/shard_map/pack/pallas_call | solution.py:96
  3.6 2.6 %collective-permute-start.9 = (bf16[128,2560]{1,0:T(8,128)(2,1)}, bf16[128,2560]{1,0:T(8,128)(2,1)S(1)}, u32[]{:S(2)}, u32[]{:S(2)}) collective-permute-start(bf16[128,2560]{1,0:T(8,128)(2,1)} %get-tuple-element.96), channel_id=1, source_target_pairs={{0,2},{1,3},{2,0},{3,1},{4,6},{5,7},{6,4},{7,5},{8,10},{9,11},{10,... | collective-permute-start | bytes 1966088 | tf_op jit(solution)/shard_map/ppermute | solution.py:21
  6.2 4.7 %copy.37 = bf16[320,8,2,768]{3,1,2,0:T(8,128)(2,1)S(1)} copy(bf16[320,8,2,768]{3,2,1,0:T(2,128)(2,1)} %bitcast.44) | data formatting | bytes 15728640
  10.9 1.1 %slice.3 = bf16[128,2560]{1,0:T(8,128)(2,1)S(1)} slice(bf16[256,2560]{1,0:T(8,128)(2,1)} %refs_0_.1), slice={[128:256], [0:2560]} | slice | bytes 1310720 | tf_op jit(solution)/shard_map/slice | solution.py:739
  12.1 2.0 %collective-permute-start.7 = (bf16[32,2560]{1,0:T(8,128)(2,1)}, bf16[32,2560]{1,0:T(8,128)(2,1)S(1)}, u32[]{:S(2)}, u32[]{:S(2)}) collective-permute-start(bf16[32,2560]{1,0:T(8,128)(2,1)} %bitcast.25), channel_id=1, source_target_pairs={{0,2},{1,3},{2,0},{3,1},{4,6},{5,7},{6,4},{7,5},{8,10},{9,11},{10,... | collective-permute-start | bytes 491528 | tf_op jit(solution)/shard_map/ppermute | solution.py:21
  14.2 7.8 %collective-permute-done.9.refs_0_ = bf16[128,2560]{1,0:T(8,128)(2,1)S(1)} collective-permute-done((bf16[128,2560]{1,0:T(8,128)(2,1)}, bf16[128,2560]{1,0:T(8,128)(2,1)S(1)}, u32[]{:S(2)}, u32[]{:S(2)}) %collective-permute-start.9) | collective-permute-done | bytes 655392 | tf_op jit(solution)/shard_map/ppermute | solution.py:21
  22.0 18.2 %collective-permute-done.4.refs_4_ = bf16[8,2560]{1,0:T(8,128)(2,1)S(1)} collective-permute-done((bf16[8,2560]{1,0:T(8,128)(2,1)S(1)}, bf16[8,2560]{1,0:T(8,128)(2,1)S(1)}, u32[]{:S(2)}, u32[]{:S(2)}) %collective-permute-start.4) | collective-permute-done | bytes 40992 | tf_op jit(solution)/shard_map/ppermute | solution.py:21
  40.2 1.2 %collective-permute-done.3.refs_3_ = bf16[8,2560]{1,0:T(8,128)(2,1)S(1)} collective-permute-done((bf16[8,2560]{1,0:T(8,128)(2,1)S(1)}, bf16[8,2560]{1,0:T(8,128)(2,1)S(1)}, u32[]{:S(2)}, u32[]{:S(2)}) %collective-permute-start.3) | collective-permute-done | bytes 40992 | tf_op jit(solution)/shard_map/ppermute | solution.py:21
  41.6 1.1 %collective-permute-done.5.refs_5_ = bf16[8,2560]{1,0:T(8,128)(2,1)S(1)} collective-permute-done((bf16[8,2560]{1,0:T(8,128)(2,1)S(1)}, bf16[8,2560]{1,0:T(8,128)(2,1)S(1)}, u32[]{:S(2)}, u32[]{:S(2)}) %collective-permute-start.5) | collective-permute-done | bytes 40992 | tf_op jit(solution)/shard_map/ppermute | solution.py:21
  43.2 1.0 %copy.38 = bf16[16,8,2,768]{3,1,2,0:T(8,128)(2,1)S(1)} copy(bf16[16,8,2,768]{3,2,1,0:T(2,128)(2,1)} %bitcast.45) | data formatting | bytes 786432
  44.5 1.3 %copy-done.2 = bf16[256,2560]{1,0:T(8,128)(2,1)S(1)} copy-done((bf16[256,2560]{1,0:T(8,128)(2,1)S(1)}, bf16[256,2560]{1,0:T(8,128)(2,1)}, u32[]{:S(2)}) %copy-start.2) | copy-done | bytes 1310744
  45.8 0.9 copy-done.4
  46.8 0.9 copy-done.5
  47.7 5.8 %project.4 = (f32[512,1024]{1,0:T(8,128)S(1)}, f32[512,128]{1,0:T(8,128)S(1)}, f32[4,16,128]{2,1,0:T(8,128)S(1)}, f32[4,16,128]{2,1,0:T(8,128)S(1)}, bf16[512,12...) custom-call(bf16[256,2560]{1,0:T(8,128)(2,1)S(1)} %copy-done.2, ...), custom_call_target="tpu_custom_call" | custom-call | flops 3355443200 | bytes 9961472 | tf_op jit(solution)/shard_map/project/pallas_call | solution.py:245
  53.5 1.8 %collective-permute-start.11 = (f32[8,1024]{1,0:T(8,128)S(1)}, f32[8,1024]{1,0:T(8,128)S(1)}, u32[]{:S(2)}, u32[]{:S(2)}) collective-permute-start(f32[8,1024]{1,0:T(8,128)S(1)} %get-tuple-element.99), channel_id=1, source_target_pairs={{0,4},{4,8},{8,12},{12,16},{16,20},{20,24},{24,28},{28,0},{1,5},{5... | collective-permute-start | bytes 98312 | tf_op jit(solution)/shard_map/ppermute | solution.py:757
  55.2 1.4 %project.7 = (f32[128,1024]{1,0:T(8,128)S(1)}, f32[128,128]{1,0:T(8,128)S(1)}, f32[1,16,128]{2,1,0:T(8,128)S(1)}, f32[1,16,128]{2,1,0:T(8,128)S(1)}, bf16[128,12...) custom-call(bf16[128,2560]{1,0:T(8,128)(2,1)S(1)} %collective-permute-done.refs_0_, ...), custom_call_target="tpu_custom_call" | custom-call | flops 838860800 | bytes 6422528 | tf_op jit(solution)/shard_map/project/pallas_call | solution.py:245
  56.6 2.3 %project.6 = (f32[256,1024]{1,0:T(8,128)S(1)}, f32[256,128]{1,0:T(8,128)S(1)}, f32[2,16,128]{2,1,0:T(8,128)S(1)}, f32[2,16,128]{2,1,0:T(8,128)S(1)}, bf16[256,12...) custom-call(bf16[128,2560]{1,0:T(8,128)(2,1)S(1)} %collective-permute-done.9.refs_0_, ...), custom_call_target="tpu_custom_call" | custom-call | flops 1677721600 | bytes 7602176 | tf_op jit(solution)/shard_map/project/pallas_call | solution.py:245
  58.9 1.3 %gate_project.4.refs_1_ = f32[256,768]{1,0:T(8,128)S(1)} custom-call(bf16[256,2560]{1,0:T(8,128)(2,1)S(1)} %get-tuple-element.139.refs_0_, bf16[256,128]{1,0:T(8,128)(2,1)S(1)} %get-tuple-element.140.refs_1_, bf16[2560,1536]{1,0:T(8,128)(2,1)S(1)} %bitcast.14, bf16[128,1536]{1,0:T(8,128)(2,1)S(1)} %bitcast.21), custom_call_target="tpu_custom_call" | custom-call | flops 1006632960 | bytes 6029312 | tf_op jit(solution)/shard_map/gate_project/pallas_call | solution.py:287
  60.2 2.4 %gate_project.3.refs_0_ = f32[512,768]{1,0:T(8,128)S(1)} custom-call(bf16[544,2560]{1,0:T(8,128)(2,1)S(1)} %get-tuple-element.137.refs_0_, bf16[512,128]{1,0:T(8,128)(2,1)S(1)} %get-tuple-element.138.refs_1_, bf16[2560,1536]{1,0:T(8,128)(2,1)S(1)} %bitcast.15, bf16[128,1536]{1,0:T(8,128)(2,1)S(1)} %bitcast.22), custom_call_target="tpu_custom_call" | custom-call | flops 2013265920 | bytes 8126464 | tf_op jit(solution)/shard_map/gate_project/pallas_call | solution.py:287
  62.7 1.4 %project.5 = (f32[128,1024]{1,0:T(8,128)S(1)}, f32[128,128]{1,0:T(8,128)S(1)}, f32[1,16,128]{2,1,0:T(8,128)S(1)}, f32[1,16,128]{2,1,0:T(8,128)S(1)}, bf16[128,12...) custom-call(bf16[128,2560]{1,0:T(8,128)(2,1)S(1)} %collective-permute-done.1.refs_0_, ...), custom_call_target="tpu_custom_call" | custom-call | flops 838860800 | bytes 6422528 | tf_op jit(solution)/shard_map/project/pallas_call | solution.py:245
  64.1 2.7 %run_states.4 = (f32[1024,1024]{1,0:T(8,128)S(1)}, f32[1024,128]{1,0:T(8,128)S(1)}, f32[8,16,128]{2,1,0:T(8,128)S(1)}, f32[8,16,128]{2,1,0:T(8,128)S(1)}, f32[8,...) custom-call(f32[512,1024]{1,0:T(8,128)S(1)} %get-tuple-element.107.z_all.older_all, ...), custom_call_target="tpu_custom_call" | custom-call | flops 786432000 | bytes 6291456 | tf_op jit(solution)/shard_map/run_states/pallas_call | solution.py:382
  66.7 1.2 %run_states.5 = (f32[1024,1024]{1,0:T(8,128)S(1)}, f32[1024,128]{1,0:T(8,128)S(1)}, f32[8,16,128]{2,1,0:T(8,128)S(1)}, f32[8,16,128]{2,1,0:T(8,128)S(1)}, f32[8,...) custom-call(f32[256,1024]{1,0:T(8,128)S(1)} %get-tuple-element.97.z_, ...), custom_call_target="tpu_custom_call", output_to_operand_aliasing={{0}: (11, {}), {1}: (12, {}), {2}: (13, {}), {3}: (14, {}),... | custom-call | flops 393216000 | bytes 3145728 | tf_op jit(solution)/shard_map/run_states/pallas_call | solution.py:382
  68.0 0.6 run_states.6
  68.6 0.6 run_states.7
  69.2 0.5 stitch.1
  69.7 2.6 %collective-permute-start.18 = (bf16[136,256]{1,0:T(8,128)(2,1)S(1)}, bf16[136,256]{1,0:T(8,128)(2,1)S(1)}, u32[]{:S(2)}, u32[]{:S(2)}) collective-permute-start(bf16[136,256]{1,0:T(8,128)(2,1)S(1)} %get-tuple-element.159), channel_id=1, source_target_pairs={{0,12},{4,8},{8,4},{12,0},{16,28},{20,24},{24,20},{28,16},{1,13},{... | collective-permute-start | bytes 208904 | tf_op jit(solution)/shard_map/ppermute | solution.py:21
  72.3 1.3 %gate_project.5.refs_2_ = f32[256,768]{1,0:T(8,128)S(1)} custom-call(bf16[128,2560]{1,0:T(8,128)(2,1)S(1)} %get-tuple-element.141.refs_0_, bf16[128,2560]{1,0:T(8,128)(2,1)S(1)} %get-tuple-element.142.refs_1_, bf16[128,128]{1,0:T(8,128)(2,1)S(1)} %get-tuple-element.143.refs_2_, bf16[128,128]{1,0:T(8,128)(2,1)S(1)} %get-tuple-element.144.refs_3_, ...), custom_call_target="tpu_custom_call" | custom-call | flops 1006632960 | bytes 6029312 | tf_op jit(solution)/shard_map/gate_project/pallas_call | solution.py:287
  73.6 0.5 collective-permute-start.17
  74.1 0.5 collective-permute-start.16
  74.6 2.6 %collective-permute-start.14 = (bf16[136,512]{1,0:T(8,128)(2,1)S(1)}, bf16[136,512]{1,0:T(8,128)(2,1)S(1)}, u32[]{:S(2)}, u32[]{:S(2)}) collective-permute-start(bf16[136,512]{1,0:T(8,128)(2,1)S(1)} %get-tuple-element.151), channel_id=1, source_target_pairs={{0,12},{4,8},{8,4},{12,0},{16,28},{20,24},{24,20},{28,16},{1,13},{... | collective-permute-start | bytes 417800 | tf_op jit(solution)/shard_map/ppermute | solution.py:21
  77.6 0.5 collective-permute-start.12
  78.1 2.4 %run_outputs.2 = (f32[1024,768]{1,0:T(8,128)S(1)}, f32[1024,768]{1,0:T(8,128)S(1)}, bf16[1024,128]{1,0:T(8,128)(2,1)S(1)}) custom-call(f32[1024,1024]{1,0:T(8,128)S(1)} %get-tuple-element.129.xc_all, f32[1024,128]{1,0:T(8,128)S(1)} %get-tuple-element.130.cum_all, f32[8,16,128]{2,1,0:T(8,128)S(1)} %get-tuple-element.131.cum_t_all, ...), custom_call_target="tpu_custom_call" | custom-call | flops 2359296000 | bytes 12582912 | tf_op jit(solution)/shard_map/run_outputs/pallas_call | solution.py:522
  80.8 0.8 combine.3
  81.6 2.6 %collective-permute-start.19 = (bf16[136,256]{1,0:T(8,128)(2,1)S(1)}, bf16[136,256]{1,0:T(8,128)(2,1)S(1)}, u32[]{:S(2)}, u32[]{:S(2)}) collective-permute-start(bf16[136,256]{1,0:T(8,128)(2,1)S(1)} %get-tuple-element.164), channel_id=1, source_target_pairs={{0,16},{4,20},{8,24},{12,28},{16,0},{20,4},{24,8},{28,12},{1,17},{... | collective-permute-start | bytes 208904 | tf_op jit(solution)/shard_map/ppermute | solution.py:21
  84.2 0.5 collective-permute-done.13.refs_1_
  84.8 1.0 combine.2
  85.7 2.1 %collective-permute-start.15 = (bf16[136,512]{1,0:T(8,128)(2,1)S(1)}, bf16[136,512]{1,0:T(8,128)(2,1)S(1)}, u32[]{:S(2)}, u32[]{:S(2)}) collective-permute-start(bf16[136,512]{1,0:T(8,128)(2,1)S(1)} %get-tuple-element.156), channel_id=1, source_target_pairs={{0,16},{4,20},{8,24},{12,28},{16,0},{20,4},{24,8},{28,12},{1,17},{... | collective-permute-start | bytes 417800 | tf_op jit(solution)/shard_map/ppermute | solution.py:21
  87.8 2.6 %run_outputs.3 = (f32[1024,768]{1,0:T(8,128)S(1)}, f32[1024,768]{1,0:T(8,128)S(1)}, bf16[1024,128]{1,0:T(8,128)(2,1)S(1)}) custom-call(f32[1024,1024]{1,0:T(8,128)S(1)} %get-tuple-element.129.xc_all, f32[1024,128]{1,0:T(8,128)S(1)} %get-tuple-element.130.cum_all, ...), custom_call_target="tpu_custom_call", output_to_operand_aliasing={{0}: (10, {}), {1}: (11, {}), {2}: (12, {})} | custom-call | flops 2359296000 | bytes 12582912 | tf_op jit(solution)/shard_map/run_outputs/pallas_call | solution.py:522
  90.4 3.9 %collective-permute-done.15.refs_0_ = bf16[136,512]{1,0:T(8,128)(2,1)S(1)} collective-permute-done((bf16[136,512]{1,0:T(8,128)(2,1)S(1)}, bf16[136,512]{1,0:T(8,128)(2,1)S(1)}, u32[]{:S(2)}, u32[]{:S(2)}) %collective-permute-start.15) | collective-permute-done | bytes 139296 | tf_op jit(solution)/shard_map/ppermute | solution.py:21
  94.3 1.3 %join.1 = (f32[1024,768]{1,0:T(8,128)S(1)}, f32[1,1024]{1,0:T(1,128)S(1)}) custom-call(f32[1024,768]{1,0:T(8,128)S(1)} %get-tuple-element.148.a_ref, f32[1024,768]{1,0:T(8,128)S(1)} %get-tuple-element.149.b_ref, bf16[1024,128]{1,0:T(8,128)(2,1)S(1)} %get-tuple-element.150.c_ref, bf16[136,512]{1,0:T(8,128)(2,1)S(1)} %collective-permute-done.15.refs_0_, ...), custom_call_target="tpu_custom_call" | custom-call | tf_op jit(solution)/shard_map/join/pallas_call | solution.py:641
  95.6 0.6 collective-permute-start.22
  96.2 1.0 collective-permute-start.21
  97.5 1.2 %collective-permute-done.22.refs_3_ = f32[1,1024]{1,0:T(1,128)S(1)} collective-permute-done((f32[1,1024]{1,0:T(1,128)S(1)}, f32[1,1024]{1,0:T(1,128)S(1)}, u32[]{:S(2)}, u32[]{:S(2)}) %collective-permute-start.22) | collective-permute-done | bytes 4128 | tf_op jit(solution)/shard_map/ppermute | solution.py:21
  98.7 1.1 %collective-permute-done.21.refs_2_ = f32[1,1024]{1,0:T(1,128)S(1)} collective-permute-done((f32[1,1024]{1,0:T(1,128)S(1)}, f32[1,1024]{1,0:T(1,128)S(1)}, u32[]{:S(2)}, u32[]{:S(2)}) %collective-permute-start.21) | collective-permute-done | bytes 4128 | tf_op jit(solution)/shard_map/ppermute | solution.py:21
  99.8 1.4 %norm.1 = bf16[1024,768]{1,0:T(8,128)(2,1)} custom-call(f32[1024,768]{1,0:T(8,128)S(1)} %get-tuple-element.167.g_ref, f32[1,768]{1,0:T(1,128)S(1)} %broadcast_in_dim.24.gain_ref, f32[1,1024]{1,0:T(1,128)S(1)} %get-tuple-element.168.refs_0_, f32[1,1024]{1,0:T(1,128)S(1)} %collective-permute-done.20.refs_1_, f32[1,1024]{1,0:T(1,128)S(1)} %collective-permute-done.21.refs_2_, ...), custom_call_target="tpu_custom_call" | custom-call | tf_op jit(solution)/shard_map/norm/pallas_call | solution.py:678
  (50 shorter events, 2.3 us)
Async XLA Ops:
  0.0 44.5 %collective-permute-start.2 = (bf16[256,2560]{1,0:T(8,128)(2,1)}, bf16[256,2560]{1,0:T(8,128)(2,1)}, u32[]{:S(2)}, u32[]{:S(2)}) collective-permute-start(bf16[256,2560]{1,0:T(8,128)(2,1)} %refs_0_.1), channel_id=1, source_target_pairs={{0,1},{1,0},{2,3},{3,2},{4,5},{5,4},{6,7},{7,6},{8,9},{9,8},{10,11... | collective-permute-start | bytes 3932168 | tf_op jit(solution)/shard_map/ppermute | solution.py:21
  0.5 1.3 %copy-start.1 = (bf16[256,2560]{1,0:T(8,128)(2,1)S(1)}, bf16[256,2560]{1,0:T(8,128)(2,1)}, u32[]{:S(2)}) copy-start(bf16[256,2560]{1,0:T(8,128)(2,1)} %refs_0_.1) | copy-start | bytes 3932164
  1.8 0.7 copy-start.10
  3.6 18.4 %collective-permute-start.9 = (bf16[128,2560]{1,0:T(8,128)(2,1)}, bf16[128,2560]{1,0:T(8,128)(2,1)S(1)}, u32[]{:S(2)}, u32[]{:S(2)}) collective-permute-start(bf16[128,2560]{1,0:T(8,128)(2,1)} %get-tuple-element.96), channel_id=1, source_target_pairs={{0,2},{1,3},{2,0},{3,1},{4,6},{5,7},{6,4},{7,5},{8,10},{9,11},{10,... | collective-permute-start | bytes 1966088 | tf_op jit(solution)/shard_map/ppermute | solution.py:21
  6.2 37.0 %copy-start.12 = (f32[768]{0:T(1024)S(1)}, f32[768]{0:T(1024)}, u32[]{:S(2)}) copy-start(f32[768]{0:T(1024)} %param.24) | copy-start | bytes 9220
  6.2 38.3 %copy-start = (bf16[2560,256]{1,0:T(8,128)(2,1)S(1)}, bf16[2560,256]{1,0:T(8,128)(2,1)}, u32[]{:S(2)}) copy-start(bf16[2560,256]{1,0:T(8,128)(2,1)} %refs_3_.3) | copy-start | bytes 3932164
  6.2 38.3 %copy-start.8 = (f32[12]{0:T(128)S(1)}, f32[12]{0:T(128)}, u32[]{:S(2)}) copy-start(f32[12]{0:T(128)} %param.26) | copy-start | bytes 148
  6.2 38.3 %copy-start.9 = (f32[12]{0:T(128)S(1)}, f32[12]{0:T(128)}, u32[]{:S(2)}) copy-start(f32[12]{0:T(128)} %param.27) | copy-start | bytes 148
  12.0 32.2 %collective-permute-start = (bf16[128,2560]{1,0:T(8,128)(2,1)S(1)}, bf16[128,2560]{1,0:T(8,128)(2,1)S(1)}, u32[]{:S(2)}, u32[]{:S(2)}) collective-permute-start(bf16[128,2560]{1,0:T(8,128)(2,1)S(1)} %slice.3), channel_id=1, source_target_pairs={{0,2},{1,3},{2,0},{3,1},{4,6},{5,7},{6,4},{7,5},{8,10},{9,11},{10,... | collective-permute-start | bytes 1966088 | tf_op jit(solution)/shard_map/ppermute | solution.py:21
  12.1 30.7 %collective-permute-start.7 = (bf16[32,2560]{1,0:T(8,128)(2,1)}, bf16[32,2560]{1,0:T(8,128)(2,1)S(1)}, u32[]{:S(2)}, u32[]{:S(2)}) collective-permute-start(bf16[32,2560]{1,0:T(8,128)(2,1)} %bitcast.25), channel_id=1, source_target_pairs={{0,2},{1,3},{2,0},{3,1},{4,6},{5,7},{6,4},{7,5},{8,10},{9,11},{10,... | collective-permute-start | bytes 491528 | tf_op jit(solution)/shard_map/ppermute | solution.py:21
  14.1 26.1 %collective-permute-start.4 = (bf16[8,2560]{1,0:T(8,128)(2,1)S(1)}, bf16[8,2560]{1,0:T(8,128)(2,1)S(1)}, u32[]{:S(2)}, u32[]{:S(2)}) collective-permute-start(bf16[8,2560]{1,0:T(8,128)(2,1)S(1)} %get-tuple-element.88.refs_2_), channel_id=1, source_target_pairs={{0,2},{1,3},{2,0},{3,1},{4,6},{5,7},{6,4},{7,5},{8,10},{9,11},{10,... | collective-permute-start | bytes 122888 | tf_op jit(solution)/shard_map/ppermute | solution.py:21
  22.0 34.6 %collective-permute-start.10 = (bf16[128,2560]{1,0:T(8,128)(2,1)S(1)}, bf16[128,2560]{1,0:T(8,128)(2,1)S(1)}, u32[]{:S(2)}, u32[]{:S(2)}) collective-permute-start(bf16[128,2560]{1,0:T(8,128)(2,1)S(1)} %collective-permute-done.9.refs_0_), channel_id=1, source_target_pairs={{0,1},{1,0},{2,3},{3,2},{4,5},{5,4},{6,7},{7,6},{8,9},{9,8},{10,11... | collective-permute-start | bytes 1966088 | tf_op jit(solution)/shard_map/ppermute | solution.py:21
  40.2 1.2 %collective-permute-start.3 = (bf16[8,2560]{1,0:T(8,128)(2,1)S(1)}, bf16[8,2560]{1,0:T(8,128)(2,1)S(1)}, u32[]{:S(2)}, u32[]{:S(2)}) collective-permute-start(bf16[8,2560]{1,0:T(8,128)(2,1)S(1)} %get-tuple-element.88.refs_2_), channel_id=1, source_target_pairs={{0,1},{1,0},{2,3},{3,2},{4,5},{5,4},{6,7},{7,6},{8,9},{9,8},{10,11... | collective-permute-start | bytes 122888 | tf_op jit(solution)/shard_map/ppermute | solution.py:21
  41.4 1.2 %collective-permute-start.5 = (bf16[8,2560]{1,0:T(8,128)(2,1)S(1)}, bf16[8,2560]{1,0:T(8,128)(2,1)S(1)}, u32[]{:S(2)}, u32[]{:S(2)}) collective-permute-start(bf16[8,2560]{1,0:T(8,128)(2,1)S(1)} %collective-permute-done.4.refs_4_), channel_id=1, source_target_pairs={{0,1},{1,0},{2,3},{3,2},{4,5},{5,4},{6,7},{7,6},{8,9},{9,8},{10,11... | collective-permute-start | bytes 122888 | tf_op jit(solution)/shard_map/ppermute | solution.py:21
  42.7 1.8 %collective-permute-start.6 = (bf16[32,2560]{1,0:T(8,128)(2,1)}, bf16[32,2560]{1,0:T(8,128)(2,1)S(1)}, u32[]{:S(2)}, u32[]{:S(2)}) collective-permute-start(bf16[32,2560]{1,0:T(8,128)(2,1)} %bitcast.26), channel_id=1, source_target_pairs={{0,1},{1,0},{2,3},{3,2},{4,5},{5,4},{6,7},{7,6},{8,9},{9,8},{10,11... | collective-permute-start | bytes 491528 | tf_op jit(solution)/shard_map/ppermute | solution.py:21
  42.8 1.7 %collective-permute-start.8 = (bf16[32,2560]{1,0:T(8,128)(2,1)S(1)}, bf16[32,2560]{1,0:T(8,128)(2,1)S(1)}, u32[]{:S(2)}, u32[]{:S(2)}) collective-permute-start(bf16[32,2560]{1,0:T(8,128)(2,1)S(1)} %collective-permute-done.7.refs_14_), channel_id=1, source_target_pairs={{0,1},{1,0},{2,3},{3,2},{4,5},{5,4},{6,7},{7,6},{8,9},{9,8},{10,11... | collective-permute-start | bytes 491528 | tf_op jit(solution)/shard_map/ppermute | solution.py:21
  44.2 18.4 %collective-permute-start.1 = (bf16[128,2560]{1,0:T(8,128)(2,1)S(1)}, bf16[128,2560]{1,0:T(8,128)(2,1)S(1)}, u32[]{:S(2)}, u32[]{:S(2)}) collective-permute-start(bf16[128,2560]{1,0:T(8,128)(2,1)S(1)} %collective-permute-done.refs_0_), channel_id=1, source_target_pairs={{0,1},{1,0},{2,3},{3,2},{4,5},{5,4},{6,7},{7,6},{8,9},{9,8},{10,11... | collective-permute-start | bytes 1966088 | tf_op jit(solution)/shard_map/ppermute | solution.py:21
  44.5 1.3 %copy-start.2 = (bf16[256,2560]{1,0:T(8,128)(2,1)S(1)}, bf16[256,2560]{1,0:T(8,128)(2,1)}, u32[]{:S(2)}) copy-start(bf16[256,2560]{1,0:T(8,128)(2,1)} %refs_0_.1) | copy-start | bytes 3932164
  45.8 0.9 copy-start.4
  46.8 0.9 copy-start.5
  53.5 10.6 %collective-permute-start.11 = (f32[8,1024]{1,0:T(8,128)S(1)}, f32[8,1024]{1,0:T(8,128)S(1)}, u32[]{:S(2)}, u32[]{:S(2)}) collective-permute-start(f32[8,1024]{1,0:T(8,128)S(1)} %get-tuple-element.99), channel_id=1, source_target_pairs={{0,4},{4,8},{8,12},{12,16},{16,20},{20,24},{24,28},{28,0},{1,5},{5... | collective-permute-start | bytes 98312 | tf_op jit(solution)/shard_map/ppermute | solution.py:757
  62.6 1.4 %copy-start.3 = (f32[4,768]{1,0:T(4,128)S(1)}, f32[4,768]{1,0:T(4,128)}, u32[]{:S(2)}) copy-start(f32[4,768]{1,0:T(4,128)} %taps_ref.7) | copy-start | bytes 36868
  62.6 1.4 %copy-start.6 = (f32[4,256]{1,0:T(4,128)S(1)}, f32[4,256]{1,0:T(4,128)}, u32[]{:S(2)}) copy-start(f32[4,256]{1,0:T(4,128)} %mtaps_ref.7) | copy-start | bytes 12292
  62.6 1.4 %copy-start.7 = (f32[256]{0:T(256)S(1)}, f32[256]{0:T(256)}, u32[]{:S(2)}) copy-start(f32[256]{0:T(256)} %param.25) | copy-start | bytes 3076
  69.7 7.9 %collective-permute-start.18 = (bf16[136,256]{1,0:T(8,128)(2,1)S(1)}, bf16[136,256]{1,0:T(8,128)(2,1)S(1)}, u32[]{:S(2)}, u32[]{:S(2)}) collective-permute-start(bf16[136,256]{1,0:T(8,128)(2,1)S(1)} %get-tuple-element.159), channel_id=1, source_target_pairs={{0,12},{4,8},{8,4},{12,0},{16,28},{20,24},{24,20},{28,16},{1,13},{... | collective-permute-start | bytes 208904 | tf_op jit(solution)/shard_map/ppermute | solution.py:21
  72.3 5.8 %copy-start.11 = (f32[12]{0:T(128)S(1)}, f32[12]{0:T(128)}, u32[]{:S(2)}) copy-start(f32[12]{0:T(128)} %param.28) | copy-start | bytes 148
  73.6 6.9 %collective-permute-start.17 = (bf16[136,256]{1,0:T(8,128)(2,1)S(1)}, bf16[136,256]{1,0:T(8,128)(2,1)S(1)}, u32[]{:S(2)}, u32[]{:S(2)}) collective-permute-start(bf16[136,256]{1,0:T(8,128)(2,1)S(1)} %get-tuple-element.159), channel_id=1, source_target_pairs={{0,8},{4,12},{8,0},{12,4},{16,24},{20,28},{24,16},{28,20},{1,9},{5... | collective-permute-start | bytes 208904 | tf_op jit(solution)/shard_map/ppermute | solution.py:21
  74.1 6.7 %collective-permute-start.16 = (bf16[136,256]{1,0:T(8,128)(2,1)S(1)}, bf16[136,256]{1,0:T(8,128)(2,1)S(1)}, u32[]{:S(2)}, u32[]{:S(2)}) collective-permute-start(bf16[136,256]{1,0:T(8,128)(2,1)S(1)} %get-tuple-element.159), channel_id=1, source_target_pairs={{0,4},{4,0},{8,12},{12,8},{16,20},{20,16},{24,28},{28,24},{1,5},{5... | collective-permute-start | bytes 208904 | tf_op jit(solution)/shard_map/ppermute | solution.py:21
  74.6 9.6 %collective-permute-start.14 = (bf16[136,512]{1,0:T(8,128)(2,1)S(1)}, bf16[136,512]{1,0:T(8,128)(2,1)S(1)}, u32[]{:S(2)}, u32[]{:S(2)}) collective-permute-start(bf16[136,512]{1,0:T(8,128)(2,1)S(1)} %get-tuple-element.151), channel_id=1, source_target_pairs={{0,12},{4,8},{8,4},{12,0},{16,28},{20,24},{24,20},{28,16},{1,13},{... | collective-permute-start | bytes 417800 | tf_op jit(solution)/shard_map/ppermute | solution.py:21
  77.2 7.6 %collective-permute-start.13 = (bf16[136,512]{1,0:T(8,128)(2,1)S(1)}, bf16[136,512]{1,0:T(8,128)(2,1)S(1)}, u32[]{:S(2)}, u32[]{:S(2)}) collective-permute-start(bf16[136,512]{1,0:T(8,128)(2,1)S(1)} %get-tuple-element.151), channel_id=1, source_target_pairs={{0,8},{4,12},{8,0},{12,4},{16,24},{20,28},{24,16},{28,20},{1,9},{5... | collective-permute-start | bytes 417800 | tf_op jit(solution)/shard_map/ppermute | solution.py:21
  77.6 7.1 %collective-permute-start.12 = (bf16[136,512]{1,0:T(8,128)(2,1)S(1)}, bf16[136,512]{1,0:T(8,128)(2,1)S(1)}, u32[]{:S(2)}, u32[]{:S(2)}) collective-permute-start(bf16[136,512]{1,0:T(8,128)(2,1)S(1)} %get-tuple-element.151), channel_id=1, source_target_pairs={{0,4},{4,0},{8,12},{12,8},{16,20},{20,16},{24,28},{28,24},{1,5},{5... | collective-permute-start | bytes 417800 | tf_op jit(solution)/shard_map/ppermute | solution.py:21
  81.6 8.8 %collective-permute-start.19 = (bf16[136,256]{1,0:T(8,128)(2,1)S(1)}, bf16[136,256]{1,0:T(8,128)(2,1)S(1)}, u32[]{:S(2)}, u32[]{:S(2)}) collective-permute-start(bf16[136,256]{1,0:T(8,128)(2,1)S(1)} %get-tuple-element.164), channel_id=1, source_target_pairs={{0,16},{4,20},{8,24},{12,28},{16,0},{20,4},{24,8},{28,12},{1,17},{... | collective-permute-start | bytes 208904 | tf_op jit(solution)/shard_map/ppermute | solution.py:21
  85.7 8.6 %collective-permute-start.15 = (bf16[136,512]{1,0:T(8,128)(2,1)S(1)}, bf16[136,512]{1,0:T(8,128)(2,1)S(1)}, u32[]{:S(2)}, u32[]{:S(2)}) collective-permute-start(bf16[136,512]{1,0:T(8,128)(2,1)S(1)} %get-tuple-element.156), channel_id=1, source_target_pairs={{0,16},{4,20},{8,24},{12,28},{16,0},{20,4},{24,8},{28,12},{1,17},{... | collective-permute-start | bytes 417800 | tf_op jit(solution)/shard_map/ppermute | solution.py:21
  94.3 3.2 %copy-start.13 = (f32[768]{0:T(1024)S(1)}, f32[768]{0:T(1024)}, u32[]{:S(2)}) copy-start(f32[768]{0:T(1024)} %param.29) | copy-start | bytes 9220
  95.6 3.0 %collective-permute-start.22 = (f32[1,1024]{1,0:T(1,128)S(1)}, f32[1,1024]{1,0:T(1,128)S(1)}, u32[]{:S(2)}, u32[]{:S(2)}) collective-permute-start(f32[1,1024]{1,0:T(1,128)S(1)} %get-tuple-element.168.refs_0_), channel_id=1, source_target_pairs={{0,3},{1,2},{2,1},{3,0},{4,7},{5,6},{6,5},{7,4},{8,11},{9,10},{10,... | collective-permute-start | bytes 12296 | tf_op jit(solution)/shard_map/ppermute | solution.py:21
  96.2 3.6 %collective-permute-start.21 = (f32[1,1024]{1,0:T(1,128)S(1)}, f32[1,1024]{1,0:T(1,128)S(1)}, u32[]{:S(2)}, u32[]{:S(2)}) collective-permute-start(f32[1,1024]{1,0:T(1,128)S(1)} %get-tuple-element.168.refs_0_), channel_id=1, source_target_pairs={{0,2},{1,3},{2,0},{3,1},{4,6},{5,7},{6,4},{7,5},{8,10},{9,11},{10,... | collective-permute-start | bytes 12296 | tf_op jit(solution)/shard_map/ppermute | solution.py:21
  97.2 2.6 %collective-permute-start.20 = (f32[1,1024]{1,0:T(1,128)S(1)}, f32[1,1024]{1,0:T(1,128)S(1)}, u32[]{:S(2)}, u32[]{:S(2)}) collective-permute-start(f32[1,1024]{1,0:T(1,128)S(1)} %get-tuple-element.168.refs_0_), channel_id=1, source_target_pairs={{0,1},{1,0},{2,3},{3,2},{4,5},{5,4},{6,7},{7,6},{8,9},{9,8},{10,11... | collective-permute-start | bytes 12296 | tf_op jit(solution)/shard_map/ppermute | solution.py:21
